TPU v7x, 32 devices: a whole 2x2x4 slice. The times are simulated.
32 devices in a mesh: grp: 4 (over x, core), fsdp: 8 (over z, y).
Axes of the slice: x: 2, y: 2, z: 4, core: 2. Of those that a mesh axis runs over, the one named last changes fastest.
Arguments:
- hidden_in: bfloat16 [8192, 2048], P(('grp', 'fsdp')), may hold values from -6 to 6
- query_weight: bfloat16 [2048, 2048], P(('grp', 'fsdp')), may hold values from -0.125 to 0.125
- key_matrix: bfloat16 [2048, 1024], P(('grp', 'fsdp')), may hold values from -0.125 to 0.125
- value_matrix: bfloat16 [2048, 1024], P(('grp', 'fsdp')), may hold values from -0.125 to 0.125
- gate_weight: bfloat16 [2048, 2048], P(('grp', 'fsdp')), may hold values from -0.125 to 0.125
- out_weight: bfloat16 [2048, 2048], P(('grp', 'fsdp')), may hold values from -2 to 2
- norm_attn: bfloat16 [2048], P(('grp', 'fsdp')), may hold values from 0.25 to 1.75
- query_gain: bfloat16 [128], P(('grp', 'fsdp')), may hold values from 0.25 to 1.75
- key_gain: bfloat16 [128], P(('grp', 'fsdp')), may hold values from 0.25 to 1.75
- norm_ffn: bfloat16 [2048], P(('grp', 'fsdp')), may hold values from 0.25 to 1.75
- ffn_gate: bfloat16 [2048, 6144], P(('grp', 'fsdp')), may hold values from -0.125 to 0.125
- ffn_up: bfloat16 [2048, 6144], P(('grp', 'fsdp')), may hold values from -0.125 to 0.125
- ffn_down: bfloat16 [6144, 2048], P(('grp', 'fsdp')), may hold values from -0.078125 to 0.078125
- cotangent: bfloat16 [8192, 2048], P(('grp', 'fsdp')), may hold values from -6 to 6
- sequence_numbers: int32 [8192], P('grp'), may hold values from 0 to 8, as said below
- positions: int32 [8192], P('grp'), may hold values from 0 to 1151, as said below
Outputs:
- output: bfloat16 [8192, 2048], P(('grp', 'fsdp'))
- input_grad: float32 [8192, 2048], P(('grp', 'fsdp'))
- grad_query: float32 [2048, 2048], P(('grp', 'fsdp'))
- grad_key: float32 [2048, 1024], P(('grp', 'fsdp'))
- grad_value: float32 [2048, 1024], P(('grp', 'fsdp'))
- grad_gate: float32 [2048, 2048], P(('grp', 'fsdp'))
- grad_out: float32 [2048, 2048], P(('grp', 'fsdp'))
- grad_norm_attn: float32 [2048], P(('grp', 'fsdp'))
- grad_query_gain: float32 [128], P(('grp', 'fsdp'))
- grad_key_gain: float32 [128], P(('grp', 'fsdp'))
- grad_norm_ffn: float32 [2048], P(('grp', 'fsdp'))
- grad_ffn_gate: float32 [2048, 6144], P(('grp', 'fsdp'))
- grad_ffn_up: float32 [2048, 6144], P(('grp', 'fsdp'))
- grad_ffn_down: float32 [6144, 2048], P(('grp', 'fsdp'))
Inputs may be any that keep to these rules, and one draw needn't show every extreme that they name: `sequence_numbers`: every aligned run of 2048 rows is one prompt group: 8 prompt blocks and 8 continuations, as blocks of 128 consecutive rows in a drawn order. A prompt block has sequence number 0; continuation c (1 to 8) has c on all its 128 tokens. Prompt tokens have positions 0 to 1023 in order within their blocks; the tokens of every continuation have positions 1024 to 1151 in order.
All inputs are finite; a program needn't handle non-finite values.
Results may differ from a plain program's by a relative error of at most 0.024.
Values may be sent and summed in bfloat16 or wider, within the bound.
A program may use at most 448 MiB of HBM per device.

v0:
```python
import math

import jax
import jax.numpy as jnp
from jax import lax
from jax.sharding import PartitionSpec as P

QUERY_HEADS = 16
KEY_VALUE_HEADS = 8
HEAD_SIZE = 128
GROUP_TOKENS = 2048


def root_mean_scale(values, gains):
    return values * lax.rsqrt(jnp.mean(values * values, axis=-1, keepdims=True) + 1e-06) * gains


def rope_tables(positions):
    steps_half = jnp.arange(HEAD_SIZE // 2).astype(jnp.float32)
    inverse = jnp.power(1000000.0, steps_half * (-2.0 / HEAD_SIZE))
    angles = positions.astype(jnp.float32)[:, None] * inverse[None, :]
    angles = jnp.concatenate([angles, angles], axis=-1)
    return (jnp.cos(angles)[:, None, :], jnp.sin(angles)[:, None, :])


def rotary_apply(values, cosine_factor, sine_factor):
    half_dim = values.shape[-1] // 2
    turned = jnp.concatenate([-values[..., half_dim:], values[..., :half_dim]], axis=-1)
    return values * cosine_factor + turned * sine_factor


def matrix_product(left, right):
    return jnp.dot(left, right, preferred_element_type=jnp.float32)


def contract_last(left, right):
    return lax.dot_general(
        left, right, (((1,), (1,)), ((), ())), preferred_element_type=jnp.float32
    )


def contract_first(left, right):
    return lax.dot_general(
        left, right, (((0,), (0,)), ((), ())), preferred_element_type=jnp.float32
    )


def shards(
    hidden_in,
    query_weight,
    key_matrix,
    value_matrix,
    gate_weight,
    out_weight,
    norm_attn,
    query_gain,
    key_gain,
    norm_ffn,
    ffn_gate,
    ffn_up,
    ffn_down,
    cotangent,
    sequence_numbers,
    positions,
):
    token_row_span = hidden_in.shape[0]
    repeat_heads = QUERY_HEADS // KEY_VALUE_HEADS
    fsdp_index = lax.axis_index("fsdp")
    start_row = fsdp_index * token_row_span
    own_group = (start_row + jnp.arange(token_row_span, dtype=jnp.int32)) // GROUP_TOKENS
    own_seq = lax.dynamic_slice_in_dim(sequence_numbers, start_row, token_row_span)
    own_pos = lax.dynamic_slice_in_dim(positions, start_row, token_row_span)
    cosine_factor, sine_factor = rope_tables(own_pos)

    def prepare_heads(raw_values, gain_values):
        return rotary_apply(root_mean_scale(raw_values, gain_values), cosine_factor, sine_factor)

    w_query, key_projection, value_projection, w_gate, gain_attn, gain_query, key_norm_gain = (
        lax.all_gather(query_weight, ("grp", "fsdp"), axis=0, tiled=True),
        lax.all_gather(key_matrix, ("grp", "fsdp"), axis=0, tiled=True),
        lax.all_gather(value_matrix, ("grp", "fsdp"), axis=0, tiled=True),
        lax.all_gather(gate_weight, ("grp", "fsdp"), axis=0, tiled=True),
        lax.all_gather(norm_attn, ("grp", "fsdp"), axis=0, tiled=True),
        lax.all_gather(query_gain, ("grp", "fsdp"), axis=0, tiled=True),
        lax.all_gather(key_gain, ("grp", "fsdp"), axis=0, tiled=True),
    )
    hidden = hidden_in.astype(jnp.float32)
    normed_input = root_mean_scale(hidden, gain_attn.astype(jnp.float32)).astype(jnp.bfloat16)
    query_f = matrix_product(normed_input, w_query).reshape(token_row_span, QUERY_HEADS, HEAD_SIZE)
    key_single = matrix_product(normed_input, key_projection).reshape(
        token_row_span, KEY_VALUE_HEADS, HEAD_SIZE
    )
    value_narrow = (
        matrix_product(normed_input, value_projection)
        .astype(jnp.bfloat16)
        .reshape(token_row_span, KEY_VALUE_HEADS, HEAD_SIZE)
    )
    gate_raw = matrix_product(normed_input, w_gate)
    query_low = (
        prepare_heads(query_f, gain_query.astype(jnp.float32))
        .astype(jnp.bfloat16)
        .reshape(token_row_span, KEY_VALUE_HEADS, repeat_heads, HEAD_SIZE)
    )
    key_low = prepare_heads(key_single, key_norm_gain.astype(jnp.float32)).astype(jnp.bfloat16)
    key_group = jnp.arange(sequence_numbers.shape[0], dtype=jnp.int32) // GROUP_TOKENS
    key_seq, key_pos = (sequence_numbers, positions)
    keys_all, values_all = (
        lax.all_gather(key_low, "fsdp", axis=0, tiled=True),
        lax.all_gather(value_narrow, "fsdp", axis=0, tiled=True),
    )
    key_total = keys_all.shape[0]
    block_row_span = min(1024, key_total)
    block_total = key_total // block_row_span
    scale_qk = 1.0 / math.sqrt(HEAD_SIZE)
    statistic_shape = (KEY_VALUE_HEADS, repeat_heads, token_row_span)

    def block_slice(source, block_index):
        return lax.dynamic_slice_in_dim(source, block_index * block_row_span, block_row_span)

    def block_active(block_index):
        group_blk = block_slice(key_group, block_index)
        return jnp.any(own_group[:, None] == group_blk[None, :])

    def block_mask(block_index):
        group_blk = block_slice(key_group, block_index)
        seq_blk = block_slice(key_seq, block_index)
        pos_blk = block_slice(key_pos, block_index)
        return (
            (own_group[:, None] == group_blk[None, :])
            & (pos_blk[None, :] <= own_pos[:, None])
            & ((seq_blk[None, :] == 0) | (seq_blk[None, :] == own_seq[:, None]))
        )

    def block_scores(block_index):
        keys_blk = block_slice(keys_all, block_index)
        return (
            jnp.einsum("qgrd,kgd->grqk", query_low, keys_blk, preferred_element_type=jnp.float32)
            * scale_qk
        )

    def stat_step(state_in, block_index):

        def active_stats(stats):
            row_peak, row_total = stats
            allowed = block_mask(block_index)
            masked = jnp.where(allowed, block_scores(block_index), -1e30)
            new_peak = jnp.maximum(row_peak, jnp.max(masked, axis=-1))
            exponent = jnp.where(allowed, jnp.exp(masked - new_peak[..., None]), 0.0)
            return (new_peak, row_total * jnp.exp(row_peak - new_peak) + jnp.sum(exponent, axis=-1))

        def skip_stats(stats):
            return stats

        return (lax.cond(block_active(block_index), active_stats, skip_stats, state_in), None)

    initial = (
        jnp.full(statistic_shape, -1e30, jnp.float32),
        jnp.zeros(statistic_shape, jnp.float32),
    )
    (row_peak, row_total), unused_stats = lax.scan(stat_step, initial, jnp.arange(block_total))

    def block_softmax(block_index):
        allowed = block_mask(block_index)
        exponent = jnp.where(allowed, jnp.exp(block_scores(block_index) - row_peak[..., None]), 0.0)
        return exponent / row_total[..., None]

    def out_step(state_in, block_index):

        def active_out(summed):
            softmax_w = block_softmax(block_index).astype(jnp.bfloat16)
            values_blk = block_slice(values_all, block_index)
            return summed + jnp.einsum(
                "grqk,kgd->qgrd", softmax_w, values_blk, preferred_element_type=jnp.float32
            )

        def skip_out(summed):
            return summed

        return (lax.cond(block_active(block_index), active_out, skip_out, state_in), None)

    empty_heads = jnp.zeros((token_row_span, KEY_VALUE_HEADS, repeat_heads, HEAD_SIZE), jnp.float32)
    attended_heads, unused_out = lax.scan(out_step, empty_heads, jnp.arange(block_total))
    attended_rows = attended_heads.reshape(token_row_span, QUERY_HEADS * HEAD_SIZE)
    gate_sig = jax.nn.sigmoid(gate_raw)
    gated_low = (attended_rows * gate_sig).astype(jnp.bfloat16)
    w_out = lax.all_gather(out_weight, ("grp", "fsdp"), axis=0, tiled=True)
    middle = hidden + matrix_product(gated_low, w_out)
    w_ffn_gate, w_ffn_up, w_ffn_down, gain_ffn = (
        lax.all_gather(ffn_gate, ("grp", "fsdp"), axis=0, tiled=True),
        lax.all_gather(ffn_up, ("grp", "fsdp"), axis=0, tiled=True),
        lax.all_gather(ffn_down, ("grp", "fsdp"), axis=0, tiled=True),
        lax.all_gather(norm_ffn, ("grp", "fsdp"), axis=0, tiled=True),
    )
    normed_two = root_mean_scale(middle, gain_ffn.astype(jnp.float32)).astype(jnp.bfloat16)
    gate_ffn = matrix_product(normed_two, w_ffn_gate)
    up_ffn = matrix_product(normed_two, w_ffn_up)
    mixed_low = (jax.nn.silu(gate_ffn) * up_ffn).astype(jnp.bfloat16)
    result = middle + matrix_product(mixed_low, w_ffn_down)
    output = result.astype(jnp.bfloat16)
    back_gate, back_up, back_down, back_gain_ffn = (
        lax.all_gather(ffn_gate, ("grp", "fsdp"), axis=0, tiled=True),
        lax.all_gather(ffn_up, ("grp", "fsdp"), axis=0, tiled=True),
        lax.all_gather(ffn_down, ("grp", "fsdp"), axis=0, tiled=True),
        lax.all_gather(norm_ffn, ("grp", "fsdp"), axis=0, tiled=True),
    )
    cotangent_f = cotangent.astype(jnp.float32)
    d_mixed = contract_last(cotangent, back_down)
    grad_down_term = contract_first(mixed_low, cotangent)
    ffn_sig = jax.nn.sigmoid(gate_ffn)
    d_up_low = (d_mixed * gate_ffn * ffn_sig).astype(jnp.bfloat16)
    d_gate_ffn_low = (d_mixed * up_ffn * ffn_sig * (1.0 + gate_ffn * (1.0 - ffn_sig))).astype(
        jnp.bfloat16
    )
    d_normed_two = contract_last(d_gate_ffn_low, back_gate) + contract_last(d_up_low, back_up)
    grad_gate_term = contract_first(normed_two, d_gate_ffn_low)
    grad_up_term = contract_first(normed_two, d_up_low)
    unused_two, norm_two_back = jax.vjp(root_mean_scale, middle, back_gain_ffn.astype(jnp.float32))
    d_middle_norm, grad_norm_two_term = norm_two_back(d_normed_two)
    d_middle = cotangent_f + d_middle_norm
    mlp_sums = (
        lax.psum_scatter(grad_gate_term, ("grp", "fsdp"), scatter_dimension=0, tiled=True),
        lax.psum_scatter(grad_up_term, ("grp", "fsdp"), scatter_dimension=0, tiled=True),
        lax.psum_scatter(grad_down_term, ("grp", "fsdp"), scatter_dimension=0, tiled=True),
        lax.psum_scatter(grad_norm_two_term, ("grp", "fsdp"), scatter_dimension=0, tiled=True),
    )
    (
        back_query,
        back_key,
        back_value,
        back_gatew,
        back_out,
        back_gain_attn,
        back_gain_query,
        back_gain_key,
    ) = (
        lax.all_gather(query_weight, ("grp", "fsdp"), axis=0, tiled=True),
        lax.all_gather(key_matrix, ("grp", "fsdp"), axis=0, tiled=True),
        lax.all_gather(value_matrix, ("grp", "fsdp"), axis=0, tiled=True),
        lax.all_gather(gate_weight, ("grp", "fsdp"), axis=0, tiled=True),
        lax.all_gather(out_weight, ("grp", "fsdp"), axis=0, tiled=True),
        lax.all_gather(norm_attn, ("grp", "fsdp"), axis=0, tiled=True),
        lax.all_gather(query_gain, ("grp", "fsdp"), axis=0, tiled=True),
        lax.all_gather(key_gain, ("grp", "fsdp"), axis=0, tiled=True),
    )
    branch_low = d_middle.astype(jnp.bfloat16)
    d_gated = contract_last(branch_low, back_out)
    grad_out_term = contract_first(gated_low, branch_low)
    grad_attention_narrow = (d_gated * gate_sig).astype(jnp.bfloat16)
    d_gate_attn_low = (d_gated * attended_rows * gate_sig * (1.0 - gate_sig)).astype(jnp.bfloat16)
    grad_attention_heads = grad_attention_narrow.reshape(
        token_row_span, KEY_VALUE_HEADS, repeat_heads, HEAD_SIZE
    )
    row_delta = jnp.transpose(
        jnp.sum(grad_attention_heads.astype(jnp.float32) * attended_heads, axis=-1), (1, 2, 0)
    )
    empty_block = jnp.zeros((block_row_span, KEY_VALUE_HEADS, HEAD_SIZE), jnp.float32)

    def grad_step(state_in, block_index):

        def active_grad(summed):
            softmax_f = block_softmax(block_index)
            softmax_low = softmax_f.astype(jnp.bfloat16)
            keys_blk = block_slice(keys_all, block_index)
            values_blk = block_slice(values_all, block_index)
            d_softmax = jnp.einsum(
                "qgrd,kgd->grqk",
                grad_attention_heads,
                values_blk,
                preferred_element_type=jnp.float32,
            )
            d_scores_low = (softmax_f * (d_softmax - row_delta[..., None])).astype(jnp.bfloat16)
            new_summed = (
                summed
                + jnp.einsum(
                    "grqk,kgd->qgrd", d_scores_low, keys_blk, preferred_element_type=jnp.float32
                )
                * scale_qk
            )
            d_keys_blk = (
                jnp.einsum(
                    "grqk,qgrd->kgd", d_scores_low, query_low, preferred_element_type=jnp.float32
                )
                * scale_qk
            )
            d_values_blk = jnp.einsum(
                "grqk,qgrd->kgd",
                softmax_low,
                grad_attention_heads,
                preferred_element_type=jnp.float32,
            )
            return (new_summed, d_keys_blk, d_values_blk)

        def skip_grad(summed):
            return (summed, empty_block, empty_block)

        new_state, d_keys_blk, d_values_blk = lax.cond(
            block_active(block_index), active_grad, skip_grad, state_in
        )
        return (new_state, (d_keys_blk, d_values_blk))

    d_query_heads, (grad_key_block_list, grad_value_block_list) = lax.scan(
        grad_step, empty_heads, jnp.arange(block_total)
    )
    grad_key_row_list = grad_key_block_list.reshape(key_total, KEY_VALUE_HEADS, HEAD_SIZE)
    grad_value_row_list = grad_value_block_list.reshape(key_total, KEY_VALUE_HEADS, HEAD_SIZE)
    d_key_rot, grad_value_full = (
        lax.psum_scatter(
            grad_key_row_list.astype(jnp.bfloat16), "fsdp", scatter_dimension=0, tiled=True
        ).astype(jnp.float32),
        lax.psum_scatter(
            grad_value_row_list.astype(jnp.bfloat16), "fsdp", scatter_dimension=0, tiled=True
        ).astype(jnp.float32),
    )
    unused_query, query_back = jax.vjp(prepare_heads, query_f, back_gain_query.astype(jnp.float32))
    d_query_raw, grad_query_gain_term = query_back(
        d_query_heads.reshape(token_row_span, QUERY_HEADS, HEAD_SIZE)
    )
    unused_key, key_back = jax.vjp(prepare_heads, key_single, back_gain_key.astype(jnp.float32))
    grad_key_unrotated, grad_key_gain_term = key_back(d_key_rot)
    d_query_low = d_query_raw.reshape(token_row_span, QUERY_HEADS * HEAD_SIZE).astype(jnp.bfloat16)
    grad_key_narrow = grad_key_unrotated.reshape(
        token_row_span, KEY_VALUE_HEADS * HEAD_SIZE
    ).astype(jnp.bfloat16)
    grad_value_narrow = grad_value_full.reshape(token_row_span, KEY_VALUE_HEADS * HEAD_SIZE).astype(
        jnp.bfloat16
    )
    d_normed = (
        contract_last(d_query_low, back_query)
        + contract_last(grad_key_narrow, back_key)
        + contract_last(grad_value_narrow, back_value)
        + contract_last(d_gate_attn_low, back_gatew)
    )
    grad_query_term = contract_first(normed_input, d_query_low)
    grad_key_term = contract_first(normed_input, grad_key_narrow)
    grad_value_term = contract_first(normed_input, grad_value_narrow)
    grad_gatew_term = contract_first(normed_input, d_gate_attn_low)
    unused_one, norm_one_back = jax.vjp(root_mean_scale, hidden, back_gain_attn.astype(jnp.float32))
    d_hidden_norm, grad_norm_one_term = norm_one_back(d_normed)
    input_grad = d_middle + d_hidden_norm
    attn_sums = (
        lax.psum_scatter(grad_query_term, ("grp", "fsdp"), scatter_dimension=0, tiled=True),
        lax.psum_scatter(grad_key_term, ("grp", "fsdp"), scatter_dimension=0, tiled=True),
        lax.psum_scatter(grad_value_term, ("grp", "fsdp"), scatter_dimension=0, tiled=True),
        lax.psum_scatter(grad_gatew_term, ("grp", "fsdp"), scatter_dimension=0, tiled=True),
        lax.psum_scatter(grad_out_term, ("grp", "fsdp"), scatter_dimension=0, tiled=True),
        lax.psum_scatter(grad_norm_one_term, ("grp", "fsdp"), scatter_dimension=0, tiled=True),
        lax.psum_scatter(grad_query_gain_term, ("grp", "fsdp"), scatter_dimension=0, tiled=True),
        lax.psum_scatter(grad_key_gain_term, ("grp", "fsdp"), scatter_dimension=0, tiled=True),
    )
    return (
        output,
        input_grad,
        attn_sums[0],
        attn_sums[1],
        attn_sums[2],
        attn_sums[3],
        attn_sums[4],
        attn_sums[5],
        attn_sums[6],
        attn_sums[7],
        mlp_sums[3],
        mlp_sums[0],
        mlp_sums[1],
        mlp_sums[2],
    )


def solution(mesh):
    placed = (
        P(("grp", "fsdp"), None),
        P(("grp", "fsdp"), None),
        P(("grp", "fsdp"), None),
        P(("grp", "fsdp"), None),
        P(("grp", "fsdp"), None),
        P(("grp", "fsdp"), None),
        P(("grp", "fsdp")),
        P(("grp", "fsdp")),
        P(("grp", "fsdp")),
        P(("grp", "fsdp")),
        P(("grp", "fsdp"), None),
        P(("grp", "fsdp"), None),
        P(("grp", "fsdp"), None),
        P(("grp", "fsdp"), None),
        P("grp"),
        P("grp"),
    )
    return jax.shard_map(
        shards,
        mesh=mesh,
        in_specs=placed,
        out_specs=(
            P(("grp", "fsdp"), None),
            P(("grp", "fsdp"), None),
            P(("grp", "fsdp"), None),
            P(("grp", "fsdp"), None),
            P(("grp", "fsdp"), None),
            P(("grp", "fsdp"), None),
            P(("grp", "fsdp"), None),
            P(("grp", "fsdp")),
            P(("grp", "fsdp")),
            P(("grp", "fsdp")),
            P(("grp", "fsdp")),
            P(("grp", "fsdp"), None),
            P(("grp", "fsdp"), None),
            P(("grp", "fsdp"), None),
        ),
        check_vma=False,
    )
```

profile of v0, /device:TPU:0, one launch (start us, length us, event | category | flops | bytes accessed | tf_op | source)
XLA Modules:
  0.0 4119.7 jit_solution(11789034147244666790)
XLA Ops:
  12.1 42.3 %all-reduce.13 = (bf16[2048]{0:T(1024)(128)(2,1)S(1)}, bf16[128]{0:T(256)(128)(2,1)S(1)}, bf16[128]{0:T(256)(128)(2,1)S(1)}, bf16[2048]{0:T(1024)(128)(2,1)S(1)}) all-reduce(bf16[2048]{0:T(1024)(128)(2,1)S(1)} %dynamic-update-slice, bf16[128]{0:T(256)(128)(2,1)S(1)} %dynamic-update-slice.1, ...), channel_id=1, replica_groups=mesh['grp'=4,'fsdp'=8] {'grp','fsdp'}, use_global_device_ids=true, to_apply=%add.4 | all-reduce | flops 4352 | bytes 17408
  57.6 18.5 all-gather.15.cloned.1.call-done
  82.6 57.2 %all-gather.11.cloned.1.call-done = bf16[2048,1024]{1,0:T(8,128)(2,1)} async-done(((bf16[64,1024]{1,0:T(8,128)(2,1)}), bf16[2048,1024]{1,0:T(8,128)(2,1)}) %all-gather.11.cloned.1.call-update) | async-done | bytes 4194320 | tf_op jit(solution)/shard_map/all_gather | solution.py:81
  149.2 65.3 %all-gather.17.cloned.1.call-done = bf16[2048,8,128]{2,1,0:T(8,128)(2,1)} async-done(((bf16[256,8,128]{2,1,0:T(8,128)(2,1)}), bf16[2048,8,128]{2,1,0:T(8,128)(2,1)}) %all-gather.17.cloned.1.call-update) | async-done | bytes 4194320 | tf_op jit(solution)/shard_map/all_gather | solution.py:108
  219.2 69.6 %all-gather.13.cloned.1.call-done = bf16[2048,8,128]{2,0,1:T(8,128)(2,1)} async-done(((bf16[256,8,128]{2,0,1:T(8,128)(2,1)}), bf16[2048,8,128]{2,0,1:T(8,128)(2,1)}) %all-gather.13.cloned.1.call-update) | async-done | bytes 4194320 | tf_op jit(solution)/shard_map/all_gather | solution.py:109
  295.3 71.9 %all-gather.19.cloned.1.call-done = bf16[2048,2048]{1,0:T(8,128)(2,1)} async-done(((bf16[64,2048]{1,0:T(8,128)(2,1)}), bf16[2048,2048]{1,0:T(8,128)(2,1)}) %all-gather.19.cloned.1.call-update) | async-done | bytes 8388624 | tf_op jit(solution)/shard_map/all_gather | solution.py:79
  388.8 25.4 while.48
  391.6 9.9 conditional.12
  404.3 9.9 conditional.12
  414.5 23.8 while.49
  417.7 8.9 conditional.13
  429.4 8.9 conditional.13
  446.1 7.8 multiply_convert_fusion.6
  453.9 71.3 %all-gather.23.cloned.1.call-done = bf16[2048,2048]{1,0:T(8,128)(2,1)} async-done(((bf16[64,2048]{1,0:T(8,128)(2,1)}), bf16[2048,2048]{1,0:T(8,128)(2,1)}) %all-gather.23.cloned.1.call-update) | async-done | bytes 8388624 | tf_op jit(solution)/shard_map/all_gather | solution.py:186
  532.7 148.7 %all-gather.25.cloned.1.call-done = bf16[2048,6144]{1,0:T(8,128)(2,1)} async-done(((bf16[64,6144]{1,0:T(8,128)(2,1)}), bf16[2048,6144]{1,0:T(8,128)(2,1)}) %all-gather.25.cloned.1.call-update) | async-done | bytes 25165840 | tf_op jit(solution)/shard_map/all_gather | solution.py:189
  681.4 14.4 fusion.113
  695.8 141.4 %all-gather.27.cloned.1.call-done = bf16[2048,6144]{1,0:T(8,128)(2,1)} async-done(((bf16[64,6144]{1,0:T(8,128)(2,1)}), bf16[2048,6144]{1,0:T(8,128)(2,1)}) %all-gather.27.cloned.1.call-update) | async-done | bytes 25165840 | tf_op jit(solution)/shard_map/all_gather | solution.py:190
  837.2 14.3 fusion.114
  851.5 141.3 %all-gather.29.cloned.1.call-done = bf16[6144,2048]{1,0:T(8,128)(2,1)} async-done(((bf16[192,2048]{1,0:T(8,128)(2,1)}), bf16[6144,2048]{1,0:T(8,128)(2,1)}) %all-gather.29.cloned.1.call-update) | async-done | bytes 25165840 | tf_op jit(solution)/shard_map/all_gather | solution.py:191
  992.8 19.5 multiply_convert_fusion
  1012.4 13.7 fusion.115
  1026.0 15.0 multiply_reduce_fusion
  1061.5 104.3 %while.50 = (s32[]{:T(128)}, f32[256,8,2,128]{0,3,2,1:T(8,128)}, bf16[2,1024,8,128]{3,2,1,0:T(8,128)(2,1)}, bf16[2,1024,8,128]{3,2,1,0:T(8,128)(2,1)}, s32[2]{0:...) while((s32[]{:T(128)}, f32[256,8,2,128]{0,3,2,1:T(8,128)}, ...), condition=%wide.region_22.23_spmd.clone.clone, body=%wide.region_18.22_spmd.clone.clone.sunk | while | flops 5407511552 | bytes 174694592 | solution.py:301
  1064.8 42.6 %conditional.14 = (f32[256,8,2,128]{0,3,2,1:T(8,128)}, bf16[1,1024,8,128]{3,1,2,0:T(8,128)(2,1)S(1)}, bf16[1,1024,8,128]{3,1,2,0:T(8,128)(2,1)}) conditional(s32[]{:T(128)} %convert_element_type.250, f32[256,8,2,128]{0,3,2,1:T(8,128)} %get-tuple-element.1405, (s32[]{:T(128)}, bf16[2048,8,128]{2,0,1:T(8,128)(2,1)}, s32[256]{0:T(256)S(1)}, ...), branch_computations={%region_20.20_spmd, %region_21.21_spmd} | conditional | flops 5406983168 | bytes 157902080 | solution.py:296
  1066.6 9.5 fusion.34
  1076.1 12.5 fusion.31
  1098.0 9.4 fusion.38
  1116.6 42.6 %conditional.14 = (f32[256,8,2,128]{0,3,2,1:T(8,128)}, bf16[1,1024,8,128]{3,1,2,0:T(8,128)(2,1)S(1)}, bf16[1,1024,8,128]{3,1,2,0:T(8,128)(2,1)}) conditional(s32[]{:T(128)} %convert_element_type.250, f32[256,8,2,128]{0,3,2,1:T(8,128)} %get-tuple-element.1405, (s32[]{:T(128)}, bf16[2048,8,128]{2,0,1:T(8,128)(2,1)}, s32[256]{0:T(256)S(1)}, ...), branch_computations={%region_20.20_spmd, %region_21.21_spmd} | conditional | flops 5406983168 | bytes 157902080 | solution.py:296
  1118.4 9.5 fusion.34
  1127.9 12.5 fusion.31
  1149.8 9.4 fusion.38
  1166.5 85.6 %reduce-scatter.11.cloned.1.call-done = bf16[256,8,128]{2,1,0:T(8,128)(2,1)} async-done(((bf16[2048,8,128]{2,1,0:T(8,128)(2,1)}), bf16[256,8,128]{2,1,0:T(8,128)(2,1)}) %reduce-scatter.11.cloned.1.call-update) | async-done | bytes 524304 | tf_op jit(solution)/shard_map/reduce_scatter | solution.py:307
  1264.0 79.7 %reduce-scatter.13.cloned.1.call-done = bf16[256,8,128]{2,1,0:T(8,128)(2,1)} async-done(((bf16[2048,8,128]{2,1,0:T(8,128)(2,1)}), bf16[256,8,128]{2,1,0:T(8,128)(2,1)}) %reduce-scatter.13.cloned.1.call-update) | async-done | bytes 524304 | tf_op jit(solution)/shard_map/reduce_scatter | solution.py:310
  1351.0 9.4 fusion.81
  1365.5 8.3 fusion.101
  1375.1 8.3 fusion.96
  1384.6 21.6 fusion.117
  1406.3 21.6 fusion.118
  1429.1 21.6 fusion.119
  1456.7 13.4 fusion.56
  1481.7 44.9 %all-reduce.12 = (f32[2048]{0:T(1024)S(1)}, f32[128]{0:T(128)S(1)}, f32[128]{0:T(128)S(1)}, f32[2048]{0:T(1024)S(1)}) all-reduce(f32[2048]{0:T(1024)S(1)} %get-tuple-element.852, f32[128]{0:T(128)S(1)} %get-tuple-element.854, f32[128]{0:T(128)S(1)} %copy-done.73, ...), channel_id=9, replica_groups=mesh['grp'=4,'fsdp'=8] {'grp','fsdp'}, use_global_device_ids=true, to_apply=%region_34.35.clone | all-reduce | flops 4352 | bytes 34816
  1532.3 187.2 %reduce-scatter.19.cloned.1.call-done = f32[64,1024]{1,0:T(8,128)} async-done(((f32[2048,1024]{1,0:T(8,128)}), f32[64,1024]{1,0:T(8,128)}) %reduce-scatter.19.cloned.1.call-update) | async-done | bytes 262160 | tf_op jit(solution)/shard_map/reduce_scatter | solution.py:343
  1719.5 360.1 %reduce-scatter.23.cloned.1.call-done = f32[64,2048]{1,0:T(8,128)} async-done(((f32[2048,2048]{1,0:T(8,128)}), f32[64,2048]{1,0:T(8,128)}) %reduce-scatter.23.cloned.1.call-update) | async-done | bytes 524304 | tf_op jit(solution)/shard_map/reduce_scatter | solution.py:345
  2079.6 360.1 %reduce-scatter.15.cloned.1.call-done = f32[64,2048]{1,0:T(8,128)} async-done(((f32[2048,2048]{1,0:T(8,128)}), f32[64,2048]{1,0:T(8,128)}) %reduce-scatter.15.cloned.1.call-update) | async-done | bytes 524304 | tf_op jit(solution)/shard_map/reduce_scatter | solution.py:341
  2439.7 360.1 %reduce-scatter.21.cloned.1.call-done = f32[64,2048]{1,0:T(8,128)} async-done(((f32[2048,2048]{1,0:T(8,128)}), f32[64,2048]{1,0:T(8,128)}) %reduce-scatter.21.cloned.1.call-update) | async-done | bytes 524304 | tf_op jit(solution)/shard_map/reduce_scatter | solution.py:344
  2799.8 437.7 %reduce-scatter.25.cloned.1.call-done = f32[64,6144]{1,0:T(8,128)} async-done(((f32[2048,6144]{1,0:T(8,128)}), f32[64,6144]{1,0:T(8,128)}) %reduce-scatter.25.cloned.1.call-update) | async-done | bytes 1572880 | tf_op jit(solution)/shard_map/reduce_scatter | solution.py:221
  3237.4 437.7 %reduce-scatter.27.cloned.1.call-done = f32[64,6144]{1,0:T(8,128)} async-done(((f32[2048,6144]{1,0:T(8,128)}), f32[64,6144]{1,0:T(8,128)}) %reduce-scatter.27.cloned.1.call-update) | async-done | bytes 1572880 | tf_op jit(solution)/shard_map/reduce_scatter | solution.py:222
  3675.1 437.3 %reduce-scatter.29.cloned.1.call-done = f32[192,2048]{1,0:T(8,128)} async-done(((f32[6144,2048]{1,0:T(8,128)}), f32[192,2048]{1,0:T(8,128)}) %reduce-scatter.29.cloned.1.call-update) | async-done | bytes 1572880 | tf_op jit(solution)/shard_map/reduce_scatter | solution.py:223
  (361 shorter events, 221.0 us)
Async XLA Ops:
  7.2 68.9 %copy-start.12 = (bf16[256,2048]{1,0:T(8,128)(2,1)S(1)}, bf16[256,2048]{1,0:T(8,128)(2,1)}, u32[]{:S(2)}) copy-start(bf16[256,2048]{1,0:T(8,128)(2,1)} %param.28) | copy-start | bytes 3145732
  7.2 68.9 %all-gather.15.cloned.1.call-start = ((), (), s32[]{:S(2)}) async-start(), calls=%async_computation.12 | async-start | bytes 4325376 | tf_op jit(solution)/shard_map/all_gather | solution.py:80
  7.9 131.9 %all-gather.11.cloned.1.call-start = ((), (), s32[]{:S(2)}) async-start(), calls=%async_computation.10 | async-start | bytes 4325376 | tf_op jit(solution)/shard_map/all_gather | solution.py:81
  8.7 205.9 %all-gather.17.cloned.1.call-start = ((), (), s32[]{:S(2)}) async-start(), calls=%async_computation.13 | async-start | bytes 4718592 | tf_op jit(solution)/shard_map/all_gather | solution.py:108
  54.4 312.8 %copy-start.51 = (f32[2048]{0:T(1024)}, f32[2048]{0:T(1024)S(1)}, u32[]{:S(2)}) copy-start(f32[2048]{0:T(1024)S(1)} %convert_element_type.126) | copy-start | bytes 24580
  55.7 20.3 copy-start.46
  55.8 20.3 copy-start.48
  55.9 330.0 %copy-start.39 = (f32[256,128]{1,0:T(8,128)}, f32[256,128]{1,0:T(8,128)S(1)}, u32[]{:S(2)}) copy-start(f32[256,128]{1,0:T(8,128)S(1)} %copy.137) | copy-start | bytes 393220
  56.0 329.9 %copy-start.41 = (f32[256,128]{1,0:T(8,128)}, f32[256,128]{1,0:T(8,128)S(1)}, u32[]{:S(2)}) copy-start(f32[256,128]{1,0:T(8,128)S(1)} %copy.138) | copy-start | bytes 393220
  56.0 25.1 copy-start.68
  57.6 22.0 copy-start.66
  57.6 309.7 %copy-start.60 = (f32[256]{0:T(256)}, f32[256]{0:T(256)S(1)}, u32[]{:S(2)}) copy-start(f32[256]{0:T(256)S(1)} %fusion.94) | copy-start | bytes 3076
  82.6 206.2 %all-gather.13.cloned.1.call-start = ((), (), s32[]{:S(2)}) async-start(), calls=%async_computation.11 | async-start | bytes 4718592 | tf_op jit(solution)/shard_map/all_gather | solution.py:109
  144.2 223.0 %all-gather.19.cloned.1.call-start = ((), (), s32[]{:S(2)}) async-start(), calls=%async_computation.14 | async-start | bytes 8650752 | tf_op jit(solution)/shard_map/all_gather | solution.py:79
  144.8 301.2 %all-gather.21.cloned.1.call-start = ((), (), s32[]{:S(2)}) async-start(), calls=%async_computation.15 | async-start | bytes 8650752 | tf_op jit(solution)/shard_map/all_gather | solution.py:82
  145.4 379.8 %all-gather.23.cloned.1.call-start = ((), (), s32[]{:S(2)}) async-start(), calls=%async_computation.16 | async-start | bytes 8650752 | tf_op jit(solution)/shard_map/all_gather | solution.py:186
  146.2 535.3 %all-gather.25.cloned.1.call-start = ((), (), s32[]{:S(2)}) async-start(), calls=%async_computation.17 | async-start | bytes 25952256 | tf_op jit(solution)/shard_map/all_gather | solution.py:189
  146.9 690.3 %all-gather.27.cloned.1.call-start = ((), (), s32[]{:S(2)}) async-start(), calls=%async_computation.18 | async-start | bytes 25952256 | tf_op jit(solution)/shard_map/all_gather | solution.py:190
  147.6 845.2 %all-gather.29.cloned.1.call-start = ((), (), s32[]{:S(2)}) async-start(), calls=%async_computation.19 | async-start | bytes 25952256 | tf_op jit(solution)/shard_map/all_gather | solution.py:191
  148.2 1103.8 %reduce-scatter.11.cloned.1.call-start = ((), (), s32[]{:S(2)}) async-start(), calls=%async_computation.20 | async-start | bytes 4718592 | tf_op jit(solution)/shard_map/reduce_scatter | solution.py:307
  148.5 237.4 %copy-start.71 = (f32[128]{0:T(128)}, f32[128]{0:T(128)S(1)}, u32[]{:S(2)}) copy-start(f32[128]{0:T(128)S(1)} %convert_element_type.133) | copy-start | bytes 1540
  453.9 77.2 %copy-start.50 = (bf16[256,2048]{1,0:T(8,128)(2,1)}, bf16[256,2048]{1,0:T(8,128)(2,1)S(1)}, u32[]{:S(2)}) copy-start(bf16[256,2048]{1,0:T(8,128)(2,1)S(1)} %get-tuple-element.983) | copy-start | bytes 3145732
  525.2 7.2 copy-start.63
  532.7 304.5 %copy-start.20 = (bf16[256,2048]{1,0:T(8,128)(2,1)}, bf16[256,2048]{1,0:T(8,128)(2,1)S(1)}, u32[]{:S(2)}) copy-start(bf16[256,2048]{1,0:T(8,128)(2,1)S(1)} %multiply_convert_fusion.5) | copy-start | bytes 3145732
  695.8 297.0 %copy-start.30 = (bf16[256,2048]{1,0:T(8,128)(2,1)S(1)}, bf16[256,2048]{1,0:T(8,128)(2,1)}, u32[]{:S(2)}) copy-start(bf16[256,2048]{1,0:T(8,128)(2,1)} %param.41) | copy-start | bytes 3145732
  1012.4 13.7 copy-start.23
  1043.7 8.0 copy-start.15
  1064.8 11.3 copy-start.8
  1076.1 12.5 copy-start.1
  1088.7 6.9 copy-start.9
  1116.6 11.3 copy-start.8
  1127.9 12.5 copy-start.1
  1165.8 177.8 %reduce-scatter.13.cloned.1.call-start = ((), (), s32[]{:S(2)}) async-start(), calls=%async_computation.21 | async-start | bytes 4718592 | tf_op jit(solution)/shard_map/reduce_scatter | solution.py:310
  1165.9 86.2 %copy-start.42 = (f32[256,128]{1,0:T(8,128)S(1)}, f32[256,128]{1,0:T(8,128)}, u32[]{:S(2)}) copy-start(f32[256,128]{1,0:T(8,128)} %copy-done.41) | copy-start | bytes 393220
  1166.4 365.9 %reduce-scatter.17.cloned.1.call-start = ((), (), s32[]{:S(2)}) async-start(), calls=%async_computation.23 | async-start | bytes 8650752 | tf_op jit(solution)/shard_map/reduce_scatter | solution.py:342
  1263.9 455.6 %reduce-scatter.19.cloned.1.call-start = ((), (), s32[]{:S(2)}) async-start(), calls=%async_computation.24 | async-start | bytes 8650752 | tf_op jit(solution)/shard_map/reduce_scatter | solution.py:343
  1349.4 730.2 %reduce-scatter.23.cloned.1.call-start = ((), (), s32[]{:S(2)}) async-start(), calls=%async_computation.26 | async-start | bytes 17301504 | tf_op jit(solution)/shard_map/reduce_scatter | solution.py:345
  1360.4 1079.3 %reduce-scatter.15.cloned.1.call-start = ((), (), s32[]{:S(2)}) async-start(), calls=%async_computation.22 | async-start | bytes 17301504 | tf_op jit(solution)/shard_map/reduce_scatter | solution.py:341
  1373.9 1425.9 %reduce-scatter.21.cloned.1.call-start = ((), (), s32[]{:S(2)}) async-start(), calls=%async_computation.25 | async-start | bytes 17301504 | tf_op jit(solution)/shard_map/reduce_scatter | solution.py:344
  1383.4 1854.0 %reduce-scatter.25.cloned.1.call-start = ((), (), s32[]{:S(2)}) async-start(), calls=%async_computation.27 | async-start | bytes 51904512 | tf_op jit(solution)/shard_map/reduce_scatter | solution.py:221
  1406.2 2268.8 %reduce-scatter.27.cloned.1.call-start = ((), (), s32[]{:S(2)}) async-start(), calls=%async_computation.28 | async-start | bytes 51904512 | tf_op jit(solution)/shard_map/reduce_scatter | solution.py:222
  1427.9 2684.5 %reduce-scatter.29.cloned.1.call-start = ((), (), s32[]{:S(2)}) async-start(), calls=%async_computation.29 | async-start | bytes 51904512 | tf_op jit(solution)/shard_map/reduce_scatter | solution.py:223
  1456.7 13.4 copy-start.28
  1456.7 13.4 copy-start.35
  1473.8 7.8 copy-start.70
  1473.8 7.8 copy-start.73
  1473.9 55.0 %copy-start.67 = (f32[256]{0:T(256)S(1)}, f32[256]{0:T(256)}, u32[]{:S(2)}) copy-start(f32[256]{0:T(256)} %copy-done.66) | copy-start | bytes 3076
  1473.9 55.0 %copy-start.17 = (f32[256,2048]{1,0:T(8,128)S(1)}, f32[256,2048]{1,0:T(8,128)}, u32[]{:S(2)}) copy-start(f32[256,2048]{1,0:T(8,128)} %copy-done.15) | copy-start | bytes 6291460
  (53 other events, 154.9 us)
Sparse Core Ops, SparseCore 0:
  11.1 64.9 all-gather.14
  79.2 60.6 all-gather.10
  142.5 71.9 all-gather.16
  217.1 71.6 all-gather.12
  291.6 75.5 all-gather.18
  370.1 75.9 all-gather.20
  449.1 76.1 all-gather.22
  528.1 153.2 all-gather.24
  684.3 152.8 all-gather.26
  839.9 152.8 all-gather.28
  1165.9 86.0 reduce-scatter.10
  1256.0 87.6 reduce-scatter.12
  1346.5 185.2 reduce-scatter.16
  1534.5 184.9 reduce-scatter.18
  1722.2 357.3 reduce-scatter.22
  2082.3 357.3 reduce-scatter.14
  2442.4 357.3 reduce-scatter.20
  2806.6 430.7 reduce-scatter.24
  3244.4 430.6 reduce-scatter.26
  3681.9 430.3 reduce-scatter.28
where the time goes:
time: 4130 us; the launch traced here: 4120 us
  waiting for transfers between devices  3540 us (86%)
  matrix products  347 us (8%)
  blocking collectives  87.1 us (2%)
  local copies, waits for them, and re-layouts  72.9 us (2%)
  other arithmetic  42.5 us (1%)
    reduce_scatter x1, waiting for transfers between devices, shards(): lax.psum_scatter(grad_up_term, ('grp', 'fsdp'), scatter_dimension=0, tile...  438 us
    reduce_scatter x1, waiting for transfers between devices, shards(): lax.psum_scatter(grad_gate_term, ('grp', 'fsdp'), scatter_dimension=0, ti...  438 us
    reduce_scatter x1, waiting for transfers between devices, shards(): lax.psum_scatter(grad_down_term, ('grp', 'fsdp'), scatter_dimension=0, ti...  437 us
    reduce_scatter x1, waiting for transfers between devices, shards(): lax.psum_scatter(grad_query_term, ('grp', 'fsdp'), scatter_dimension=0, t...  360 us
    reduce_scatter x1, waiting for transfers between devices, shards(): lax.psum_scatter(grad_gatew_term, ('grp', 'fsdp'), scatter_dimension=0, t...  360 us
    reduce_scatter x1, waiting for transfers between devices, shards(): lax.psum_scatter(grad_out_term, ('grp', 'fsdp'), scatter_dimension=0, til...  360 us
    reduce_scatter x1, waiting for transfers between devices, shards(): lax.psum_scatter(grad_value_term, ('grp', 'fsdp'), scatter_dimension=0, t...  187 us
    all_gather x1, waiting for transfers between devices, shards(): lax.all_gather(ffn_gate, ('grp', 'fsdp'), axis=0, tiled=True)  149 us
  transfers between devices with their start and end apart: 20, of which 19 were waited for; matrix products, arithmetic and copies ran while one was open for 7% of the time, Pallas kernels for 0%

commit v1 on v0

v1 whole, which is shorter than its diff:
```python
import math

import jax
import jax.numpy as jnp
from jax import lax
from jax.sharding import Mesh
from jax.sharding import PartitionSpec as P

QUERY_HEADS = 16
KEY_VALUE_HEADS = 8
HEAD_SIZE = 128
GROUP_TOKENS = 2048
CORNERS = 2
PLANES = 4
ALL = ("x", "core", "cell", "z", "y")
TENSOR = ("x", "core", "y")
DATA = ("cell", "z")
RANKS = CORNERS**3


def root_mean_scale(values, gains):
    return values * lax.rsqrt(jnp.mean(values * values, axis=-1, keepdims=True) + 1e-06) * gains


def rope_tables(positions):
    steps_half = jnp.arange(HEAD_SIZE // 2).astype(jnp.float32)
    inverse = jnp.power(1000000.0, steps_half * (-2.0 / HEAD_SIZE))
    angles = positions.astype(jnp.float32)[..., None] * inverse
    angles = jnp.concatenate([angles, angles], axis=-1)
    return (jnp.cos(angles)[..., None, :], jnp.sin(angles)[..., None, :])


def rotary_apply(values, cosine_factor, sine_factor):
    half_dim = values.shape[-1] // 2
    turned = jnp.concatenate([-values[..., half_dim:], values[..., :half_dim]], axis=-1)
    return values * cosine_factor + turned * sine_factor


def matrix_product(left, right):
    return jnp.dot(left, right, preferred_element_type=jnp.float32)


def contract_last(left, right):
    return lax.dot_general(
        left, right, (((1,), (1,)), ((), ())), preferred_element_type=jnp.float32
    )


def contract_first(left, right):
    return lax.dot_general(
        left, right, (((0,), (0,)), ((), ())), preferred_element_type=jnp.float32
    )


def low(values):
    return values.astype(jnp.bfloat16)


def make_shards(cells):
    data_total = cells * PLANES

    def gather_tokens(rows):
        return lax.all_gather(rows, TENSOR, axis=0, tiled=True)

    def scatter_tokens(terms):
        return lax.psum_scatter(low(terms), TENSOR, scatter_dimension=0, tiled=True).astype(
            jnp.float32
        )

    def split_units(weight):
        rows, units = weight.shape
        piece = units // (RANKS * data_total)
        split = weight.reshape(rows, CORNERS**2, data_total, CORNERS, piece)
        return jnp.transpose(split, (0, 1, 3, 2, 4)).reshape(rows, RANKS, units // RANKS)

    def join_units(parts):
        ranks, rows, units = parts.shape
        split = parts.reshape(CORNERS**2, CORNERS, rows, data_total, units // data_total)
        return jnp.transpose(split, (2, 0, 3, 1, 4)).reshape(rows, ranks * units)

    def split_columns(weight):
        return weight.reshape(weight.shape[0], RANKS, -1)

    def join_columns(parts):
        return jnp.transpose(parts, (1, 0, 2)).reshape(parts.shape[1], -1)

    def gather_columns(pieces):
        sent = jnp.transpose(jnp.concatenate(pieces, axis=-1), (1, 0, 2))
        mine = lax.all_to_all(sent, TENSOR, split_axis=0, concat_axis=0, tiled=True)
        rows, columns = mine.shape[1:]
        every = lax.all_gather(mine, DATA, axis=0, tiled=False)
        every = every.reshape(data_total, CORNERS**2, CORNERS, rows, columns)
        return jnp.transpose(every, (1, 0, 2, 3, 4)).reshape(-1, columns)

    def scatter_columns(term):
        rows = term.shape[0] // (RANKS * data_total)
        split = low(term).reshape(CORNERS**2, data_total, CORNERS, rows, -1)
        split = jnp.transpose(split, (1, 0, 2, 3, 4)).reshape(data_total * RANKS, rows, -1)
        mine = lax.psum_scatter(split, DATA, scatter_dimension=0, tiled=True)
        return lax.all_to_all(mine, TENSOR, split_axis=0, concat_axis=0, tiled=True).astype(
            jnp.float32
        )

    inner = CORNERS * data_total
    to_rank = []
    for source in range(inner):
        rank_y, place = divmod(source, data_total)
        to_rank.append((source, place * CORNERS + rank_y))
    from_rank = [(b, a) for a, b in to_rank]
    INNER = ("cell", "z", "y")

    def shards(
        hidden_in,
        query_weight,
        key_matrix,
        value_matrix,
        gate_weight,
        out_weight,
        norm_attn,
        query_gain,
        key_gain,
        norm_ffn,
        ffn_gate,
        ffn_up,
        ffn_down,
        cotangent,
        sequence_numbers,
        positions,
    ):
        rows = hidden_in.shape[0]
        tokens = rows * RANKS
        groups = CORNERS**2
        window = GROUP_TOKENS // PLANES
        repeat = QUERY_HEADS // KEY_VALUE_HEADS
        query_columns = QUERY_HEADS * HEAD_SIZE // RANKS
        key_columns = KEY_VALUE_HEADS * HEAD_SIZE // RANKS
        scale_qk = 1.0 / math.sqrt(HEAD_SIZE)

        sizes = [norm_attn.shape[0], norm_ffn.shape[0], query_gain.shape[0], key_gain.shape[0]]
        gains = lax.all_gather(
            jnp.concatenate([norm_attn, norm_ffn, query_gain, key_gain]), ALL, axis=0, tiled=False
        ).astype(jnp.float32)
        cuts = [0]
        for size in sizes:
            cuts.append(cuts[-1] + size)
        gain_attn, gain_ffn, gain_query, gain_key = (
            gains[:, a:b].reshape(-1) for a, b in zip(cuts[:-1], cuts[1:])
        )

        w_attn = gather_columns(
            [
                split_columns(query_weight),
                split_columns(key_matrix),
                split_columns(value_matrix),
                split_columns(gate_weight),
            ]
        )
        w_out = lax.all_gather(
            lax.ppermute(out_weight, INNER, to_rank), DATA, axis=0, tiled=True
        )
        w_ffn = gather_columns([split_units(ffn_gate), split_units(ffn_up)])
        w_down = lax.all_gather(ffn_down, DATA, axis=0, tiled=True)

        plane = lax.axis_index("z")
        group_start = lax.axis_index("cell") * GROUP_TOKENS
        marks = jnp.stack(
            [
                lax.dynamic_slice_in_dim(sequence_numbers, group_start, GROUP_TOKENS),
                lax.dynamic_slice_in_dim(positions, group_start, GROUP_TOKENS),
            ]
        )
        marks = lax.all_gather(marks, ("x", "core"), axis=0, tiled=False)
        key_seq, key_pos = marks[:, 0], marks[:, 1]
        own = lax.dynamic_slice_in_dim(marks, plane * window, window, axis=2)
        own_seq, own_pos = own[:, 0], own[:, 1]
        cosine_factor, sine_factor = rope_tables(own_pos)
        allowed = (key_pos[:, None, :] <= own_pos[:, :, None]) & (
            (key_seq[:, None, :] == 0) | (key_seq[:, None, :] == own_seq[:, :, None])
        )

        def prepare_heads(raw_values, gain_values):
            return rotary_apply(
                root_mean_scale(raw_values, gain_values), cosine_factor, sine_factor
            )

        hidden = hidden_in.astype(jnp.float32)
        normed_input = gather_tokens(low(root_mean_scale(hidden, gain_attn)))
        raw = matrix_product(normed_input, w_attn)
        a, b, c = query_columns, query_columns + key_columns, query_columns + 2 * key_columns
        query_raw = raw[:, :a].reshape(groups, window, repeat, HEAD_SIZE)
        key_raw = raw[:, a:b].reshape(groups, window, 1, HEAD_SIZE)
        value_low = low(raw[:, b:c]).reshape(groups, window, HEAD_SIZE)
        gate_sig = jax.nn.sigmoid(raw[:, c:])
        query_low = low(prepare_heads(query_raw, gain_query))
        key_low = low(prepare_heads(key_raw, gain_key)).reshape(groups, window, HEAD_SIZE)
        pair = lax.all_gather(
            jnp.concatenate([key_low, value_low], axis=-1), "z", axis=0, tiled=False
        )
        pair = jnp.transpose(pair, (1, 0, 2, 3)).reshape(groups, GROUP_TOKENS, 2 * HEAD_SIZE)
        keys_all, values_all = pair[..., :HEAD_SIZE], pair[..., HEAD_SIZE:]

        scores = (
            jnp.einsum("gqrd,gkd->grqk", query_low, keys_all, preferred_element_type=jnp.float32)
            * scale_qk
        )
        masked = jnp.where(allowed[:, None], scores, -1e30)
        peak = jnp.max(masked, axis=-1, keepdims=True)
        exponent = jnp.exp(masked - peak)
        probs = exponent / jnp.sum(exponent, axis=-1, keepdims=True)
        probs_low = low(probs)
        attended = jnp.einsum(
            "grqk,gkd->gqrd", probs_low, values_all, preferred_element_type=jnp.float32
        )
        attended_rows = attended.reshape(tokens, query_columns)
        gated_low = low(attended_rows * gate_sig)
        middle = hidden + scatter_tokens(matrix_product(gated_low, w_out))

        normed_two = gather_tokens(low(root_mean_scale(middle, gain_ffn)))
        both = matrix_product(normed_two, w_ffn)
        units = both.shape[1] // 2
        gate_ffn, up_ffn = both[:, :units], both[:, units:]
        ffn_sig = jax.nn.sigmoid(gate_ffn)
        mixed_low = low(gate_ffn * ffn_sig * up_ffn)
        output = low(middle + scatter_tokens(matrix_product(mixed_low, w_down)))

        cotangent_all = gather_tokens(cotangent)
        d_mixed = contract_last(cotangent_all, w_down)
        d_up_low = low(d_mixed * gate_ffn * ffn_sig)
        d_gate_ffn_low = low(d_mixed * up_ffn * ffn_sig * (1.0 + gate_ffn * (1.0 - ffn_sig)))
        d_both = jnp.concatenate([d_gate_ffn_low, d_up_low], axis=-1)
        d_normed_two = scatter_tokens(contract_last(d_both, w_ffn))
        grad_down = lax.psum_scatter(
            low(contract_first(mixed_low, cotangent_all)), DATA, scatter_dimension=0, tiled=True
        ).astype(jnp.float32)
        grad_both = scatter_columns(contract_first(normed_two, d_both))
        grad_gate = join_units(grad_both[..., :units])
        grad_up = join_units(grad_both[..., units:])
        unused_two, norm_two_back = jax.vjp(root_mean_scale, middle, gain_ffn)
        d_middle_norm, grad_norm_two_term = norm_two_back(d_normed_two)
        d_middle = cotangent.astype(jnp.float32) + d_middle_norm

        branch_all = gather_tokens(low(d_middle))
        d_gated = contract_last(branch_all, w_out)
        grad_out = lax.psum_scatter(
            low(contract_first(gated_low, branch_all)), DATA, scatter_dimension=0, tiled=True
        )
        grad_out = lax.ppermute(grad_out, INNER, from_rank).astype(jnp.float32)
        d_attended = low(d_gated * gate_sig)
        d_gate_low = low(d_gated * attended_rows * gate_sig * (1.0 - gate_sig))
        d_heads = d_attended.reshape(groups, window, repeat, HEAD_SIZE)
        row_delta = jnp.transpose(
            jnp.sum(d_heads.astype(jnp.float32) * attended, axis=-1), (0, 2, 1)
        )
        d_probs = jnp.einsum(
            "gqrd,gkd->grqk", d_heads, values_all, preferred_element_type=jnp.float32
        )
        d_scores = low(probs * (d_probs - row_delta[..., None]))
        d_query_rot = (
            jnp.einsum("grqk,gkd->gqrd", d_scores, keys_all, preferred_element_type=jnp.float32)
            * scale_qk
        )
        d_keys = (
            jnp.einsum("grqk,gqrd->gkd", d_scores, query_low, preferred_element_type=jnp.float32)
            * scale_qk
        )
        d_values = jnp.einsum(
            "grqk,gqrd->gkd", probs_low, d_heads, preferred_element_type=jnp.float32
        )
        d_pair = low(jnp.concatenate([d_keys, d_values], axis=-1))
        d_pair = jnp.transpose(
            d_pair.reshape(groups, PLANES, window, 2 * HEAD_SIZE), (1, 0, 2, 3)
        )
        d_pair = lax.psum_scatter(d_pair, "z", scatter_dimension=0, tiled=True)
        d_pair = d_pair.reshape(groups, window, 2 * HEAD_SIZE).astype(jnp.float32)
        d_key_rot, d_value = d_pair[..., :HEAD_SIZE], d_pair[..., HEAD_SIZE:]
        unused_query, query_back = jax.vjp(prepare_heads, query_raw, gain_query)
        d_query_raw, grad_query_gain_term = query_back(d_query_rot)
        unused_key, key_back = jax.vjp(prepare_heads, key_raw, gain_key)
        d_key_raw, grad_key_gain_term = key_back(d_key_rot[:, :, None, :])
        d_raw = jnp.concatenate(
            [
                low(d_query_raw.reshape(tokens, query_columns)),
                low(d_key_raw.reshape(tokens, key_columns)),
                low(d_value.reshape(tokens, key_columns)),
                d_gate_low,
            ],
            axis=-1,
        )
        d_normed = scatter_tokens(contract_last(d_raw, w_attn))
        grad_attn = scatter_columns(contract_first(normed_input, d_raw))
        grad_query = join_columns(grad_attn[..., :a])
        grad_key = join_columns(grad_attn[..., a:b])
        grad_value = join_columns(grad_attn[..., b:c])
        grad_gatew = join_columns(grad_attn[..., c:])
        unused_one, norm_one_back = jax.vjp(root_mean_scale, hidden, gain_attn)
        d_hidden_norm, grad_norm_one_term = norm_one_back(d_normed)
        input_grad = d_middle + d_hidden_norm

        terms = jnp.concatenate(
            [
                t.reshape(RANKS * data_total, -1)
                for t in (
                    grad_norm_one_term,
                    grad_norm_two_term,
                    grad_query_gain_term,
                    grad_key_gain_term,
                )
            ],
            axis=-1,
        )
        small = lax.psum_scatter(terms, ALL, scatter_dimension=0, tiled=True).reshape(-1)
        grad_norm_attn, grad_norm_ffn, grad_query_gain, grad_key_gain = (
            small[s:e] for s, e in zip(cuts[:-1], cuts[1:])
        )
        return (
            output,
            input_grad,
            grad_query,
            grad_key,
            grad_value,
            grad_gatew,
            grad_out,
            grad_norm_attn,
            grad_query_gain,
            grad_key_gain,
            grad_norm_ffn,
            grad_gate,
            grad_up,
            grad_down,
        )

    return shards


def solution(mesh):
    cells = mesh.shape["fsdp"] // (PLANES * CORNERS)
    split = Mesh(
        mesh.devices.reshape(CORNERS, CORNERS, cells, PLANES, CORNERS),
        ALL,
    )
    rows, flat, group = P(ALL, None), P(ALL), P(("x", "core"))
    return jax.shard_map(
        make_shards(cells),
        mesh=split,
        in_specs=(rows,) * 6 + (flat,) * 4 + (rows,) * 4 + (group,) * 2,
        out_specs=(rows,) * 7 + (flat,) * 4 + (rows,) * 3,
        check_vma=False,
    )
```

time: 4130 us -> 1420 us (0.34)
  waiting for transfers between devices: 3540 us -> 815 us
  matrix products: 347 us -> 218 us
  blocking collectives: 87.1 us -> 162 us
    reduce_scatter x10 -> x9, waiting for transfers between devices: 2750 us -> 386 us  [the longest x4 182 us: scatter_tokens(): lax.psum_scatter(low(terms), TENSOR, scatter_dimension=0, tiled=True)]
    all_gather x10 -> x9, waiting for transfers between devices: 789 us -> 428 us  [the longest x4 210 us: gather_tokens(): return lax.all_gather(rows, TENSOR, axis=0, tiled=True)]
    all_to_all x0 -> x3, blocking collectives: none -> 73.2 us  [the longest x2 49.5 us: gather_columns(): mine = lax.all_to_all(sent, TENSOR, split_axis=0, concat_axis=0, tiled=True)]
    dot_general x8 -> x4, matrix products: 101 us -> 46.6 us  [contract_first(): lax.dot_general(left, right, (((0,), (0,)), ((), ())), preferred_element_...]
    dot_general x14 -> x5, matrix products: 104 us -> 49.5 us  [the longest x1 18.9 us: shards(): jnp.einsum('gqrd,gkd->grqk', d_heads, values_all, preferred_element_type=...]
  transfers between devices with their start and end apart: 20 -> 21, of which waited for: 19 -> 17; matrix products, arithmetic and copies ran while one was open for 7% -> 19% of each run, Pallas kernels for 0% -> 0%
where the time goes in v1:
time: 1420 us; the launch traced here: 1410 us
  waiting for transfers between devices  815 us (57%)
  matrix products  218 us (15%)
  blocking collectives  162 us (11%)
  local copies, waits for them, and re-layouts  109 us (8%)
  other arithmetic  81.4 us (6%)
  between operations  15.7 us (1%)
    all_gather x4, waiting for transfers between devices, gather_tokens(): return lax.all_gather(rows, TENSOR, axis=0, tiled=True)  210 us
    reduce_scatter x4, waiting for transfers between devices, scatter_tokens(): lax.psum_scatter(low(terms), TENSOR, scatter_dimension=0, tiled=True)  182 us
    all_gather x2, waiting for transfers between devices, gather_columns(): every = lax.all_gather(mine, DATA, axis=0, tiled=False)  124 us
    unnamed x2, blocking collectives  83.7 us
    reduce_scatter x2, waiting for transfers between devices, scatter_columns(): mine = lax.psum_scatter(split, DATA, scatter_dimension=0, tiled=True)  62.4 us
    reduce_scatter x1, waiting for transfers between devices, shards(): lax.psum_scatter(low(contract_first(mixed_low, cotangent_all)), DATA, sca...  58.9 us
    dot_general x4, matrix products, contract_last(): lax.dot_general(left, right, (((1,), (1,)), ((), ())), preferred_element_...  55.6 us
    reduce_scatter x1, waiting for transfers between devices, shards(): d_pair = lax.psum_scatter(d_pair, 'z', scatter_dimension=0, tiled=True)  55.3 us
  transfers between devices with their start and end apart: 21, of which 17 were waited for; matrix products, arithmetic and copies ran while one was open for 19% of the time, Pallas kernels for 0%

profile of v1, /device:TPU:0, one launch (start us, length us, event | category | flops | bytes accessed | tf_op | source)
XLA Modules:
  0.0 1408.2 jit_solution(437829805743148016)
XLA Ops:
  11.5 16.7 %all_to_all.20 = bf16[8,64,768]{2,1,0:T(8,128)(2,1)} all-to-all(bf16[8,64,768]{2,1,0:T(8,128)(2,1)S(1)} %copy.270), channel_id=1, replica_groups=mesh['x'=2,'core'=2,'cell'=1,'z'=4,'y'=2] {'x','core','y'}, dimensions={0} | all-to-all | bytes 1572864 | tf_op jit(solution)/shard_map/all_to_all | solution.py:89
  28.6 44.0 %all-reduce.4 = bf16[4352]{0:T(1024)(128)(2,1)S(1)} all-reduce(bf16[4352]{0:T(1024)(128)(2,1)S(1)} %dynamic-update-slice), channel_id=2, replica_groups=mesh['x'=2,'core'=2,'cell'=1,'z'=4,'y'=2] {'x','core','cell','z','y'}, use_global_device_ids=true, to_apply=%add.4 | all-reduce | flops 4352 | bytes 17408
  74.8 5.5 all-gather.5
  80.8 12.4 all-gather.28.cloned.1.call-done
  97.1 51.4 %all-gather.16.cloned.1.call-done = bf16[2048,2048]{1,0:T(8,128)(2,1)} async-done(((bf16[256,2048]{1,0:T(8,128)(2,1)}), bf16[2048,2048]{1,0:T(8,128)(2,1)}) %all-gather.16.cloned.1.call-update) | async-done | bytes 8388624 | tf_op jit(solution)/shard_map/all_gather | solution.py:63
  148.6 10.0 fusion.69
  164.1 5.8 fusion.44
  172.0 6.7 or_and_fusion
  203.9 48.0 %all-gather.30.cloned.1.call-done = bf16[16,512,256]{2,1,0:T(8,128)(2,1)} async-done(((bf16[4,512,256]{2,1,0:T(8,128)(2,1)}), bf16[16,512,256]{2,1,0:T(8,128)(2,1)}) %all-gather.30.cloned.1.call-update) | async-done | bytes 4194320 | tf_op jit(solution)/shard_map/all_gather | solution.py:196
  256.6 18.4 %fusion.68 = (f32[4,2,512]{2,1,0:T(2,128)S(1)}, f32[4,2,512,2048]{2,3,1,0:T(8,128)}) fusion(pred[4,512,2048]{1,2,0:T(8,128)(4,1)} %or_and_fusion, bf16[4,512,2,128]{1,3,2,0:T(8,128)(2,1)S(1)} %copy-done.28, bf16[4,2048,256]{2,1,0:T(8,128)(2,1)} %bitcast.225), kind=kOutput, calls=%fused_computation.172 | convolution fusion | flops 2181040128 | bytes 40910848 | tf_op jit(solution)/shard_map/sub | solution.py:208
  275.0 12.7 fusion.7
  287.7 5.8 copy-done
  302.3 7.2 convolution_convert_fusion.3
  321.4 32.8 %all_to_all.21 = bf16[8,64,1536]{2,1,0:T(8,128)(2,1)} all-to-all(bf16[8,64,1536]{2,1,0:T(8,128)(2,1)S(1)} %copy.284), channel_id=1, replica_groups=mesh['x'=2,'core'=2,'cell'=1,'z'=4,'y'=2] {'x','core','y'}, dimensions={0} | all-to-all | bytes 3145728 | tf_op jit(solution)/shard_map/all_to_all | solution.py:89
  354.4 33.2 %reduce-scatter.10.cloned.1.call-done = bf16[256,2048]{1,0:T(8,128)(2,1)} async-done(((bf16[2048,2048]{1,0:T(8,128)(2,1)}), bf16[256,2048]{1,0:T(8,128)(2,1)}) %reduce-scatter.10.cloned.1.call-update) | async-done | bytes 1048592 | tf_op jit(solution)/shard_map/reduce_scatter | solution.py:66
  393.4 111.1 %all-gather.32.cloned.1.call-done = bf16[32,64,1536]{2,1,0:T(8,128)(2,1)} async-done(((bf16[8,64,1536]{2,1,0:T(8,128)(2,1)}), bf16[32,64,1536]{2,1,0:T(8,128)(2,1)}) %all-gather.32.cloned.1.call-update) | async-done | bytes 6291472 | tf_op jit(solution)/shard_map/all_gather | solution.py:91
  504.4 6.0 copy.285
  510.5 49.2 %all-gather.20.cloned.1.call-done = bf16[2048,2048]{1,0:T(8,128)(2,1)} async-done(((bf16[256,2048]{1,0:T(8,128)(2,1)}), bf16[2048,2048]{1,0:T(8,128)(2,1)}) %all-gather.20.cloned.1.call-update) | async-done | bytes 8388624 | tf_op jit(solution)/shard_map/all_gather | solution.py:63
  559.7 19.4 %fusion.70 = f32[2048,1536]{0,1:T(8,128)} fusion(bf16[2048,2048]{1,0:T(8,128)(2,1)} %all-gather.20.cloned.1.call-done, bf16[2048,1536]{1,0:T(8,128)(2,1)} %bitcast.238), kind=kOutput, calls=%fused_computation.174 | convolution fusion | flops 12884901888 | bytes 27262976 | tf_op jit(solution)/shard_map/dot_general | solution.py:40
  579.2 45.7 %all-gather.22.cloned.1.call-done = bf16[768,2048]{1,0:T(8,128)(2,1)} async-done(((bf16[192,2048]{1,0:T(8,128)(2,1)}), bf16[768,2048]{1,0:T(8,128)(2,1)}) %all-gather.22.cloned.1.call-update) | async-done | bytes 3145744 | tf_op jit(solution)/shard_map/all_gather | solution.py:162
  624.9 55.1 %all-gather.24.cloned.1.call-done = bf16[2048,2048]{1,0:T(8,128)(2,1)} async-done(((bf16[256,2048]{1,0:T(8,128)(2,1)}), bf16[2048,2048]{1,0:T(8,128)(2,1)}) %all-gather.24.cloned.1.call-update) | async-done | bytes 8388624 | tf_op jit(solution)/shard_map/all_gather | solution.py:63
  680.0 18.5 %multiply_convert_fusion.1 = (bf16[2048,768]{0,1:T(8,128)(2,1)}, bf16[2048,768]{0,1:T(8,128)(2,1)}, bf16[2048,768]{0,1:T(8,128)(2,1)}) fusion(f32[2048,1536]{0,1:T(8,128)} %fusion.70, bf16[2048,2048]{1,0:T(8,128)(2,1)} %all-gather.24.cloned.1.call-done, bf16[768,2048]{1,0:T(8,128)(2,1)} %all-gather.22.cloned.1.call-done), kind=kOutput, calls=%fused_computation.20 | convolution fusion | flops 6467616768 | bytes 33554432 | tf_op jit(solution)/shard_map/dot_general | solution.py:44
  698.5 17.5 %convolution_convert_fusion.1 = bf16[2048,2048]{1,0:T(8,128)(2,1)} fusion(bf16[2048,1536]{1,0:T(8,128)(2,1)S(1)} %bitcast.239, bf16[2048,768]{0,1:T(8,128)(2,1)} %get-tuple-element.25, bf16[2048,768]{0,1:T(8,128)(2,1)} %get-tuple-element.24), kind=kOutput, calls=%fused_computation.14 | convolution fusion | flops 12901679104 | bytes 20971520 | tf_op jit(solution)/shard_map/dot_general | solution.py:44
  716.1 71.4 %reduce-scatter.14.cloned.1.call-done = bf16[256,2048]{1,0:T(8,128)(2,1)} async-done(((bf16[2048,2048]{1,0:T(8,128)(2,1)}), bf16[256,2048]{1,0:T(8,128)(2,1)}) %reduce-scatter.14.cloned.1.call-update) | async-done | bytes 1048592 | tf_op jit(solution)/shard_map/reduce_scatter | solution.py:66
  793.0 54.5 %all-gather.26.cloned.1.call-done = bf16[2048,2048]{1,0:T(8,128)(2,1)} async-done(((bf16[256,2048]{1,0:T(8,128)(2,1)}), bf16[2048,2048]{1,0:T(8,128)(2,1)}) %all-gather.26.cloned.1.call-update) | async-done | bytes 8388624 | tf_op jit(solution)/shard_map/all_gather | solution.py:63
  847.5 8.8 multiply_convert_fusion.3
  860.6 8.5 bitcast_convert_fusion
  869.1 18.9 %fusion.2 = bf16[4,2,512,2048]{2,3,1,0:T(8,128)(2,1)} fusion(bf16[4,512,2,128]{1,3,2,0:T(8,128)(2,1)S(1)} %copy.288, f32[4,2,512]{2,1,0:T(2,128)S(1)} %bitcast.274, f32[4,2,512,2048]{2,3,1,0:T(8,128)} %get-tuple-element.68, f32[4,2,512]{2,1,0:T(2,128)S(1)} %get-tuple-element.67, bf16[4,2048,256]{2,1,0:T(8,128)(2,1)S(1)} %bitcast.228), kind=kOutput, calls=%fused_computation.3 | convolution fusion | flops 2181038080 | bytes 53510144 | tf_op jit(solution)/shard_map/gqrd,gkd->grqk/dot_general | solution.py:254
  888.0 10.5 fusion.8
  900.9 18.3 %convolution_convert_fusion.4 = bf16[2048,1536]{1,0:T(8,128)(2,1)S(1)} fusion(bf16[2048,2048]{1,0:T(8,128)(2,1)} %all-gather.20.cloned.1.call-done, bf16[2048,768]{0,1:T(8,128)(2,1)} %get-tuple-element.25, bf16[2048,768]{0,1:T(8,128)(2,1)} %get-tuple-element.24), kind=kOutput, calls=%fused_computation.17 | convolution fusion | flops 12900630528 | bytes 20971520 | tf_op jit(solution)/shard_map/dot_general | solution.py:50
  922.6 55.3 %reduce-scatter.16.cloned.1.call-done = bf16[1,4,512,256]{3,2,1,0:T(8,128)(2,1)} async-done(((bf16[4,4,512,256]{3,2,1,0:T(8,128)(2,1)}), bf16[1,4,512,256]{3,2,1,0:T(8,128)(2,1)}) %reduce-scatter.16.cloned.1.call-update) | async-done | bytes 1048592 | tf_op jit(solution)/shard_map/reduce_scatter | solution.py:273
  979.7 5.9 broadcast_multiply_fusion.1
  988.8 9.1 bitcast_multiply_fusion.3
  1006.9 5.7 multiply_reduce_fusion.5
  1014.4 9.7 convolution_convert_fusion.6
  1026.1 11.9 convolution_convert_fusion.5
  1039.3 6.7 convolution_convert_fusion.7
  1046.1 10.8 convolution_convert_fusion
  1057.0 11.4 convolution_convert_fusion.2
  1068.4 23.1 %reduce-scatter.24.cloned.1.call-done = bf16[8,64,1536]{2,1,0:T(8,128)(2,1)} async-done(((bf16[32,64,1536]{2,1,0:T(8,128)(2,1)}), bf16[8,64,1536]{2,1,0:T(8,128)(2,1)}) %reduce-scatter.24.cloned.1.call-update) | async-done | bytes 1572880 | tf_op jit(solution)/shard_map/reduce_scatter | solution.py:99
  1091.5 23.7 %all_to_all.22 = bf16[8,64,1536]{2,1,0:T(8,128)(2,1)S(1)} all-to-all(bf16[8,64,1536]{2,1,0:T(8,128)(2,1)} %reduce-scatter.24.cloned.1.call-done), channel_id=1, replica_groups=mesh['x'=2,'core'=2,'cell'=1,'z'=4,'y'=2] {'x','core','y'}, dimensions={0} | all-to-all | bytes 3145728 | tf_op jit(solution)/shard_map/all_to_all | solution.py:100
  1115.2 39.3 %reduce-scatter.20.cloned.1.call-done = bf16[8,64,768]{2,1,0:T(8,128)(2,1)} async-done(((bf16[32,64,768]{2,1,0:T(8,128)(2,1)}), bf16[8,64,768]{2,1,0:T(8,128)(2,1)}) %reduce-scatter.20.cloned.1.call-update) | async-done | bytes 786448 | tf_op jit(solution)/shard_map/reduce_scatter | solution.py:99
  1158.2 58.9 %reduce-scatter.26.cloned.1.call-done = bf16[192,2048]{1,0:T(8,128)(2,1)} async-done(((bf16[768,2048]{1,0:T(8,128)(2,1)}), bf16[192,2048]{1,0:T(8,128)(2,1)}) %reduce-scatter.26.cloned.1.call-update) | async-done | bytes 786448 | tf_op jit(solution)/shard_map/reduce_scatter | solution.py:232
  1219.7 27.5 %reduce-scatter.22.cloned.1.call-done = bf16[64,2048]{1,0:T(8,128)(2,1)} async-done(((bf16[256,2048]{1,0:T(8,128)(2,1)}), bf16[64,2048]{1,0:T(8,128)(2,1)}) %reduce-scatter.22.cloned.1.call-update) | async-done | bytes 262160 | tf_op jit(solution)/shard_map/reduce_scatter | solution.py:244
  1275.6 44.9 %reduce-scatter.18.cloned.1.call-done = bf16[256,2048]{1,0:T(8,128)(2,1)} async-done(((bf16[2048,2048]{1,0:T(8,128)(2,1)}), bf16[256,2048]{1,0:T(8,128)(2,1)}) %reduce-scatter.18.cloned.1.call-update) | async-done | bytes 1048592 | tf_op jit(solution)/shard_map/reduce_scatter | solution.py:66
  1322.8 39.7 %all-reduce.5 = f32[32,136]{1,0:T(8,128)S(1)} all-reduce(f32[32,136]{1,0:T(8,128)S(1)} %pad_maximum_fusion.9), channel_id=14, replica_groups=mesh['x'=2,'core'=2,'cell'=1,'z'=4,'y'=2] {'x','core','cell','z','y'}, use_global_device_ids=true, to_apply=%region_22.23.clone | all-reduce | flops 4352 | bytes 34816
  1363.8 32.3 %reduce-scatter.12.cloned.1.call-done = bf16[256,2048]{1,0:T(8,128)(2,1)} async-done(((bf16[2048,2048]{1,0:T(8,128)(2,1)}), bf16[256,2048]{1,0:T(8,128)(2,1)}) %reduce-scatter.12.cloned.1.call-update) | async-done | bytes 1048592 | tf_op jit(solution)/shard_map/reduce_scatter | solution.py:66
  1396.1 5.1 fusion.21
  (284 shorter events, 147.5 us)
Async XLA Ops:
  7.2 86.0 %all-gather.28.cloned.1.call-start = ((), (), s32[]{:S(2)}) async-start(), calls=%async_computation.28 | async-start | bytes 3932160 | tf_op jit(solution)/shard_map/all_gather | solution.py:91
  9.2 19.1 %copy-start.59 = (bf16[4]{0:T(256)(128)(2,1)S(1)}, bf16[4]{0:T(256)(128)(2,1)}, u32[]{:S(2)}) copy-start(bf16[4]{0:T(256)(128)(2,1)} %param.24) | copy-start | bytes 28
  9.2 19.1 %copy-start.60 = (bf16[4]{0:T(256)(128)(2,1)S(1)}, bf16[4]{0:T(256)(128)(2,1)}, u32[]{:S(2)}) copy-start(bf16[4]{0:T(256)(128)(2,1)} %param.23) | copy-start | bytes 28
  9.3 19.1 %copy-start.61 = (bf16[64]{0:T(256)(128)(2,1)S(1)}, bf16[64]{0:T(256)(128)(2,1)}, u32[]{:S(2)}) copy-start(bf16[64]{0:T(256)(128)(2,1)} %param.25) | copy-start | bytes 388
  9.3 19.1 %copy-start.62 = (bf16[64]{0:T(256)(128)(2,1)S(1)}, bf16[64]{0:T(256)(128)(2,1)}, u32[]{:S(2)}) copy-start(bf16[64]{0:T(256)(128)(2,1)} %param.22) | copy-start | bytes 388
  9.3 63.6 %copy-start.1 = (bf16[256,2048]{1,0:T(8,128)(2,1)S(1)}, bf16[256,2048]{1,0:T(8,128)(2,1)}, u32[]{:S(2)}) copy-start(bf16[256,2048]{1,0:T(8,128)(2,1)} %param.16) | copy-start | bytes 3145732
  11.5 63.3 %copy-start.57 = (s32[2048]{0:T(1024)S(1)}, s32[2048]{0:T(1024)}, u32[]{:S(2)}) copy-start(s32[2048]{0:T(1024)} %param.31) | copy-start | bytes 24580
  11.5 63.3 %copy-start.58 = (s32[2048]{0:T(1024)S(1)}, s32[2048]{0:T(1024)}, u32[]{:S(2)}) copy-start(s32[2048]{0:T(1024)} %param.30) | copy-start | bytes 24580
  28.2 120.3 %all-gather.16.cloned.1.call-start = ((), (), s32[]{:S(2)}) async-start(), calls=%async_computation.13 | async-start | bytes 9437184 | tf_op jit(solution)/shard_map/all_gather | solution.py:63
  74.5 177.5 %all-gather.30.cloned.1.call-start = ((), (), s32[]{:S(2)}) async-start(), calls=%async_computation.29 | async-start | bytes 5242880 | tf_op jit(solution)/shard_map/all_gather | solution.py:196
  74.7 89.4 %copy-start.49 = (f32[128]{0:T(128)}, f32[128]{0:T(128)S(1)}, u32[]{:S(2)}) copy-start(f32[128]{0:T(128)S(1)} %mul.456) | copy-start | bytes 1540
  80.8 83.4 %copy-start.12 = (f32[4,512,64]{2,1,0:T(8,128)}, f32[4,512,64]{2,1,0:T(8,128)S(1)}, u32[]{:S(2)}) copy-start(f32[4,512,64]{2,1,0:T(8,128)S(1)} %broadcast_multiply_fusion.2) | copy-start | bytes 1572868
  171.1 131.3 %all-gather.18.cloned.1.call-start = ((), (), s32[]{:S(2)}) async-start(), calls=%async_computation.14 | async-start | bytes 1310720 | tf_op jit(solution)/shard_map/all_gather | solution.py:158
  171.1 7.7 collective-permute-start
  178.8 22.1 %copy-start.51 = (f32[128]{0:T(128)}, f32[128]{0:T(128)S(1)}, u32[]{:S(2)}) copy-start(f32[128]{0:T(128)S(1)} %mul.474) | copy-start | bytes 1540
  179.5 208.0 %reduce-scatter.10.cloned.1.call-start = ((), (), s32[]{:S(2)}) async-start(), calls=%async_computation.15 | async-start | bytes 9437184 | tf_op jit(solution)/shard_map/reduce_scatter | solution.py:66
  275.0 18.5 %copy-start.10 = (bf16[4,4,512,256]{3,2,0,1:T(8,128)(2,1)S(1)}, bf16[4,4,512,256]{3,2,0,1:T(8,128)(2,1)}, u32[]{:S(2)}) copy-start(bf16[4,4,512,256]{3,2,0,1:T(8,128)(2,1)} %copy.272) | copy-start | bytes 12582916
  309.5 194.9 %all-gather.32.cloned.1.call-start = ((), (), s32[]{:S(2)}) async-start(), calls=%async_computation.30 | async-start | bytes 7864320 | tf_op jit(solution)/shard_map/all_gather | solution.py:91
  354.2 205.5 %all-gather.20.cloned.1.call-start = ((), (), s32[]{:S(2)}) async-start(), calls=%async_computation.16 | async-start | bytes 9437184 | tf_op jit(solution)/shard_map/all_gather | solution.py:63
  354.4 436.0 %copy-start.36 = (f32[2048]{0:T(1024)}, f32[2048]{0:T(1024)S(1)}, u32[]{:S(2)}) copy-start(f32[2048]{0:T(1024)S(1)} %mul.488) | copy-start | bytes 24580
  389.2 401.2 %copy-start.45 = (f32[256]{0:T(256)}, f32[256]{0:T(256)S(1)}, u32[]{:S(2)}) copy-start(f32[256]{0:T(256)S(1)} %fusion.50) | copy-start | bytes 3076
  391.8 233.1 %all-gather.22.cloned.1.call-start = ((), (), s32[]{:S(2)}) async-start(), calls=%async_computation.17 | async-start | bytes 3932160 | tf_op jit(solution)/shard_map/all_gather | solution.py:162
  392.6 287.4 %all-gather.24.cloned.1.call-start = ((), (), s32[]{:S(2)}) async-start(), calls=%async_computation.19 | async-start | bytes 9437184 | tf_op jit(solution)/shard_map/all_gather | solution.py:63
  393.3 394.2 %reduce-scatter.14.cloned.1.call-start = ((), (), s32[]{:S(2)}) async-start(), calls=%async_computation.20 | async-start | bytes 9437184 | tf_op jit(solution)/shard_map/reduce_scatter | solution.py:66
  680.0 18.5 %copy-start.21 = (bf16[4,4,2,64,1536]{4,3,2,1,0:T(8,128)(2,1)S(1)}, bf16[4,4,2,64,1536]{4,3,2,1,0:T(8,128)(2,1)}, u32[]{:S(2)}) copy-start(bf16[4,4,2,64,1536]{4,3,2,1,0:T(8,128)(2,1)} %copy.285) | copy-start | bytes 18874372
  716.0 71.5 %copy-start.5 = (bf16[256,2048]{1,0:T(8,128)(2,1)S(1)}, bf16[256,2048]{1,0:T(8,128)(2,1)}, u32[]{:S(2)}) copy-start(bf16[256,2048]{1,0:T(8,128)(2,1)} %reduce-scatter.10.cloned.1.call-done) | copy-start | bytes 3145732
  716.0 74.9 %copy-start.16 = (bf16[256,2048]{1,0:T(8,128)(2,1)S(1)}, bf16[256,2048]{1,0:T(8,128)(2,1)}, u32[]{:S(2)}) copy-start(bf16[256,2048]{1,0:T(8,128)(2,1)} %param.29) | copy-start | bytes 3145732
  716.1 131.4 %all-gather.26.cloned.1.call-start = ((), (), s32[]{:S(2)}) async-start(), calls=%async_computation.21 | async-start | bytes 9437184 | tf_op jit(solution)/shard_map/all_gather | solution.py:63
  793.0 184.9 %reduce-scatter.16.cloned.1.call-start = ((), (), s32[]{:S(2)}) async-start(), calls=%async_computation.22 | async-start | bytes 5242880 | tf_op jit(solution)/shard_map/reduce_scatter | solution.py:273
  900.9 190.6 %reduce-scatter.24.cloned.1.call-start = ((), (), s32[]{:S(2)}) async-start(), calls=%async_computation.26 | async-start | bytes 7864320 | tf_op jit(solution)/shard_map/reduce_scatter | solution.py:99
  922.5 57.2 %copy-start.13 = (f32[4,512,64]{2,1,0:T(8,128)S(1)}, f32[4,512,64]{2,1,0:T(8,128)}, u32[]{:S(2)}) copy-start(f32[4,512,64]{2,1,0:T(8,128)} %copy-done.12) | copy-start | bytes 1572868
  922.5 232.1 %reduce-scatter.20.cloned.1.call-start = ((), (), s32[]{:S(2)}) async-start(), calls=%async_computation.24 | async-start | bytes 3932160 | tf_op jit(solution)/shard_map/reduce_scatter | solution.py:99
  1026.1 191.1 %reduce-scatter.26.cloned.1.call-start = ((), (), s32[]{:S(2)}) async-start(), calls=%async_computation.27 | async-start | bytes 3932160 | tf_op jit(solution)/shard_map/reduce_scatter | solution.py:232
  1038.1 209.1 %reduce-scatter.22.cloned.1.call-start = ((), (), s32[]{:S(2)}) async-start(), calls=%async_computation.25 | async-start | bytes 1310720 | tf_op jit(solution)/shard_map/reduce_scatter | solution.py:244
  1046.0 274.4 %reduce-scatter.18.cloned.1.call-start = ((), (), s32[]{:S(2)}) async-start(), calls=%async_computation.23 | async-start | bytes 9437184 | tf_op jit(solution)/shard_map/reduce_scatter | solution.py:66
  1056.9 339.1 %reduce-scatter.12.cloned.1.call-start = ((), (), s32[]{:S(2)}) async-start(), calls=%async_computation.18 | async-start | bytes 9437184 | tf_op jit(solution)/shard_map/reduce_scatter | solution.py:66
  1068.4 151.2 %copy-start.44 = (f32[2048]{0:T(1024)S(1)}, f32[2048]{0:T(1024)}, u32[]{:S(2)}) copy-start(f32[2048]{0:T(1024)} %get-tuple-element.16) | copy-start | bytes 24580
  1154.6 117.5 %all-to-all-start.2 = ((bf16[8,64,768]{2,1,0:T(8,128)(2,1)}), bf16[8,64,768]{2,1,0:T(8,128)(2,1)S(1)}, u32[]{:S(2)}, u32[]{:S(2)}) async-start(bf16[8,64,768]{2,1,0:T(8,128)(2,1)} %reduce-scatter.20.cloned.1.call-done), calls=%async_computation.8 | async-start | bytes 1572864 | tf_op jit(solution)/shard_map/all_to_all | solution.py:100
  1247.2 23.8 %collective-permute-start.1 = (bf16[64,2048]{1,0:T(8,128)(2,1)}, bf16[64,2048]{1,0:T(8,128)(2,1)S(1)}, u32[]{:S(2)}, u32[]{:S(2)}) collective-permute-start(bf16[64,2048]{1,0:T(8,128)(2,1)} %reduce-scatter.22.cloned.1.call-done), channel_id=1, source_target_pairs={{0,0},{2,1},{4,2},{6,3},{1,4},{3,5},{5,6},{7,7},{8,8},{10,9},{12,1... | collective-permute-start | bytes 786440 | tf_op jit(solution)/shard_map/ppermute | solution.py:247
  1272.2 48.2 %copy-start.2 = (bf16[256,2048]{1,0:T(8,128)(2,1)S(1)}, bf16[256,2048]{1,0:T(8,128)(2,1)}, u32[]{:S(2)}) copy-start(bf16[256,2048]{1,0:T(8,128)(2,1)} %param.16) | copy-start | bytes 3145732
  1272.2 48.2 %copy-start.41 = (f32[2048]{0:T(1024)S(1)}, f32[2048]{0:T(1024)}, u32[]{:S(2)}) copy-start(f32[2048]{0:T(1024)} %copy-done.40) | copy-start | bytes 24580
  1272.2 48.2 %copy-start.48 = (f32[256]{0:T(256)S(1)}, f32[256]{0:T(256)}, u32[]{:S(2)}) copy-start(f32[256]{0:T(256)} %copy-done.47) | copy-start | bytes 3076
  1272.3 91.4 %copy-start.56 = (f32[256]{0:T(256)S(1)}, f32[256]{0:T(256)}, u32[]{:S(2)}) copy-start(f32[256]{0:T(256)} %copy-done.55) | copy-start | bytes 3076
  1272.3 123.7 %copy-start.6 = (bf16[256,2048]{1,0:T(8,128)(2,1)S(1)}, bf16[256,2048]{1,0:T(8,128)(2,1)}, u32[]{:S(2)}) copy-start(bf16[256,2048]{1,0:T(8,128)(2,1)} %reduce-scatter.10.cloned.1.call-done) | copy-start | bytes 3145732
  1272.3 123.7 %copy-start.17 = (bf16[256,2048]{1,0:T(8,128)(2,1)S(1)}, bf16[256,2048]{1,0:T(8,128)(2,1)}, u32[]{:S(2)}) copy-start(bf16[256,2048]{1,0:T(8,128)(2,1)} %param.29) | copy-start | bytes 3145732
  1272.3 123.7 %copy-start.37 = (f32[2048]{0:T(1024)S(1)}, f32[2048]{0:T(1024)}, u32[]{:S(2)}) copy-start(f32[2048]{0:T(1024)} %copy-done.36) | copy-start | bytes 24580
  1272.3 123.7 %copy-start.46 = (f32[256]{0:T(256)S(1)}, f32[256]{0:T(256)}, u32[]{:S(2)}) copy-start(f32[256]{0:T(256)} %copy-done.45) | copy-start | bytes 3076
  1272.4 123.7 %copy-start.54 = (f32[256]{0:T(256)S(1)}, f32[256]{0:T(256)}, u32[]{:S(2)}) copy-start(f32[256]{0:T(256)} %copy-done.53) | copy-start | bytes 3076
  (38 other events, 128.6 us)
Sparse Core Ops, SparseCore 0:
  28.4 64.7 all-gather.27
  95.6 52.8 all-gather.15
  171.2 80.7 all-gather.29
  254.0 27.4 all-gather.17
  309.7 77.8 reduce-scatter.9
  389.1 115.3 all-gather.31
  507.1 52.6 all-gather.19
  561.3 63.4 all-gather.21
  626.9 53.0 all-gather.23
  716.2 71.2 reduce-scatter.13
  793.1 54.3 all-gather.25
  901.0 76.7 reduce-scatter.15
  980.2 111.2 reduce-scatter.23
  1093.8 60.7 reduce-scatter.19
  1156.8 60.2 reduce-scatter.25
  1220.0 27.1 reduce-scatter.21
  1250.5 69.8 reduce-scatter.17
  1324.1 71.8 reduce-scatter.11

commit v2 on v1

--- a/solution.py
+++ b/solution.py
@@ -1,8 +1,11 @@
+import functools
 import math
 
 import jax
 import jax.numpy as jnp
 from jax import lax
+from jax.experimental import pallas as pl
+from jax.experimental.pallas import tpu as pltpu
 from jax.sharding import Mesh
 from jax.sharding import PartitionSpec as P
 
@@ -16,6 +19,498 @@
 TENSOR = ("x", "core", "y")
 DATA = ("cell", "z")
 RANKS = CORNERS**3
+CHUNKS = 4
+MESH_ID = pl.DeviceIdType.MESH
+
+
+def remote(source, target, send, receive, device):
+    return pltpu.make_async_remote_copy(src_ref=source, dst_ref=target, send_sem=send, recv_sem=receive,
+        device_id=device, device_id_type=MESH_ID)
+
+def greet(devices):
+    barrier = pltpu.get_barrier_semaphore()
+    for device in devices:
+        pl.semaphore_signal(barrier, inc=1, device_id=device, device_id_type=MESH_ID)
+    pl.semaphore_wait(barrier, len(devices))
+
+def corner():
+    x, c, y = lax.axis_index("x"), lax.axis_index("core"), lax.axis_index("y")
+    return x, c, y, {"x": 1 - x}, {"y": 1 - y}, {"core": 1 - c}
+
+def slot(x, c, y):
+    return (x * 2 + c) * 2 + y
+
+def gather_kernel(rows, in_ref, out_ref, send_x, send_y, send_c, recv_x, recv_y, recv_c, local):
+    x, c, y, dev_x, dev_y, dev_c = corner()
+    chunk = rows // CHUNKS
+    def at(index, k):
+        return out_ref.at[pl.ds(pl.multiple_of(index * rows + k * chunk, chunk), chunk), :]
+    own, beside_x, beside_y = slot(x, c, y), slot(1 - x, c, y), slot(x, c, 1 - y)
+    across = slot(1 - x, c, 1 - y)
+    mirror = [slot(x, 1 - c, y), slot(1 - x, 1 - c, y), slot(x, 1 - c, 1 - y), slot(1 - x, 1 - c, 1 - y)]
+    greet([dev_x, dev_y, dev_c])
+    keep = pltpu.make_async_copy(in_ref, out_ref.at[pl.ds(pl.multiple_of(own * rows, rows), rows), :], local)
+    keep.start()
+    sent = []
+    def go(copy):
+        copy.start(); sent.append(copy)
+    half = CHUNKS // 2
+    order_x = list(range(CHUNKS)); order_y = order_x[half:] + order_x[:half]
+    def mine(k):
+        return in_ref.at[pl.ds(k * chunk, chunk), :]
+    for i in range(CHUNKS):
+        k = order_x[i]; go(remote(mine(k), at(own, k), send_x.at[k], recv_x.at[k], dev_x))
+        k = order_y[i]; go(remote(mine(k), at(own, k), send_y.at[k], recv_y.at[k], dev_y))
+    for k in range(CHUNKS):
+        go(remote(mine(k), at(own, k), send_c.at[k], recv_c.at[k], dev_c))
+    def landed(index, k, sem, device):
+        remote(at(index, k), at(index, k), sem, sem, device).wait_recv()
+    for i in range(CHUNKS):
+        k = order_x[i]
+        landed(beside_x, k, recv_x.at[k], dev_x)
+        if k < half:
+            go(remote(at(beside_x, k), at(beside_x, k), send_y.at[CHUNKS + k], recv_y.at[CHUNKS + k], dev_y))
+        go(remote(at(beside_x, k), at(beside_x, k), send_c.at[CHUNKS + k], recv_c.at[CHUNKS + k], dev_c))
+        k = order_y[i]
+        landed(beside_y, k, recv_y.at[k], dev_y)
+        if k >= half:
+            go(remote(at(beside_y, k), at(beside_y, k), send_x.at[half + k], recv_x.at[half + k], dev_x))
+        go(remote(at(beside_y, k), at(beside_y, k), send_c.at[2 * CHUNKS + k], recv_c.at[2 * CHUNKS + k], dev_c))
+    for i in range(half):
+        k = i
+        landed(across, k, recv_y.at[CHUNKS + k], dev_y)
+        go(remote(at(across, k), at(across, k), send_c.at[3 * CHUNKS + k], recv_c.at[3 * CHUNKS + k], dev_c))
+        k = half + i
+        landed(across, k, recv_x.at[half + k], dev_x)
+        go(remote(at(across, k), at(across, k), send_c.at[3 * CHUNKS + k], recv_c.at[3 * CHUNKS + k], dev_c))
+    for b in range(4):
+        for k in range(CHUNKS):
+            landed(mirror[b], k, recv_c.at[b * CHUNKS + k], dev_c)
+    for copy in sent:
+        copy.wait_send()
+    keep.wait()
+
+def gather_tokens(block):
+    rows, columns = block.shape
+    dma = pltpu.SemaphoreType.DMA
+    n = CHUNKS
+    return pl.pallas_call(
+        functools.partial(gather_kernel, rows),
+        out_shape=jax.ShapeDtypeStruct((8 * rows, columns), block.dtype),
+        in_specs=[pl.BlockSpec(memory_space=pltpu.VMEM)],
+        out_specs=pl.BlockSpec(memory_space=pl.ANY),
+        scratch_shapes=[dma((n + n // 2,)), dma((n + n // 2,)), dma((4 * n,)), dma((n + n // 2,)), dma((n + n // 2,)), dma((4 * n,)), dma(())],
+        compiler_params=pltpu.CompilerParams(collective_id=0, has_side_effects=True),
+    )(block)
+
+def scatter_kernel(rows, part_ref, out_ref, core_buf, x_buf, y_buf, x_diag, y_diag, d_sum, x_sum, y_sum,
+                   send_c, recv_c, send_x, recv_x, send_y, recv_y):
+    x, c, y, dev_x, dev_y, dev_c = corner()
+    chunk = rows // CHUNKS
+    half = CHUNKS // 2
+    D, X, Y, O = range(4)
+    place = [(1 - x, 1 - y), (1 - x, y), (x, 1 - y), (x, y)]
+    mine = [slot(px, c, py) for px, py in place]
+    theirs = [slot(px, 1 - c, py) for px, py in place]
+    f32 = jnp.float32
+    columns = out_ref.shape[1]
+    def piece(k):
+        return pl.ds(k * chunk, chunk)
+    greet([dev_x, dev_y, dev_c])
+    sent = []
+    def go(copy):
+        copy.start(); sent.append(copy)
+    orders = {D: [0, 2, 1, 3], X: [0, 1, 2, 3], Y: [2, 3, 0, 1], O: [0, 1, 2, 3]}
+    orders = orders if CHUNKS == 4 else {b: list(range(CHUNKS)) for b in range(4)}
+    for b in (D, X, Y, O):
+        for k in orders[b]:
+            go(remote(part_ref.at[theirs[b], piece(k), :], core_buf.at[b, piece(k), :], send_c.at[b * CHUNKS + k], recv_c.at[b * CHUNKS + k], dev_c))
+    def got(ref, sem, device):
+        remote(ref, ref, sem, sem, device).wait_recv()
+    step = 16
+    def total(target, k, *sources, dtype):
+        def body(i, carry):
+            r = pl.multiple_of(k * chunk + i * step, step)
+            acc = None
+            for source in sources:
+                v = source(r).astype(f32)
+                acc = v if acc is None else acc + v
+            target[pl.ds(r, step), :] = acc.astype(dtype)
+            return carry
+        lax.fori_loop(0, chunk // step, body, 0)
+    def own_part(b):
+        return lambda r: part_ref[mine[b], pl.ds(r, step), :]
+    def core_part(b):
+        return lambda r: core_buf[b, pl.ds(r, step), :]
+    def from_(ref, shift=0):
+        return lambda r: ref[pl.ds(r - shift if shift else r, step), :]
+    bf = jnp.bfloat16
+    for k in orders[D]:
+        got(core_buf.at[D, piece(k), :], recv_c.at[D * CHUNKS + k], dev_c)
+        total(d_sum, k, own_part(D), core_part(D), dtype=bf)
+        if k < half:
+            go(remote(d_sum.at[piece(k), :], x_diag.at[pl.ds(k * chunk, chunk), :], send_x.at[CHUNKS + k], recv_x.at[CHUNKS + k], dev_x))
+        else:
+            go(remote(d_sum.at[piece(k), :], y_diag.at[pl.ds((k - half) * chunk, chunk), :], send_y.at[half + k], recv_y.at[half + k], dev_y))
+    for i in range(half):
+        k = i
+        got(core_buf.at[X, piece(k), :], recv_c.at[X * CHUNKS + k], dev_c)
+        total(x_sum, k, own_part(X), core_part(X), dtype=bf)
+        go(remote(x_sum.at[piece(k), :], x_buf.at[piece(k), :], send_x.at[k], recv_x.at[k], dev_x))
+        k = half + i
+        got(core_buf.at[Y, piece(k), :], recv_c.at[Y * CHUNKS + k], dev_c)
+        total(y_sum, k, own_part(Y), core_part(Y), dtype=bf)
+        go(remote(y_sum.at[piece(k), :], y_buf.at[piece(k), :], send_y.at[k], recv_y.at[k], dev_y))
+    for i in range(half):
+        k = half + i
+        got(core_buf.at[X, piece(k), :], recv_c.at[X * CHUNKS + k], dev_c)
+        got(y_diag.at[pl.ds(i * chunk, chunk), :], recv_y.at[half + k], dev_y)
+        total(x_sum, k, own_part(X), core_part(X), from_(y_diag, half * chunk), dtype=bf)
+        go(remote(x_sum.at[piece(k), :], x_buf.at[piece(k), :], send_x.at[k], recv_x.at[k], dev_x))
+        k = i
+        got(core_buf.at[Y, piece(k), :], recv_c.at[Y * CHUNKS + k], dev_c)
+        got(x_diag.at[pl.ds(i * chunk, chunk), :], recv_x.at[CHUNKS + k], dev_x)
+        total(y_sum, k, own_part(Y), core_part(Y), from_(x_diag), dtype=bf)
+        go(remote(y_sum.at[piece(k), :], y_buf.at[piece(k), :], send_y.at[k], recv_y.at[k], dev_y))
+    for k in range(CHUNKS):
+        got(core_buf.at[O, piece(k), :], recv_c.at[O * CHUNKS + k], dev_c)
+        got(x_buf.at[piece(k), :], recv_x.at[k], dev_x)
+        got(y_buf.at[piece(k), :], recv_y.at[k], dev_y)
+        total(out_ref, k, own_part(O), core_part(O), from_(x_buf), from_(y_buf), dtype=out_ref.dtype)
+    for copy in sent:
+        copy.wait_send()
+
+def scatter_blocks(terms):
+    ranks, rows, columns = terms.shape
+    dma = pltpu.SemaphoreType.DMA
+    n = CHUNKS
+    vm = lambda *s: pltpu.VMEM(s, jnp.bfloat16)
+    return pl.pallas_call(
+        functools.partial(scatter_kernel, rows),
+        out_shape=jax.ShapeDtypeStruct((rows, columns), jnp.float32),
+        in_specs=[pl.BlockSpec(memory_space=pltpu.VMEM)],
+        out_specs=pl.BlockSpec(memory_space=pltpu.VMEM),
+        scratch_shapes=[vm(4, rows, columns), vm(rows, columns), vm(rows, columns), vm(rows // 2, columns), vm(rows // 2, columns),
+            vm(rows, columns), vm(rows, columns), vm(rows, columns),
+            dma((4 * n,)), dma((4 * n,)), dma((n + n // 2,)), dma((n + n // 2,)), dma((n + n // 2,)), dma((n + n // 2,))],
+        compiler_params=pltpu.CompilerParams(collective_id=1, has_side_effects=True, vmem_limit_bytes=40 << 20),
+    )(terms)
+
+OTHERS = [(dx, dc, dy) for dx in (0, 1) for dc in (0, 1) for dy in (0, 1) if dx + dc + dy]
+
+def flip(value, bit):
+    return 1 - value if bit else value
+
+def hello_kernel(total, gains_ref, marks_ref, weight_ref, gains_out, marks_out, weight_out,
+                 gain_send, gain_recv, mark_send, mark_recv, weight_send, weight_recv, local):
+    x, c, y, dev_x, dev_y, dev_c = corner()
+    me, device = everyone(total)
+    own = slot(x, c, y)
+    group = x * 2 + c
+    keeps = [
+        pltpu.make_async_copy(gains_ref, gains_out.at[me], local.at[0]),
+        pltpu.make_async_copy(marks_ref, marks_out.at[group], local.at[1]),
+        pltpu.make_async_copy(weight_ref.at[own], weight_out.at[own], local.at[2]),
+    ]
+    for keep in keeps:
+        keep.start()
+    sent = []
+    for i, (dx, dc, dy) in enumerate(OTHERS):
+        there = {"x": flip(x, dx), "core": flip(c, dc), "y": flip(y, dy)}
+        other = slot(flip(x, dx), flip(c, dc), flip(y, dy))
+        copy = remote(weight_ref.at[other], weight_out.at[own], weight_send.at[i], weight_recv.at[i], there)
+        copy.start(); sent.append(copy)
+        if not dy:
+            copy = remote(marks_ref, marks_out.at[group], mark_send.at[i], mark_recv.at[i], there)
+            copy.start(); sent.append(copy)
+    def send_gain(d, carry):
+        remote(gains_ref, gains_out.at[me], gain_send.at[d], gain_recv.at[d], device(lax.rem(me + d, total))).start()
+        return carry
+    lax.fori_loop(1, total, send_gain, 0)
+    def take_gain(d, carry):
+        source = lax.rem(me + total - d, total)
+        remote(gains_out.at[source], gains_out.at[source], gain_recv.at[d], gain_recv.at[d], device(source)).wait_recv()
+        remote(gains_ref, gains_out.at[me], gain_send.at[d], gain_recv.at[d], device(lax.rem(me + d, total))).wait_send()
+        return carry
+    lax.fori_loop(1, total, take_gain, 0)
+    for i, (dx, dc, dy) in enumerate(OTHERS):
+        there = {"x": flip(x, dx), "core": flip(c, dc), "y": flip(y, dy)}
+        other = slot(flip(x, dx), flip(c, dc), flip(y, dy))
+        remote(weight_out.at[other], weight_out.at[other], weight_recv.at[i], weight_recv.at[i], there).wait_recv()
+        if not dy:
+            theirs = flip(x, dx) * 2 + flip(c, dc)
+            remote(marks_out.at[theirs], marks_out.at[theirs], mark_recv.at[i], mark_recv.at[i], there).wait_recv()
+    for copy in sent:
+        copy.wait_send()
+    for keep in keeps:
+        keep.wait()
+
+def hello(total, gains, marks, weight, collective_id):
+    dma = pltpu.SemaphoreType.DMA
+    vmem, anyspace = pl.BlockSpec(memory_space=pltpu.VMEM), pl.BlockSpec(memory_space=pl.ANY)
+    n = len(OTHERS)
+    return pl.pallas_call(
+        functools.partial(hello_kernel, total),
+        out_shape=[jax.ShapeDtypeStruct((total,) + gains.shape, gains.dtype),
+                   jax.ShapeDtypeStruct((4,) + marks.shape, marks.dtype),
+                   jax.ShapeDtypeStruct(weight.shape, weight.dtype)],
+        in_specs=[vmem, vmem, vmem], out_specs=[vmem, vmem, anyspace],
+        scratch_shapes=[dma((total,)), dma((total,)), dma((n,)), dma((n,)), dma((n,)), dma((n,)), dma((3,))],
+        compiler_params=pltpu.CompilerParams(collective_id=collective_id, has_side_effects=True),
+    )(gains, marks, weight)
+
+def swap_kernel(in_ref, out_ref, send, recv, local):
+    x, c, y, dev_x, dev_y, dev_c = corner()
+    own = slot(x, c, y)
+    places = [({"x": flip(x, dx), "core": flip(c, dc), "y": flip(y, dy)}, slot(flip(x, dx), flip(c, dc), flip(y, dy))) for dx, dc, dy in OTHERS]
+    greet([p for p, _ in places])
+    keep = pltpu.make_async_copy(in_ref.at[own], out_ref.at[own], local)
+    keep.start()
+    sent = []
+    for i, (there, other) in enumerate(places):
+        copy = remote(in_ref.at[other], out_ref.at[own], send.at[i], recv.at[i], there)
+        copy.start(); sent.append(copy)
+    for i, (there, other) in enumerate(places):
+        remote(out_ref.at[other], out_ref.at[other], recv.at[i], recv.at[i], there).wait_recv()
+    for copy in sent:
+        copy.wait_send()
+    keep.wait()
+
+def swap(blocks, collective_id):
+    dma = pltpu.SemaphoreType.DMA
+    n = len(OTHERS)
+    return pl.pallas_call(
+        swap_kernel, out_shape=jax.ShapeDtypeStruct(blocks.shape, blocks.dtype),
+        in_specs=[pl.BlockSpec(memory_space=pltpu.VMEM)], out_specs=pl.BlockSpec(memory_space=pl.ANY),
+        scratch_shapes=[dma((n,)), dma((n,)), dma(())],
+        compiler_params=pltpu.CompilerParams(collective_id=collective_id, has_side_effects=True),
+    )(blocks)
+
+LINE = 4
+def line_greet(z):
+    barrier = pltpu.get_barrier_semaphore()
+    @pl.when(z > 0)
+    def _():
+        pl.semaphore_signal(barrier, inc=1, device_id={"z": z - 1}, device_id_type=MESH_ID)
+    @pl.when(z < LINE - 1)
+    def _():
+        pl.semaphore_signal(barrier, inc=1, device_id={"z": z + 1}, device_id_type=MESH_ID)
+    @pl.when((z == 0) | (z == LINE - 1))
+    def _():
+        pl.semaphore_wait(barrier, 1)
+    @pl.when((z > 0) & (z < LINE - 1))
+    def _():
+        pl.semaphore_wait(barrier, 2)
+
+def line_gather_kernel(pieces, in_ref, out_ref, up_send, up_recv, down_send, down_recv, local):
+    z = lax.axis_index("z")
+    rows = in_ref.shape[0] // pieces
+    line_greet(z)
+    keep = pltpu.make_async_copy(in_ref, out_ref.at[z], local)
+    keep.start()
+    def at(block, k):
+        return out_ref.at[block, pl.ds(k * rows, rows), :]
+    def up(t, k, source=None):
+        s = at(z - t, k) if source is None else source
+        return remote(s, at(z - t, k), up_send.at[t * pieces + k], up_recv.at[t * pieces + k], {"z": z + 1})
+    def down(t, k, source=None):
+        s = at(z + t, k) if source is None else source
+        return remote(s, at(z + t, k), down_send.at[t * pieces + k], down_recv.at[t * pieces + k], {"z": z - 1})
+    for k in range(pieces):
+        mine = in_ref.at[pl.ds(k * rows, rows), :]
+        @pl.when(z < LINE - 1)
+        def _():
+            up(0, k, mine).start()
+        @pl.when(z > 0)
+        def _():
+            down(0, k, mine).start()
+    for t in range(LINE - 1):
+        for k in range(pieces):
+            @pl.when(z - 1 - t >= 0)
+            def _():
+                i = t * pieces + k
+                remote(at(z - 1 - t, k), at(z - 1 - t, k), up_recv.at[i], up_recv.at[i], {"z": z - 1}).wait_recv()
+                @pl.when(z < LINE - 1)
+                def _():
+                    if t + 1 < LINE - 1:
+                        up(t + 1, k).start()
+            @pl.when(z + 1 + t < LINE)
+            def _():
+                i = t * pieces + k
+                remote(at(z + 1 + t, k), at(z + 1 + t, k), down_recv.at[i], down_recv.at[i], {"z": z + 1}).wait_recv()
+                @pl.when(z > 0)
+                def _():
+                    if t + 1 < LINE - 1:
+                        down(t + 1, k).start()
+    for t in range(LINE - 1):
+        for k in range(pieces):
+            @pl.when((z < LINE - 1) & (z - t >= 0))
+            def _():
+                up(t, k).wait_send()
+            @pl.when((z > 0) & (z + t < LINE))
+            def _():
+                down(t, k).wait_send()
+    keep.wait()
+
+def line_gather(block, collective_id, pieces=4):
+    dma = pltpu.SemaphoreType.DMA
+    n = (LINE - 1) * pieces
+    return pl.pallas_call(
+        functools.partial(line_gather_kernel, pieces), out_shape=jax.ShapeDtypeStruct((LINE,) + block.shape, block.dtype),
+        in_specs=[pl.BlockSpec(memory_space=pltpu.VMEM)], out_specs=pl.BlockSpec(memory_space=pl.ANY),
+        scratch_shapes=[dma((n,)), dma((n,)), dma((n,)), dma((n,)), dma(())],
+        compiler_params=pltpu.CompilerParams(collective_id=collective_id, has_side_effects=True),
+    )(block)
+
+def line_scatter_kernel(pieces, in_ref, out_ref, up_buf, down_buf, up_stage, down_stage, up_send, up_recv, down_send, down_recv):
+    z = lax.axis_index("z")
+    rows = in_ref.shape[1] // pieces
+    step = 32
+    f32, bf = jnp.float32, jnp.bfloat16
+    line_greet(z)
+    def cut(k):
+        return pl.ds(k * rows, rows)
+    def add(target, index, a, b, k):
+        def body(i, carry):
+            r = pl.ds(pl.multiple_of(k * rows + i * step, step), step)
+            target[index, r, :] = (a(r).astype(f32) + b(r).astype(f32)).astype(target.dtype)
+            return carry
+        lax.fori_loop(0, rows // step, body, 0)
+    for d in range(LINE - 1, 0, -1):
+        for k in range(pieces):
+            i = (d - 1) * pieces + k
+            @pl.when(z + d < LINE)
+            def _():
+                @pl.when(z == 0)
+                def _():
+                    remote(in_ref.at[z + d, cut(k), :], up_buf.at[d - 1, cut(k), :], up_send.at[i], up_recv.at[i], {"z": z + 1}).start()
+                @pl.when(z > 0)
+                def _():
+                    if d + 1 < LINE:
+                        j = d * pieces + k
+                        remote(up_buf.at[d, cut(k), :], up_buf.at[d, cut(k), :], up_recv.at[j], up_recv.at[j], {"z": z - 1}).wait_recv()
+                        add(up_stage, d - 1, lambda r: in_ref[z + d, r, :], lambda r: up_buf[d, r, :], k)
+                        remote(up_stage.at[d - 1, cut(k), :], up_buf.at[d - 1, cut(k), :], up_send.at[i], up_recv.at[i], {"z": z + 1}).start()
+            @pl.when(z - d >= 0)
+            def _():
+                @pl.when(z == LINE - 1)
+                def _():
+                    remote(in_ref.at[z - d, cut(k), :], down_buf.at[d - 1, cut(k), :], down_send.at[i], down_recv.at[i], {"z": z - 1}).start()
+                @pl.when(z < LINE - 1)
+                def _():
+                    if d + 1 < LINE:
+                        j = d * pieces + k
+                        remote(down_buf.at[d, cut(k), :], down_buf.at[d, cut(k), :], down_recv.at[j], down_recv.at[j], {"z": z + 1}).wait_recv()
+                        add(down_stage, d - 1, lambda r: in_ref[z - d, r, :], lambda r: down_buf[d, r, :], k)
+                        remote(down_stage.at[d - 1, cut(k), :], down_buf.at[d - 1, cut(k), :], down_send.at[i], down_recv.at[i], {"z": z - 1}).start()
+    for k in range(pieces):
+        @pl.when(z > 0)
+        def _():
+            remote(up_buf.at[0, cut(k), :], up_buf.at[0, cut(k), :], up_recv.at[k], up_recv.at[k], {"z": z - 1}).wait_recv()
+        @pl.when(z < LINE - 1)
+        def _():
+            remote(down_buf.at[0, cut(k), :], down_buf.at[0, cut(k), :], down_recv.at[k], down_recv.at[k], {"z": z + 1}).wait_recv()
+        def body(i, carry):
+            r = pl.ds(pl.multiple_of(k * rows + i * step, step), step)
+            own = in_ref[z, r, :].astype(f32)
+            @pl.when(z == 0)
+            def _():
+                out_ref[r, :] = own + down_buf[0, r, :].astype(f32)
+            @pl.when(z == LINE - 1)
+            def _():
+                out_ref[r, :] = own + up_buf[0, r, :].astype(f32)
+            @pl.when((z > 0) & (z < LINE - 1))
+            def _():
+                out_ref[r, :] = own + up_buf[0, r, :].astype(f32) + down_buf[0, r, :].astype(f32)
+            return carry
+        lax.fori_loop(0, rows // step, body, 0)
+    for d in range(LINE - 1, 0, -1):
+        for k in range(pieces):
+            i = (d - 1) * pieces + k
+            @pl.when(z + d < LINE)
+            def _():
+                remote(up_stage.at[d - 1, cut(k), :], up_buf.at[d - 1, cut(k), :], up_send.at[i], up_recv.at[i], {"z": z + 1}).wait_send()
+            @pl.when(z - d >= 0)
+            def _():
+                remote(down_stage.at[d - 1, cut(k), :], down_buf.at[d - 1, cut(k), :], down_send.at[i], down_recv.at[i], {"z": z - 1}).wait_send()
+
+def line_scatter(terms, collective_id, pieces=4):
+    dma = pltpu.SemaphoreType.DMA
+    line, rows, columns = terms.shape
+    n = (LINE - 1) * pieces
+    vm = pltpu.VMEM((LINE - 1, rows, columns), jnp.bfloat16)
+    return pl.pallas_call(
+        functools.partial(line_scatter_kernel, pieces), out_shape=jax.ShapeDtypeStruct((rows, columns), jnp.float32),
+        in_specs=[pl.BlockSpec(memory_space=pltpu.VMEM)], out_specs=pl.BlockSpec(memory_space=pltpu.VMEM),
+        scratch_shapes=[vm, vm, vm, vm, dma((n,)), dma((n,)), dma((n,)), dma((n,))],
+        compiler_params=pltpu.CompilerParams(collective_id=collective_id, has_side_effects=True, vmem_limit_bytes=40 << 20),
+    )(terms)
+
+
+def everyone(total):
+    names = ALL
+    sizes = [lax.axis_size(n) for n in names]
+    me = 0
+    for n, size in zip(names, sizes):
+        me = me * size + lax.axis_index(n)
+
+    def device(index):
+        where = {}
+        for n, size in reversed(list(zip(names, sizes))):
+            where[n] = lax.rem(index, size)
+            index = index // size
+        return where
+
+    barrier = pltpu.get_barrier_semaphore()
+
+    def greet_one(d, carry):
+        pl.semaphore_signal(barrier, inc=1, device_id=device(lax.rem(me + d, total)), device_id_type=MESH_ID)
+        return carry
+
+    lax.fori_loop(1, total, greet_one, 0)
+    pl.semaphore_wait(barrier, total - 1)
+    return me, device
+
+
+def spread_kernel(total, in_ref, out_ref, buffer, send, recv):
+    me, device = everyone(total)
+
+    def put(d, carry):
+        other = lax.rem(me + d, total)
+        remote(in_ref.at[other], buffer.at[me], send.at[d], recv.at[d], device(other)).start()
+        return carry
+
+    lax.fori_loop(1, total, put, 0)
+
+    def take(d, carry):
+        source = lax.rem(me + total - d, total)
+        other = lax.rem(me + d, total)
+        remote(buffer.at[source], buffer.at[source], recv.at[d], recv.at[d], device(source)).wait_recv()
+        remote(in_ref.at[other], buffer.at[me], send.at[d], recv.at[d], device(other)).wait_send()
+        return carry
+
+    lax.fori_loop(1, total, take, 0)
+    out_ref[...] = in_ref[me]
+
+    def add(d, carry):
+        out_ref[...] += buffer[lax.rem(me + d, total)]
+        return carry
+
+    lax.fori_loop(1, total, add, 0)
+
+
+def spread_sum(tiles, collective_id):
+    dma = pltpu.SemaphoreType.DMA
+    total = tiles.shape[0]
+    vmem = pl.BlockSpec(memory_space=pltpu.VMEM)
+    return pl.pallas_call(
+        functools.partial(spread_kernel, total),
+        out_shape=jax.ShapeDtypeStruct(tiles.shape[1:], tiles.dtype),
+        in_specs=[vmem],
+        out_specs=vmem,
+        scratch_shapes=[pltpu.VMEM(tiles.shape, tiles.dtype), dma((total,)), dma((total,))],
+        compiler_params=pltpu.CompilerParams(collective_id=collective_id, has_side_effects=True),
+    )(tiles)
 
 
 def root_mean_scale(values, gains):
@@ -59,13 +554,8 @@
 def make_shards(cells):
     data_total = cells * PLANES
 
-    def gather_tokens(rows):
-        return lax.all_gather(rows, TENSOR, axis=0, tiled=True)
-
     def scatter_tokens(terms):
-        return lax.psum_scatter(low(terms), TENSOR, scatter_dimension=0, tiled=True).astype(
-            jnp.float32
-        )
+        return scatter_blocks(low(terms).reshape(RANKS, -1, terms.shape[1]))
 
     def split_units(weight):
         rows, units = weight.shape
@@ -84,22 +574,21 @@
     def join_columns(parts):
         return jnp.transpose(parts, (1, 0, 2)).reshape(parts.shape[1], -1)
 
-    def gather_columns(pieces):
-        sent = jnp.transpose(jnp.concatenate(pieces, axis=-1), (1, 0, 2))
-        mine = lax.all_to_all(sent, TENSOR, split_axis=0, concat_axis=0, tiled=True)
+    def send_columns(pieces):
+        return jnp.transpose(jnp.concatenate(pieces, axis=-1), (1, 0, 2))
+
+    def gather_columns(mine):
         rows, columns = mine.shape[1:]
         every = lax.all_gather(mine, DATA, axis=0, tiled=False)
         every = every.reshape(data_total, CORNERS**2, CORNERS, rows, columns)
         return jnp.transpose(every, (1, 0, 2, 3, 4)).reshape(-1, columns)
 
-    def scatter_columns(term):
+    def scatter_columns(term, collective_id):
         rows = term.shape[0] // (RANKS * data_total)
         split = low(term).reshape(CORNERS**2, data_total, CORNERS, rows, -1)
         split = jnp.transpose(split, (1, 0, 2, 3, 4)).reshape(data_total * RANKS, rows, -1)
         mine = lax.psum_scatter(split, DATA, scatter_dimension=0, tiled=True)
-        return lax.all_to_all(mine, TENSOR, split_axis=0, concat_axis=0, tiled=True).astype(
-            jnp.float32
-        )
+        return swap(mine, collective_id).astype(jnp.float32)
 
     inner = CORNERS * data_total
     to_rank = []
@@ -137,39 +626,46 @@
         scale_qk = 1.0 / math.sqrt(HEAD_SIZE)
 
         sizes = [norm_attn.shape[0], norm_ffn.shape[0], query_gain.shape[0], key_gain.shape[0]]
-        gains = lax.all_gather(
-            jnp.concatenate([norm_attn, norm_ffn, query_gain, key_gain]), ALL, axis=0, tiled=False
-        ).astype(jnp.float32)
         cuts = [0]
         for size in sizes:
             cuts.append(cuts[-1] + size)
-        gain_attn, gain_ffn, gain_query, gain_key = (
-            gains[:, a:b].reshape(-1) for a, b in zip(cuts[:-1], cuts[1:])
-        )
-
-        w_attn = gather_columns(
-            [
-                split_columns(query_weight),
-                split_columns(key_matrix),
-                split_columns(value_matrix),
-                split_columns(gate_weight),
-            ]
-        )
-        w_out = lax.all_gather(
-            lax.ppermute(out_weight, INNER, to_rank), DATA, axis=0, tiled=True
-        )
-        w_ffn = gather_columns([split_units(ffn_gate), split_units(ffn_up)])
-        w_down = lax.all_gather(ffn_down, DATA, axis=0, tiled=True)
-
+        tile = (8, HEAD_SIZE)
+        pad = tile[0] * tile[1] - cuts[-1]
+        own_gains = jnp.concatenate([norm_attn, norm_ffn, query_gain, key_gain]).astype(jnp.float32)
+        own_gains = jnp.pad(own_gains, (0, pad)).reshape(tile)
         plane = lax.axis_index("z")
         group_start = lax.axis_index("cell") * GROUP_TOKENS
-        marks = jnp.stack(
+        marks = jnp.concatenate(
             [
                 lax.dynamic_slice_in_dim(sequence_numbers, group_start, GROUP_TOKENS),
                 lax.dynamic_slice_in_dim(positions, group_start, GROUP_TOKENS),
             ]
-        )
-        marks = lax.all_gather(marks, ("x", "core"), axis=0, tiled=False)
+        ).reshape(-1, HEAD_SIZE)
+        gains, marks, attn_columns = hello(
+            RANKS * data_total,
+            own_gains,
+            marks,
+            send_columns(
+                [
+                    split_columns(query_weight),
+                    split_columns(key_matrix),
+                    split_columns(value_matrix),
+                    split_columns(gate_weight),
+                ]
+            ),
+            2,
+        )
+        gains = gains.reshape(RANKS * data_total, -1)
+        gain_attn, gain_ffn, gain_query, gain_key = (
+            gains[:, a:b].reshape(-1) for a, b in zip(cuts[:-1], cuts[1:])
+        )
+        w_attn = gather_columns(attn_columns)
+        w_out = lax.all_gather(
+            lax.ppermute(out_weight, INNER, to_rank), DATA, axis=0, tiled=True
+        )
+        w_down = lax.all_gather(ffn_down, DATA, axis=0, tiled=True)
+
+        marks = marks.reshape(groups, 2, GROUP_TOKENS)
         key_seq, key_pos = marks[:, 0], marks[:, 1]
         own = lax.dynamic_slice_in_dim(marks, plane * window, window, axis=2)
         own_seq, own_pos = own[:, 0], own[:, 1]
@@ -185,6 +681,7 @@
 
         hidden = hidden_in.astype(jnp.float32)
         normed_input = gather_tokens(low(root_mean_scale(hidden, gain_attn)))
+        w_ffn = gather_columns(swap(send_columns([split_units(ffn_gate), split_units(ffn_up)]), 3))
         raw = matrix_product(normed_input, w_attn)
         a, b, c = query_columns, query_columns + key_columns, query_columns + 2 * key_columns
         query_raw = raw[:, :a].reshape(groups, window, repeat, HEAD_SIZE)
@@ -193,9 +690,10 @@
         gate_sig = jax.nn.sigmoid(raw[:, c:])
         query_low = low(prepare_heads(query_raw, gain_query))
         key_low = low(prepare_heads(key_raw, gain_key)).reshape(groups, window, HEAD_SIZE)
-        pair = lax.all_gather(
-            jnp.concatenate([key_low, value_low], axis=-1), "z", axis=0, tiled=False
-        )
+        pair = line_gather(
+            jnp.concatenate([key_low, value_low], axis=-1).reshape(tokens, 2 * HEAD_SIZE), 5
+        )
+        pair = pair.reshape(PLANES, groups, window, 2 * HEAD_SIZE)
         pair = jnp.transpose(pair, (1, 0, 2, 3)).reshape(groups, GROUP_TOKENS, 2 * HEAD_SIZE)
         keys_all, values_all = pair[..., :HEAD_SIZE], pair[..., HEAD_SIZE:]
 
@@ -232,7 +730,7 @@
         grad_down = lax.psum_scatter(
             low(contract_first(mixed_low, cotangent_all)), DATA, scatter_dimension=0, tiled=True
         ).astype(jnp.float32)
-        grad_both = scatter_columns(contract_first(normed_two, d_both))
+        grad_both = scatter_columns(contract_first(normed_two, d_both), 3)
         grad_gate = join_units(grad_both[..., :units])
         grad_up = join_units(grad_both[..., units:])
         unused_two, norm_two_back = jax.vjp(root_mean_scale, middle, gain_ffn)
@@ -270,8 +768,8 @@
         d_pair = jnp.transpose(
             d_pair.reshape(groups, PLANES, window, 2 * HEAD_SIZE), (1, 0, 2, 3)
         )
-        d_pair = lax.psum_scatter(d_pair, "z", scatter_dimension=0, tiled=True)
-        d_pair = d_pair.reshape(groups, window, 2 * HEAD_SIZE).astype(jnp.float32)
+        d_pair = line_scatter(d_pair.reshape(PLANES, tokens, 2 * HEAD_SIZE), 6)
+        d_pair = d_pair.reshape(groups, window, 2 * HEAD_SIZE)
         d_key_rot, d_value = d_pair[..., :HEAD_SIZE], d_pair[..., HEAD_SIZE:]
         unused_query, query_back = jax.vjp(prepare_heads, query_raw, gain_query)
         d_query_raw, grad_query_gain_term = query_back(d_query_rot)
@@ -287,7 +785,7 @@
             axis=-1,
         )
         d_normed = scatter_tokens(contract_last(d_raw, w_attn))
-        grad_attn = scatter_columns(contract_first(normed_input, d_raw))
+        grad_attn = scatter_columns(contract_first(normed_input, d_raw), 4)
         grad_query = join_columns(grad_attn[..., :a])
         grad_key = join_columns(grad_attn[..., a:b])
         grad_value = join_columns(grad_attn[..., b:c])
@@ -308,7 +806,8 @@
             ],
             axis=-1,
         )
-        small = lax.psum_scatter(terms, ALL, scatter_dimension=0, tiled=True).reshape(-1)
+        terms = jnp.pad(terms, ((0, 0), (0, pad))).reshape((-1,) + tile)
+        small = spread_sum(terms, 7).reshape(-1)
         grad_norm_attn, grad_norm_ffn, grad_query_gain, grad_key_gain = (
             small[s:e] for s, e in zip(cuts[:-1], cuts[1:])
         )

time: 1420 us -> 1140 us (0.80)
  waiting for transfers between devices: 815 us -> 40.9 us
  Pallas kernels: 0 us -> 664 us
  blocking collectives: 162 us -> 0 us
    pallas_call x0 -> x15, Pallas kernels: none -> 664 us  [the longest x4 162 us: gather_tokens(): pl.pallas_call(functools.partial(gather_kernel, rows), out_shape=jax.Shap...]
    all_gather x5 -> x0, waiting for transfers between devices: 258 us -> none  [the longest x4 210 us: gather_tokens(): return lax.all_gather(rows, TENSOR, axis=0, tiled=True)]
    reduce_scatter x5 -> x0, waiting for transfers between devices: 237 us -> none  [the longest x4 182 us: scatter_tokens(): lax.psum_scatter(low(terms), TENSOR, scatter_dimension=0, tiled=True)]
    all_gather x2, waiting for transfers between devices: 124 us -> 0.02 us  [gather_columns(): every = lax.all_gather(mine, DATA, axis=0, tiled=False)]
    unnamed x2 -> x0, blocking collectives: 83.7 us -> none
    all_to_all x3 -> x0, blocking collectives: 73.2 us -> none  [the longest x2 49.5 us: gather_columns(): mine = lax.all_to_all(sent, TENSOR, split_axis=0, concat_axis=0, tiled=True)]
    reduce_scatter x1, waiting for transfers between devices: 58.9 us -> 0.01 us  [shards(): lax.psum_scatter(low(contract_first(mixed_low, cotangent_all)), DATA, sca...]
    all_gather x1, waiting for transfers between devices: 45.7 us -> 0.01 us  [shards(): w_down = lax.all_gather(ffn_down, DATA, axis=0, tiled=True)]
  transfers between devices with their start and end apart: 21 -> 10, of which waited for: 17 -> 1; matrix products, arithmetic and copies ran while one was open for 19% -> 23% of each run, Pallas kernels for 0% -> 48%
where the time goes in v2:
time: 1140 us; the launch traced here: 1120 us
  Pallas kernels  664 us (58%)
  matrix products  206 us (18%)
  local copies, waits for them, and re-layouts  105 us (9%)
  other arithmetic  90.1 us (8%)
  waiting for transfers between devices  40.9 us (4%)
  between operations  15.8 us (1%)
    pallas_call x4, Pallas kernels, gather_tokens(): pl.pallas_call(functools.partial(gather_kernel, rows), out_shape=jax.Shap...  162 us
    pallas_call x4, Pallas kernels, scatter_blocks(): pl.pallas_call(functools.partial(scatter_kernel, rows), out_shape=jax.Sha...  161 us
    pallas_call x1, Pallas kernels, line_gather(): pl.pallas_call(functools.partial(line_gather_kernel, pieces), out_shape=j...  129 us
    pallas_call x3, Pallas kernels, swap(): pl.pallas_call(swap_kernel, out_shape=jax.ShapeDtypeStruct(blocks.shape,...  95.3 us
    pallas_call x1, Pallas kernels, line_scatter(): pl.pallas_call(functools.partial(line_scatter_kernel, pieces), out_shape=...  78.1 us
    dot_general x4, matrix products, contract_last(): lax.dot_general(left, right, (((1,), (1,)), ((), ())), preferred_element_...  54.7 us
    dot_general x4, matrix products, contract_first(): lax.dot_general(left, right, (((0,), (0,)), ((), ())), preferred_element_...  43.6 us
    reduce_scatter x2, waiting for transfers between devices, scatter_columns(): mine = lax.psum_scatter(split, DATA, scatter_dimension=0, tiled=True)  40.2 us
  transfers between devices with their start and end apart: 10, of which 1 were waited for; matrix products, arithmetic and copies ran while one was open for 23% of the time, Pallas kernels for 48%

profile of v2, /device:TPU:0, one launch (start us, length us, event | category | flops | bytes accessed | tf_op | source)
XLA Modules:
  0.0 1124.7 jit_solution(11184572925641843917)
XLA Ops:
  13.1 21.7 %shard_map.263 = (f32[32,8,128]{2,1,0:T(8,128)}, s32[4,32,128]{2,1,0:T(8,128)}, bf16[8,64,768]{2,1,0:T(8,128)(2,1)}) custom-call(f32[8,128]{1,0:T(8,128)} %fusion.50.gains_ref, s32[32,128]{1,0:T(8,128)} %pad_add_fusion.marks_ref, bf16[8,64,768]{2,1,0:T(8,128)(2,1)} %maximum_bitcast_fusion.1.weight_ref), custom_call_target="tpu_custom_call" | custom-call | tf_op jit(solution)/shard_map/pallas_call | solution.py:252
  38.9 3.5 reshape.424
  45.1 40.1 %shard_map.268 = bf16[8,64,1536]{2,1,0:T(8,128)(2,1)} custom-call(bf16[8,64,1536]{2,1,0:T(8,128)(2,1)} %maximum_bitcast_fusion.in_ref), custom_call_target="tpu_custom_call" | custom-call | tf_op jit(solution)/shard_map/pallas_call | solution.py:282
  89.3 4.2 fusion.38
  97.4 41.6 %shard_map.264 = bf16[2048,2048]{1,0:T(8,128)(2,1)} custom-call(bf16[256,2048]{1,0:T(8,128)(2,1)} %fusion.13.in_ref), custom_call_target="tpu_custom_call" | custom-call | tf_op jit(solution)/shard_map/pallas_call | solution.py:97
  139.0 40.6 %shard_map.270 = bf16[2048,2048]{1,0:T(8,128)(2,1)} custom-call(bf16[256,2048]{1,0:T(8,128)(2,1)} %in_ref.1), custom_call_target="tpu_custom_call" | custom-call | tf_op jit(solution)/shard_map/pallas_call | solution.py:97
  179.5 6.7 or_and_fusion
  188.5 10.2 fusion.75
  221.6 6.8 fusion.35
  229.5 128.6 %shard_map.265 = bf16[4,2048,256]{2,1,0:T(8,128)(2,1)} custom-call(bf16[2048,256]{1,0:T(8,128)(2,1)} %pad_maximum_fusion.6.in_ref), custom_call_target="tpu_custom_call" | custom-call | tf_op jit(solution)/shard_map/pallas_call | solution.py:358
  358.1 4.7 copy.230
  364.7 18.5 %fusion.74 = (f32[4,2,512]{2,1,0:T(2,128)S(1)}, f32[4,2,512,2048]{2,3,1,0:T(8,128)}) fusion(pred[4,512,2048]{1,2,0:T(8,128)(4,1)} %or_and_fusion, bf16[4,512,2,128]{1,3,2,0:T(8,128)(2,1)} %fusion.28, bf16[4,2048,256]{2,1,0:T(8,128)(2,1)} %bitcast.249), kind=kOutput, calls=%fused_computation.180 | convolution fusion | flops 2181040128 | bytes 40910848 | tf_op jit(solution)/shard_map/sub | solution.py:706
  383.2 12.4 %fusion.7 = bf16[4,2,512,2048]{2,3,1,0:T(8,128)(2,1)S(1)} fusion(f32[4,2,512,2048]{2,3,1,0:T(8,128)} %get-tuple-element.78, f32[4,2,512]{2,1,0:T(2,128)S(1)} %get-tuple-element.77), kind=kLoop, calls=%fused_computation.12 | loop fusion | flops 16777216 | bytes 50348032 | tf_op jit(solution)/shard_map/convert_element_type | solution.py:551
  395.6 5.8 copy-done.7
  406.6 3.7 fusion.20
  410.3 3.9 convolution_convert_fusion.3
  414.2 40.4 %shard_map.266 = f32[256,2048]{1,0:T(8,128)S(1)} custom-call(bf16[8,256,2048]{2,1,0:T(8,128)(2,1)S(1)} %bitcast.240), custom_call_target="tpu_custom_call" | custom-call | tf_op jit(solution)/shard_map/pallas_call | solution.py:188
  456.4 40.1 %shard_map.267 = bf16[2048,2048]{1,0:T(8,128)(2,1)} custom-call(bf16[256,2048]{1,0:T(8,128)(2,1)} %multiply_convert_fusion.4.in_ref), custom_call_target="tpu_custom_call" | custom-call | tf_op jit(solution)/shard_map/pallas_call | solution.py:97
  496.6 3.6 copy.243
  503.2 16.7 %fusion.76 = f32[2048,1536]{0,1:T(8,128)} fusion(bf16[2048,2048]{1,0:T(8,128)(2,1)S(1)} %copy-done.24, bf16[2048,1536]{1,0:T(8,128)(2,1)S(1)} %bitcast.261), kind=kOutput, calls=%fused_computation.182 | convolution fusion | flops 12884901888 | bytes 27262976 | tf_op jit(solution)/shard_map/dot_general | solution.py:535
  519.9 18.0 %multiply_convert_fusion.1 = (bf16[2048,768]{0,1:T(8,128)(2,1)S(1)}, bf16[2048,768]{0,1:T(8,128)(2,1)}, bf16[2048,768]{0,1:T(8,128)(2,1)}) fusion(f32[2048,1536]{0,1:T(8,128)} %fusion.76, bf16[2048,2048]{1,0:T(8,128)(2,1)} %shard_map.270, bf16[768,2048]{1,0:T(8,128)(2,1)} %all-gather.9.cloned.1.call-done), kind=kOutput, calls=%fused_computation.20 | convolution fusion | flops 6467616768 | bytes 33554432 | tf_op jit(solution)/shard_map/dot_general | solution.py:539
  537.9 19.7 %convolution_convert_fusion.1 = bf16[2048,2048]{1,0:T(8,128)(2,1)} fusion(bf16[2048,1536]{1,0:T(8,128)(2,1)} %bitcast.262, bf16[2048,768]{0,1:T(8,128)(2,1)} %get-tuple-element.35, bf16[2048,768]{0,1:T(8,128)(2,1)S(1)} %get-tuple-element.34), kind=kOutput, calls=%fused_computation.14 | convolution fusion | flops 12901679104 | bytes 20971520 | tf_op jit(solution)/shard_map/dot_general | solution.py:539
  557.5 3.4 copy-done.6
  560.9 40.0 %shard_map.271 = f32[256,2048]{1,0:T(8,128)S(1)} custom-call(bf16[8,256,2048]{2,1,0:T(8,128)(2,1)S(1)} %bitcast.247), custom_call_target="tpu_custom_call" | custom-call | tf_op jit(solution)/shard_map/pallas_call | solution.py:188
  604.6 39.9 %shard_map.272 = bf16[2048,2048]{1,0:T(8,128)(2,1)} custom-call(bf16[256,2048]{1,0:T(8,128)(2,1)} %fusion.61.in_ref), custom_call_target="tpu_custom_call" | custom-call | tf_op jit(solution)/shard_map/pallas_call | solution.py:97
  644.5 6.9 convolution_convert_fusion.7
  651.4 8.2 multiply_convert_fusion.3
  660.7 8.5 bitcast_convert_fusion
  669.6 19.0 %fusion.2 = bf16[4,2,512,2048]{2,3,1,0:T(8,128)(2,1)} fusion(bf16[4,512,2,128]{1,3,2,0:T(8,128)(2,1)S(1)} %copy.246, f32[4,2,512]{2,1,0:T(2,128)S(1)} %bitcast.295, f32[4,2,512,2048]{2,3,1,0:T(8,128)} %get-tuple-element.78, f32[4,2,512]{2,1,0:T(2,128)S(1)} %get-tuple-element.77, bf16[4,2048,256]{2,1,0:T(8,128)(2,1)S(1)} %bitcast.252), kind=kOutput, calls=%fused_computation.3 | convolution fusion | flops 2181038080 | bytes 53510144 | tf_op jit(solution)/shard_map/gqrd,gkd->grqk/dot_general | solution.py:752
  688.8 10.7 fusion.8
  700.4 78.1 %shard_map.273 = f32[2048,256]{1,0:T(8,128)S(1)} custom-call(bf16[4,2048,256]{2,1,0:T(8,128)(2,1)S(1)} %bitcast.241), custom_call_target="tpu_custom_call" | custom-call | tf_op jit(solution)/shard_map/pallas_call | solution.py:442
  778.5 5.0 broadcast_multiply_fusion.1
  788.6 9.1 bitcast_multiply_fusion.3
  803.0 6.1 multiply_reduce_fusion.7
  814.9 9.6 convolution_convert_fusion.6
  828.2 10.2 convolution_convert_fusion.5
  840.3 16.9 %convolution_convert_fusion.4 = bf16[2048,1536]{1,0:T(8,128)(2,1)S(1)} fusion(bf16[2048,2048]{1,0:T(8,128)(2,1)} %shard_map.267, bf16[2048,768]{0,1:T(8,128)(2,1)} %get-tuple-element.35, bf16[2048,768]{0,1:T(8,128)(2,1)S(1)} %copy-done.78), kind=kOutput, calls=%fused_computation.17 | convolution fusion | flops 12900630528 | bytes 20971520 | tf_op jit(solution)/shard_map/dot_general | solution.py:545
  862.5 8.9 convolution_convert_fusion.2
  871.4 40.7 %shard_map.269 = f32[256,2048]{1,0:T(8,128)S(1)} custom-call(bf16[8,256,2048]{2,1,0:T(8,128)(2,1)S(1)} %bitcast.246), custom_call_target="tpu_custom_call" | custom-call | tf_op jit(solution)/shard_map/pallas_call | solution.py:188
  913.6 8.9 convolution_convert_fusion
  922.5 39.8 %shard_map.274 = f32[256,2048]{1,0:T(8,128)S(1)} custom-call(bf16[8,256,2048]{2,1,0:T(8,128)(2,1)S(1)} %bitcast.245), custom_call_target="tpu_custom_call" | custom-call | tf_op jit(solution)/shard_map/pallas_call | solution.py:188
  965.3 17.7 %shard_map.276 = f32[8,128]{1,0:T(8,128)} custom-call(f32[32,8,128]{2,1,0:T(8,128)} %bitcast.281), custom_call_target="tpu_custom_call" | custom-call | tf_op jit(solution)/shard_map/pallas_call | solution.py:506
  983.0 5.9 fusion.17
  992.6 33.1 %shard_map.275 = bf16[8,64,768]{2,1,0:T(8,128)(2,1)} custom-call(bf16[8,64,768]{2,1,0:T(8,128)(2,1)} %reduce-scatter.5.cloned.1.call-done.in_ref), custom_call_target="tpu_custom_call" | custom-call | tf_op jit(solution)/shard_map/pallas_call | solution.py:282
  1032.8 40.2 %reduce-scatter.9.cloned.1.call-done.in_ref = bf16[8,64,1536]{2,1,0:T(8,128)(2,1)} async-done(((bf16[32,64,1536]{2,1,0:T(8,128)(2,1)}), bf16[8,64,1536]{2,1,0:T(8,128)(2,1)}) %reduce-scatter.9.cloned.1.call-update) | async-done | bytes 1572880 | tf_op jit(solution)/shard_map/reduce_scatter | solution.py:590
  1073.0 22.0 %shard_map.277 = bf16[8,64,1536]{2,1,0:T(8,128)(2,1)} custom-call(bf16[8,64,1536]{2,1,0:T(8,128)(2,1)} %reduce-scatter.9.cloned.1.call-done.in_ref), custom_call_target="tpu_custom_call" | custom-call | tf_op jit(solution)/shard_map/pallas_call | solution.py:282
  1104.0 4.0 reshape.451
  1113.6 4.0 reshape.449
  (288 shorter events, 121.2 us)
Async XLA Ops:
  7.2 27.6 %copy-start.74 = (bf16[64,2048]{1,0:T(8,128)(2,1)S(1)}, bf16[64,2048]{1,0:T(8,128)(2,1)}, u32[]{:S(2)}) copy-start(bf16[64,2048]{1,0:T(8,128)(2,1)} %param.21) | copy-start | bytes 786436
  7.2 29.1 %copy-start.41 = (bf16[64,6144]{1,0:T(8,128)(2,1)S(1)}, bf16[64,6144]{1,0:T(8,128)(2,1)}, u32[]{:S(2)}) copy-start(bf16[64,6144]{1,0:T(8,128)(2,1)} %param.26) | copy-start | bytes 2359300
  7.2 179.0 %all-gather.11.cloned.1.call-start = ((), (), s32[]{:S(2)}) async-start(), calls=%async_computation.10 | async-start | bytes 3932160 | tf_op jit(solution)/shard_map/all_gather | solution.py:582
  34.8 375.6 %all-gather.7.cloned.1.call-start = ((), (), s32[]{:S(2)}) async-start(), calls=%async_computation.4 | async-start | bytes 1310720 | tf_op jit(solution)/shard_map/all_gather | solution.py:663
  34.8 0.7 collective-permute-start
  36.3 460.3 %all-gather.13.cloned.1.call-start = ((), (), s32[]{:S(2)}) async-start(), calls=%async_computation.11 | async-start | bytes 7864320 | tf_op jit(solution)/shard_map/all_gather | solution.py:582
  45.1 40.8 %copy-start.53 = (f32[32,8,128]{2,1,0:T(8,128)S(1)}, f32[32,8,128]{2,1,0:T(8,128)}, u32[]{:S(2)}) copy-start(f32[32,8,128]{2,1,0:T(8,128)} %get-tuple-element.17) | copy-start | bytes 393220
  45.1 41.0 %copy-start.58 = (s32[4,32,128]{2,1,0:T(8,128)S(1)}, s32[4,32,128]{2,1,0:T(8,128)}, u32[]{:S(2)}) copy-start(s32[4,32,128]{2,1,0:T(8,128)} %get-tuple-element.19) | copy-start | bytes 196612
  45.1 41.1 %copy-start.11 = (bf16[256,2048]{1,0:T(8,128)(2,1)S(1)}, bf16[256,2048]{1,0:T(8,128)(2,1)}, u32[]{:S(2)}) copy-start(bf16[256,2048]{1,0:T(8,128)(2,1)} %param.16) | copy-start | bytes 3145732
  85.2 434.7 %all-gather.9.cloned.1.call-start = ((), (), s32[]{:S(2)}) async-start(), calls=%async_computation.5 | async-start | bytes 3932160 | tf_op jit(solution)/shard_map/all_gather | solution.py:666
  85.8 903.2 %reduce-scatter.7.cloned.1.call-start = ((), (), s32[]{:S(2)}) async-start(), calls=%async_computation.7 | async-start | bytes 1310720 | tf_op jit(solution)/shard_map/reduce_scatter | solution.py:742
  87.1 9.0 copy-start.62
  87.2 514.9 %copy-start.47 = (f32[2048]{0:T(1024)}, f32[2048]{0:T(1024)S(1)}, u32[]{:S(2)}) copy-start(f32[2048]{0:T(1024)S(1)} %mul.504) | copy-start | bytes 24580
  87.3 133.3 %copy-start.64 = (f32[128]{0:T(128)}, f32[128]{0:T(128)S(1)}, u32[]{:S(2)}) copy-start(f32[128]{0:T(128)S(1)} %mul.469) | copy-start | bytes 1540
  87.4 275.4 %copy-start.66 = (f32[128]{0:T(128)}, f32[128]{0:T(128)S(1)}, u32[]{:S(2)}) copy-start(f32[128]{0:T(128)S(1)} %mul.487) | copy-start | bytes 1540
  87.5 8.6 copy-start.51
  188.4 10.2 copy-start.37
  212.9 149.9 %copy-start.9 = (f32[4,512,2,128]{1,3,2,0:T(8,128)}, f32[4,512,2,128]{1,3,2,0:T(8,128)S(1)}, u32[]{:S(2)}) copy-start(f32[4,512,2,128]{1,3,2,0:T(8,128)S(1)} %copy.234) | copy-start | bytes 6291460
  218.5 144.3 %copy-start.44 = (f32[4,512,2]{1,2,0:T(2,128)}, f32[4,512,2]{1,2,0:T(2,128)S(1)}, u32[]{:S(2)}) copy-start(f32[4,512,2]{1,2,0:T(2,128)S(1)} %copy.233) | copy-start | bytes 49156
  220.6 7.8 copy-start.39
  383.2 18.3 %copy-start.16 = (bf16[4,4,512,256]{3,2,1,0:T(8,128)(2,1)S(1)}, bf16[4,4,512,256]{3,2,1,0:T(8,128)(2,1)}, u32[]{:S(2)}) copy-start(bf16[4,4,512,256]{3,2,1,0:T(8,128)(2,1)} %copy.230) | copy-start | bytes 12582916
  403.9 6.4 copy-start.13
  455.0 147.1 %copy-start.8 = (f32[256,2048]{1,0:T(8,128)}, f32[256,2048]{1,0:T(8,128)S(1)}, u32[]{:S(2)}) copy-start(f32[256,2048]{1,0:T(8,128)S(1)} %get-tuple-element.31) | copy-start | bytes 6291460
  455.0 147.1 %copy-start.60 = (f32[256]{0:T(256)}, f32[256]{0:T(256)S(1)}, u32[]{:S(2)}) copy-start(f32[256]{0:T(256)S(1)} %fusion.52) | copy-start | bytes 3076
  496.6 6.6 copy-start.24
  537.9 19.7 %copy-start.77 = (bf16[2048,768]{0,1:T(8,128)(2,1)}, bf16[2048,768]{0,1:T(8,128)(2,1)S(1)}, u32[]{:S(2)}) copy-start(bf16[2048,768]{0,1:T(8,128)(2,1)S(1)} %get-tuple-element.34) | copy-start | bytes 9437188
  604.6 39.9 %copy-start.20 = (bf16[2048,256]{1,0:T(8,128)(2,1)S(1)}, bf16[2048,256]{1,0:T(8,128)(2,1)}, u32[]{:S(2)}) copy-start(bf16[2048,256]{1,0:T(8,128)(2,1)} %fusion.20) | copy-start | bytes 3145732
  644.5 6.9 copy-start.25
  660.7 8.5 copy-start.14
  660.7 8.9 copy-start.17
  688.6 304.0 %reduce-scatter.5.cloned.1.call-start = ((), (), s32[]{:S(2)}) async-start(), calls=%async_computation.6 | async-start | bytes 3932160 | tf_op jit(solution)/shard_map/reduce_scatter | solution.py:590
  700.4 78.1 %copy-start.19 = (f32[4,512,64]{2,1,0:T(8,128)S(1)}, f32[4,512,64]{2,1,0:T(8,128)}, u32[]{:S(2)}) copy-start(f32[4,512,64]{2,1,0:T(8,128)} %copy-done.18) | copy-start | bytes 1572868
  812.6 11.9 %copy-start.40 = (bf16[256,8,2,128]{3,1,2,0:T(8,128)(2,1)}, bf16[256,8,2,128]{3,1,2,0:T(8,128)(2,1)S(1)}, u32[]{:S(2)}) copy-start(bf16[256,8,2,128]{3,1,2,0:T(8,128)(2,1)S(1)} %copy.323) | copy-start | bytes 3145732
  814.8 9.6 copy-start.43
  826.4 203.9 %reduce-scatter.11.cloned.1.call-start = ((), (), s32[]{:S(2)}) async-start(), calls=%async_computation.9 | async-start | bytes 3932160 | tf_op jit(solution)/shard_map/reduce_scatter | solution.py:730
  838.5 234.5 %reduce-scatter.9.cloned.1.call-start = ((), (), s32[]{:S(2)}) async-start(), calls=%async_computation.8 | async-start | bytes 7864320 | tf_op jit(solution)/shard_map/reduce_scatter | solution.py:590
  871.4 42.2 %copy-start.38 = (bf16[4,4,2,64,768]{4,3,2,1,0:T(8,128)(2,1)S(1)}, bf16[4,4,2,64,768]{4,3,2,1,0:T(8,128)(2,1)}, u32[]{:S(2)}) copy-start(bf16[4,4,2,64,768]{4,3,2,1,0:T(8,128)(2,1)} %copy-done.37) | copy-start | bytes 9437188
  922.5 41.1 %copy-start.12 = (bf16[256,2048]{1,0:T(8,128)(2,1)S(1)}, bf16[256,2048]{1,0:T(8,128)(2,1)}, u32[]{:S(2)}) copy-start(bf16[256,2048]{1,0:T(8,128)(2,1)} %param.16) | copy-start | bytes 3145732
  922.5 41.1 %copy-start.52 = (f32[2048]{0:T(1024)S(1)}, f32[2048]{0:T(1024)}, u32[]{:S(2)}) copy-start(f32[2048]{0:T(1024)} %copy-done.51) | copy-start | bytes 24580
  922.5 41.1 %copy-start.63 = (f32[256]{0:T(256)S(1)}, f32[256]{0:T(256)}, u32[]{:S(2)}) copy-start(f32[256]{0:T(256)} %copy-done.62) | copy-start | bytes 3076
  963.7 19.3 %copy-start.71 = (f32[256]{0:T(256)S(1)}, f32[256]{0:T(256)}, u32[]{:S(2)}) copy-start(f32[256]{0:T(256)} %copy-done.70) | copy-start | bytes 3076
  963.7 19.3 %copy-start.3 = (f32[256,2048]{1,0:T(8,128)S(1)}, f32[256,2048]{1,0:T(8,128)}, u32[]{:S(2)}) copy-start(f32[256,2048]{1,0:T(8,128)} %copy-done.2) | copy-start | bytes 6291460
  963.7 19.3 %copy-start.48 = (f32[2048]{0:T(1024)S(1)}, f32[2048]{0:T(1024)}, u32[]{:S(2)}) copy-start(f32[2048]{0:T(1024)} %copy-done.47) | copy-start | bytes 24580
  963.7 19.3 %copy-start.61 = (f32[256]{0:T(256)S(1)}, f32[256]{0:T(256)}, u32[]{:S(2)}) copy-start(f32[256]{0:T(256)} %copy-done.60) | copy-start | bytes 3076
  963.7 19.3 %copy-start.69 = (f32[256]{0:T(256)S(1)}, f32[256]{0:T(256)}, u32[]{:S(2)}) copy-start(f32[256]{0:T(256)} %copy-done.68) | copy-start | bytes 3076
  983.0 7.6 copy-start.72
  989.0 2.8 collective-permute-start.1
  1110.7 6.9 copy-start.1
  (41 other events, 96.5 us)
Sparse Core Ops, SparseCore 0:
  34.9 63.3 all-gather.10
  100.4 25.2 all-gather.6
  127.3 121.4 all-gather.12
  250.2 89.2 all-gather.8
  688.7 36.2 reduce-scatter.6
  826.5 62.7 reduce-scatter.4
  891.7 60.2 reduce-scatter.10
  954.4 118.4 reduce-scatter.8

commit v3 on v1

--- a/solution.py
+++ b/solution.py
@@ -1,8 +1,11 @@
+import functools
 import math
 
 import jax
 import jax.numpy as jnp
 from jax import lax
+from jax.experimental import pallas as pl
+from jax.experimental.pallas import tpu as pltpu
 from jax.sharding import Mesh
 from jax.sharding import PartitionSpec as P
 
@@ -16,6 +19,694 @@
 TENSOR = ("x", "core", "y")
 DATA = ("cell", "z")
 RANKS = CORNERS**3
+CHUNKS = 4
+MESH_ID = pl.DeviceIdType.MESH
+OTHERS = [(dx, dc, dy) for dx in (0, 1) for dc in (0, 1) for dy in (0, 1) if dx + dc + dy]
+DMA = pltpu.SemaphoreType.DMA
+VMEM = pl.BlockSpec(memory_space=pltpu.VMEM)
+ANYWHERE = pl.BlockSpec(memory_space=pl.ANY)
+
+
+def remote(source, target, send, receive, device):
+    return pltpu.make_async_remote_copy(
+        src_ref=source,
+        dst_ref=target,
+        send_sem=send,
+        recv_sem=receive,
+        device_id=device,
+        device_id_type=MESH_ID,
+    )
+
+
+def landed(ref, sem, device):
+    remote(ref, ref, sem, sem, device).wait_recv()
+
+
+def corner():
+    return lax.axis_index("x"), lax.axis_index("core"), lax.axis_index("y")
+
+
+def slot(x, c, y):
+    return (x * CORNERS + c) * CORNERS + y
+
+
+def flip(value, bit):
+    return 1 - value if bit else value
+
+
+def neighbours():
+    x, c, y = corner()
+    return {"x": 1 - x}, {"y": 1 - y}, {"core": 1 - c}
+
+
+def plane_peers():
+    x, c, y = corner()
+    peers = []
+    for dx, dc, dy in OTHERS:
+        px, pc, py = flip(x, dx), flip(c, dc), flip(y, dy)
+        peers.append(({"x": px, "core": pc, "y": py}, slot(px, pc, py)))
+    return peers
+
+
+def greet(plane, line):
+    barrier = pltpu.get_barrier_semaphore()
+    near = {"near": neighbours(), "all": [p for p, _ in plane_peers()], None: []}[plane]
+    for device in near:
+        pl.semaphore_signal(barrier, inc=1, device_id=device, device_id_type=MESH_ID)
+    if not line:
+        pl.semaphore_wait(barrier, len(near))
+        return
+    z = lax.axis_index("z")
+
+    @pl.when(z > 0)
+    def _():
+        pl.semaphore_signal(barrier, inc=1, device_id={"z": z - 1}, device_id_type=MESH_ID)
+
+    @pl.when(z < PLANES - 1)
+    def _():
+        pl.semaphore_signal(barrier, inc=1, device_id={"z": z + 1}, device_id_type=MESH_ID)
+
+    edge = (z == 0) | (z == PLANES - 1)
+
+    @pl.when(edge)
+    def _():
+        pl.semaphore_wait(barrier, len(near) + 1)
+
+    @pl.when(jnp.logical_not(edge))
+    def _():
+        pl.semaphore_wait(barrier, len(near) + 2)
+
+
+class Part:
+    def __init__(self, inputs, outs, scratch, steps, plane=None, line=False):
+        self.inputs = inputs
+        self.outs = outs
+        self.scratch = scratch
+        self.steps = steps
+        self.plane, self.line = plane, line
+
+
+def run_kernel(parts, kept, *refs):
+    refs = list(refs)
+
+    def take(counts):
+        groups = []
+        for count in counts:
+            groups.append(refs[:count])
+            del refs[:count]
+        return groups
+
+    ins = take([len(p.inputs) for p in parts])
+    outs = take([len(p.outs) for p in parts])
+    scratch = take([len(p.scratch) for p in parts])
+    ranks = [None, "near", "all"]
+    plane = ranks[max(ranks.index(p.plane) for p in parts)]
+    greet(plane, any(p.line for p in parts))
+    plans = [p.steps(i, o, s) for p, i, o, s in zip(parts, ins, outs, scratch)]
+    for first, _, _ in plans:
+        first()
+    ordered = []
+    for _, middle, _ in plans:
+        ordered += [((n + 0.5) / len(middle), step) for n, step in enumerate(middle)]
+    for _, step in sorted(ordered, key=lambda pair: pair[0]):
+        step()
+    for _, _, last in plans:
+        last()
+
+
+def run(parts, collective_id, vmem=None):
+    inputs = [pair for p in parts for pair in p.inputs]
+    outs = [pair for p in parts for pair in p.outs]
+    return pl.pallas_call(
+        functools.partial(run_kernel, parts, None),
+        out_shape=[shape for shape, _ in outs],
+        in_specs=[spec for _, spec in inputs],
+        out_specs=[spec for _, spec in outs],
+        scratch_shapes=[s for p in parts for s in p.scratch],
+        compiler_params=pltpu.CompilerParams(
+            collective_id=collective_id,
+            has_side_effects=True,
+            vmem_limit_bytes=None if vmem is None else vmem << 20,
+        ),
+    )(*[array for array, _ in inputs])
+
+
+def gather_part(block):
+    rows, columns = block.shape
+    n, half = CHUNKS, CHUNKS // 2
+    chunk = rows // n
+
+    def steps(ins, outs, scratch):
+        (in_ref,), (out_ref,) = ins, outs
+        send_x, send_y, send_c, recv_x, recv_y, recv_c, local = scratch
+        x, c, y = corner()
+        dev_x, dev_y, dev_c = neighbours()
+
+        def at(index, k):
+            start = pl.multiple_of(index * rows + k * chunk, chunk)
+            return out_ref.at[pl.ds(start, chunk), :]
+
+        own, beside_x, beside_y = slot(x, c, y), slot(1 - x, c, y), slot(x, c, 1 - y)
+        across = slot(1 - x, c, 1 - y)
+        mirror = [
+            slot(x, 1 - c, y),
+            slot(1 - x, 1 - c, y),
+            slot(x, 1 - c, 1 - y),
+            slot(1 - x, 1 - c, 1 - y),
+        ]
+        start = pl.multiple_of(own * rows, rows)
+        keep = pltpu.make_async_copy(in_ref, out_ref.at[pl.ds(start, rows), :], local)
+        sent = []
+
+        def go(copy):
+            copy.start()
+            sent.append(copy)
+
+        def share(index, k, b):
+            go(remote(at(index, k), at(index, k), send_c.at[b * n + k], recv_c.at[b * n + k], dev_c))
+
+        order_x = list(range(n))
+        order_y = order_x[half:] + order_x[:half]
+
+        def first():
+            keep.start()
+
+            def mine(k):
+                return in_ref.at[pl.ds(k * chunk, chunk), :]
+
+            for k, j in zip(order_x, order_y):
+                go(remote(mine(k), at(own, k), send_x.at[k], recv_x.at[k], dev_x))
+                go(remote(mine(j), at(own, j), send_y.at[j], recv_y.at[j], dev_y))
+            for k in range(n):
+                go(remote(mine(k), at(own, k), send_c.at[k], recv_c.at[k], dev_c))
+
+        def straight(k, j):
+            landed(at(beside_x, k), recv_x.at[k], dev_x)
+            if k < half:
+                to = at(beside_x, k)
+                go(remote(to, to, send_y.at[n + k], recv_y.at[n + k], dev_y))
+            share(beside_x, k, 1)
+            landed(at(beside_y, j), recv_y.at[j], dev_y)
+            if j >= half:
+                to = at(beside_y, j)
+                go(remote(to, to, send_x.at[half + j], recv_x.at[half + j], dev_x))
+            share(beside_y, j, 2)
+
+        def diagonal(k):
+            landed(at(across, k), recv_y.at[n + k], dev_y)
+            share(across, k, 3)
+            landed(at(across, half + k), recv_x.at[n + k], dev_x)
+            share(across, half + k, 3)
+
+        def last():
+            for b in range(4):
+                for k in range(n):
+                    landed(at(mirror[b], k), recv_c.at[b * n + k], dev_c)
+            for copy in sent:
+                copy.wait_send()
+            keep.wait()
+
+        middle = [functools.partial(straight, k, j) for k, j in zip(order_x, order_y)]
+        middle += [functools.partial(diagonal, k) for k in range(half)]
+        return first, middle, last
+
+    link = DMA((n + half,))
+    core = DMA((4 * n,))
+    return Part(
+        [(block, VMEM)],
+        [(jax.ShapeDtypeStruct((RANKS * rows, columns), block.dtype), ANYWHERE)],
+        [link, link, core, link, link, core, DMA(())],
+        steps,
+        plane="near",
+    )
+
+
+def add_rows(target, start, count, sources, step=16):
+    def body(i, carry):
+        r = pl.multiple_of(start + i * step, step)
+        total = None
+        for ref, shift in sources:
+            value = ref[pl.ds(r - shift if shift else r, step), :].astype(jnp.float32)
+            total = value if total is None else total + value
+        target[pl.ds(r, step), :] = total.astype(target.dtype)
+        return carry
+
+    lax.fori_loop(0, count // step, body, 0)
+
+
+def scatter_part(terms):
+    ranks, rows, columns = terms.shape
+    n, half = CHUNKS, CHUNKS // 2
+    chunk = rows // n
+    middle_row = half * chunk
+
+    def steps(ins, outs, scratch):
+        (part_ref,), (out_ref,) = ins, outs
+        core_buf, x_buf, y_buf, x_diag, y_diag, d_sum, x_sum, y_sum = scratch[:8]
+        send_c, recv_c, send_x, recv_x, send_y, recv_y = scratch[8:]
+        x, c, y = corner()
+        dev_x, dev_y, dev_c = neighbours()
+        D, X, Y, O = range(4)
+        place = [(1 - x, 1 - y), (1 - x, y), (x, 1 - y), (x, y)]
+        mine = [slot(px, c, py) for px, py in place]
+        theirs = [slot(px, 1 - c, py) for px, py in place]
+        orders = {D: [], X: list(range(n)), O: list(range(n))}
+        for k in range(half):
+            orders[D] += [k, half + k]
+        orders[Y] = orders[X][half:] + orders[X][:half]
+        sent = []
+
+        def go(copy):
+            copy.start()
+            sent.append(copy)
+
+        def piece(k):
+            return pl.ds(k * chunk, chunk)
+
+        def first():
+            for b in (D, X, Y, O):
+                for k in orders[b]:
+                    source = part_ref.at[theirs[b], piece(k), :]
+                    i = b * n + k
+                    go(remote(source, core_buf.at[b, piece(k), :], send_c.at[i], recv_c.at[i], dev_c))
+
+        def chip(target, b, k, *more):
+            landed(core_buf.at[b, piece(k), :], recv_c.at[b * n + k], dev_c)
+            sources = [(part_ref.at[mine[b]], 0), (core_buf.at[b], 0), *more]
+            add_rows(target, k * chunk, chunk, sources)
+
+        def to_x(k):
+            go(remote(x_sum.at[piece(k), :], x_buf.at[piece(k), :], send_x.at[k], recv_x.at[k], dev_x))
+
+        def to_y(k):
+            go(remote(y_sum.at[piece(k), :], y_buf.at[piece(k), :], send_y.at[k], recv_y.at[k], dev_y))
+
+        def diagonal(k):
+            chip(d_sum, D, k)
+            source = d_sum.at[piece(k), :]
+            if k < half:
+                go(remote(source, x_diag.at[piece(k), :], send_x.at[n + k], recv_x.at[n + k], dev_x))
+            else:
+                to = y_diag.at[piece(k - half), :]
+                go(remote(source, to, send_y.at[half + k], recv_y.at[half + k], dev_y))
+
+        def direct(k):
+            chip(x_sum, X, k)
+            to_x(k)
+            chip(y_sum, Y, half + k)
+            to_y(half + k)
+
+        def relayed(k):
+            landed(y_diag.at[piece(k), :], recv_y.at[n + k], dev_y)
+            chip(x_sum, X, half + k, (y_diag, middle_row))
+            to_x(half + k)
+            landed(x_diag.at[piece(k), :], recv_x.at[n + k], dev_x)
+            chip(y_sum, Y, k, (x_diag, 0))
+            to_y(k)
+
+        def own(k):
+            landed(x_buf.at[piece(k), :], recv_x.at[k], dev_x)
+            landed(y_buf.at[piece(k), :], recv_y.at[k], dev_y)
+            chip(out_ref, O, k, (x_buf, 0), (y_buf, 0))
+
+        def last():
+            for copy in sent:
+                copy.wait_send()
+
+        middle = [functools.partial(diagonal, k) for k in orders[D]]
+        middle += [functools.partial(direct, k) for k in range(half)]
+        middle += [functools.partial(relayed, k) for k in range(half)]
+        middle += [functools.partial(own, k) for k in range(n)]
+        return first, middle, last
+
+    def low_vmem(*shape):
+        return pltpu.VMEM(shape, jnp.bfloat16)
+
+    whole, part = low_vmem(rows, columns), low_vmem(rows // 2, columns)
+    link = DMA((n + half,))
+    core = DMA((4 * n,))
+    return Part(
+        [(terms, VMEM)],
+        [(jax.ShapeDtypeStruct((rows, columns), jnp.float32), VMEM)],
+        [low_vmem(4, rows, columns), whole, whole, part, part, whole, whole, whole]
+        + [core, core, link, link, link, link],
+        steps,
+        plane="near",
+    )
+
+
+def swap_part(blocks):
+    def steps(ins, outs, scratch):
+        (in_ref,), (out_ref,) = ins, outs
+        send, recv, local = scratch
+        own = slot(*corner())
+        keep = pltpu.make_async_copy(in_ref.at[own], out_ref.at[own], local)
+        peers = plane_peers()
+        sent = []
+
+        def first():
+            keep.start()
+            for i, (there, other) in enumerate(peers):
+                copy = remote(in_ref.at[other], out_ref.at[own], send.at[i], recv.at[i], there)
+                copy.start()
+                sent.append(copy)
+
+        def last():
+            for i, (there, other) in enumerate(peers):
+                landed(out_ref.at[other], recv.at[i], there)
+            for copy in sent:
+                copy.wait_send()
+            keep.wait()
+
+        return first, [], last
+
+    n = len(OTHERS)
+    return Part(
+        [(blocks, VMEM)],
+        [(jax.ShapeDtypeStruct(blocks.shape, blocks.dtype), ANYWHERE)],
+        [DMA((n,)), DMA((n,)), DMA(())],
+        steps,
+        plane="all",
+    )
+
+
+def line_gather_part(block, pieces=4):
+    rows = block.shape[0] // pieces
+
+    def steps(ins, outs, scratch):
+        (in_ref,), (out_ref,) = ins, outs
+        up_send, up_recv, down_send, down_recv, local = scratch
+        z = lax.axis_index("z")
+        keep = pltpu.make_async_copy(in_ref, out_ref.at[z], local)
+
+        def at(block, k):
+            return out_ref.at[block, pl.ds(k * rows, rows), :]
+
+        def up(t, k, source=None):
+            s = at(z - t, k) if source is None else source
+            i = t * pieces + k
+            return remote(s, at(z - t, k), up_send.at[i], up_recv.at[i], {"z": z + 1})
+
+        def down(t, k, source=None):
+            s = at(z + t, k) if source is None else source
+            i = t * pieces + k
+            return remote(s, at(z + t, k), down_send.at[i], down_recv.at[i], {"z": z - 1})
+
+        def first():
+            keep.start()
+            for k in range(pieces):
+                mine = in_ref.at[pl.ds(k * rows, rows), :]
+
+                @pl.when(z < PLANES - 1)
+                def _():
+                    up(0, k, mine).start()
+
+                @pl.when(z > 0)
+                def _():
+                    down(0, k, mine).start()
+
+        def arrive(t, k):
+            i = t * pieces + k
+            on = t + 1 < PLANES - 1
+
+            @pl.when(z - 1 - t >= 0)
+            def _():
+                landed(at(z - 1 - t, k), up_recv.at[i], {"z": z - 1})
+                if on:
+
+                    @pl.when(z < PLANES - 1)
+                    def _():
+                        up(t + 1, k).start()
+
+            @pl.when(z + 1 + t < PLANES)
+            def _():
+                landed(at(z + 1 + t, k), down_recv.at[i], {"z": z + 1})
+                if on:
+
+                    @pl.when(z > 0)
+                    def _():
+                        down(t + 1, k).start()
+
+        def last():
+            for t in range(PLANES - 1):
+                for k in range(pieces):
+
+                    @pl.when((z < PLANES - 1) & (z - t >= 0))
+                    def _():
+                        up(t, k).wait_send()
+
+                    @pl.when((z > 0) & (z + t < PLANES))
+                    def _():
+                        down(t, k).wait_send()
+
+            keep.wait()
+
+        middle = [
+            functools.partial(arrive, t, k) for t in range(PLANES - 1) for k in range(pieces)
+        ]
+        return first, middle, last
+
+    sems = DMA(((PLANES - 1) * pieces,))
+    return Part(
+        [(block, VMEM)],
+        [(jax.ShapeDtypeStruct((PLANES,) + block.shape, block.dtype), ANYWHERE)],
+        [sems, sems, sems, sems, DMA(())],
+        steps,
+        line=True,
+    )
+
+
+def line_scatter_part(terms, pieces=4):
+    line, all_rows, columns = terms.shape
+    rows = all_rows // pieces
+    step = 32
+
+    def steps(ins, outs, scratch):
+        (in_ref,), (out_ref,) = ins, outs
+        up_buf, down_buf, up_stage, down_stage, up_send, up_recv, down_send, down_recv = scratch
+        z = lax.axis_index("z")
+        f32 = jnp.float32
+
+        def cut(k):
+            return pl.ds(k * rows, rows)
+
+        def send_up(source, d, k):
+            i = (d - 1) * pieces + k
+            return remote(source, up_buf.at[d - 1, cut(k), :], up_send.at[i], up_recv.at[i], {"z": z + 1})
+
+        def send_down(source, d, k):
+            i = (d - 1) * pieces + k
+            to = down_buf.at[d - 1, cut(k), :]
+            return remote(source, to, down_send.at[i], down_recv.at[i], {"z": z - 1})
+
+        def first():
+            pass
+
+        def pass_on(d, k):
+            @pl.when(z + d < line)
+            def _():
+                @pl.when(z == 0)
+                def _():
+                    send_up(in_ref.at[z + d, cut(k), :], d, k).start()
+
+                if d + 1 < line:
+
+                    @pl.when(z > 0)
+                    def _():
+                        landed(up_buf.at[d, cut(k), :], up_recv.at[d * pieces + k], {"z": z - 1})
+                        sources = [(in_ref.at[z + d], 0), (up_buf.at[d], 0)]
+                        add_rows(up_stage.at[d - 1], k * rows, rows, sources, step)
+                        send_up(up_stage.at[d - 1, cut(k), :], d, k).start()
+
+            @pl.when(z - d >= 0)
+            def _():
+                @pl.when(z == line - 1)
+                def _():
+                    send_down(in_ref.at[z - d, cut(k), :], d, k).start()
+
+                if d + 1 < line:
+
+                    @pl.when(z < line - 1)
+                    def _():
+                        landed(down_buf.at[d, cut(k), :], down_recv.at[d * pieces + k], {"z": z + 1})
+                        sources = [(in_ref.at[z - d], 0), (down_buf.at[d], 0)]
+                        add_rows(down_stage.at[d - 1], k * rows, rows, sources, step)
+                        send_down(down_stage.at[d - 1, cut(k), :], d, k).start()
+
+        def own(k):
+            @pl.when(z > 0)
+            def _():
+                landed(up_buf.at[0, cut(k), :], up_recv.at[k], {"z": z - 1})
+
+            @pl.when(z < line - 1)
+            def _():
+                landed(down_buf.at[0, cut(k), :], down_recv.at[k], {"z": z + 1})
+
+            mine, below, above = (in_ref.at[z], 0), (up_buf.at[0], 0), (down_buf.at[0], 0)
+
+            @pl.when(z == 0)
+            def _():
+                add_rows(out_ref, k * rows, rows, [mine, above], step)
+
+            @pl.when(z == line - 1)
+            def _():
+                add_rows(out_ref, k * rows, rows, [mine, below], step)
+
+            @pl.when((z > 0) & (z < line - 1))
+            def _():
+                add_rows(out_ref, k * rows, rows, [mine, below, above], step)
+
+        def last():
+            for d in range(line - 1, 0, -1):
+                for k in range(pieces):
+
+                    @pl.when(z + d < line)
+                    def _():
+                        send_up(up_stage.at[d - 1, cut(k), :], d, k).wait_send()
+
+                    @pl.when(z - d >= 0)
+                    def _():
+                        send_down(down_stage.at[d - 1, cut(k), :], d, k).wait_send()
+
+        middle = [
+            functools.partial(pass_on, d, k) for d in range(line - 1, 0, -1) for k in range(pieces)
+        ]
+        middle += [functools.partial(own, k) for k in range(pieces)]
+        return first, middle, last
+
+    sems = DMA(((line - 1) * pieces,))
+    buffer = pltpu.VMEM((line - 1, all_rows, columns), jnp.bfloat16)
+    return Part(
+        [(terms, VMEM)],
+        [(jax.ShapeDtypeStruct((all_rows, columns), jnp.float32), VMEM)],
+        [buffer, buffer, buffer, buffer, sems, sems, sems, sems],
+        steps,
+        line=True,
+    )
+
+
+def everyone(total):
+    sizes = [lax.axis_size(n) for n in ALL]
+    me = 0
+    for n, size in zip(ALL, sizes):
+        me = me * size + lax.axis_index(n)
+
+    def device(index):
+        where = {}
+        for n, size in reversed(list(zip(ALL, sizes))):
+            where[n] = lax.rem(index, size)
+            index = index // size
+        return where
+
+    barrier = pltpu.get_barrier_semaphore()
+
+    def greet_one(d, carry):
+        other = device(lax.rem(me + d, total))
+        pl.semaphore_signal(barrier, inc=1, device_id=other, device_id_type=MESH_ID)
+        return carry
+
+    lax.fori_loop(1, total, greet_one, 0)
+    pl.semaphore_wait(barrier, total - 1)
+    return me, device
+
+
+def hello_kernel(total, gains_ref, marks_ref, gains_out, marks_out, g_send, g_recv, m_send, m_recv, local):
+    me, device = everyone(total)
+    x, c, y = corner()
+    group = x * CORNERS + c
+    keeps = [
+        pltpu.make_async_copy(gains_ref, gains_out.at[me], local.at[0]),
+        pltpu.make_async_copy(marks_ref, marks_out.at[group], local.at[1]),
+    ]
+    for keep in keeps:
+        keep.start()
+    sent = []
+    near = [(i, dx, dc) for i, (dx, dc) in enumerate([(0, 1), (1, 0), (1, 1)])]
+    for i, dx, dc in near:
+        there = {"x": flip(x, dx), "core": flip(c, dc)}
+        copy = remote(marks_ref, marks_out.at[group], m_send.at[i], m_recv.at[i], there)
+        copy.start()
+        sent.append(copy)
+
+    def give(d):
+        other = device(lax.rem(me + d, total))
+        return remote(gains_ref, gains_out.at[me], g_send.at[d], g_recv.at[d], other)
+
+    def put(d, carry):
+        give(d).start()
+        return carry
+
+    lax.fori_loop(1, total, put, 0)
+
+    def take(d, carry):
+        source = lax.rem(me + total - d, total)
+        landed(gains_out.at[source], g_recv.at[d], device(source))
+        give(d).wait_send()
+        return carry
+
+    lax.fori_loop(1, total, take, 0)
+    for i, dx, dc in near:
+        there = {"x": flip(x, dx), "core": flip(c, dc)}
+        landed(marks_out.at[flip(x, dx) * CORNERS + flip(c, dc)], m_recv.at[i], there)
+    for copy in sent:
+        copy.wait_send()
+    for keep in keeps:
+        keep.wait()
+
+
+def hello(total, gains, marks, collective_id):
+    return pl.pallas_call(
+        functools.partial(hello_kernel, total),
+        out_shape=[
+            jax.ShapeDtypeStruct((total,) + gains.shape, gains.dtype),
+            jax.ShapeDtypeStruct((CORNERS**2,) + marks.shape, marks.dtype),
+        ],
+        in_specs=[VMEM, VMEM],
+        out_specs=[VMEM, VMEM],
+        scratch_shapes=[DMA((total,)), DMA((total,)), DMA((3,)), DMA((3,)), DMA((2,))],
+        compiler_params=pltpu.CompilerParams(collective_id=collective_id, has_side_effects=True),
+    )(gains, marks)
+
+
+def spread_kernel(total, in_ref, out_ref, buffer, send, recv):
+    me, device = everyone(total)
+
+    def give(d):
+        other = lax.rem(me + d, total)
+        return remote(in_ref.at[other], buffer.at[me], send.at[d], recv.at[d], device(other))
+
+    def put(d, carry):
+        give(d).start()
+        return carry
+
+    lax.fori_loop(1, total, put, 0)
+
+    def take(d, carry):
+        source = lax.rem(me + total - d, total)
+        landed(buffer.at[source], recv.at[d], device(source))
+        give(d).wait_send()
+        return carry
+
+    lax.fori_loop(1, total, take, 0)
+    out_ref[...] = in_ref[me]
+
+    def add(d, carry):
+        out_ref[...] += buffer[lax.rem(me + d, total)]
+        return carry
+
+    lax.fori_loop(1, total, add, 0)
+
+
+def spread_sum(tiles, collective_id):
+    total = tiles.shape[0]
+    return pl.pallas_call(
+        functools.partial(spread_kernel, total),
+        out_shape=jax.ShapeDtypeStruct(tiles.shape[1:], tiles.dtype),
+        in_specs=[VMEM],
+        out_specs=VMEM,
+        scratch_shapes=[pltpu.VMEM(tiles.shape, tiles.dtype), DMA((total,)), DMA((total,))],
+        compiler_params=pltpu.CompilerParams(collective_id=collective_id, has_side_effects=True),
+    )(tiles)
 
 
 def root_mean_scale(values, gains):
@@ -59,13 +750,14 @@
 def make_shards(cells):
     data_total = cells * PLANES
 
+    def blocks(terms):
+        return low(terms).reshape(RANKS, -1, terms.shape[1])
+
     def gather_tokens(rows):
-        return lax.all_gather(rows, TENSOR, axis=0, tiled=True)
+        return run([gather_part(rows)], 0)[0]
 
     def scatter_tokens(terms):
-        return lax.psum_scatter(low(terms), TENSOR, scatter_dimension=0, tiled=True).astype(
-            jnp.float32
-        )
+        return run([scatter_part(blocks(terms))], 1, 40)[0]
 
     def split_units(weight):
         rows, units = weight.shape
@@ -84,22 +776,20 @@
     def join_columns(parts):
         return jnp.transpose(parts, (1, 0, 2)).reshape(parts.shape[1], -1)
 
-    def gather_columns(pieces):
-        sent = jnp.transpose(jnp.concatenate(pieces, axis=-1), (1, 0, 2))
-        mine = lax.all_to_all(sent, TENSOR, split_axis=0, concat_axis=0, tiled=True)
+    def send_columns(pieces):
+        return jnp.transpose(jnp.concatenate(pieces, axis=-1), (1, 0, 2))
+
+    def gather_columns(mine):
         rows, columns = mine.shape[1:]
         every = lax.all_gather(mine, DATA, axis=0, tiled=False)
         every = every.reshape(data_total, CORNERS**2, CORNERS, rows, columns)
         return jnp.transpose(every, (1, 0, 2, 3, 4)).reshape(-1, columns)
 
-    def scatter_columns(term):
+    def sum_columns(term):
         rows = term.shape[0] // (RANKS * data_total)
         split = low(term).reshape(CORNERS**2, data_total, CORNERS, rows, -1)
         split = jnp.transpose(split, (1, 0, 2, 3, 4)).reshape(data_total * RANKS, rows, -1)
-        mine = lax.psum_scatter(split, DATA, scatter_dimension=0, tiled=True)
-        return lax.all_to_all(mine, TENSOR, split_axis=0, concat_axis=0, tiled=True).astype(
-            jnp.float32
-        )
+        return lax.psum_scatter(split, DATA, scatter_dimension=0, tiled=True)
 
     inner = CORNERS * data_total
     to_rank = []
@@ -137,17 +827,22 @@
         scale_qk = 1.0 / math.sqrt(HEAD_SIZE)
 
         sizes = [norm_attn.shape[0], norm_ffn.shape[0], query_gain.shape[0], key_gain.shape[0]]
-        gains = lax.all_gather(
-            jnp.concatenate([norm_attn, norm_ffn, query_gain, key_gain]), ALL, axis=0, tiled=False
-        ).astype(jnp.float32)
         cuts = [0]
         for size in sizes:
             cuts.append(cuts[-1] + size)
-        gain_attn, gain_ffn, gain_query, gain_key = (
-            gains[:, a:b].reshape(-1) for a, b in zip(cuts[:-1], cuts[1:])
-        )
-
-        w_attn = gather_columns(
+        tile = (8, HEAD_SIZE)
+        pad = tile[0] * tile[1] - cuts[-1]
+        own_gains = jnp.concatenate([norm_attn, norm_ffn, query_gain, key_gain]).astype(jnp.float32)
+        own_gains = jnp.pad(own_gains, (0, pad)).reshape(tile)
+        plane = lax.axis_index("z")
+        group_start = lax.axis_index("cell") * GROUP_TOKENS
+        marks = jnp.concatenate(
+            [
+                lax.dynamic_slice_in_dim(sequence_numbers, group_start, GROUP_TOKENS),
+                lax.dynamic_slice_in_dim(positions, group_start, GROUP_TOKENS),
+            ]
+        ).reshape(-1, HEAD_SIZE)
+        attn_columns = send_columns(
             [
                 split_columns(query_weight),
                 split_columns(key_matrix),
@@ -155,21 +850,19 @@
                 split_columns(gate_weight),
             ]
         )
+        (attn_columns,) = run([swap_part(attn_columns)], 4)
+        attn_columns, own_gains = lax.optimization_barrier((attn_columns, own_gains))
+        gains, marks = hello(RANKS * data_total, own_gains, marks, 2)
+        gains = gains.reshape(RANKS * data_total, -1)
+        gain_attn, gain_ffn, gain_query, gain_key = (
+            gains[:, a:b].reshape(-1) for a, b in zip(cuts[:-1], cuts[1:])
+        )
+        w_attn = gather_columns(attn_columns)
         w_out = lax.all_gather(
             lax.ppermute(out_weight, INNER, to_rank), DATA, axis=0, tiled=True
         )
-        w_ffn = gather_columns([split_units(ffn_gate), split_units(ffn_up)])
-        w_down = lax.all_gather(ffn_down, DATA, axis=0, tiled=True)
-
-        plane = lax.axis_index("z")
-        group_start = lax.axis_index("cell") * GROUP_TOKENS
-        marks = jnp.stack(
-            [
-                lax.dynamic_slice_in_dim(sequence_numbers, group_start, GROUP_TOKENS),
-                lax.dynamic_slice_in_dim(positions, group_start, GROUP_TOKENS),
-            ]
-        )
-        marks = lax.all_gather(marks, ("x", "core"), axis=0, tiled=False)
+
+        marks = marks.reshape(groups, 2, GROUP_TOKENS)
         key_seq, key_pos = marks[:, 0], marks[:, 1]
         own = lax.dynamic_slice_in_dim(marks, plane * window, window, axis=2)
         own_seq, own_pos = own[:, 0], own[:, 1]
@@ -193,9 +886,15 @@
         gate_sig = jax.nn.sigmoid(raw[:, c:])
         query_low = low(prepare_heads(query_raw, gain_query))
         key_low = low(prepare_heads(key_raw, gain_key)).reshape(groups, window, HEAD_SIZE)
-        pair = lax.all_gather(
-            jnp.concatenate([key_low, value_low], axis=-1), "z", axis=0, tiled=False
-        )
+        pair = jnp.concatenate([key_low, value_low], axis=-1).reshape(tokens, 2 * HEAD_SIZE)
+        ffn_columns = send_columns([split_units(ffn_gate), split_units(ffn_up)])
+        pair, cotangent_all, ffn_columns = run(
+            [line_gather_part(pair), gather_part(cotangent), swap_part(ffn_columns)], 3
+        )
+        w_ffn = gather_columns(ffn_columns)
+        own_down, pair = lax.optimization_barrier((ffn_down, pair))
+        w_down = lax.all_gather(own_down, DATA, axis=0, tiled=True)
+        pair = pair.reshape(PLANES, groups, window, 2 * HEAD_SIZE)
         pair = jnp.transpose(pair, (1, 0, 2, 3)).reshape(groups, GROUP_TOKENS, 2 * HEAD_SIZE)
         keys_all, values_all = pair[..., :HEAD_SIZE], pair[..., HEAD_SIZE:]
 
@@ -221,20 +920,23 @@
         gate_ffn, up_ffn = both[:, :units], both[:, units:]
         ffn_sig = jax.nn.sigmoid(gate_ffn)
         mixed_low = low(gate_ffn * ffn_sig * up_ffn)
-        output = low(middle + scatter_tokens(matrix_product(mixed_low, w_down)))
-
-        cotangent_all = gather_tokens(cotangent)
+        down_terms = blocks(matrix_product(mixed_low, w_down))
+
         d_mixed = contract_last(cotangent_all, w_down)
         d_up_low = low(d_mixed * gate_ffn * ffn_sig)
         d_gate_ffn_low = low(d_mixed * up_ffn * ffn_sig * (1.0 + gate_ffn * (1.0 - ffn_sig)))
         d_both = jnp.concatenate([d_gate_ffn_low, d_up_low], axis=-1)
-        d_normed_two = scatter_tokens(contract_last(d_both, w_ffn))
-        grad_down = lax.psum_scatter(
-            low(contract_first(mixed_low, cotangent_all)), DATA, scatter_dimension=0, tiled=True
-        ).astype(jnp.float32)
-        grad_both = scatter_columns(contract_first(normed_two, d_both))
-        grad_gate = join_units(grad_both[..., :units])
-        grad_up = join_units(grad_both[..., units:])
+        both_term = low(contract_first(normed_two, d_both))
+        down_term = low(contract_first(mixed_low, cotangent_all))
+        two_terms = blocks(contract_last(d_both, w_ffn))
+        two_terms, both_term, down_term = lax.optimization_barrier(
+            (two_terms, both_term, down_term)
+        )
+        grad_both = sum_columns(both_term)
+        grad_down = lax.psum_scatter(down_term, DATA, scatter_dimension=0, tiled=True).astype(
+            jnp.float32
+        )
+        (d_normed_two,) = run([scatter_part(two_terms)], 1, 40)
         unused_two, norm_two_back = jax.vjp(root_mean_scale, middle, gain_ffn)
         d_middle_norm, grad_norm_two_term = norm_two_back(d_normed_two)
         d_middle = cotangent.astype(jnp.float32) + d_middle_norm
@@ -270,8 +972,20 @@
         d_pair = jnp.transpose(
             d_pair.reshape(groups, PLANES, window, 2 * HEAD_SIZE), (1, 0, 2, 3)
         )
-        d_pair = lax.psum_scatter(d_pair, "z", scatter_dimension=0, tiled=True)
-        d_pair = d_pair.reshape(groups, window, 2 * HEAD_SIZE).astype(jnp.float32)
+        d_pair, result, grad_both = run(
+            [
+                line_scatter_part(d_pair.reshape(PLANES, tokens, 2 * HEAD_SIZE)),
+                scatter_part(down_terms),
+                swap_part(grad_both),
+            ],
+            5,
+            56,
+        )
+        output = low(middle + result)
+        grad_both = grad_both.astype(jnp.float32)
+        grad_gate = join_units(grad_both[..., :units])
+        grad_up = join_units(grad_both[..., units:])
+        d_pair = d_pair.reshape(groups, window, 2 * HEAD_SIZE)
         d_key_rot, d_value = d_pair[..., :HEAD_SIZE], d_pair[..., HEAD_SIZE:]
         unused_query, query_back = jax.vjp(prepare_heads, query_raw, gain_query)
         d_query_raw, grad_query_gain_term = query_back(d_query_rot)
@@ -286,8 +1000,13 @@
             ],
             axis=-1,
         )
-        d_normed = scatter_tokens(contract_last(d_raw, w_attn))
-        grad_attn = scatter_columns(contract_first(normed_input, d_raw))
+        attn_term = low(contract_first(normed_input, d_raw))
+        one_terms = blocks(contract_last(d_raw, w_attn))
+        one_terms, attn_term = lax.optimization_barrier((one_terms, attn_term))
+        grad_attn = sum_columns(attn_term)
+        (d_normed,) = run([scatter_part(one_terms)], 1, 40)
+        (grad_attn,) = run([swap_part(grad_attn)], 4)
+        grad_attn = grad_attn.astype(jnp.float32)
         grad_query = join_columns(grad_attn[..., :a])
         grad_key = join_columns(grad_attn[..., a:b])
         grad_value = join_columns(grad_attn[..., b:c])
@@ -308,7 +1027,8 @@
             ],
             axis=-1,
         )
-        small = lax.psum_scatter(terms, ALL, scatter_dimension=0, tiled=True).reshape(-1)
+        terms = jnp.pad(terms, ((0, 0), (0, pad))).reshape((-1,) + tile)
+        small = spread_sum(terms, 7).reshape(-1)
         grad_norm_attn, grad_norm_ffn, grad_query_gain, grad_key_gain = (
             small[s:e] for s, e in zip(cuts[:-1], cuts[1:])
         )

time: 1420 us -> 977 us (0.69)
  waiting for transfers between devices: 815 us -> 3.71 us
  Pallas kernels: 0 us -> 520 us
  blocking collectives: 162 us -> 0 us
  local copies, waits for them, and re-layouts: 109 us -> 125 us
    pallas_call x0 -> x12, Pallas kernels: none -> 520 us  [the longest x10 480 us: run(): pl.pallas_call(functools.partial(run_kernel, parts, None), out_shape=[sha...]
    reduce_scatter x8 -> x3, waiting for transfers between devices: 358 us -> 0.01 us  [the longest x2 0.01 us: sum_columns(): return lax.psum_scatter(split, DATA, scatter_dimension=0, tiled=True)]
    all_gather x6 -> x1, waiting for transfers between devices: 304 us -> 3.51 us  [shards(): w_down = lax.all_gather(own_down, DATA, axis=0, tiled=True)]
    all_gather x2, waiting for transfers between devices: 124 us -> 0.04 us  [gather_columns(): every = lax.all_gather(mine, DATA, axis=0, tiled=False)]
    unnamed x2 -> x0, blocking collectives: 83.7 us -> none
    all_to_all x3 -> x0, blocking collectives: 73.2 us -> none  [the longest x2 49.5 us: gather_columns(): mine = lax.all_to_all(sent, TENSOR, split_axis=0, concat_axis=0, tiled=True)]
    reduce_scatter x1, waiting for transfers between devices: 27.5 us -> 0.02 us  [shards(): lax.psum_scatter(low(contract_first(gated_low, branch_all)), DATA, scatte...]
  transfers between devices with their start and end apart: 21 -> 10, of which waited for: 17 -> 1; matrix products, arithmetic and copies ran while one was open for 19% -> 33% of each run, Pallas kernels for 0% -> 52%
where the time goes in v3:
time: 977 us; the launch traced here: 968 us
  Pallas kernels  520 us (53%)
  matrix products  209 us (21%)
  local copies, waits for them, and re-layouts  125 us (13%)
  other arithmetic  90.2 us (9%)
  between operations  15.6 us (2%)
    pallas_call x10, Pallas kernels, run(): pl.pallas_call(functools.partial(run_kernel, parts, None), out_shape=[sha...  480 us
    dot_general x4, matrix products, contract_last(): lax.dot_general(left, right, (((1,), (1,)), ((), ())), preferred_element_...  55.5 us
    dot_general x4, matrix products, contract_first(): lax.dot_general(left, right, (((0,), (0,)), ((), ())), preferred_element_...  42.8 us
    dot_general x4, matrix products, matrix_product(): return jnp.dot(left, right, preferred_element_type=jnp.float32)  42.2 us
    convert_element_type x9, other arithmetic, low(): return values.astype(jnp.bfloat16)  32.6 us
    unnamed x154, local copies, waits for them, and re-layouts  28.3 us
    pallas_call x1, Pallas kernels, spread_sum(): pl.pallas_call(functools.partial(spread_kernel, total), out_shape=jax.Sha...  26.8 us
  transfers between devices with their start and end apart: 10, of which 1 were waited for; matrix products, arithmetic and copies ran while one was open for 33% of the time, Pallas kernels for 52%

profile of v3, /device:TPU:0, one launch (start us, length us, event | category | flops | bytes accessed | tf_op | source)
XLA Modules:
  0.0 968.2 jit_solution(2664237870248348837)
XLA Ops:
  12.1 16.6 %shard_map.263 = bf16[8,64,768]{2,1,0:T(8,128)(2,1)} custom-call(bf16[8,64,768]{2,1,0:T(8,128)(2,1)} %maximum_bitcast_fusion.1.refs_0_), custom_call_target="tpu_custom_call" | custom-call | tf_op jit(solution)/shard_map/pallas_call | solution.py:140
  30.2 12.7 %shard_map.264 = (f32[32,8,128]{2,1,0:T(8,128)}, s32[4,32,128]{2,1,0:T(8,128)}) custom-call(f32[8,128]{1,0:T(8,128)} %fusion.50.gains_ref, s32[32,128]{1,0:T(8,128)} %pad_add_fusion.marks_ref), custom_call_target="tpu_custom_call" | custom-call | tf_op jit(solution)/shard_map/pallas_call | solution.py:658
  56.1 4.0 fusion.38
  64.3 39.8 %shard_map.265 = bf16[2048,2048]{1,0:T(8,128)(2,1)} custom-call(bf16[256,2048]{1,0:T(8,128)(2,1)} %fusion.13.refs_0_), custom_call_target="tpu_custom_call" | custom-call | tf_op jit(solution)/shard_map/pallas_call | solution.py:140
  105.5 6.6 or_and_fusion
  117.0 10.2 %fusion.75 = f32[2048,768]{1,0:T(8,128)S(1)} fusion(bf16[2048,2048]{1,0:T(8,128)(2,1)} %shard_map.265, bf16[2048,768]{1,0:T(8,128)(2,1)S(1)} %bitcast.272), kind=kOutput, calls=%fused_computation.181 | convolution fusion | flops 6442450944 | bytes 17825792 | tf_op jit(solution)/shard_map/dot_general | solution.py:731
  136.8 6.8 fusion.35
  144.8 73.9 %shard_map.266 = (bf16[4,2048,256]{2,1,0:T(8,128)(2,1)}, bf16[2048,2048]{1,0:T(8,128)(2,1)}, bf16[8,64,1536]{2,1,0:T(8,128)(2,1)}) custom-call(bf16[2048,256]{1,0:T(8,128)(2,1)} %pad_maximum_fusion.6.refs_0_, bf16[256,2048]{1,0:T(8,128)(2,1)} %refs_1_.1, bf16[8,64,1536]{2,1,0:T(8,128)(2,1)} %maximum_bitcast_fusion.refs_2_), custom_call_target="tpu_custom_call" | custom-call | tf_op jit(solution)/shard_map/pallas_call | solution.py:140
  228.1 4.9 copy.232
  237.0 18.5 %fusion.74 = (f32[4,2,512]{2,1,0:T(2,128)S(1)}, f32[4,2,512,2048]{2,3,1,0:T(8,128)}) fusion(pred[4,512,2048]{1,2,0:T(8,128)(4,1)} %or_and_fusion, bf16[4,512,2,128]{1,3,2,0:T(8,128)(2,1)} %fusion.28, bf16[4,2048,256]{2,1,0:T(8,128)(2,1)} %bitcast.244), kind=kOutput, calls=%fused_computation.180 | convolution fusion | flops 2181040128 | bytes 40910848 | tf_op jit(solution)/shard_map/sub | solution.py:907
  255.5 12.6 %fusion.7 = bf16[4,2,512,2048]{2,3,1,0:T(8,128)(2,1)S(1)} fusion(f32[4,2,512,2048]{2,3,1,0:T(8,128)} %get-tuple-element.106, f32[4,2,512]{2,1,0:T(2,128)S(1)} %get-tuple-element.105), kind=kLoop, calls=%fused_computation.12 | loop fusion | flops 16777216 | bytes 50348032 | tf_op jit(solution)/shard_map/convert_element_type | solution.py:747
  268.1 5.8 copy-done.5
  279.3 3.7 fusion.20
  283.1 3.9 convolution_convert_fusion.3
  287.0 39.4 %shard_map.267 = f32[256,2048]{1,0:T(8,128)S(1)} custom-call(bf16[8,256,2048]{2,1,0:T(8,128)(2,1)S(1)} %bitcast.240), custom_call_target="tpu_custom_call" | custom-call | tf_op jit(solution)/shard_map/pallas_call | solution.py:140
  329.3 40.3 %shard_map.268 = bf16[2048,2048]{1,0:T(8,128)(2,1)} custom-call(bf16[256,2048]{1,0:T(8,128)(2,1)} %multiply_convert_fusion.4.refs_0_), custom_call_target="tpu_custom_call" | custom-call | tf_op jit(solution)/shard_map/pallas_call | solution.py:140
  376.5 16.5 %fusion.76 = f32[2048,1536]{0,1:T(8,128)} fusion(bf16[2048,2048]{1,0:T(8,128)(2,1)S(1)} %copy-done.23, bf16[2048,1536]{1,0:T(8,128)(2,1)S(1)} %bitcast.259), kind=kOutput, calls=%fused_computation.182 | convolution fusion | flops 12884901888 | bytes 27262976 | tf_op jit(solution)/shard_map/dot_general | solution.py:731
  396.5 18.1 %multiply_convert_fusion.2 = (bf16[2048,768]{0,1:T(8,128)(2,1)}, bf16[2048,768]{0,1:T(8,128)(2,1)}, bf16[2048,768]{0,1:T(8,128)(2,1)S(1)}) fusion(f32[2048,1536]{0,1:T(8,128)} %fusion.76, bf16[2048,2048]{1,0:T(8,128)(2,1)} %get-tuple-element.37, bf16[768,2048]{1,0:T(8,128)(2,1)} %all-gather.9.cloned.1.call-done), kind=kOutput, calls=%fused_computation.21 | convolution fusion | flops 6467616768 | bytes 33554432 | tf_op jit(solution)/shard_map/dot_general | solution.py:735
  414.6 18.2 %convolution_convert_fusion.4 = bf16[2048,1536]{1,0:T(8,128)(2,1)} fusion(bf16[2048,2048]{1,0:T(8,128)(2,1)S(1)} %copy-done.24, bf16[2048,768]{0,1:T(8,128)(2,1)} %get-tuple-element.63, bf16[2048,768]{0,1:T(8,128)(2,1)} %get-tuple-element.62), kind=kOutput, calls=%fused_computation.17 | convolution fusion | flops 12900630528 | bytes 20971520 | tf_op jit(solution)/shard_map/dot_general | solution.py:741
  432.8 19.2 %convolution_convert_fusion.2 = bf16[2048,2048]{1,0:T(8,128)(2,1)} fusion(bf16[2048,1536]{1,0:T(8,128)(2,1)} %bitcast.260, bf16[2048,768]{0,1:T(8,128)(2,1)} %get-tuple-element.63, bf16[2048,768]{0,1:T(8,128)(2,1)} %get-tuple-element.62), kind=kOutput, calls=%fused_computation.15 | convolution fusion | flops 12901679104 | bytes 20971520 | tf_op jit(solution)/shard_map/dot_general | solution.py:735
  452.0 10.4 %convolution_convert_fusion.5 = bf16[768,2048]{1,0:T(8,128)(2,1)} fusion(bf16[2048,768]{0,1:T(8,128)(2,1)S(1)} %get-tuple-element.64, bf16[2048,2048]{1,0:T(8,128)(2,1)} %get-tuple-element.37), kind=kOutput, calls=%fused_computation.33 | convolution fusion | flops 6444023808 | bytes 14680064 | tf_op jit(solution)/shard_map/dot_general | solution.py:741
  462.4 6.2 copy.251
  472.0 39.8 %shard_map.269 = f32[256,2048]{1,0:T(8,128)S(1)} custom-call(bf16[8,256,2048]{2,1,0:T(8,128)(2,1)S(1)} %bitcast.242), custom_call_target="tpu_custom_call" | custom-call | tf_op jit(solution)/shard_map/pallas_call | solution.py:140
  514.8 40.6 %shard_map.270 = bf16[2048,2048]{1,0:T(8,128)(2,1)} custom-call(bf16[256,2048]{1,0:T(8,128)(2,1)} %fusion.61.refs_0_), custom_call_target="tpu_custom_call" | custom-call | tf_op jit(solution)/shard_map/pallas_call | solution.py:140
  555.3 8.8 fusion.23
  565.2 3.7 copy.246
  571.3 6.8 convolution_convert_fusion.7
  578.1 19.4 %fusion.2 = bf16[4,2,512,2048]{2,3,1,0:T(8,128)(2,1)} fusion(bf16[4,512,2,128]{1,3,2,0:T(8,128)(2,1)} %copy.246, f32[4,2,512]{2,1,0:T(2,128)S(1)} %bitcast.297, f32[4,2,512,2048]{2,3,1,0:T(8,128)} %get-tuple-element.106, f32[4,2,512]{2,1,0:T(2,128)S(1)} %copy-done.53, bf16[4,2048,256]{2,1,0:T(8,128)(2,1)} %bitcast.245), kind=kOutput, calls=%fused_computation.3 | convolution fusion | flops 2181038080 | bytes 53510144 | tf_op jit(solution)/shard_map/gqrd,gkd->grqk/dot_general | solution.py:956
  597.6 8.8 bitcast_convert_fusion
  606.4 8.5 fusion.8
  617.9 11.5 %convolution_convert_fusion.1 = bf16[2048,2048]{1,0:T(8,128)(2,1)} fusion(bf16[2048,768]{0,1:T(8,128)(2,1)} %copy-done.70, bf16[768,2048]{1,0:T(8,128)(2,1)} %all-gather.9.cloned.1.call-done), kind=kOutput, calls=%fused_computation.14 | convolution fusion | flops 6446645248 | bytes 14680064 | tf_op jit(solution)/shard_map/dot_general | solution.py:731
  629.4 121.6 %shard_map.271 = (f32[2048,256]{1,0:T(8,128)}, f32[256,2048]{1,0:T(8,128)}, bf16[8,64,1536]{2,1,0:T(8,128)(2,1)}) custom-call(bf16[4,2048,256]{2,1,0:T(8,128)(2,1)} %bitcast.248, bf16[8,256,2048]{2,1,0:T(8,128)(2,1)} %bitcast.250, bf16[8,64,1536]{2,1,0:T(8,128)(2,1)} %reduce-scatter.5.cloned.1.call-done.refs_2_), custom_call_target="tpu_custom_call" | custom-call | tf_op jit(solution)/shard_map/pallas_call | solution.py:140
  751.0 6.5 broadcast_multiply_fusion.1
  760.1 11.1 %bitcast_multiply_fusion.3 = (f32[4,512,2,128]{1,3,2,0:T(8,128)}, f32[4,128,2,512]{3,1,2,0:T(8,128)}) fusion(f32[4,512,128]{1,2,0:T(8,128)} %copy.255, bf16[4,2,512,2048]{2,3,1,0:T(8,128)(2,1)} %fusion.2, bf16[4,2048,256]{2,1,0:T(8,128)(2,1)} %bitcast.246), kind=kOutput, calls=%fused_computation.64 | convolution fusion | flops 2148007936 | bytes 24117248 | tf_op jit(solution)/shard_map/grqk,gkd->gqrd/dot_general | solution.py:961
  782.8 3.7 copy.260
  788.4 5.9 multiply_reduce_fusion.7
  796.1 7.4 convolution_convert_fusion.6
  803.6 9.5 convolution_convert_fusion
  823.6 54.8 %shard_map.272 = f32[256,2048]{1,0:T(8,128)S(1)} custom-call(bf16[8,256,2048]{2,1,0:T(8,128)(2,1)S(1)} %bitcast.241), custom_call_target="tpu_custom_call" | custom-call | tf_op jit(solution)/shard_map/pallas_call | solution.py:140
  881.4 26.8 %shard_map.274 = f32[8,128]{1,0:T(8,128)} custom-call(f32[32,8,128]{2,1,0:T(8,128)} %bitcast.283), custom_call_target="tpu_custom_call" | custom-call | tf_op jit(solution)/shard_map/pallas_call | solution.py:702
  911.6 3.6 reshape.451
  915.2 4.6 copy.268
  919.8 4.0 reshape.452
  923.7 3.6 reshape.449
  927.4 4.6 copy.267
  931.9 4.2 reshape.450
  937.3 5.9 fusion.17
  943.2 13.3 %shard_map.273 = bf16[8,64,768]{2,1,0:T(8,128)(2,1)} custom-call(bf16[8,64,768]{2,1,0:T(8,128)(2,1)} %reduce-scatter.7.cloned.1.call-done.refs_0_), custom_call_target="tpu_custom_call" | custom-call | tf_op jit(solution)/shard_map/pallas_call | solution.py:140
  (274 shorter events, 125.0 us)
Async XLA Ops:
  7.2 21.6 %copy-start.67 = (bf16[64]{0:T(256)(128)(2,1)S(1)}, bf16[64]{0:T(256)(128)(2,1)}, u32[]{:S(2)}) copy-start(bf16[64]{0:T(256)(128)(2,1)} %param.25) | copy-start | bytes 388
  7.2 21.6 %copy-start.65 = (bf16[4]{0:T(256)(128)(2,1)S(1)}, bf16[4]{0:T(256)(128)(2,1)}, u32[]{:S(2)}) copy-start(bf16[4]{0:T(256)(128)(2,1)} %param.24) | copy-start | bytes 28
  7.2 21.6 %copy-start.66 = (bf16[4]{0:T(256)(128)(2,1)S(1)}, bf16[4]{0:T(256)(128)(2,1)}, u32[]{:S(2)}) copy-start(bf16[4]{0:T(256)(128)(2,1)} %param.23) | copy-start | bytes 28
  7.2 21.6 %copy-start.68 = (bf16[64]{0:T(256)(128)(2,1)S(1)}, bf16[64]{0:T(256)(128)(2,1)}, u32[]{:S(2)}) copy-start(bf16[64]{0:T(256)(128)(2,1)} %param.22) | copy-start | bytes 388
  7.2 22.3 %copy-start.63 = (s32[2048]{0:T(1024)S(1)}, s32[2048]{0:T(1024)}, u32[]{:S(2)}) copy-start(s32[2048]{0:T(1024)} %param.31) | copy-start | bytes 24580
  7.2 22.3 %copy-start.64 = (s32[2048]{0:T(1024)S(1)}, s32[2048]{0:T(1024)}, u32[]{:S(2)}) copy-start(s32[2048]{0:T(1024)} %param.30) | copy-start | bytes 24580
  7.3 107.5 %all-gather.11.cloned.1.call-start = ((), (), s32[]{:S(2)}) async-start(), calls=%async_computation.10 | async-start | bytes 3932160 | tf_op jit(solution)/shard_map/all_gather | solution.py:784
  7.3 106.2 %collective-permute-start = (bf16[64,2048]{1,0:T(8,128)(2,1)}, bf16[64,2048]{1,0:T(8,128)(2,1)S(1)}, u32[]{:S(2)}, u32[]{:S(2)}) collective-permute-start(bf16[64,2048]{1,0:T(8,128)(2,1)} %param.21), channel_id=1, source_target_pairs={{0,0},{1,2},{2,4},{3,6},{4,1},{5,3},{6,5},{7,7},{8,8},{9,10},{10,1... | collective-permute-start | bytes 786440 | tf_op jit(solution)/shard_map/ppermute | solution.py:862
  10.0 37.7 %copy-start.36 = (bf16[64,6144]{1,0:T(8,128)(2,1)S(1)}, bf16[64,6144]{1,0:T(8,128)(2,1)}, u32[]{:S(2)}) copy-start(bf16[64,6144]{1,0:T(8,128)(2,1)} %param.26) | copy-start | bytes 2359300
  29.5 253.6 %all-gather.7.cloned.1.call-start = ((), (), s32[]{:S(2)}) async-start(), calls=%async_computation.4 | async-start | bytes 1310720 | tf_op jit(solution)/shard_map/all_gather | solution.py:861
  44.1 7.1 copy-start.37
  45.4 17.6 %copy-start.44 = (f32[2048]{0:T(1024)}, f32[2048]{0:T(1024)S(1)}, u32[]{:S(2)}) copy-start(f32[2048]{0:T(1024)S(1)} %mul.463) | copy-start | bytes 24580
  64.3 41.2 %copy-start.46 = (s32[4,1,2048]{2,0,1:T(4,128)S(1)}, s32[4,1,2048]{2,0,1:T(4,128)}, u32[]{:S(2)}) copy-start(s32[4,1,2048]{2,0,1:T(4,128)} %copy.329) | copy-start | bytes 98308
  64.3 41.2 %copy-start.47 = (s32[4,1,2048]{2,0,1:T(4,128)S(1)}, s32[4,1,2048]{2,0,1:T(4,128)}, u32[]{:S(2)}) copy-start(s32[4,1,2048]{2,0,1:T(4,128)} %copy.330) | copy-start | bytes 98308
  104.2 8.0 copy-start.32
  104.2 8.0 copy-start.33
  114.2 255.5 %all-gather.13.cloned.1.call-start = ((), (), s32[]{:S(2)}) async-start(), calls=%async_computation.11 | async-start | bytes 7864320 | tf_op jit(solution)/shard_map/all_gather | solution.py:784
  117.0 10.3 %copy-start.30 = (bf16[4,4,2,64,768]{4,3,2,1,0:T(8,128)(2,1)}, bf16[4,4,2,64,768]{4,3,2,1,0:T(8,128)(2,1)S(1)}, u32[]{:S(2)}) copy-start(bf16[4,4,2,64,768]{4,3,2,1,0:T(8,128)(2,1)S(1)} %copy.229) | copy-start | bytes 9437188
  134.1 84.9 %copy-start.13 = (f32[4,512,2,128]{3,2,1,0:T(2,128)}, f32[4,512,2,128]{3,2,1,0:T(2,128)S(1)}, u32[]{:S(2)}) copy-start(f32[4,512,2,128]{3,2,1,0:T(2,128)S(1)} %reshape.424) | copy-start | bytes 6291460
  136.8 6.9 copy-start.34
  218.7 177.8 %all-gather.9.cloned.1.call-start = ((), (), s32[]{:S(2)}) async-start(), calls=%async_computation.5 | async-start | bytes 3932160 | tf_op jit(solution)/shard_map/all_gather | solution.py:896
  225.0 8.9 copy-start.8
  255.5 12.6 %copy-start.52 = (f32[4,2,512]{2,1,0:T(2,128)}, f32[4,2,512]{2,1,0:T(2,128)S(1)}, u32[]{:S(2)}) copy-start(f32[4,2,512]{2,1,0:T(2,128)S(1)} %get-tuple-element.105) | copy-start | bytes 49156
  255.5 18.4 %copy-start.14 = (bf16[4,4,512,256]{3,2,1,0:T(8,128)(2,1)S(1)}, bf16[4,4,512,256]{3,2,1,0:T(8,128)(2,1)}, u32[]{:S(2)}) copy-start(bf16[4,4,512,256]{3,2,1,0:T(8,128)(2,1)} %copy.232) | copy-start | bytes 12582916
  276.4 6.7 copy-start.12
  279.1 350.3 %reduce-scatter.5.cloned.1.call-start = ((), (), s32[]{:S(2)}) async-start(), calls=%async_computation.6 | async-start | bytes 7864320 | tf_op jit(solution)/shard_map/reduce_scatter | solution.py:792
  369.7 6.8 copy-start.23
  396.5 18.1 %copy-start.24 = (bf16[2048,2048]{1,0:T(8,128)(2,1)S(1)}, bf16[2048,2048]{1,0:T(8,128)(2,1)}, u32[]{:S(2)}) copy-start(bf16[2048,2048]{1,0:T(8,128)(2,1)} %shard_map.268) | copy-start | bytes 25165828
  414.6 37.4 %copy-start.70 = (bf16[2048,768]{0,1:T(8,128)(2,1)}, bf16[2048,768]{0,1:T(8,128)(2,1)S(1)}, u32[]{:S(2)}) copy-start(bf16[2048,768]{0,1:T(8,128)(2,1)S(1)} %get-tuple-element.64) | copy-start | bytes 9437188
  468.6 346.4 %reduce-scatter.9.cloned.1.call-start = ((), (), s32[]{:S(2)}) async-start(), calls=%async_computation.8 | async-start | bytes 1310720 | tf_op jit(solution)/shard_map/reduce_scatter | solution.py:946
  472.0 39.9 %copy-start.7 = (f32[256,2048]{1,0:T(8,128)S(1)}, f32[256,2048]{1,0:T(8,128)}, u32[]{:S(2)}) copy-start(f32[256,2048]{1,0:T(8,128)} %copy-done.6) | copy-start | bytes 6291460
  571.3 6.8 copy-start.53
  578.1 19.5 %copy-start.19 = (bf16[4,512,2,128]{1,3,2,0:T(8,128)(2,1)S(1)}, bf16[4,512,2,128]{1,3,2,0:T(8,128)(2,1)}, u32[]{:S(2)}) copy-start(bf16[4,512,2,128]{1,3,2,0:T(8,128)(2,1)} %copy.246) | copy-start | bytes 3145732
  597.5 220.0 %reduce-scatter.11.cloned.1.call-start = ((), (), s32[]{:S(2)}) async-start(), calls=%async_computation.9 | async-start | bytes 3932160 | tf_op jit(solution)/shard_map/reduce_scatter | solution.py:936
  597.6 8.9 copy-start.35
  617.8 325.4 %reduce-scatter.7.cloned.1.call-start = ((), (), s32[]{:S(2)}) async-start(), calls=%async_computation.7 | async-start | bytes 3932160 | tf_op jit(solution)/shard_map/reduce_scatter | solution.py:792
  629.4 121.6 %copy-start.16 = (f32[4,512,64]{2,1,0:T(8,128)S(1)}, f32[4,512,64]{2,1,0:T(8,128)}, u32[]{:S(2)}) copy-start(f32[4,512,64]{2,1,0:T(8,128)} %copy-done.15) | copy-start | bytes 1572868
  786.4 9.6 slice-start
  788.4 7.7 slice-start.1
  788.4 7.7 copy-start.38
  788.4 7.7 copy-start.69
  796.1 7.4 copy-start.31
  814.9 1.7 collective-permute-start.1
  823.6 56.2 %copy-start.11 = (bf16[256,2048]{1,0:T(8,128)(2,1)S(1)}, bf16[256,2048]{1,0:T(8,128)(2,1)}, u32[]{:S(2)}) copy-start(bf16[256,2048]{1,0:T(8,128)(2,1)} %param.16) | copy-start | bytes 3145732
  823.6 56.2 %copy-start.45 = (f32[2048]{0:T(1024)S(1)}, f32[2048]{0:T(1024)}, u32[]{:S(2)}) copy-start(f32[2048]{0:T(1024)} %copy-done.44) | copy-start | bytes 24580
  823.6 56.2 %copy-start.55 = (f32[256]{0:T(256)S(1)}, f32[256]{0:T(256)}, u32[]{:S(2)}) copy-start(f32[256]{0:T(256)} %copy-done.54) | copy-start | bytes 3076
  927.4 8.8 copy-start.61
  927.4 8.8 copy-start.62
  (35 other events, 105.7 us)
Sparse Core Ops, SparseCore 0:
  29.6 64.4 all-gather.10
  114.3 27.2 all-gather.6
  218.9 114.4 all-gather.12
  334.8 61.7 all-gather.8
  468.7 109.3 reduce-scatter.4
  597.6 25.1 reduce-scatter.8
  625.3 101.9 reduce-scatter.10
  815.0 64.5 reduce-scatter.6

commit v4 on v3

--- a/solution.py
+++ b/solution.py
@@ -12,6 +12,7 @@
 QUERY_HEADS = 16
 KEY_VALUE_HEADS = 8
 HEAD_SIZE = 128
+REPEAT = QUERY_HEADS // KEY_VALUE_HEADS
 GROUP_TOKENS = 2048
 CORNERS = 2
 PLANES = 4
@@ -69,6 +70,9 @@
 
 
 def greet(plane, line):
+    if plane == "world":
+        everyone(math.prod(lax.axis_size(n) for n in ALL))
+        return
     barrier = pltpu.get_barrier_semaphore()
     near = {"near": neighbours(), "all": [p for p, _ in plane_peers()], None: []}[plane]
     for device in near:
@@ -106,7 +110,7 @@
         self.plane, self.line = plane, line
 
 
-def run_kernel(parts, kept, *refs):
+def run_kernel(parts, *refs):
     refs = list(refs)
 
     def take(counts):
@@ -119,7 +123,7 @@
     ins = take([len(p.inputs) for p in parts])
     outs = take([len(p.outs) for p in parts])
     scratch = take([len(p.scratch) for p in parts])
-    ranks = [None, "near", "all"]
+    ranks = [None, "near", "all", "world"]
     plane = ranks[max(ranks.index(p.plane) for p in parts)]
     greet(plane, any(p.line for p in parts))
     plans = [p.steps(i, o, s) for p, i, o, s in zip(parts, ins, outs, scratch)]
@@ -134,11 +138,15 @@
         last()
 
 
-def run(parts, collective_id, vmem=None):
+def expected(micros):
+    return pl.CostEstimate(flops=0, bytes_accessed=int(micros * 3.5e6), transcendentals=0)
+
+
+def run(parts, collective_id, vmem=None, micros=40):
     inputs = [pair for p in parts for pair in p.inputs]
     outs = [pair for p in parts for pair in p.outs]
     return pl.pallas_call(
-        functools.partial(run_kernel, parts, None),
+        functools.partial(run_kernel, parts),
         out_shape=[shape for shape, _ in outs],
         in_specs=[spec for _, spec in inputs],
         out_specs=[spec for _, spec in outs],
@@ -148,6 +156,7 @@
             has_side_effects=True,
             vmem_limit_bytes=None if vmem is None else vmem << 20,
         ),
+        cost_estimate=expected(micros),
     )(*[array for array, _ in inputs])
 
 
@@ -585,7 +594,7 @@
     )
 
 
-def everyone(total):
+def places():
     sizes = [lax.axis_size(n) for n in ALL]
     me = 0
     for n, size in zip(ALL, sizes):
@@ -598,6 +607,11 @@
             index = index // size
         return where
 
+    return me, device
+
+
+def everyone(total):
+    me, device = places()
     barrier = pltpu.get_barrier_semaphore()
 
     def greet_one(d, carry):
@@ -610,103 +624,222 @@
     return me, device
 
 
-def hello_kernel(total, gains_ref, marks_ref, gains_out, marks_out, g_send, g_recv, m_send, m_recv, local):
-    me, device = everyone(total)
-    x, c, y = corner()
-    group = x * CORNERS + c
-    keeps = [
-        pltpu.make_async_copy(gains_ref, gains_out.at[me], local.at[0]),
-        pltpu.make_async_copy(marks_ref, marks_out.at[group], local.at[1]),
-    ]
-    for keep in keeps:
-        keep.start()
-    sent = []
-    near = [(i, dx, dc) for i, (dx, dc) in enumerate([(0, 1), (1, 0), (1, 1)])]
-    for i, dx, dc in near:
-        there = {"x": flip(x, dx), "core": flip(c, dc)}
-        copy = remote(marks_ref, marks_out.at[group], m_send.at[i], m_recv.at[i], there)
-        copy.start()
-        sent.append(copy)
-
-    def give(d):
-        other = device(lax.rem(me + d, total))
-        return remote(gains_ref, gains_out.at[me], g_send.at[d], g_recv.at[d], other)
-
-    def put(d, carry):
-        give(d).start()
-        return carry
-
-    lax.fori_loop(1, total, put, 0)
-
-    def take(d, carry):
-        source = lax.rem(me + total - d, total)
-        landed(gains_out.at[source], g_recv.at[d], device(source))
-        give(d).wait_send()
-        return carry
-
-    lax.fori_loop(1, total, take, 0)
-    for i, dx, dc in near:
-        there = {"x": flip(x, dx), "core": flip(c, dc)}
-        landed(marks_out.at[flip(x, dx) * CORNERS + flip(c, dc)], m_recv.at[i], there)
-    for copy in sent:
-        copy.wait_send()
-    for keep in keeps:
-        keep.wait()
-
-
-def hello(total, gains, marks, collective_id):
-    return pl.pallas_call(
-        functools.partial(hello_kernel, total),
-        out_shape=[
-            jax.ShapeDtypeStruct((total,) + gains.shape, gains.dtype),
-            jax.ShapeDtypeStruct((CORNERS**2,) + marks.shape, marks.dtype),
+def hello_part(total, gains, marks):
+    def steps(ins, outs, scratch):
+        gains_ref, marks_ref = ins
+        gains_out, marks_out = outs
+        g_send, g_recv, m_send, m_recv, local = scratch
+        me, device = places()
+        x, c, y = corner()
+        group = x * CORNERS + c
+        keeps = [
+            pltpu.make_async_copy(gains_ref, gains_out.at[me], local.at[0]),
+            pltpu.make_async_copy(marks_ref, marks_out.at[group], local.at[1]),
+        ]
+        near = [(i, dx, dc) for i, (dx, dc) in enumerate([(0, 1), (1, 0), (1, 1)])]
+        sent = []
+
+        def give(d):
+            other = device(lax.rem(me + d, total))
+            return remote(gains_ref, gains_out.at[me], g_send.at[d], g_recv.at[d], other)
+
+        def first():
+            for keep in keeps:
+                keep.start()
+            for i, dx, dc in near:
+                there = {"x": flip(x, dx), "core": flip(c, dc)}
+                copy = remote(marks_ref, marks_out.at[group], m_send.at[i], m_recv.at[i], there)
+                copy.start()
+                sent.append(copy)
+
+            def put(d, carry):
+                give(d).start()
+                return carry
+
+            lax.fori_loop(1, total, put, 0)
+
+        def last():
+            def take(d, carry):
+                source = lax.rem(me + total - d, total)
+                landed(gains_out.at[source], g_recv.at[d], device(source))
+                give(d).wait_send()
+                return carry
+
+            lax.fori_loop(1, total, take, 0)
+            for i, dx, dc in near:
+                there = {"x": flip(x, dx), "core": flip(c, dc)}
+                theirs = flip(x, dx) * CORNERS + flip(c, dc)
+                landed(marks_out.at[theirs], m_recv.at[i], there)
+            for copy in sent:
+                copy.wait_send()
+            for keep in keeps:
+                keep.wait()
+
+        return first, [], last
+
+    return Part(
+        [(gains, VMEM), (marks, VMEM)],
+        [
+            (jax.ShapeDtypeStruct((total,) + gains.shape, gains.dtype), VMEM),
+            (jax.ShapeDtypeStruct((CORNERS**2,) + marks.shape, marks.dtype), VMEM),
         ],
-        in_specs=[VMEM, VMEM],
-        out_specs=[VMEM, VMEM],
-        scratch_shapes=[DMA((total,)), DMA((total,)), DMA((3,)), DMA((3,)), DMA((2,))],
-        compiler_params=pltpu.CompilerParams(collective_id=collective_id, has_side_effects=True),
-    )(gains, marks)
-
-
-def spread_kernel(total, in_ref, out_ref, buffer, send, recv):
-    me, device = everyone(total)
-
-    def give(d):
-        other = lax.rem(me + d, total)
-        return remote(in_ref.at[other], buffer.at[me], send.at[d], recv.at[d], device(other))
-
-    def put(d, carry):
-        give(d).start()
-        return carry
-
-    lax.fori_loop(1, total, put, 0)
-
-    def take(d, carry):
-        source = lax.rem(me + total - d, total)
-        landed(buffer.at[source], recv.at[d], device(source))
-        give(d).wait_send()
-        return carry
-
-    lax.fori_loop(1, total, take, 0)
-    out_ref[...] = in_ref[me]
-
-    def add(d, carry):
-        out_ref[...] += buffer[lax.rem(me + d, total)]
-        return carry
-
-    lax.fori_loop(1, total, add, 0)
-
-
-def spread_sum(tiles, collective_id):
+        [DMA((total,)), DMA((total,)), DMA((3,)), DMA((3,)), DMA((2,))],
+        steps,
+        plane="world",
+    )
+
+
+def columns_part(blocks):
+    ranks, rows, columns = blocks.shape
+
+    def steps(ins, outs, scratch):
+        (in_ref,), (out_ref,) = ins, outs
+        send, recv, up_send, up_recv, down_send, down_recv, local = scratch
+        x, c, y = corner()
+        z = lax.axis_index("z")
+        own = slot(x, c, y)
+        peers = plane_peers()
+        spots = [(x * CORNERS + c, y)]
+        spots += [(flip(x, dx) * CORNERS + flip(c, dc), flip(y, dy)) for dx, dc, dy in OTHERS]
+
+        def at(i, plane):
+            return out_ref.at[spots[i][0], plane, spots[i][1]]
+
+        keep = pltpu.make_async_copy(in_ref.at[own], at(0, z), local)
+        sent = []
+
+        def up(t, i, source=None):
+            s = at(i, z - t) if source is None else source
+            n = t * RANKS + i
+            return remote(s, at(i, z - t), up_send.at[n], up_recv.at[n], {"z": z + 1})
+
+        def down(t, i, source=None):
+            s = at(i, z + t) if source is None else source
+            n = t * RANKS + i
+            return remote(s, at(i, z + t), down_send.at[n], down_recv.at[n], {"z": z - 1})
+
+        def begin(i, source=None):
+            @pl.when(z < PLANES - 1)
+            def _():
+                up(0, i, source).start()
+
+            @pl.when(z > 0)
+            def _():
+                down(0, i, source).start()
+
+        def first():
+            keep.start()
+            for i, (there, other) in enumerate(peers):
+                copy = remote(in_ref.at[other], at(0, z), send.at[i], recv.at[i], there)
+                copy.start()
+                sent.append(copy)
+            begin(0, in_ref.at[own])
+
+        def swapped(i):
+            landed(at(i, z), recv.at[i - 1], peers[i - 1][0])
+            begin(i)
+
+        def arrive(t, i):
+            n = t * RANKS + i
+            on = t + 1 < PLANES - 1
+
+            @pl.when(z - 1 - t >= 0)
+            def _():
+                landed(at(i, z - 1 - t), up_recv.at[n], {"z": z - 1})
+                if on:
+
+                    @pl.when(z < PLANES - 1)
+                    def _():
+                        up(t + 1, i).start()
+
+            @pl.when(z + 1 + t < PLANES)
+            def _():
+                landed(at(i, z + 1 + t), down_recv.at[n], {"z": z + 1})
+                if on:
+
+                    @pl.when(z > 0)
+                    def _():
+                        down(t + 1, i).start()
+
+        def last():
+            for copy in sent:
+                copy.wait_send()
+            for t in range(PLANES - 1):
+                for i in range(RANKS):
+
+                    @pl.when((z < PLANES - 1) & (z - t >= 0))
+                    def _():
+                        up(t, i).wait_send()
+
+                    @pl.when((z > 0) & (z + t < PLANES))
+                    def _():
+                        down(t, i).wait_send()
+
+            keep.wait()
+
+        middle = [functools.partial(swapped, i) for i in range(1, RANKS)]
+        middle += [
+            functools.partial(arrive, t, i) for t in range(PLANES - 1) for i in range(RANKS)
+        ]
+        return first, middle, last
+
+    n = len(OTHERS)
+    sems = DMA(((PLANES - 1) * RANKS,))
+    shape = (CORNERS**2, PLANES, CORNERS, rows, columns)
+    return Part(
+        [(blocks, VMEM)],
+        [(jax.ShapeDtypeStruct(shape, blocks.dtype), ANYWHERE)],
+        [DMA((n,)), DMA((n,)), sems, sems, sems, sems, DMA(())],
+        steps,
+        plane="all",
+        line=True,
+    )
+
+
+def spread_part(tiles):
     total = tiles.shape[0]
-    return pl.pallas_call(
-        functools.partial(spread_kernel, total),
-        out_shape=jax.ShapeDtypeStruct(tiles.shape[1:], tiles.dtype),
-        in_specs=[VMEM],
-        out_specs=VMEM,
-        scratch_shapes=[pltpu.VMEM(tiles.shape, tiles.dtype), DMA((total,)), DMA((total,))],
-        compiler_params=pltpu.CompilerParams(collective_id=collective_id, has_side_effects=True),
-    )(tiles)
+
+    def steps(ins, outs, scratch):
+        (in_ref,), (out_ref,) = ins, outs
+        buffer, send, recv = scratch
+        me, device = places()
+
+        def give(d):
+            other = lax.rem(me + d, total)
+            return remote(in_ref.at[other], buffer.at[me], send.at[d], recv.at[d], device(other))
+
+        def first():
+            def put(d, carry):
+                give(d).start()
+                return carry
+
+            lax.fori_loop(1, total, put, 0)
+
+        def last():
+            def take(d, carry):
+                source = lax.rem(me + total - d, total)
+                landed(buffer.at[source], recv.at[d], device(source))
+                give(d).wait_send()
+                return carry
+
+            lax.fori_loop(1, total, take, 0)
+            out_ref[...] = in_ref[me]
+
+            def add(d, carry):
+                out_ref[...] += buffer[lax.rem(me + d, total)]
+                return carry
+
+            lax.fori_loop(1, total, add, 0)
+
+        return first, [], last
+
+    return Part(
+        [(tiles, VMEM)],
+        [(jax.ShapeDtypeStruct(tiles.shape[1:], tiles.dtype), VMEM)],
+        [pltpu.VMEM(tiles.shape, tiles.dtype), DMA((total,)), DMA((total,))],
+        steps,
+        plane="world",
+    )
 
 
 def root_mean_scale(values, gains):
@@ -714,17 +847,12 @@
 
 
 def rope_tables(positions):
-    steps_half = jnp.arange(HEAD_SIZE // 2).astype(jnp.float32)
+    half = HEAD_SIZE // 2
+    steps_half = jnp.arange(half).astype(jnp.float32)
     inverse = jnp.power(1000000.0, steps_half * (-2.0 / HEAD_SIZE))
-    angles = positions.astype(jnp.float32)[..., None] * inverse
-    angles = jnp.concatenate([angles, angles], axis=-1)
-    return (jnp.cos(angles)[..., None, :], jnp.sin(angles)[..., None, :])
-
-
-def rotary_apply(values, cosine_factor, sine_factor):
-    half_dim = values.shape[-1] // 2
-    turned = jnp.concatenate([-values[..., half_dim:], values[..., :half_dim]], axis=-1)
-    return values * cosine_factor + turned * sine_factor
+    angles = positions.astype(jnp.float32)[:, None] * inverse[None, :]
+    cosine, sine = jnp.cos(angles), jnp.sin(angles)
+    return jnp.concatenate([cosine, cosine], axis=-1), jnp.concatenate([-sine, sine], axis=-1)
 
 
 def matrix_product(left, right):
@@ -746,6 +874,341 @@
 def low(values):
     return values.astype(jnp.bfloat16)
 
+def turn(values, cosine, sine):
+    return values * cosine + pltpu.roll(values, HEAD_SIZE // 2, 1) * sine
+
+
+def turn_back(grads, cosine, sine):
+    return grads * cosine + pltpu.roll(grads * sine, HEAD_SIZE // 2, 1)
+
+
+def unit_scale(values):
+    return lax.rsqrt(jnp.mean(values * values, axis=-1, keepdims=True) + 1e-06)
+
+
+def norm_back(raw, gain, grads):
+    scale = unit_scale(raw)
+    unit = raw * scale
+    inner = grads * gain
+    d_raw = scale * (inner - unit * jnp.mean(inner * unit, axis=-1, keepdims=True))
+    return d_raw, grads * unit
+
+
+def head(index):
+    return slice(index * HEAD_SIZE, (index + 1) * HEAD_SIZE)
+
+
+def dot(left, right):
+    return jnp.dot(left, right, preferred_element_type=jnp.float32)
+
+
+def dot_rows(left, right):
+    return lax.dot_general(
+        left, right, (((1,), (1,)), ((), ())), preferred_element_type=jnp.float32
+    )
+
+
+def prepare_kernel(
+    x_ref, gain_ref, w_ref, cos_ref, sin_ref, qg_ref, kg_ref, x_out, q_ref, kv_ref, raw_ref, gate_ref
+):
+    hidden = x_ref[...].astype(jnp.float32)
+    x_out[...] = low(hidden * unit_scale(hidden) * gain_ref[...])
+    raw = dot(x_out[...], w_ref[...])
+    cosine, sine = cos_ref[...], sin_ref[...]
+
+    def prepare(values, gain):
+        return low(turn(values * unit_scale(values) * gain, cosine, sine))
+
+    for h in range(REPEAT):
+        q_ref[:, head(h)] = prepare(raw[:, head(h)], qg_ref[...])
+    kv_ref[:, head(0)] = prepare(raw[:, head(REPEAT)], kg_ref[...])
+    kv_ref[:, head(1)] = low(raw[:, head(REPEAT + 1)])
+    raw_ref[...] = raw[:, : (REPEAT + 1) * HEAD_SIZE]
+    gate_ref[...] = raw[:, (REPEAT + 2) * HEAD_SIZE :]
+
+
+def rows_spec(rows, columns):
+    return pl.BlockSpec((rows, columns), lambda i: (i, 0))
+
+
+def fixed_spec(*shape):
+    return pl.BlockSpec(shape, lambda i: (0,) * len(shape))
+
+
+def kernel_params(vmem):
+    return pltpu.CompilerParams(vmem_limit_bytes=vmem << 20)
+
+
+def prepare_attention(hidden, gain_attn, w_attn, cosine, sine, gain_query, gain_key):
+    tokens, width = hidden.shape
+    columns = w_attn.shape[1]
+    q_columns = REPEAT * HEAD_SIZE
+    rows = tokens // RANKS
+    shape = jax.ShapeDtypeStruct
+    return pl.pallas_call(
+        prepare_kernel,
+        grid=(RANKS,),
+        out_shape=[
+            shape((tokens, width), jnp.bfloat16),
+            shape((tokens, q_columns), jnp.bfloat16),
+            shape((tokens, 2 * HEAD_SIZE), jnp.bfloat16),
+            shape((tokens, q_columns + HEAD_SIZE), jnp.float32),
+            shape((tokens, q_columns), jnp.float32),
+        ],
+        in_specs=[
+            rows_spec(rows, width),
+            fixed_spec(1, width),
+            fixed_spec(width, columns),
+            rows_spec(rows, HEAD_SIZE),
+            rows_spec(rows, HEAD_SIZE),
+            fixed_spec(1, HEAD_SIZE),
+            fixed_spec(1, HEAD_SIZE),
+        ],
+        out_specs=[
+            rows_spec(rows, width),
+            rows_spec(rows, q_columns),
+            rows_spec(rows, 2 * HEAD_SIZE),
+            rows_spec(rows, q_columns + HEAD_SIZE),
+            rows_spec(rows, q_columns),
+        ],
+        compiler_params=kernel_params(32),
+        cost_estimate=expected(12),
+    )(hidden, gain_attn[None], w_attn, cosine, sine, gain_query[None], gain_key[None])
+
+
+EXPONENT = math.log2(math.e) / math.sqrt(HEAD_SIZE)
+
+
+def allowed_keys(own_ref, keys_ref, z, window):
+    seq, pos = own_ref[0, :, 0:1], own_ref[0, :, 1:2]
+    key_seq = keys_ref[0, 0:1, z * window : (z + 1) * window]
+    key_pos = keys_ref[0, 1:2, z * window : (z + 1) * window]
+    return (key_pos <= pos) & ((key_seq == 0) | (key_seq == seq))
+
+
+def attend_kernel(q_ref, kv_ref, gate_ref, own_ref, keys_ref, wo_ref, terms_ref, att_ref, log_ref, gated_ref):
+    planes, window = kv_ref.shape[0], kv_ref.shape[1]
+    totals = [None] * REPEAT
+    ones = jnp.ones((window, HEAD_SIZE), jnp.bfloat16)
+    for z in range(planes):
+        allowed = allowed_keys(own_ref, keys_ref, z, window)
+        keys = kv_ref[z, :, head(0)]
+        values = jnp.concatenate([kv_ref[z, :, head(1)], ones], axis=1)
+        for h in range(REPEAT):
+            scores = dot_rows(q_ref[:, head(h)], keys) * EXPONENT
+            exponent = low(jnp.where(allowed, jnp.exp2(scores), 0.0))
+            part = dot(exponent, values)
+            totals[h] = part if totals[h] is None else totals[h] + part
+    for h in range(REPEAT):
+        weight = totals[h][:, head(1)]
+        attended = totals[h][:, head(0)] / weight
+        att_ref[:, head(h)] = attended
+        log_ref[:, head(h)] = jnp.log2(weight)
+        gated_ref[:, head(h)] = low(attended * jax.nn.sigmoid(gate_ref[:, head(h)]))
+    terms_ref[...] = low(dot(gated_ref[...], wo_ref[...]))
+
+
+def group_specs(window):
+    return [
+        pl.BlockSpec((PLANES, window, 2 * HEAD_SIZE), lambda i: (0, i, 0)),
+        pl.BlockSpec((1, window, 2), lambda i: (i, 0, 0)),
+        pl.BlockSpec((1, 2, PLANES * window), lambda i: (i, 0, 0)),
+    ]
+
+
+def attend(query, pair, gate, own, keys, w_out):
+    tokens, q_columns = query.shape
+    groups = own.shape[0]
+    window = tokens // groups
+    width = w_out.shape[1]
+    kv, mine, marks = group_specs(window)
+    shape = jax.ShapeDtypeStruct
+    columns = rows_spec(window, q_columns)
+    return pl.pallas_call(
+        attend_kernel,
+        grid=(groups,),
+        out_shape=[
+            shape((tokens, width), jnp.bfloat16),
+            shape((tokens, q_columns), jnp.float32),
+            shape((tokens, q_columns), jnp.float32),
+            shape((tokens, q_columns), jnp.bfloat16),
+        ],
+        in_specs=[columns, kv, columns, mine, marks, fixed_spec(q_columns, width)],
+        out_specs=[rows_spec(window, width), columns, columns, columns],
+        compiler_params=kernel_params(48),
+        cost_estimate=expected(18),
+    )(query, pair, gate, own, keys, w_out)
+
+
+def attend_back_kernel(
+    branch_ref, wo_ref, q_ref, kv_ref, gate_ref, own_ref, keys_ref, att_ref, log_ref, raw_ref,
+    cos_ref, sin_ref, qg_ref, dq_ref, dgate_ref, dkv_ref, gain_ref,
+):
+    planes, window = kv_ref.shape[0], kv_ref.shape[1]
+    scale = 1.0 / math.sqrt(HEAD_SIZE)
+    d_gated = dot_rows(branch_ref[...], wo_ref[...])
+    gate = jax.nn.sigmoid(gate_ref[...])
+    attended = att_ref[...]
+    d_attended = low(d_gated * gate)
+    dgate_ref[...] = low(d_gated * attended * gate * (1.0 - gate))
+    product = d_attended.astype(jnp.float32) * attended
+    delta = [jnp.sum(product[:, head(h)], axis=-1, keepdims=True) for h in range(REPEAT)]
+    turned_q = [jnp.transpose(q_ref[:, head(h)]) for h in range(REPEAT)]
+    turned_d = [jnp.transpose(d_attended[:, head(h)]) for h in range(REPEAT)]
+    d_query = [None] * REPEAT
+    for z in range(planes):
+        allowed = allowed_keys(own_ref, keys_ref, z, window)
+        keys, values = kv_ref[z, :, head(0)], kv_ref[z, :, head(1)]
+        d_keys, d_values = None, None
+        for h in range(REPEAT):
+            scores = dot_rows(q_ref[:, head(h)], keys) * EXPONENT - log_ref[:, h * HEAD_SIZE : h * HEAD_SIZE + 1]
+            probs = jnp.where(allowed, jnp.exp2(scores), 0.0)
+            d_probs = dot_rows(d_attended[:, head(h)], values)
+            d_scores = low(probs * (d_probs - delta[h]))
+            part = dot(d_scores, keys)
+            d_query[h] = part if d_query[h] is None else d_query[h] + part
+            part = dot(turned_q[h], d_scores)
+            d_keys = part if d_keys is None else d_keys + part
+            part = dot(turned_d[h], low(probs))
+            d_values = part if d_values is None else d_values + part
+        dkv_ref[z, :, head(0)] = low(jnp.transpose(d_keys * scale))
+        dkv_ref[z, :, head(1)] = low(jnp.transpose(d_values))
+    cosine, sine = cos_ref[...], sin_ref[...]
+    total = jnp.zeros((1, HEAD_SIZE), jnp.float32)
+    for h in range(REPEAT):
+        grads = turn_back(d_query[h] * scale, cosine, sine)
+        d_raw, by_row = norm_back(raw_ref[:, head(h)], qg_ref[...], grads)
+        dq_ref[:, head(h)] = low(d_raw)
+        total += jnp.sum(by_row, axis=0, keepdims=True)
+    gain_ref[0] = jnp.broadcast_to(total, gain_ref.shape[1:])
+
+
+def attend_back(branch, w_out, query, pair, gate, own, keys, attended, log, raw, cosine, sine, gain):
+    tokens, q_columns = query.shape
+    groups = own.shape[0]
+    window = tokens // groups
+    width = w_out.shape[1]
+    kv, mine, marks = group_specs(window)
+    shape = jax.ShapeDtypeStruct
+    columns = rows_spec(window, q_columns)
+    table = rows_spec(window, HEAD_SIZE)
+    return pl.pallas_call(
+        attend_back_kernel,
+        grid=(groups,),
+        out_shape=[
+            shape((tokens, q_columns), jnp.bfloat16),
+            shape((tokens, q_columns), jnp.bfloat16),
+            shape(pair.shape, jnp.bfloat16),
+            shape((groups, 8, HEAD_SIZE), jnp.float32),
+        ],
+        in_specs=[
+            rows_spec(window, width), fixed_spec(q_columns, width), columns, kv, columns, mine, marks,
+            columns, columns, rows_spec(window, raw.shape[1]), table, table, fixed_spec(1, HEAD_SIZE),
+        ],
+        out_specs=[columns, columns, kv, pl.BlockSpec((1, 8, HEAD_SIZE), lambda i: (i, 0, 0))],
+        compiler_params=kernel_params(56),
+        cost_estimate=expected(35),
+    )(branch, w_out, query, pair, gate, own, keys, attended, log, raw, cosine, sine, gain[None])
+
+
+def finish_kernel(dkv_ref, raw_ref, cos_ref, sin_ref, kg_ref, dq_ref, dgate_ref, out_ref, gain_ref):
+    grads = turn_back(dkv_ref[:, head(0)], cos_ref[...], sin_ref[...])
+    d_raw, by_row = norm_back(raw_ref[:, head(REPEAT)], kg_ref[...], grads)
+    out_ref[:, : REPEAT * HEAD_SIZE] = dq_ref[...]
+    out_ref[:, head(REPEAT)] = low(d_raw)
+    out_ref[:, head(REPEAT + 1)] = low(dkv_ref[:, head(1)])
+    out_ref[:, (REPEAT + 2) * HEAD_SIZE :] = dgate_ref[...]
+    gain_ref[0] = jnp.broadcast_to(jnp.sum(by_row, axis=0, keepdims=True), gain_ref.shape[1:])
+
+
+def finish_attention(d_pair, raw, cosine, sine, gain, d_query, d_gate, steps=4):
+    tokens, q_columns = d_query.shape
+    rows = tokens // steps
+    shape = jax.ShapeDtypeStruct
+    table = rows_spec(rows, HEAD_SIZE)
+    columns = 2 * q_columns + 2 * HEAD_SIZE
+    return pl.pallas_call(
+        finish_kernel,
+        grid=(steps,),
+        out_shape=[shape((tokens, columns), jnp.bfloat16), shape((steps, 8, HEAD_SIZE), jnp.float32)],
+        in_specs=[
+            rows_spec(rows, 2 * HEAD_SIZE), rows_spec(rows, raw.shape[1]), table, table,
+            fixed_spec(1, HEAD_SIZE), rows_spec(rows, q_columns), rows_spec(rows, q_columns),
+        ],
+        out_specs=[rows_spec(rows, columns), pl.BlockSpec((1, 8, HEAD_SIZE), lambda i: (i, 0, 0))],
+        compiler_params=kernel_params(32),
+        cost_estimate=expected(5),
+    )(d_pair, raw, cosine, sine, gain[None], d_query, d_gate)
+
+
+def split_kernel(pieces, gate_ref, up_ref, out_ref):
+    units = gate_ref.shape[1] // CORNERS
+    piece = units // pieces
+    for y in range(CORNERS):
+        for at, ref in ((0, gate_ref), (units, up_ref)):
+            starts = [(d * CORNERS + y) * piece for d in range(pieces)]
+            parts = [ref[:, start : start + piece] for start in starts]
+            out_ref[y, :, at : at + units] = jnp.concatenate(parts, axis=1)
+
+
+def split_units(gate, up, pieces):
+    rows, units = gate.shape
+    width = units // CORNERS**2
+    narrow = pl.BlockSpec((rows, width), lambda i: (0, i))
+    return pl.pallas_call(
+        functools.partial(split_kernel, pieces),
+        grid=(CORNERS**2,),
+        out_shape=jax.ShapeDtypeStruct((RANKS, rows, width), gate.dtype),
+        in_specs=[narrow, narrow],
+        out_specs=pl.BlockSpec((CORNERS, rows, width), lambda i: (i, 0, 0)),
+        cost_estimate=expected(3),
+    )(gate, up)
+
+
+def join_kernel(pieces, in_ref, gate_ref, up_ref):
+    units = gate_ref.shape[1] // CORNERS
+    piece = units // pieces
+    for at, ref in ((0, gate_ref), (units, up_ref)):
+        parts = []
+        for d in range(pieces):
+            for y in range(CORNERS):
+                parts.append(in_ref[y, :, at + d * piece : at + (d + 1) * piece].astype(jnp.float32))
+        ref[...] = jnp.concatenate(parts, axis=1)
+
+
+def join_units(parts, pieces):
+    ranks, rows, width = parts.shape
+    narrow = pl.BlockSpec((rows, width), lambda i: (0, i))
+    shape = jax.ShapeDtypeStruct((rows, width * CORNERS**2), jnp.float32)
+    return pl.pallas_call(
+        functools.partial(join_kernel, pieces),
+        grid=(CORNERS**2,),
+        out_shape=[shape, shape],
+        in_specs=[pl.BlockSpec((CORNERS, rows, width), lambda i: (i, 0, 0))],
+        out_specs=[narrow, narrow],
+        cost_estimate=expected(4),
+    )(parts)
+
+
+def widen_kernel(in_ref, *out_refs):
+    start = 0
+    for ref in out_refs:
+        width = ref.shape[1]
+        ref[...] = in_ref[0, :, start : start + width].astype(jnp.float32)
+        start += width
+
+
+def widen_columns(parts, widths):
+    ranks, rows, columns = parts.shape
+    return pl.pallas_call(
+        widen_kernel,
+        grid=(ranks,),
+        out_shape=[jax.ShapeDtypeStruct((rows, ranks * w), jnp.float32) for w in widths],
+        in_specs=[pl.BlockSpec((1, rows, columns), lambda i: (i, 0, 0))],
+        out_specs=[pl.BlockSpec((rows, w), lambda i: (0, i)) for w in widths],
+        cost_estimate=expected(3),
+    )(parts)
+
 
 def make_shards(cells):
     data_total = cells * PLANES
@@ -759,25 +1222,17 @@
     def scatter_tokens(terms):
         return run([scatter_part(blocks(terms))], 1, 40)[0]
 
-    def split_units(weight):
-        rows, units = weight.shape
-        piece = units // (RANKS * data_total)
-        split = weight.reshape(rows, CORNERS**2, data_total, CORNERS, piece)
-        return jnp.transpose(split, (0, 1, 3, 2, 4)).reshape(rows, RANKS, units // RANKS)
-
-    def join_units(parts):
-        ranks, rows, units = parts.shape
-        split = parts.reshape(CORNERS**2, CORNERS, rows, data_total, units // data_total)
-        return jnp.transpose(split, (2, 0, 3, 1, 4)).reshape(rows, ranks * units)
-
     def split_columns(weight):
         return weight.reshape(weight.shape[0], RANKS, -1)
 
-    def join_columns(parts):
-        return jnp.transpose(parts, (1, 0, 2)).reshape(parts.shape[1], -1)
-
     def send_columns(pieces):
         return jnp.transpose(jnp.concatenate(pieces, axis=-1), (1, 0, 2))
+
+    def join_cells(rows):
+        if cells > 1:
+            rows = lax.all_gather(rows, "cell", axis=0, tiled=False)
+            rows = jnp.transpose(rows, (1, 0, 2, 3, 4, 5))
+        return rows.reshape(-1, rows.shape[-1])
 
     def gather_columns(mine):
         rows, columns = mine.shape[1:]
@@ -821,10 +1276,6 @@
         tokens = rows * RANKS
         groups = CORNERS**2
         window = GROUP_TOKENS // PLANES
-        repeat = QUERY_HEADS // KEY_VALUE_HEADS
-        query_columns = QUERY_HEADS * HEAD_SIZE // RANKS
-        key_columns = KEY_VALUE_HEADS * HEAD_SIZE // RANKS
-        scale_qk = 1.0 / math.sqrt(HEAD_SIZE)
 
         sizes = [norm_attn.shape[0], norm_ffn.shape[0], query_gain.shape[0], key_gain.shape[0]]
         cuts = [0]
@@ -850,69 +1301,45 @@
                 split_columns(gate_weight),
             ]
         )
-        (attn_columns,) = run([swap_part(attn_columns)], 4)
-        attn_columns, own_gains = lax.optimization_barrier((attn_columns, own_gains))
-        gains, marks = hello(RANKS * data_total, own_gains, marks, 2)
+        attn_rows, hidden_all, gains, marks = run(
+            [
+                columns_part(attn_columns),
+                gather_part(hidden_in),
+                hello_part(RANKS * data_total, own_gains, marks),
+            ],
+            2,
+            micros=70,
+        )
+        attn_rows, out_rows, down_rows = lax.optimization_barrier(
+            (attn_rows, lax.ppermute(out_weight, INNER, to_rank), ffn_down)
+        )
+        w_attn = join_cells(attn_rows)
         gains = gains.reshape(RANKS * data_total, -1)
         gain_attn, gain_ffn, gain_query, gain_key = (
             gains[:, a:b].reshape(-1) for a, b in zip(cuts[:-1], cuts[1:])
         )
-        w_attn = gather_columns(attn_columns)
-        w_out = lax.all_gather(
-            lax.ppermute(out_weight, INNER, to_rank), DATA, axis=0, tiled=True
+        w_out = lax.all_gather(out_rows, DATA, axis=0, tiled=True)
+        w_down = lax.all_gather(down_rows, DATA, axis=0, tiled=True)
+
+        marks = marks.reshape(groups, 2, GROUP_TOKENS)
+        own_marks = lax.dynamic_slice_in_dim(marks, plane * window, window, axis=2)
+        cosine, sine = rope_tables(own_marks[:, 1].reshape(tokens))
+        own_marks = jnp.transpose(own_marks, (0, 2, 1))
+
+        hidden = hidden_in.astype(jnp.float32)
+        normed_input, query_low, pair, raw, gate_raw = prepare_attention(
+            hidden_all, gain_attn, w_attn, cosine, sine, gain_query, gain_key
         )
-
-        marks = marks.reshape(groups, 2, GROUP_TOKENS)
-        key_seq, key_pos = marks[:, 0], marks[:, 1]
-        own = lax.dynamic_slice_in_dim(marks, plane * window, window, axis=2)
-        own_seq, own_pos = own[:, 0], own[:, 1]
-        cosine_factor, sine_factor = rope_tables(own_pos)
-        allowed = (key_pos[:, None, :] <= own_pos[:, :, None]) & (
-            (key_seq[:, None, :] == 0) | (key_seq[:, None, :] == own_seq[:, :, None])
-        )
-
-        def prepare_heads(raw_values, gain_values):
-            return rotary_apply(
-                root_mean_scale(raw_values, gain_values), cosine_factor, sine_factor
-            )
-
-        hidden = hidden_in.astype(jnp.float32)
-        normed_input = gather_tokens(low(root_mean_scale(hidden, gain_attn)))
-        raw = matrix_product(normed_input, w_attn)
-        a, b, c = query_columns, query_columns + key_columns, query_columns + 2 * key_columns
-        query_raw = raw[:, :a].reshape(groups, window, repeat, HEAD_SIZE)
-        key_raw = raw[:, a:b].reshape(groups, window, 1, HEAD_SIZE)
-        value_low = low(raw[:, b:c]).reshape(groups, window, HEAD_SIZE)
-        gate_sig = jax.nn.sigmoid(raw[:, c:])
-        query_low = low(prepare_heads(query_raw, gain_query))
-        key_low = low(prepare_heads(key_raw, gain_key)).reshape(groups, window, HEAD_SIZE)
-        pair = jnp.concatenate([key_low, value_low], axis=-1).reshape(tokens, 2 * HEAD_SIZE)
-        ffn_columns = send_columns([split_units(ffn_gate), split_units(ffn_up)])
+        ffn_columns = split_units(ffn_gate, ffn_up, data_total)
         pair, cotangent_all, ffn_columns = run(
-            [line_gather_part(pair), gather_part(cotangent), swap_part(ffn_columns)], 3
+            [line_gather_part(pair), gather_part(cotangent), swap_part(ffn_columns)], 3, micros=75
         )
         w_ffn = gather_columns(ffn_columns)
-        own_down, pair = lax.optimization_barrier((ffn_down, pair))
-        w_down = lax.all_gather(own_down, DATA, axis=0, tiled=True)
-        pair = pair.reshape(PLANES, groups, window, 2 * HEAD_SIZE)
-        pair = jnp.transpose(pair, (1, 0, 2, 3)).reshape(groups, GROUP_TOKENS, 2 * HEAD_SIZE)
-        keys_all, values_all = pair[..., :HEAD_SIZE], pair[..., HEAD_SIZE:]
-
-        scores = (
-            jnp.einsum("gqrd,gkd->grqk", query_low, keys_all, preferred_element_type=jnp.float32)
-            * scale_qk
+        out_terms, attended, log_weight, gated_low = attend(
+            query_low, pair, gate_raw, own_marks, marks, w_out
         )
-        masked = jnp.where(allowed[:, None], scores, -1e30)
-        peak = jnp.max(masked, axis=-1, keepdims=True)
-        exponent = jnp.exp(masked - peak)
-        probs = exponent / jnp.sum(exponent, axis=-1, keepdims=True)
-        probs_low = low(probs)
-        attended = jnp.einsum(
-            "grqk,gkd->gqrd", probs_low, values_all, preferred_element_type=jnp.float32
-        )
-        attended_rows = attended.reshape(tokens, query_columns)
-        gated_low = low(attended_rows * gate_sig)
-        middle = hidden + scatter_tokens(matrix_product(gated_low, w_out))
+        out_terms = out_terms.reshape(RANKS, rows, -1)
+        middle = hidden + run([scatter_part(out_terms)], 1, 40)[0]
 
         normed_two = gather_tokens(low(root_mean_scale(middle, gain_ffn)))
         both = matrix_product(normed_two, w_ffn)
@@ -922,95 +1349,57 @@
         mixed_low = low(gate_ffn * ffn_sig * up_ffn)
         down_terms = blocks(matrix_product(mixed_low, w_down))
 
+        down_term = low(contract_first(mixed_low, cotangent_all))
+        down_term, cotangent_all = lax.optimization_barrier((down_term, cotangent_all))
+        grad_down = lax.psum_scatter(down_term, DATA, scatter_dimension=0, tiled=True).astype(
+            jnp.float32
+        )
         d_mixed = contract_last(cotangent_all, w_down)
         d_up_low = low(d_mixed * gate_ffn * ffn_sig)
         d_gate_ffn_low = low(d_mixed * up_ffn * ffn_sig * (1.0 + gate_ffn * (1.0 - ffn_sig)))
         d_both = jnp.concatenate([d_gate_ffn_low, d_up_low], axis=-1)
         both_term = low(contract_first(normed_two, d_both))
-        down_term = low(contract_first(mixed_low, cotangent_all))
+        both_term, d_both = lax.optimization_barrier((both_term, d_both))
         two_terms = blocks(contract_last(d_both, w_ffn))
-        two_terms, both_term, down_term = lax.optimization_barrier(
-            (two_terms, both_term, down_term)
-        )
         grad_both = sum_columns(both_term)
-        grad_down = lax.psum_scatter(down_term, DATA, scatter_dimension=0, tiled=True).astype(
-            jnp.float32
-        )
+        two_terms, grad_down = lax.optimization_barrier((two_terms, grad_down))
         (d_normed_two,) = run([scatter_part(two_terms)], 1, 40)
         unused_two, norm_two_back = jax.vjp(root_mean_scale, middle, gain_ffn)
         d_middle_norm, grad_norm_two_term = norm_two_back(d_normed_two)
         d_middle = cotangent.astype(jnp.float32) + d_middle_norm
 
         branch_all = gather_tokens(low(d_middle))
-        d_gated = contract_last(branch_all, w_out)
         grad_out = lax.psum_scatter(
             low(contract_first(gated_low, branch_all)), DATA, scatter_dimension=0, tiled=True
         )
         grad_out = lax.ppermute(grad_out, INNER, from_rank).astype(jnp.float32)
-        d_attended = low(d_gated * gate_sig)
-        d_gate_low = low(d_gated * attended_rows * gate_sig * (1.0 - gate_sig))
-        d_heads = d_attended.reshape(groups, window, repeat, HEAD_SIZE)
-        row_delta = jnp.transpose(
-            jnp.sum(d_heads.astype(jnp.float32) * attended, axis=-1), (0, 2, 1)
-        )
-        d_probs = jnp.einsum(
-            "gqrd,gkd->grqk", d_heads, values_all, preferred_element_type=jnp.float32
-        )
-        d_scores = low(probs * (d_probs - row_delta[..., None]))
-        d_query_rot = (
-            jnp.einsum("grqk,gkd->gqrd", d_scores, keys_all, preferred_element_type=jnp.float32)
-            * scale_qk
-        )
-        d_keys = (
-            jnp.einsum("grqk,gqrd->gkd", d_scores, query_low, preferred_element_type=jnp.float32)
-            * scale_qk
-        )
-        d_values = jnp.einsum(
-            "grqk,gqrd->gkd", probs_low, d_heads, preferred_element_type=jnp.float32
-        )
-        d_pair = low(jnp.concatenate([d_keys, d_values], axis=-1))
-        d_pair = jnp.transpose(
-            d_pair.reshape(groups, PLANES, window, 2 * HEAD_SIZE), (1, 0, 2, 3)
+        d_query, d_gate, d_pair, query_gain_terms = attend_back(
+            branch_all, w_out, query_low, pair, gate_raw, own_marks, marks,
+            attended, log_weight, raw, cosine, sine, gain_query,
         )
         d_pair, result, grad_both = run(
             [
-                line_scatter_part(d_pair.reshape(PLANES, tokens, 2 * HEAD_SIZE)),
+                line_scatter_part(d_pair),
                 scatter_part(down_terms),
                 swap_part(grad_both),
             ],
             5,
             56,
+            75,
         )
         output = low(middle + result)
-        grad_both = grad_both.astype(jnp.float32)
-        grad_gate = join_units(grad_both[..., :units])
-        grad_up = join_units(grad_both[..., units:])
-        d_pair = d_pair.reshape(groups, window, 2 * HEAD_SIZE)
-        d_key_rot, d_value = d_pair[..., :HEAD_SIZE], d_pair[..., HEAD_SIZE:]
-        unused_query, query_back = jax.vjp(prepare_heads, query_raw, gain_query)
-        d_query_raw, grad_query_gain_term = query_back(d_query_rot)
-        unused_key, key_back = jax.vjp(prepare_heads, key_raw, gain_key)
-        d_key_raw, grad_key_gain_term = key_back(d_key_rot[:, :, None, :])
-        d_raw = jnp.concatenate(
-            [
-                low(d_query_raw.reshape(tokens, query_columns)),
-                low(d_key_raw.reshape(tokens, key_columns)),
-                low(d_value.reshape(tokens, key_columns)),
-                d_gate_low,
-            ],
-            axis=-1,
+        d_raw, key_gain_terms = finish_attention(
+            d_pair, raw, cosine, sine, gain_key, d_query, d_gate
         )
+        grad_query_gain_term = jnp.sum(query_gain_terms[:, 0], axis=0)
+        grad_key_gain_term = jnp.sum(key_gain_terms[:, 0], axis=0)
+        a = REPEAT * HEAD_SIZE
+        b, c = a + HEAD_SIZE, a + 2 * HEAD_SIZE
         attn_term = low(contract_first(normed_input, d_raw))
+        attn_term, d_raw = lax.optimization_barrier((attn_term, d_raw))
         one_terms = blocks(contract_last(d_raw, w_attn))
-        one_terms, attn_term = lax.optimization_barrier((one_terms, attn_term))
         grad_attn = sum_columns(attn_term)
         (d_normed,) = run([scatter_part(one_terms)], 1, 40)
-        (grad_attn,) = run([swap_part(grad_attn)], 4)
-        grad_attn = grad_attn.astype(jnp.float32)
-        grad_query = join_columns(grad_attn[..., :a])
-        grad_key = join_columns(grad_attn[..., a:b])
-        grad_value = join_columns(grad_attn[..., b:c])
-        grad_gatew = join_columns(grad_attn[..., c:])
         unused_one, norm_one_back = jax.vjp(root_mean_scale, hidden, gain_attn)
         d_hidden_norm, grad_norm_one_term = norm_one_back(d_normed)
         input_grad = d_middle + d_hidden_norm
@@ -1028,7 +1417,11 @@
             axis=-1,
         )
         terms = jnp.pad(terms, ((0, 0), (0, pad))).reshape((-1,) + tile)
-        small = spread_sum(terms, 7).reshape(-1)
+        grad_attn, small = run([swap_part(grad_attn), spread_part(terms)], 4, micros=15)
+        small = small.reshape(-1)
+        grad_query, grad_key, grad_value, grad_gatew = widen_columns(grad_attn, (a, b - a, c - b, a))
+        grad_both, d_normed = lax.optimization_barrier((grad_both, d_normed))
+        grad_gate, grad_up = join_units(grad_both, data_total)
         grad_norm_attn, grad_norm_ffn, grad_query_gain, grad_key_gain = (
             small[s:e] for s, e in zip(cuts[:-1], cuts[1:])
         )

time: 977 us -> 810 us (0.83)
  matrix products: 209 us -> 117 us
  local copies, waits for them, and re-layouts: 125 us -> 52.9 us
  other arithmetic: 90.2 us -> 29.3 us
  Pallas kernels: 520 us -> 551 us
  waiting for transfers between devices: 3.71 us -> 32.2 us
    dot_general x5 -> x0, matrix products: 50.3 us -> none  [the longest x1 19.4 us: shards(): jnp.einsum('gqrd,gkd->grqk', d_heads, values_all, preferred_element_type=...]
    reshape x18 -> x0, local copies, waits for them, and re-layouts: 35.4 us -> none  [the longest x2 8.16 us: join_units(): return jnp.transpose(split, (2, 0, 3, 1, 4)).reshape(rows, ranks * units)]
    pallas_call x12 -> x16, Pallas kernels: 520 us -> 551 us  [the longest x9 471 us: run(): pl.pallas_call(functools.partial(run_kernel, parts), out_shape=[shape for...]
    convert_element_type x9 -> x3, other arithmetic: 32.6 us -> 4.9 us  [low(): return values.astype(jnp.bfloat16)]
    all_gather x2, waiting for transfers between devices: 3.51 us -> 23.2 us  [the longest x1 23.2 us: shards(): w_down = lax.all_gather(down_rows, DATA, axis=0, tiled=True)]
    sub x1 -> x0, matrix products: 18.5 us -> none  [shards(): exponent = jnp.exp(masked - peak)]
    transpose x4 -> x2, local copies, waits for them, and re-layouts: 16.7 us -> 0.37 us  [shards(): own_marks = jnp.transpose(own_marks, (0, 2, 1))]
    dot_general x4 -> x2, matrix products: 42.2 us -> 28.5 us  [matrix_product(): return jnp.dot(left, right, preferred_element_type=jnp.float32)]
  transfers between devices with their start and end apart: 10 -> 9, of which waited for: 1 -> 3; matrix products, arithmetic and copies ran while one was open for 33% -> 20% of each run, Pallas kernels for 52% -> 64%
where the time goes in v4:
time: 810 us; the launch traced here: 801 us
  Pallas kernels  551 us (68%)
  matrix products  117 us (14%)
  local copies, waits for them, and re-layouts  52.9 us (7%)
  waiting for transfers between devices  32.2 us (4%)
  other arithmetic  29.3 us (4%)
  between operations  15.2 us (2%)
    pallas_call x9, Pallas kernels, run(): pl.pallas_call(functools.partial(run_kernel, parts), out_shape=[shape for...  471 us
    dot_general x3, matrix products, contract_last(): lax.dot_general(left, right, (((1,), (1,)), ((), ())), preferred_element_...  44.6 us
    dot_general x4, matrix products, contract_first(): lax.dot_general(left, right, (((0,), (0,)), ((), ())), preferred_element_...  44 us
    pallas_call x1, Pallas kernels, attend_back(): pl.pallas_call(attend_back_kernel, grid=(groups,), out_shape=[shape((toke...  35.3 us
    unnamed x80, local copies, waits for them, and re-layouts  34.2 us
    dot_general x2, matrix products, matrix_product(): return jnp.dot(left, right, preferred_element_type=jnp.float32)  28.5 us
    all_gather x1, waiting for transfers between devices, shards(): w_down = lax.all_gather(down_rows, DATA, axis=0, tiled=True)  23.2 us
    pallas_call x1, Pallas kernels, attend(): pl.pallas_call(attend_kernel, grid=(groups,), out_shape=[shape((tokens, w...  17.2 us
  transfers between devices with their start and end apart: 9, of which 3 were waited for; matrix products, arithmetic and copies ran while one was open for 20% of the time, Pallas kernels for 64%

profile of v4, /device:TPU:0, one launch (start us, length us, event | category | flops | bytes accessed | tf_op | source)
XLA Modules:
  0.0 801.5 jit_solution(17202293506311910183)
XLA Ops:
  7.2 1.6 collective-permute-start
  14.6 74.0 %shard_map.263 = (bf16[4,4,2,64,768]{4,3,2,1,0:T(8,128)(2,1)}, bf16[2048,2048]{1,0:T(8,128)(2,1)}, f32[32,8,128]{2,1,0:T(8,128)}, s32[4,32,128]{2,1,0:T(8,128)}) custom-call(bf16[8,64,768]{2,1,0:T(8,128)(2,1)} %maximum_bitcast_fusion.refs_0_, bf16[256,2048]{1,0:T(8,128)(2,1)} %refs_1_.2, f32[8,128]{1,0:T(8,128)} %fusion.16.refs_2_, ...), custom_call_target="tpu_custom_call" | custom-call | bytes 245000000 | tf_op jit(solution)/shard_map/pallas_call | solution.py:148
  91.6 3.9 shard_map.265.refs_2_
  95.6 3.7 fusion.6
  100.1 1.9 copy-done.15
  102.0 12.6 %shard_map.264 = (bf16[2048,2048]{1,0:T(8,128)(2,1)S(1)}, bf16[2048,256]{1,0:T(8,128)(2,1)S(1)}, bf16[2048,256]{1,0:T(8,128)(2,1)S(1)}, f32[2048,384]{1,0:T(8,128)S(1)}, f32[2048,256]{1,0:T(8,128)S(1)}) custom-call(bf16[2048,2048]{1,0:T(8,128)(2,1)} %get-tuple-element.59.x_ref, f32[1,2048]{1,0:T(1,128)S(1)} %broadcast_in_dim_reshape.6.gain_ref, ...), custom_call_target="tpu_custom_call" | custom-call | bytes 42000000 | tf_op jit(solution)/shard_map/pallas_call | solution.py:948
  114.6 1.7 copy-done.7
  118.6 3.2 copy-done.24
  121.8 73.2 %shard_map.266 = (bf16[4,2048,256]{2,1,0:T(8,128)(2,1)}, bf16[2048,2048]{1,0:T(8,128)(2,1)}, bf16[8,64,1536]{2,1,0:T(8,128)(2,1)}) custom-call(bf16[2048,256]{1,0:T(8,128)(2,1)} %copy-done.19, bf16[256,2048]{1,0:T(8,128)(2,1)} %refs_1_.3, bf16[8,64,1536]{2,1,0:T(8,128)(2,1)} %shard_map.265.refs_2_), custom_call_target="tpu_custom_call" | custom-call | bytes 262500000 | tf_op jit(solution)/shard_map/pallas_call | solution.py:148
  197.2 17.2 %shard_map.267 = (bf16[2048,2048]{1,0:T(8,128)(2,1)}, f32[2048,256]{1,0:T(8,128)}, f32[2048,256]{1,0:T(8,128)}, bf16[2048,256]{1,0:T(8,128)(2,1)S(1)}) custom-call(bf16[2048,256]{1,0:T(8,128)(2,1)S(1)} %get-tuple-element.64.q_ref, bf16[4,2048,256]{2,1,0:T(8,128)(2,1)} %get-tuple-element.66.kv_ref, f32[2048,256]{1,0:T(8,128)} %copy-done.12, ...), custom_call_target="tpu_custom_call" | custom-call | bytes 63000000 | tf_op jit(solution)/shard_map/pallas_call | solution.py:1027
  214.5 3.4 copy-done.11
  217.9 38.4 %shard_map.268 = f32[256,2048]{1,0:T(8,128)S(1)} custom-call(bf16[8,256,2048]{2,1,0:T(8,128)(2,1)S(1)} %bitcast.71), custom_call_target="tpu_custom_call" | custom-call | bytes 140000000 | tf_op jit(solution)/shard_map/pallas_call | solution.py:148
  259.9 40.8 %shard_map.269 = bf16[2048,2048]{1,0:T(8,128)(2,1)} custom-call(bf16[256,2048]{1,0:T(8,128)(2,1)} %multiply_convert_fusion.3.refs_0_), custom_call_target="tpu_custom_call" | custom-call | bytes 140000000 | tf_op jit(solution)/shard_map/pallas_call | solution.py:148
  300.7 8.1 %all-gather.9.cloned.1.call-done = bf16[32,64,1536]{2,1,0:T(8,128)(2,1)} async-done(((bf16[8,64,1536]{2,1,0:T(8,128)(2,1)}), bf16[32,64,1536]{2,1,0:T(8,128)(2,1)}) %all-gather.9.cloned.1.call-update) | async-done | bytes 6291472 | tf_op jit(solution)/shard_map/all_gather | solution.py:1239
  308.9 6.6 copy.56
  315.5 16.7 %fusion.24 = f32[2048,1536]{0,1:T(8,128)S(1)} fusion(bf16[2048,2048]{1,0:T(8,128)(2,1)S(1)} %copy-done.32, bf16[2048,1536]{1,0:T(8,128)(2,1)} %bitcast.79), kind=kOutput, calls=%fused_computation.73 | convolution fusion | flops 12884901888 | bytes 27262976 | tf_op jit(solution)/shard_map/dot_general | solution.py:859
  332.2 2.0 multiply_convert_fusion.2
  334.3 2.5 copy-done.30
  336.8 1.8 copy-done.34
  338.6 10.3 %convolution_convert_fusion.4 = bf16[768,2048]{1,0:T(8,128)(2,1)} fusion(bf16[2048,768]{0,1:T(8,128)(2,1)S(1)} %multiply_convert_fusion.2, bf16[2048,2048]{1,0:T(8,128)(2,1)} %get-tuple-element.72), kind=kOutput, calls=%fused_computation.14 | convolution fusion | flops 6444023808 | bytes 14680064 | tf_op jit(solution)/shard_map/dot_general | solution.py:869
  349.0 23.2 %all-gather.7.cloned.1.call-done = bf16[768,2048]{1,0:T(8,128)(2,1)} async-done(((bf16[192,2048]{1,0:T(8,128)(2,1)}), bf16[768,2048]{1,0:T(8,128)(2,1)}) %all-gather.7.cloned.1.call-update) | async-done | bytes 3145744 | tf_op jit(solution)/shard_map/all_gather | solution.py:1322
  372.2 15.6 %multiply_convert_fusion.1 = (bf16[2048,768]{0,1:T(8,128)(2,1)S(1)}, bf16[2048,768]{0,1:T(8,128)(2,1)S(1)}) fusion(f32[2048,1536]{0,1:T(8,128)} %copy-done.30, bf16[2048,2048]{1,0:T(8,128)(2,1)} %get-tuple-element.72, bf16[768,2048]{1,0:T(8,128)(2,1)} %all-gather.7.cloned.1.call-done), kind=kOutput, calls=%fused_computation.6 | convolution fusion | flops 6462898176 | bytes 30408704 | tf_op jit(solution)/shard_map/dot_general | solution.py:863
  387.9 1.6 copy-done.33
  389.5 3.8 pad_maximum_fusion
  393.3 16.5 %convolution_convert_fusion.3 = bf16[2048,1536]{1,0:T(8,128)(2,1)S(1)} fusion(bf16[2048,2048]{1,0:T(8,128)(2,1)} %shard_map.269, bf16[2048,768]{0,1:T(8,128)(2,1)} %copy-done.33, bf16[2048,768]{0,1:T(8,128)(2,1)S(1)} %get-tuple-element.110), kind=kOutput, calls=%fused_computation.3 | convolution fusion | flops 12900630528 | bytes 20971520 | tf_op jit(solution)/shard_map/dot_general | solution.py:869
  409.8 3.3 copy.58
  413.2 19.6 %convolution_convert_fusion.2 = bf16[2048,2048]{1,0:T(8,128)(2,1)} fusion(bf16[2048,1536]{0,1:T(8,128)(2,1)} %pad_maximum_fusion, bf16[2048,1536]{1,0:T(8,128)(2,1)} %bitcast.80), kind=kOutput, calls=%fused_computation.2 | convolution fusion | flops 12889096192 | bytes 20971520 | tf_op jit(solution)/shard_map/dot_general | solution.py:863
  433.3 2.5 convert_element_type.85
  435.8 3.4 copy-done.10
  439.1 39.7 %shard_map.270 = f32[256,2048]{1,0:T(8,128)S(1)} custom-call(bf16[8,256,2048]{2,1,0:T(8,128)(2,1)S(1)} %bitcast.70), custom_call_target="tpu_custom_call" | custom-call | bytes 140000000 | tf_op jit(solution)/shard_map/pallas_call | solution.py:148
  480.0 1.7 fusion.19.refs_0_
  481.7 40.6 %shard_map.271.branch_ref = bf16[2048,2048]{1,0:T(8,128)(2,1)} custom-call(bf16[256,2048]{1,0:T(8,128)(2,1)} %fusion.19.refs_0_), custom_call_target="tpu_custom_call" | custom-call | bytes 140000000 | tf_op jit(solution)/shard_map/pallas_call | solution.py:148
  522.3 6.7 convolution_convert_fusion.6
  529.1 11.8 %convolution_convert_fusion.1 = bf16[2048,2048]{1,0:T(8,128)(2,1)} fusion(bf16[2048,768]{0,1:T(8,128)(2,1)} %copy-done.34, bf16[768,2048]{1,0:T(8,128)(2,1)} %all-gather.7.cloned.1.call-done), kind=kOutput, calls=%fused_computation.1 | convolution fusion | flops 6446645248 | bytes 14680064 | tf_op jit(solution)/shard_map/dot_general | solution.py:859
  540.9 35.3 %shard_map.272 = (bf16[2048,256]{1,0:T(8,128)(2,1)}, bf16[2048,256]{1,0:T(8,128)(2,1)}, bf16[4,2048,256]{2,1,0:T(8,128)(2,1)}, f32[4,8,128]{2,1,0:T(8,128)}) custom-call(bf16[2048,2048]{1,0:T(8,128)(2,1)} %shard_map.271.branch_ref, bf16[256,2048]{1,0:T(8,128)(2,1)} %all-gather.5.cloned.1.call-done.wo_ref, bf16[2048,256]{1,0:T(8,128)(2,1)} %copy-done.14, ...), custom_call_target="tpu_custom_call" | custom-call | bytes 122500000 | tf_op jit(solution)/shard_map/pallas_call | solution.py:1095
  576.3 77.9 %shard_map.273 = (f32[2048,256]{1,0:T(8,128)}, f32[256,2048]{1,0:T(8,128)}, bf16[8,64,1536]{2,1,0:T(8,128)(2,1)}) custom-call(bf16[4,2048,256]{2,1,0:T(8,128)(2,1)} %get-tuple-element.80.refs_0_, bf16[8,256,2048]{2,1,0:T(8,128)(2,1)} %bitcast.77, bf16[8,64,1536]{2,1,0:T(8,128)(2,1)} %reduce-scatter.7.cloned.1.call-done.refs_2_), custom_call_target="tpu_custom_call" | custom-call | bytes 262500000 | tf_op jit(solution)/shard_map/pallas_call | solution.py:148
  654.2 1.9 copy-done.8
  656.1 1.6 copy-done.16
  658.9 1.5 shard_map.274
  660.4 10.4 %convolution_convert_fusion.5 = bf16[2048,768]{1,0:T(8,128)(2,1)S(1)} fusion(bf16[2048,2048]{1,0:T(8,128)(2,1)} %copy-done.24, bf16[2048,768]{1,0:T(8,128)(2,1)S(1)} %get-tuple-element.88), kind=kOutput, calls=%fused_computation.15 | convolution fusion | flops 6444023808 | bytes 14680064 | tf_op jit(solution)/shard_map/dot_general | solution.py:869
  670.8 2.0 copy.59
  673.5 1.6 collective-permute-start.1
  677.0 9.4 %convolution_convert_fusion = bf16[2048,2048]{1,0:T(8,128)(2,1)S(1)} fusion(bf16[2048,768]{1,0:T(8,128)(2,1)} %copy-done.25, bf16[2048,768]{1,0:T(8,128)(2,1)} %bitcast.73), kind=kOutput, calls=%fused_computation | convolution fusion | flops 6446645248 | bytes 14680064 | tf_op jit(solution)/shard_map/dot_general | solution.py:863
  686.4 54.5 %shard_map.275 = f32[256,2048]{1,0:T(8,128)S(1)} custom-call(bf16[8,256,2048]{2,1,0:T(8,128)(2,1)S(1)} %bitcast.72), custom_call_target="tpu_custom_call" | custom-call | bytes 140000000 | tf_op jit(solution)/shard_map/pallas_call | solution.py:148
  743.8 4.0 shard_map.278
  747.8 5.9 fusion.1
  753.7 32.5 %shard_map.276 = (bf16[8,64,768]{2,1,0:T(8,128)(2,1)}, f32[8,128]{1,0:T(8,128)}) custom-call(bf16[8,64,768]{2,1,0:T(8,128)(2,1)} %reduce-scatter.9.cloned.1.call-done.refs_0_, f32[32,8,128]{2,1,0:T(8,128)} %bitcast.83), custom_call_target="tpu_custom_call" | custom-call | bytes 52500000 | tf_op jit(solution)/shard_map/pallas_call | solution.py:148
  789.0 5.2 shard_map.277
  (128 shorter events, 29.2 us)
Async XLA Ops:
  7.2 1.7 copy-start
  7.2 188.8 %all-gather.5.cloned.1.call-start = ((), (), s32[]{:S(2)}) async-start(), calls=%async_computation.4 | async-start | bytes 1310720 | tf_op jit(solution)/shard_map/all_gather | solution.py:1321
  7.2 82.2 %collective-permute-start = (bf16[64,2048]{1,0:T(8,128)(2,1)}, bf16[64,2048]{1,0:T(8,128)(2,1)S(1)}, u32[]{:S(2)}, u32[]{:S(2)}) collective-permute-start(bf16[64,2048]{1,0:T(8,128)(2,1)} %param.21), channel_id=1, source_target_pairs={{0,0},{1,2},{2,4},{3,6},{4,1},{5,3},{6,5},{7,7},{8,8},{9,10},{10,1... | collective-permute-start | bytes 786440 | tf_op jit(solution)/shard_map/ppermute | solution.py:1314
  89.5 0.7 copy-start.35
  90.2 218.7 %all-gather.9.cloned.1.call-start = ((), (), s32[]{:S(2)}) async-start(), calls=%async_computation.10 | async-start | bytes 7864320 | tf_op jit(solution)/shard_map/all_gather | solution.py:1239
  90.4 9.6 %copy-start.22 = (f32[1,128]{1,0:T(1,128)}, f32[1,128]{1,0:T(1,128)S(1)}, u32[]{:S(2)}) copy-start(f32[1,128]{1,0:T(1,128)S(1)} %broadcast_in_dim_reshape.16.kg_ref) | copy-start | bytes 1540
  90.5 9.5 %copy-start.21 = (f32[1,128]{1,0:T(1,128)}, f32[1,128]{1,0:T(1,128)S(1)}, u32[]{:S(2)}) copy-start(f32[1,128]{1,0:T(1,128)S(1)} %broadcast_in_dim_reshape.7.qg_ref) | copy-start | bytes 1540
  90.6 8.7 %copy-start.36 = (f32[32,64]{1,0:T(8,128)}, f32[32,64]{1,0:T(8,128)S(1)}, u32[]{:S(2)}) copy-start(f32[32,64]{1,0:T(8,128)S(1)} %get-tuple-element.116) | copy-start | bytes 24580
  91.6 104.4 %copy-start.20 = (s32[4,2,2048]{2,1,0:T(2,128)}, s32[4,2,2048]{2,1,0:T(2,128)S(1)}, u32[]{:S(2)}) copy-start(s32[4,2,2048]{2,1,0:T(2,128)S(1)} %reshape.167.keys_ref) | copy-start | bytes 196612
  99.3 2.6 copy-start.15
  99.7 14.9 %copy-start.5 = (f32[2048,128]{1,0:T(8,128)}, f32[2048,128]{1,0:T(8,128)S(1)}, u32[]{:S(2)}) copy-start(f32[2048,128]{1,0:T(8,128)S(1)} %pad_maximum_fusion.1.cos_ref) | copy-start | bytes 3145732
  100.0 14.6 %copy-start.3 = (f32[2048,128]{1,0:T(8,128)}, f32[2048,128]{1,0:T(8,128)S(1)}, u32[]{:S(2)}) copy-start(f32[2048,128]{1,0:T(8,128)S(1)} %pad_maximum_fusion.2.sin_ref) | copy-start | bytes 3145732
  114.6 1.7 copy-start.7
  116.3 1.3 copy-start.12
  117.6 1.0 copy-start.19
  118.6 3.2 copy-start.24
  121.8 74.2 %copy-start.14 = (bf16[2048,256]{1,0:T(8,128)(2,1)}, bf16[2048,256]{1,0:T(8,128)(2,1)S(1)}, u32[]{:S(2)}) copy-start(bf16[2048,256]{1,0:T(8,128)(2,1)S(1)} %get-tuple-element.64.q_ref) | copy-start | bytes 3145732
  195.0 177.2 %all-gather.7.cloned.1.call-start = ((), (), s32[]{:S(2)}) async-start(), calls=%async_computation.5 | async-start | bytes 3932160 | tf_op jit(solution)/shard_map/all_gather | solution.py:1322
  195.5 19.0 %copy-start.9 = (s32[4,512,2]{2,1,0:T(8,128)}, s32[4,512,2]{2,1,0:T(8,128)S(1)}, u32[]{:S(2)}) copy-start(s32[4,512,2]{2,1,0:T(8,128)S(1)} %copy.55.own_ref) | copy-start | bytes 49156
  195.7 237.6 %reduce-scatter.5.cloned.1.call-start = ((), (), s32[]{:S(2)}) async-start(), calls=%async_computation.6 | async-start | bytes 3932160 | tf_op jit(solution)/shard_map/reduce_scatter | solution.py:1354
  196.0 1.2 copy-start.13
  214.5 3.4 copy-start.11
  217.9 38.4 %copy-start.28 = (bf16[256,2048]{1,0:T(8,128)(2,1)S(1)}, bf16[256,2048]{1,0:T(8,128)(2,1)}, u32[]{:S(2)}) copy-start(bf16[256,2048]{1,0:T(8,128)(2,1)} %refs_1_.2) | copy-start | bytes 3145732
  257.4 1.3 copy-start.26
  308.9 6.7 copy-start.32
  332.2 4.6 copy-start.30
  336.8 1.8 copy-start.34
  348.9 227.3 %reduce-scatter.7.cloned.1.call-start = ((), (), s32[]{:S(2)}) async-start(), calls=%async_computation.7 | async-start | bytes 7864320 | tf_op jit(solution)/shard_map/reduce_scatter | solution.py:1247
  387.8 1.6 copy-start.33
  413.1 260.4 %reduce-scatter.11.cloned.1.call-start = ((), (), s32[]{:S(2)}) async-start(), calls=%async_computation.9 | async-start | bytes 1310720 | tf_op jit(solution)/shard_map/reduce_scatter | solution.py:1372
  435.8 3.4 copy-start.10
  439.1 39.7 %copy-start.27 = (f32[256,2048]{1,0:T(8,128)S(1)}, f32[256,2048]{1,0:T(8,128)}, u32[]{:S(2)}) copy-start(f32[256,2048]{1,0:T(8,128)} %copy-done.26) | copy-start | bytes 6291460
  478.8 1.2 copy-start.31
  529.0 224.7 %reduce-scatter.9.cloned.1.call-start = ((), (), s32[]{:S(2)}) async-start(), calls=%async_computation.8 | async-start | bytes 3932160 | tf_op jit(solution)/shard_map/reduce_scatter | solution.py:1247
  576.2 77.9 %copy-start.4 = (f32[2048,128]{1,0:T(8,128)S(1)}, f32[2048,128]{1,0:T(8,128)}, u32[]{:S(2)}) copy-start(f32[2048,128]{1,0:T(8,128)} %copy-done.3) | copy-start | bytes 3145732
  576.2 77.9 %copy-start.6 = (f32[2048,128]{1,0:T(8,128)S(1)}, f32[2048,128]{1,0:T(8,128)}, u32[]{:S(2)}) copy-start(f32[2048,128]{1,0:T(8,128)} %copy-done.5) | copy-start | bytes 3145732
  576.3 77.9 %copy-start.17 = (bf16[2048,256]{1,0:T(8,128)(2,1)S(1)}, bf16[2048,256]{1,0:T(8,128)(2,1)}, u32[]{:S(2)}) copy-start(bf16[2048,256]{1,0:T(8,128)(2,1)} %get-tuple-element.85.dq_ref) | copy-start | bytes 3145732
  576.3 77.9 %copy-start.23 = (f32[1,128]{1,0:T(1,128)S(1)}, f32[1,128]{1,0:T(1,128)}, u32[]{:S(2)}) copy-start(f32[1,128]{1,0:T(1,128)} %copy-done.22) | copy-start | bytes 1540
  654.2 1.9 copy-start.8
  656.1 1.6 copy-start.16
  657.7 1.2 copy-start.18
  660.4 10.4 %copy-start.25 = (bf16[2048,768]{1,0:T(8,128)(2,1)}, bf16[2048,768]{1,0:T(8,128)(2,1)S(1)}, u32[]{:S(2)}) copy-start(bf16[2048,768]{1,0:T(8,128)(2,1)S(1)} %get-tuple-element.88) | copy-start | bytes 9437188
  672.8 0.7 copy-start.37
  672.8 2.4 copy-start.38
  673.5 2.5 collective-permute-start.1
  686.4 55.8 %copy-start.29 = (bf16[256,2048]{1,0:T(8,128)(2,1)S(1)}, bf16[256,2048]{1,0:T(8,128)(2,1)}, u32[]{:S(2)}) copy-start(bf16[256,2048]{1,0:T(8,128)(2,1)} %refs_1_.2) | copy-start | bytes 3145732
  740.9 1.3 copy-start.2
  747.8 46.4 %copy-start.1 = (bf16[64,1024]{1,0:T(8,128)(2,1)S(1)}, bf16[64,1024]{1,0:T(8,128)(2,1)}, u32[]{:S(2)}) copy-start(bf16[64,1024]{1,0:T(8,128)(2,1)} %param.18) | copy-start | bytes 393220
Sparse Core Ops, SparseCore 0:
  90.3 26.3 all-gather.4
  195.1 113.7 all-gather.8
  310.4 61.7 all-gather.6
  374.4 58.8 reduce-scatter.4
  435.4 110.7 reduce-scatter.6
  548.4 27.6 reduce-scatter.10
  672.9 65.8 reduce-scatter.8

commit v5 on v4

--- a/solution.py
+++ b/solution.py
@@ -103,6 +103,7 @@
 
 class Part:
     def __init__(self, inputs, outs, scratch, steps, plane=None, line=False):
+        self.begin = 0.0
         self.inputs = inputs
         self.outs = outs
         self.scratch = scratch
@@ -127,11 +128,11 @@
     plane = ranks[max(ranks.index(p.plane) for p in parts)]
     greet(plane, any(p.line for p in parts))
     plans = [p.steps(i, o, s) for p, i, o, s in zip(parts, ins, outs, scratch)]
-    for first, _, _ in plans:
-        first()
     ordered = []
-    for _, middle, _ in plans:
-        ordered += [((n + 0.5) / len(middle), step) for n, step in enumerate(middle)]
+    for p, (first, middle, _) in zip(parts, plans):
+        ordered.append((p.begin - 1.0 if p.begin == 0 else p.begin, first))
+        for n, step in enumerate(middle):
+            ordered.append((p.begin + (1.0 - p.begin) * (n + 0.5) / len(middle), step))
     for _, step in sorted(ordered, key=lambda pair: pair[0]):
         step()
     for _, _, last in plans:
@@ -160,6 +161,11 @@
     )(*[array for array, _ in inputs])
 
 
+def later(part, begin):
+    part.begin = begin
+    return part
+
+
 def gather_part(block):
     rows, columns = block.shape
     n, half = CHUNKS, CHUNKS // 2
@@ -263,14 +269,23 @@
     lax.fori_loop(0, count // step, body, 0)
 
 
-def scatter_part(terms):
-    ranks, rows, columns = terms.shape
+def scatter_part(terms=None, product=None, transposed=False, tile=512):
+    if product is None:
+        ranks, rows, columns = terms.shape
+    else:
+        left, right = product
+        rows, columns = left.shape[0] // RANKS, right.shape[0 if transposed else 1]
     n, half = CHUNKS, CHUNKS // 2
     chunk = rows // n
     middle_row = half * chunk
 
     def steps(ins, outs, scratch):
-        (part_ref,), (out_ref,) = ins, outs
+        (out_ref,) = outs
+        if product is None:
+            (part_ref,) = ins
+        else:
+            left_ref, right_ref = ins
+            part_ref, scratch = scratch[-1], scratch[:-1]
         core_buf, x_buf, y_buf, x_diag, y_diag, d_sum, x_sum, y_sum = scratch[:8]
         send_c, recv_c, send_x, recv_x, send_y, recv_y = scratch[8:]
         x, c, y = corner()
@@ -292,12 +307,36 @@
         def piece(k):
             return pl.ds(k * chunk, chunk)
 
+        def make(index):
+            def body(j, carry):
+                at = pl.ds(pl.multiple_of(j * tile, tile), tile)
+                some = left_ref[pl.ds(pl.multiple_of(index * rows, rows), rows), :]
+                if transposed:
+                    value = dot_rows(some, right_ref[at, :])
+                else:
+                    value = dot(some, right_ref[:, at])
+                part_ref[index, :, at] = low(value)
+                return carry
+
+            lax.fori_loop(0, columns // tile, body, 0)
+
+        def to_core(b):
+            for k in orders[b]:
+                source = part_ref.at[theirs[b], piece(k), :]
+                i = b * n + k
+                go(remote(source, core_buf.at[b, piece(k), :], send_c.at[i], recv_c.at[i], dev_c))
+
+        def made_for_core(b):
+            make(theirs[b])
+            to_core(b)
+
         def first():
-            for b in (D, X, Y, O):
-                for k in orders[b]:
-                    source = part_ref.at[theirs[b], piece(k), :]
-                    i = b * n + k
-                    go(remote(source, core_buf.at[b, piece(k), :], send_c.at[i], recv_c.at[i], dev_c))
+            if product is None:
+                for b in (D, X, Y, O):
+                    to_core(b)
+            else:
+                made_for_core(D)
+                make(mine[D])
 
         def chip(target, b, k, *more):
             landed(core_buf.at[b, piece(k), :], recv_c.at[b * n + k], dev_c)
@@ -342,8 +381,15 @@
             for copy in sent:
                 copy.wait_send()
 
+        def makes(b):
+            if product is None:
+                return []
+            return [functools.partial(made_for_core, b), functools.partial(make, mine[b])]
+
         middle = [functools.partial(diagonal, k) for k in orders[D]]
+        middle += makes(X) + makes(Y)
         middle += [functools.partial(direct, k) for k in range(half)]
+        middle += makes(O)
         middle += [functools.partial(relayed, k) for k in range(half)]
         middle += [functools.partial(own, k) for k in range(n)]
         return first, middle, last
@@ -354,11 +400,13 @@
     whole, part = low_vmem(rows, columns), low_vmem(rows // 2, columns)
     link = DMA((n + half,))
     core = DMA((4 * n,))
+    made = [] if product is None else [low_vmem(RANKS, rows, columns)]
     return Part(
-        [(terms, VMEM)],
+        [(terms, VMEM)] if product is None else [(left, VMEM), (right, VMEM)],
         [(jax.ShapeDtypeStruct((rows, columns), jnp.float32), VMEM)],
         [low_vmem(4, rows, columns), whole, whole, part, part, whole, whole, whole]
-        + [core, core, link, link, link, link],
+        + [core, core, link, link, link, link]
+        + made,
         steps,
         plane="near",
     )
@@ -396,6 +444,51 @@
         [DMA((n,)), DMA((n,)), DMA(())],
         steps,
         plane="all",
+    )
+
+
+def owners_part(block):
+    def steps(ins, outs, scratch):
+        (in_ref,), (out_ref,) = ins, outs
+        send, recv, local = scratch
+        cells = lax.axis_size("cell")
+        total = cells * PLANES
+        y, place = lax.axis_index("y"), lax.axis_index("cell") * PLANES + lax.axis_index("z")
+        here = place * CORNERS + y
+        to = y * total + place
+        whence = lax.rem(here, total) * CORNERS + here // total
+
+        def device(index):
+            planes = index // CORNERS
+            return {"cell": planes // PLANES, "z": lax.rem(planes, PLANES), "y": lax.rem(index, CORNERS)}
+
+        def first():
+            @pl.when(to == here)
+            def _():
+                pltpu.make_async_copy(in_ref, out_ref, local).start()
+
+            @pl.when(to != here)
+            def _():
+                remote(in_ref, out_ref, send, recv, device(to)).start()
+
+        def last():
+            @pl.when(to == here)
+            def _():
+                pltpu.make_async_copy(in_ref, out_ref, local).wait()
+
+            @pl.when(to != here)
+            def _():
+                landed(out_ref, recv, device(whence))
+                remote(in_ref, out_ref, send, recv, device(to)).wait_send()
+
+        return first, [], last
+
+    return Part(
+        [(block, VMEM)],
+        [(jax.ShapeDtypeStruct(block.shape, block.dtype), VMEM)],
+        [DMA(()), DMA(()), DMA(())],
+        steps,
+        plane="world",
     )
 
 
@@ -1141,53 +1234,80 @@
     )(d_pair, raw, cosine, sine, gain[None], d_query, d_gate)
 
 
-def split_kernel(pieces, gate_ref, up_ref, out_ref):
-    units = gate_ref.shape[1] // CORNERS
+def split_part(gate, up, pieces):
+    rows, every = gate.shape
+    units = every // RANKS
     piece = units // pieces
-    for y in range(CORNERS):
-        for at, ref in ((0, gate_ref), (units, up_ref)):
-            starts = [(d * CORNERS + y) * piece for d in range(pieces)]
-            parts = [ref[:, start : start + piece] for start in starts]
-            out_ref[y, :, at : at + units] = jnp.concatenate(parts, axis=1)
-
-
-def split_units(gate, up, pieces):
-    rows, units = gate.shape
-    width = units // CORNERS**2
-    narrow = pl.BlockSpec((rows, width), lambda i: (0, i))
-    return pl.pallas_call(
-        functools.partial(split_kernel, pieces),
-        grid=(CORNERS**2,),
-        out_shape=jax.ShapeDtypeStruct((RANKS, rows, width), gate.dtype),
-        in_specs=[narrow, narrow],
-        out_specs=pl.BlockSpec((CORNERS, rows, width), lambda i: (i, 0, 0)),
+
+    def steps(ins, outs, scratch):
+        (out_ref,) = outs
+
+        def some(corner_at):
+            for y in range(CORNERS):
+                for at, ref in ((0, ins[0]), (units, ins[1])):
+                    starts = [((corner_at * pieces + d) * CORNERS + y) * piece for d in range(pieces)]
+                    parts = [ref[:, start : start + piece] for start in starts]
+                    out_ref[corner_at * CORNERS + y, :, at : at + units] = jnp.concatenate(parts, axis=1)
+
+        return (lambda: None), [functools.partial(some, i) for i in range(CORNERS**2)], (lambda: None)
+
+    return Part(
+        [(gate, VMEM), (up, VMEM)],
+        [(jax.ShapeDtypeStruct((RANKS, rows, 2 * units), gate.dtype), VMEM)],
+        [],
+        steps,
+    )
+
+
+def join_part(blocks, pieces):
+    ranks, rows, width = blocks.shape
+    units = width // 2
+    piece = units // pieces
+
+    def steps(ins, outs, scratch):
+        (in_ref,) = ins
+
+        def some(corner_at):
+            for at, ref in ((0, outs[0]), (units, outs[1])):
+                parts = []
+                for d in range(pieces):
+                    for y in range(CORNERS):
+                        here = slice(at + d * piece, at + (d + 1) * piece)
+                        parts.append(in_ref[corner_at * CORNERS + y, :, here].astype(jnp.float32))
+                wide = CORNERS * units
+                ref[:, corner_at * wide : (corner_at + 1) * wide] = jnp.concatenate(parts, axis=1)
+
+        return (lambda: None), [functools.partial(some, i) for i in range(CORNERS**2)], (lambda: None)
+
+    out = (jax.ShapeDtypeStruct((rows, ranks * units), jnp.float32), VMEM)
+    return Part([(blocks, VMEM)], [out, out], [], steps)
+
+
+def norm_rows_kernel(x_ref, gain_ref, grads_ref, more_ref, out_ref, term_ref):
+    values = x_ref[...].astype(jnp.float32)
+    d_values, by_row = norm_back(values, gain_ref[...], grads_ref[...])
+    out_ref[...] = more_ref[...].astype(jnp.float32) + d_values
+
+    @pl.when(pl.program_id(0) == 0)
+    def _():
+        term_ref[...] = jnp.zeros_like(term_ref)
+
+    term_ref[...] += jnp.sum(by_row.reshape(-1, *term_ref.shape), axis=0)
+
+
+def norm_rows_back(values, gain, grads, more, steps=4):
+    rows, width = values.shape
+    some = rows_spec(rows // steps, width)
+    d_values, term = pl.pallas_call(
+        norm_rows_kernel,
+        grid=(steps,),
+        out_shape=[jax.ShapeDtypeStruct(values.shape, jnp.float32), jax.ShapeDtypeStruct((8, width), jnp.float32)],
+        in_specs=[some, fixed_spec(1, width), some, some],
+        out_specs=[some, fixed_spec(8, width)],
+        compiler_params=kernel_params(32),
         cost_estimate=expected(3),
-    )(gate, up)
-
-
-def join_kernel(pieces, in_ref, gate_ref, up_ref):
-    units = gate_ref.shape[1] // CORNERS
-    piece = units // pieces
-    for at, ref in ((0, gate_ref), (units, up_ref)):
-        parts = []
-        for d in range(pieces):
-            for y in range(CORNERS):
-                parts.append(in_ref[y, :, at + d * piece : at + (d + 1) * piece].astype(jnp.float32))
-        ref[...] = jnp.concatenate(parts, axis=1)
-
-
-def join_units(parts, pieces):
-    ranks, rows, width = parts.shape
-    narrow = pl.BlockSpec((rows, width), lambda i: (0, i))
-    shape = jax.ShapeDtypeStruct((rows, width * CORNERS**2), jnp.float32)
-    return pl.pallas_call(
-        functools.partial(join_kernel, pieces),
-        grid=(CORNERS**2,),
-        out_shape=[shape, shape],
-        in_specs=[pl.BlockSpec((CORNERS, rows, width), lambda i: (i, 0, 0))],
-        out_specs=[narrow, narrow],
-        cost_estimate=expected(4),
-    )(parts)
+    )(values, gain[None], grads, more)
+    return d_values, jnp.sum(term, axis=0)
 
 
 def widen_kernel(in_ref, *out_refs):
@@ -1251,7 +1371,6 @@
     for source in range(inner):
         rank_y, place = divmod(source, data_total)
         to_rank.append((source, place * CORNERS + rank_y))
-    from_rank = [(b, a) for a, b in to_rank]
     INNER = ("cell", "z", "y")
 
     def shards(
@@ -1301,11 +1420,12 @@
                 split_columns(gate_weight),
             ]
         )
-        attn_rows, hidden_all, gains, marks = run(
+        attn_rows, hidden_all, gains, marks, ffn_columns = run(
             [
                 columns_part(attn_columns),
-                gather_part(hidden_in),
+                later(gather_part(hidden_in), 0.22),
                 hello_part(RANKS * data_total, own_gains, marks),
+                split_part(ffn_gate, ffn_up, data_total),
             ],
             2,
             micros=70,
@@ -1330,7 +1450,6 @@
         normed_input, query_low, pair, raw, gate_raw = prepare_attention(
             hidden_all, gain_attn, w_attn, cosine, sine, gain_query, gain_key
         )
-        ffn_columns = split_units(ffn_gate, ffn_up, data_total)
         pair, cotangent_all, ffn_columns = run(
             [line_gather_part(pair), gather_part(cotangent), swap_part(ffn_columns)], 3, micros=75
         )
@@ -1347,7 +1466,6 @@
         gate_ffn, up_ffn = both[:, :units], both[:, units:]
         ffn_sig = jax.nn.sigmoid(gate_ffn)
         mixed_low = low(gate_ffn * ffn_sig * up_ffn)
-        down_terms = blocks(matrix_product(mixed_low, w_down))
 
         down_term = low(contract_first(mixed_low, cotangent_all))
         down_term, cotangent_all = lax.optimization_barrier((down_term, cotangent_all))
@@ -1360,19 +1478,12 @@
         d_both = jnp.concatenate([d_gate_ffn_low, d_up_low], axis=-1)
         both_term = low(contract_first(normed_two, d_both))
         both_term, d_both = lax.optimization_barrier((both_term, d_both))
-        two_terms = blocks(contract_last(d_both, w_ffn))
         grad_both = sum_columns(both_term)
-        two_terms, grad_down = lax.optimization_barrier((two_terms, grad_down))
-        (d_normed_two,) = run([scatter_part(two_terms)], 1, 40)
-        unused_two, norm_two_back = jax.vjp(root_mean_scale, middle, gain_ffn)
-        d_middle_norm, grad_norm_two_term = norm_two_back(d_normed_two)
-        d_middle = cotangent.astype(jnp.float32) + d_middle_norm
+        (d_normed_two,) = run([scatter_part(product=(d_both, w_ffn), transposed=True)], 6, 48, 45)
+        d_middle, grad_norm_two_term = norm_rows_back(middle, gain_ffn, d_normed_two, cotangent)
 
         branch_all = gather_tokens(low(d_middle))
-        grad_out = lax.psum_scatter(
-            low(contract_first(gated_low, branch_all)), DATA, scatter_dimension=0, tiled=True
-        )
-        grad_out = lax.ppermute(grad_out, INNER, from_rank).astype(jnp.float32)
+        branch_all, grad_down = lax.optimization_barrier((branch_all, grad_down))
         d_query, d_gate, d_pair, query_gain_terms = attend_back(
             branch_all, w_out, query_low, pair, gate_raw, own_marks, marks,
             attended, log_weight, raw, cosine, sine, gain_query,
@@ -1380,13 +1491,16 @@
         d_pair, result, grad_both = run(
             [
                 line_scatter_part(d_pair),
-                scatter_part(down_terms),
+                scatter_part(product=(mixed_low, w_down)),
                 swap_part(grad_both),
             ],
             5,
             56,
             75,
         )
+        branch_all, d_pair = lax.optimization_barrier((branch_all, d_pair))
+        out_term = low(contract_first(gated_low, branch_all))
+        grad_out = lax.psum_scatter(out_term, DATA, scatter_dimension=0, tiled=True)
         output = low(middle + result)
         d_raw, key_gain_terms = finish_attention(
             d_pair, raw, cosine, sine, gain_key, d_query, d_gate
@@ -1397,12 +1511,23 @@
         b, c = a + HEAD_SIZE, a + 2 * HEAD_SIZE
         attn_term = low(contract_first(normed_input, d_raw))
         attn_term, d_raw = lax.optimization_barrier((attn_term, d_raw))
-        one_terms = blocks(contract_last(d_raw, w_attn))
-        grad_attn = sum_columns(attn_term)
-        (d_normed,) = run([scatter_part(one_terms)], 1, 40)
-        unused_one, norm_one_back = jax.vjp(root_mean_scale, hidden, gain_attn)
-        d_hidden_norm, grad_norm_one_term = norm_one_back(d_normed)
-        input_grad = d_middle + d_hidden_norm
+        split = attn_term.reshape(CORNERS**2, cells, PLANES, CORNERS, -1, attn_term.shape[1])
+        split = jnp.transpose(split, (2, 1, 0, 3, 4, 5)).reshape(PLANES, -1, attn_term.shape[1])
+        d_normed, grad_attn, grad_gate, grad_up = run(
+            [
+                scatter_part(product=(d_raw, w_attn), transposed=True),
+                line_scatter_part(split),
+                join_part(grad_both, data_total),
+            ],
+            7,
+            56,
+            60,
+        )
+        grad_attn = low(grad_attn)
+        if cells > 1:
+            grad_attn = lax.psum_scatter(grad_attn, "cell", scatter_dimension=0, tiled=True)
+        grad_attn = grad_attn.reshape(RANKS, -1, attn_term.shape[1])
+        input_grad, grad_norm_one_term = norm_rows_back(hidden_in, gain_attn, d_normed, d_middle)
 
         terms = jnp.concatenate(
             [
@@ -1417,11 +1542,12 @@
             axis=-1,
         )
         terms = jnp.pad(terms, ((0, 0), (0, pad))).reshape((-1,) + tile)
-        grad_attn, small = run([swap_part(grad_attn), spread_part(terms)], 4, micros=15)
+        grad_attn, small, grad_out = run(
+            [swap_part(grad_attn), spread_part(terms), owners_part(grad_out)], 4, micros=18
+        )
+        grad_out = grad_out.astype(jnp.float32)
         small = small.reshape(-1)
         grad_query, grad_key, grad_value, grad_gatew = widen_columns(grad_attn, (a, b - a, c - b, a))
-        grad_both, d_normed = lax.optimization_barrier((grad_both, d_normed))
-        grad_gate, grad_up = join_units(grad_both, data_total)
         grad_norm_attn, grad_norm_ffn, grad_query_gain, grad_key_gain = (
             small[s:e] for s, e in zip(cuts[:-1], cuts[1:])
         )

time: 810 us -> 779 us (0.962)
  matrix products: 117 us -> 71.1 us
  waiting for transfers between devices: 32.2 us -> 40.7 us
    dot_general x3 -> x1, matrix products: 44.6 us -> 14.2 us  [contract_last(): lax.dot_general(left, right, (((1,), (1,)), ((), ())), preferred_element_...]
    dot_general x2 -> x1, matrix products: 28.5 us -> 13.4 us  [matrix_product(): return jnp.dot(left, right, preferred_element_type=jnp.float32)]
    pallas_call x9, Pallas kernels: 471 us -> 481 us  [run(): pl.pallas_call(functools.partial(run_kernel, parts), out_shape=[shape for...]
    unnamed x80 -> x76, local copies, waits for them, and re-layouts: 34.2 us -> 39.7 us
  transfers between devices with their start and end apart: 9 -> 7, of which waited for: 3 -> 3; matrix products, arithmetic and copies ran while one was open for 20% -> 14% of each run, Pallas kernels for 64% -> 58%
where the time goes in v5:
time: 779 us; the launch traced here: 770 us
  Pallas kernels  558 us (72%)
  matrix products  71.1 us (9%)
  local copies, waits for them, and re-layouts  55.6 us (7%)
  waiting for transfers between devices  40.7 us (5%)
  other arithmetic  28 us (4%)
  between operations  14.8 us (2%)
    pallas_call x9, Pallas kernels, run(): pl.pallas_call(functools.partial(run_kernel, parts), out_shape=[shape for...  481 us
    dot_general x4, matrix products, contract_first(): lax.dot_general(left, right, (((0,), (0,)), ((), ())), preferred_element_...  43.5 us
    unnamed x76, local copies, waits for them, and re-layouts  39.7 us
    pallas_call x1, Pallas kernels, attend_back(): pl.pallas_call(attend_back_kernel, grid=(groups,), out_shape=[shape((toke...  35.7 us
    all_gather x1, waiting for transfers between devices, shards(): w_down = lax.all_gather(down_rows, DATA, axis=0, tiled=True)  26.5 us
    pallas_call x1, Pallas kernels, attend(): pl.pallas_call(attend_kernel, grid=(groups,), out_shape=[shape((tokens, w...  17.3 us
  transfers between devices with their start and end apart: 7, of which 3 were waited for; matrix products, arithmetic and copies ran while one was open for 14% of the time, Pallas kernels for 58%

profile of v5, /device:TPU:0, one launch (start us, length us, event | category | flops | bytes accessed | tf_op | source)
XLA Modules:
  0.0 770.5 jit_solution(7770129315380146819)
XLA Ops:
  7.2 1.6 collective-permute-start
  14.6 69.6 %shard_map.263 = (bf16[4,4,2,64,768]{4,3,2,1,0:T(8,128)(2,1)}, bf16[2048,2048]{1,0:T(8,128)(2,1)}, f32[32,8,128]{2,1,0:T(8,128)}, s32[4,32,128]{2,1,0:T(8,128)}, bf16[8,64,1536]{2,1,0:T(8,128)(2,1)}) custom-call(bf16[8,64,768]{2,1,0:T(8,128)(2,1)} %maximum_bitcast_fusion.refs_0_, bf16[256,2048]{1,0:T(8,128)(2,1)} %x_ref.1, f32[8,128]{1,0:T(8,128)} %fusion.10.refs_2_, ...), custom_call_target="tpu_custom_call" | custom-call | bytes 245000000 | tf_op jit(solution)/shard_map/pallas_call | solution.py:149
  87.4 3.7 fusion
  91.8 13.0 %shard_map.264 = (bf16[2048,2048]{1,0:T(8,128)(2,1)S(1)}, bf16[2048,256]{1,0:T(8,128)(2,1)S(1)}, bf16[2048,256]{1,0:T(8,128)(2,1)S(1)}, f32[2048,384]{1,0:T(8,128)S(1)}, f32[2048,256]{1,0:T(8,128)S(1)}) custom-call(bf16[2048,2048]{1,0:T(8,128)(2,1)} %get-tuple-element.68.x_ref, f32[1,2048]{1,0:T(1,128)S(1)} %broadcast_in_dim_reshape.16.gain_ref, ...), custom_call_target="tpu_custom_call" | custom-call | bytes 42000000 | tf_op jit(solution)/shard_map/pallas_call | solution.py:1041
  104.9 1.7 copy-done.6
  108.9 3.2 copy-done.30
  112.1 74.1 %shard_map.265 = (bf16[4,2048,256]{2,1,0:T(8,128)(2,1)}, bf16[2048,2048]{1,0:T(8,128)(2,1)}, bf16[8,64,1536]{2,1,0:T(8,128)(2,1)}) custom-call(bf16[2048,256]{1,0:T(8,128)(2,1)} %copy-done.25, bf16[256,2048]{1,0:T(8,128)(2,1)} %more_ref.1, bf16[8,64,1536]{2,1,0:T(8,128)(2,1)} %get-tuple-element.75.refs_2_), custom_call_target="tpu_custom_call" | custom-call | bytes 262500000 | tf_op jit(solution)/shard_map/pallas_call | solution.py:149
  188.8 17.3 %shard_map.266 = (bf16[2048,2048]{1,0:T(8,128)(2,1)}, f32[2048,256]{1,0:T(8,128)}, f32[2048,256]{1,0:T(8,128)}, bf16[2048,256]{1,0:T(8,128)(2,1)S(1)}) custom-call(bf16[2048,256]{1,0:T(8,128)(2,1)S(1)} %get-tuple-element.73.q_ref, bf16[4,2048,256]{2,1,0:T(8,128)(2,1)} %get-tuple-element.76.kv_ref, f32[2048,256]{1,0:T(8,128)} %copy-done.15, ...), custom_call_target="tpu_custom_call" | custom-call | bytes 63000000 | tf_op jit(solution)/shard_map/pallas_call | solution.py:1120
  207.1 3.5 copy-done.12
  210.6 38.8 %shard_map.267 = f32[256,2048]{1,0:T(8,128)S(1)} custom-call(bf16[8,256,2048]{2,1,0:T(8,128)(2,1)S(1)} %bitcast.64), custom_call_target="tpu_custom_call" | custom-call | bytes 140000000 | tf_op jit(solution)/shard_map/pallas_call | solution.py:149
  251.0 40.6 %shard_map.268 = bf16[2048,2048]{1,0:T(8,128)(2,1)} custom-call(bf16[256,2048]{1,0:T(8,128)(2,1)} %multiply_convert_fusion.3.refs_0_), custom_call_target="tpu_custom_call" | custom-call | bytes 140000000 | tf_op jit(solution)/shard_map/pallas_call | solution.py:149
  291.6 8.7 %all-gather.9.cloned.1.call-done = bf16[32,64,1536]{2,1,0:T(8,128)(2,1)} async-done(((bf16[8,64,1536]{2,1,0:T(8,128)(2,1)}), bf16[32,64,1536]{2,1,0:T(8,128)(2,1)}) %all-gather.9.cloned.1.call-update) | async-done | bytes 6291472 | tf_op jit(solution)/shard_map/all_gather | solution.py:1359
  300.3 3.6 copy.57
  303.9 3.0 copy-done.34
  306.9 13.4 %fusion.15 = f32[2048,1536]{1,0:T(8,128)S(1)} fusion(bf16[2048,2048]{1,0:T(8,128)(2,1)S(1)} %copy-done.34, bf16[2048,1536]{1,0:T(8,128)(2,1)S(1)} %bitcast.66), kind=kOutput, calls=%fused_computation.50 | convolution fusion | flops 12884901888 | bytes 27262976 | tf_op jit(solution)/shard_map/dot_general | solution.py:952
  320.3 2.1 multiply_convert_fusion.2.refs_1_
  322.4 2.5 copy-done.32
  324.9 1.7 copy-done.33
  326.6 10.5 %convolution_convert_fusion.1 = bf16[768,2048]{1,0:T(8,128)(2,1)} fusion(bf16[2048,768]{1,0:T(8,128)(2,1)S(1)} %multiply_convert_fusion.2.refs_1_, bf16[2048,2048]{1,0:T(8,128)(2,1)} %get-tuple-element.82), kind=kOutput, calls=%fused_computation.6 | convolution fusion | flops 6444023808 | bytes 14680064 | tf_op jit(solution)/shard_map/dot_general | solution.py:962
  337.1 26.5 %all-gather.7.cloned.1.call-done.refs_2_ = bf16[768,2048]{1,0:T(8,128)(2,1)} async-done(((bf16[192,2048]{1,0:T(8,128)(2,1)}), bf16[768,2048]{1,0:T(8,128)(2,1)}) %all-gather.7.cloned.1.call-update) | async-done | bytes 3145744 | tf_op jit(solution)/shard_map/all_gather | solution.py:1442
  363.6 14.2 %multiply_convert_fusion.1 = (bf16[2048,768]{1,0:T(8,128)(2,1)S(1)}, bf16[2048,768]{1,0:T(8,128)(2,1)S(1)}) fusion(f32[2048,1536]{1,0:T(8,128)} %copy-done.32, bf16[2048,2048]{1,0:T(8,128)(2,1)} %get-tuple-element.82, bf16[768,2048]{1,0:T(8,128)(2,1)} %all-gather.7.cloned.1.call-done.refs_2_), kind=kOutput, calls=%fused_computation.3 | convolution fusion | flops 6462898176 | bytes 30408704 | tf_op jit(solution)/shard_map/dot_general | solution.py:956
  377.8 3.2 pad_maximum_fusion.refs_0_
  381.0 15.5 %convolution_convert_fusion = bf16[2048,1536]{1,0:T(8,128)(2,1)S(1)} fusion(bf16[2048,2048]{1,0:T(8,128)(2,1)} %shard_map.268, bf16[2048,768]{1,0:T(8,128)(2,1)S(1)} %get-tuple-element.125, bf16[2048,768]{1,0:T(8,128)(2,1)S(1)} %get-tuple-element.124), kind=kOutput, calls=%fused_computation | convolution fusion | flops 12900630528 | bytes 20971520 | tf_op jit(solution)/shard_map/dot_general | solution.py:962
  396.5 3.4 copy.63
  400.0 48.0 %shard_map.269.grads_ref = f32[256,2048]{1,0:T(8,128)S(1)} custom-call(bf16[2048,1536]{1,0:T(8,128)(2,1)} %pad_maximum_fusion.refs_0_, bf16[2048,1536]{1,0:T(8,128)(2,1)} %bitcast.67), custom_call_target="tpu_custom_call" | custom-call | bytes 157500000 | tf_op jit(solution)/shard_map/pallas_call | solution.py:149
  448.1 1.5 shard_map.270
  451.1 2.7 convert_element_type.74.refs_0_
  453.8 39.6 %shard_map.271.branch_ref = bf16[2048,2048]{1,0:T(8,128)(2,1)} custom-call(bf16[256,2048]{1,0:T(8,128)(2,1)} %convert_element_type.74.refs_0_), custom_call_target="tpu_custom_call" | custom-call | bytes 140000000 | tf_op jit(solution)/shard_map/pallas_call | solution.py:149
  493.4 2.5 convert_element_type.75
  495.8 35.7 %shard_map.272 = (bf16[2048,256]{1,0:T(8,128)(2,1)}, bf16[2048,256]{1,0:T(8,128)(2,1)}, bf16[4,2048,256]{2,1,0:T(8,128)(2,1)}, f32[4,8,128]{2,1,0:T(8,128)}) custom-call(bf16[2048,2048]{1,0:T(8,128)(2,1)} %shard_map.271.branch_ref, bf16[256,2048]{1,0:T(8,128)(2,1)} %all-gather.5.cloned.1.call-done.wo_ref, bf16[2048,256]{1,0:T(8,128)(2,1)} %copy-done.18, ...), custom_call_target="tpu_custom_call" | custom-call | bytes 122500000 | tf_op jit(solution)/shard_map/pallas_call | solution.py:1188
  532.4 5.3 reduce-scatter.6.cloned.1.call-done.refs_3_
  537.7 81.1 %shard_map.273 = (f32[2048,256]{1,0:T(8,128)}, f32[256,2048]{1,0:T(8,128)}, bf16[8,64,1536]{2,1,0:T(8,128)(2,1)}) custom-call(bf16[4,2048,256]{2,1,0:T(8,128)(2,1)} %get-tuple-element.91.refs_0_, bf16[2048,768]{1,0:T(8,128)(2,1)} %copy-done.33, bf16[768,2048]{1,0:T(8,128)(2,1)} %all-gather.7.cloned.1.call-done.refs_2_, ...), custom_call_target="tpu_custom_call" | custom-call | bytes 262500000 | tf_op jit(solution)/shard_map/pallas_call | solution.py:149
  618.8 7.1 convolution_convert_fusion.3
  627.2 1.9 copy-done.7
  629.1 1.6 copy-done.21
  634.7 10.4 %convolution_convert_fusion.2 = bf16[2048,768]{1,0:T(8,128)(2,1)S(1)} fusion(bf16[2048,2048]{1,0:T(8,128)(2,1)} %copy-done.30, bf16[2048,768]{1,0:T(8,128)(2,1)S(1)} %get-tuple-element.100.refs_0_), kind=kOutput, calls=%fused_computation.7 | convolution fusion | flops 6444023808 | bytes 14680064 | tf_op jit(solution)/shard_map/dot_general | solution.py:962
  645.1 2.0 copy.64
  647.1 65.1 %shard_map.275 = (f32[256,2048]{1,0:T(8,128)}, f32[512,768]{1,0:T(8,128)}, f32[64,6144]{1,0:T(8,128)}, f32[64,6144]{1,0:T(8,128)}) custom-call(bf16[2048,768]{1,0:T(8,128)(2,1)} %copy-done.19, bf16[2048,768]{1,0:T(8,128)(2,1)} %bitcast.62, bf16[4,512,768]{2,1,0:T(8,128)(2,1)} %bitcast.68, bf16[8,64,1536]{2,1,0:T(8,128)(2,1)} %get-tuple-element.102.refs_3_), custom_call_target="tpu_custom_call" | custom-call | bytes 210000000 | tf_op jit(solution)/shard_map/pallas_call | solution.py:149
  712.3 1.6 copy-done.14
  713.9 1.6 copy-done.22
  715.5 2.6 shard_map.276
  719.1 2.4 convert_element_type.78
  721.4 2.8 add_convert_fusion
  724.3 24.2 %shard_map.277 = (bf16[8,64,768]{2,1,0:T(8,128)(2,1)}, f32[8,128]{1,0:T(8,128)}, bf16[64,2048]{1,0:T(8,128)(2,1)}) custom-call(bf16[8,64,768]{2,1,0:T(8,128)(2,1)} %bitcast.72, f32[32,8,128]{2,1,0:T(8,128)} %bitcast.73, bf16[64,2048]{1,0:T(8,128)(2,1)} %reduce-scatter.8.cloned.1.call-done.refs_2_), custom_call_target="tpu_custom_call" | custom-call | bytes 63000000 | tf_op jit(solution)/shard_map/pallas_call | solution.py:149
  751.1 1.8 convert_element_type.80
  752.9 5.2 shard_map.278
  758.1 2.7 copy.81
  760.8 2.7 copy.82
  (114 shorter events, 28.4 us)
Async XLA Ops:
  7.2 1.7 copy-start
  7.2 180.4 %all-gather.5.cloned.1.call-start = ((), (), s32[]{:S(2)}) async-start(), calls=%async_computation.3 | async-start | bytes 1310720 | tf_op jit(solution)/shard_map/all_gather | solution.py:1441
  7.2 77.9 %collective-permute-start = (bf16[64,2048]{1,0:T(8,128)(2,1)}, bf16[64,2048]{1,0:T(8,128)(2,1)S(1)}, u32[]{:S(2)}, u32[]{:S(2)}) collective-permute-start(bf16[64,2048]{1,0:T(8,128)(2,1)} %param.21), channel_id=1, source_target_pairs={{0,0},{1,2},{2,4},{3,6},{4,1},{5,3},{6,5},{7,7},{8,8},{9,10},{10,1... | collective-permute-start | bytes 786440 | tf_op jit(solution)/shard_map/ppermute | solution.py:1434
  85.2 0.7 copy-start.35
  85.9 214.4 %all-gather.9.cloned.1.call-start = ((), (), s32[]{:S(2)}) async-start(), calls=%async_computation.8 | async-start | bytes 7864320 | tf_op jit(solution)/shard_map/all_gather | solution.py:1359
  86.1 18.8 %copy-start.27 = (f32[1,2048]{1,0:T(1,128)}, f32[1,2048]{1,0:T(1,128)S(1)}, u32[]{:S(2)}) copy-start(f32[1,2048]{1,0:T(1,128)S(1)} %broadcast_in_dim_reshape.16.gain_ref) | copy-start | bytes 24580
  86.4 18.5 %copy-start.29 = (f32[1,128]{1,0:T(1,128)}, f32[1,128]{1,0:T(1,128)S(1)}, u32[]{:S(2)}) copy-start(f32[1,128]{1,0:T(1,128)S(1)} %broadcast_in_dim_reshape.17.qg_ref) | copy-start | bytes 1540
  87.3 100.3 %copy-start.26 = (s32[4,2,2048]{2,1,0:T(2,128)}, s32[4,2,2048]{2,1,0:T(2,128)S(1)}, u32[]{:S(2)}) copy-start(s32[4,2,2048]{2,1,0:T(2,128)S(1)} %reshape.128.keys_ref) | copy-start | bytes 196612
  87.3 4.6 copy-start.8
  91.5 13.4 %copy-start.4 = (f32[2048,128]{1,0:T(8,128)}, f32[2048,128]{1,0:T(8,128)S(1)}, u32[]{:S(2)}) copy-start(f32[2048,128]{1,0:T(8,128)S(1)} %pad_maximum_fusion.1.cos_ref) | copy-start | bytes 3145732
  91.8 13.1 %copy-start.2 = (f32[2048,128]{1,0:T(8,128)}, f32[2048,128]{1,0:T(8,128)S(1)}, u32[]{:S(2)}) copy-start(f32[2048,128]{1,0:T(8,128)S(1)} %pad_maximum_fusion.2.sin_ref) | copy-start | bytes 3145732
  104.9 1.7 copy-start.6
  106.6 1.3 copy-start.15
  108.0 1.0 copy-start.25
  108.9 3.2 copy-start.30
  112.1 93.9 %copy-start.18 = (bf16[2048,256]{1,0:T(8,128)(2,1)}, bf16[2048,256]{1,0:T(8,128)(2,1)S(1)}, u32[]{:S(2)}) copy-start(bf16[2048,256]{1,0:T(8,128)(2,1)S(1)} %get-tuple-element.73.q_ref) | copy-start | bytes 3145732
  186.3 177.3 %all-gather.7.cloned.1.call-start = ((), (), s32[]{:S(2)}) async-start(), calls=%async_computation.4 | async-start | bytes 3932160 | tf_op jit(solution)/shard_map/all_gather | solution.py:1442
  186.8 62.6 %copy-start.9 = (s32[4,512,2]{2,1,0:T(8,128)}, s32[4,512,2]{2,1,0:T(8,128)S(1)}, u32[]{:S(2)}) copy-start(s32[4,512,2]{2,1,0:T(8,128)S(1)} %copy.56.own_ref) | copy-start | bytes 49156
  187.0 306.4 %reduce-scatter.4.cloned.1.call-start = ((), (), s32[]{:S(2)}) async-start(), calls=%async_computation.5 | async-start | bytes 3932160 | tf_op jit(solution)/shard_map/reduce_scatter | solution.py:1472
  187.6 1.2 copy-start.17
  206.1 1.0 copy-start.20
  207.1 42.3 %copy-start.10 = (bf16[256,2048]{1,0:T(8,128)(2,1)S(1)}, bf16[256,2048]{1,0:T(8,128)(2,1)}, u32[]{:S(2)}) copy-start(bf16[256,2048]{1,0:T(8,128)(2,1)} %x_ref.1) | copy-start | bytes 3145732
  207.1 3.5 copy-start.12
  300.3 6.6 copy-start.34
  303.9 16.4 %copy-start.31 = (bf16[4,4,2,64,1536]{4,3,2,0,1:T(8,128)(2,1)}, bf16[4,4,2,64,1536]{4,3,2,0,1:T(8,128)(2,1)S(1)}, u32[]{:S(2)}) copy-start(bf16[4,4,2,64,1536]{4,3,2,0,1:T(8,128)(2,1)S(1)} %copy.57) | copy-start | bytes 18874372
  320.3 4.6 copy-start.32
  324.9 1.7 copy-start.33
  337.1 200.6 %reduce-scatter.6.cloned.1.call-start = ((), (), s32[]{:S(2)}) async-start(), calls=%async_computation.6 | async-start | bytes 7864320 | tf_op jit(solution)/shard_map/reduce_scatter | solution.py:1367
  399.9 324.4 %reduce-scatter.8.cloned.1.call-start = ((), (), s32[]{:S(2)}) async-start(), calls=%async_computation.7 | async-start | bytes 1310720 | tf_op jit(solution)/shard_map/reduce_scatter | solution.py:1503
  400.0 48.0 %copy-start.16 = (bf16[256,2048]{1,0:T(8,128)(2,1)S(1)}, bf16[256,2048]{1,0:T(8,128)(2,1)}, u32[]{:S(2)}) copy-start(bf16[256,2048]{1,0:T(8,128)(2,1)} %more_ref.1) | copy-start | bytes 3145732
  449.6 1.4 copy-start.13
  618.8 7.1 copy-start.3
  626.0 1.2 copy-start.5
  627.2 1.9 copy-start.7
  629.1 1.6 copy-start.21
  630.7 1.2 copy-start.23
  631.9 1.3 copy-start.24
  634.7 10.4 %copy-start.19 = (bf16[2048,768]{1,0:T(8,128)(2,1)}, bf16[2048,768]{1,0:T(8,128)(2,1)S(1)}, u32[]{:S(2)}) copy-start(bf16[2048,768]{1,0:T(8,128)(2,1)S(1)} %get-tuple-element.100.refs_0_) | copy-start | bytes 9437188
  647.1 65.1 %copy-start.11 = (bf16[256,2048]{1,0:T(8,128)(2,1)S(1)}, bf16[256,2048]{1,0:T(8,128)(2,1)}, u32[]{:S(2)}) copy-start(bf16[256,2048]{1,0:T(8,128)(2,1)} %x_ref.1) | copy-start | bytes 3145732
  647.1 65.1 %copy-start.28 = (f32[1,2048]{1,0:T(1,128)S(1)}, f32[1,2048]{1,0:T(1,128)}, u32[]{:S(2)}) copy-start(f32[1,2048]{1,0:T(1,128)} %copy-done.27) | copy-start | bytes 24580
  712.3 1.6 copy-start.14
  713.9 1.6 copy-start.22
  721.4 42.0 %copy-start.1 = (bf16[64,1024]{1,0:T(8,128)(2,1)S(1)}, bf16[64,1024]{1,0:T(8,128)(2,1)}, u32[]{:S(2)}) copy-start(bf16[64,1024]{1,0:T(8,128)(2,1)} %param.18) | copy-start | bytes 393220
Sparse Core Ops, SparseCore 0:
  86.0 26.4 all-gather.4
  186.4 113.8 all-gather.8
  301.8 61.7 all-gather.6
  365.8 58.9 reduce-scatter.3
  426.9 110.7 reduce-scatter.5
  626.1 27.9 reduce-scatter.7

commit v6 on v5

--- a/solution.py
+++ b/solution.py
@@ -103,7 +103,7 @@
 
 class Part:
     def __init__(self, inputs, outs, scratch, steps, plane=None, line=False):
-        self.begin = 0.0
+        self.begin, self.end = 0.0, 1.0
         self.inputs = inputs
         self.outs = outs
         self.scratch = scratch
@@ -132,7 +132,7 @@
     for p, (first, middle, _) in zip(parts, plans):
         ordered.append((p.begin - 1.0 if p.begin == 0 else p.begin, first))
         for n, step in enumerate(middle):
-            ordered.append((p.begin + (1.0 - p.begin) * (n + 0.5) / len(middle), step))
+            ordered.append((p.begin + (p.end - p.begin) * (n + 0.5) / len(middle), step))
     for _, step in sorted(ordered, key=lambda pair: pair[0]):
         step()
     for _, _, last in plans:
@@ -161,8 +161,8 @@
     )(*[array for array, _ in inputs])
 
 
-def later(part, begin):
-    part.begin = begin
+def between(part, begin, end):
+    part.begin, part.end = begin, end
     return part
 
 
@@ -447,48 +447,44 @@
     )
 
 
-def owners_part(block):
+def halves_part(term, owners):
+    rows = term.shape[0] // owners
+    half = owners // CORNERS
+
     def steps(ins, outs, scratch):
         (in_ref,), (out_ref,) = ins, outs
         send, recv, local = scratch
-        cells = lax.axis_size("cell")
-        total = cells * PLANES
-        y, place = lax.axis_index("y"), lax.axis_index("cell") * PLANES + lax.axis_index("z")
-        here = place * CORNERS + y
-        to = y * total + place
-        whence = lax.rem(here, total) * CORNERS + here // total
-
-        def device(index):
-            planes = index // CORNERS
-            return {"cell": planes // PLANES, "z": lax.rem(planes, PLANES), "y": lax.rem(index, CORNERS)}
+        y = lax.axis_index("y")
+        dev_y = neighbours()[1]
+
+        def rows_of(i, side):
+            return in_ref.at[pl.ds(pl.multiple_of((i * CORNERS + side) * rows, rows), rows), :]
+
+        def keep(i):
+            return pltpu.make_async_copy(rows_of(i, y), out_ref.at[y * half + i], local.at[i])
+
+        def give(i):
+            return remote(rows_of(i, 1 - y), out_ref.at[y * half + i], send.at[i], recv.at[i], dev_y)
 
         def first():
-            @pl.when(to == here)
-            def _():
-                pltpu.make_async_copy(in_ref, out_ref, local).start()
-
-            @pl.when(to != here)
-            def _():
-                remote(in_ref, out_ref, send, recv, device(to)).start()
+            for i in range(half):
+                keep(i).start()
+                give(i).start()
 
         def last():
-            @pl.when(to == here)
-            def _():
-                pltpu.make_async_copy(in_ref, out_ref, local).wait()
-
-            @pl.when(to != here)
-            def _():
-                landed(out_ref, recv, device(whence))
-                remote(in_ref, out_ref, send, recv, device(to)).wait_send()
+            for i in range(half):
+                landed(out_ref.at[(1 - y) * half + i], recv.at[i], dev_y)
+                give(i).wait_send()
+                keep(i).wait()
 
         return first, [], last
 
     return Part(
-        [(block, VMEM)],
-        [(jax.ShapeDtypeStruct(block.shape, block.dtype), VMEM)],
-        [DMA(()), DMA(()), DMA(())],
+        [(term, VMEM)],
+        [(jax.ShapeDtypeStruct((owners, rows, term.shape[1]), term.dtype), VMEM)],
+        [DMA((half,)), DMA((half,)), DMA((half,))],
         steps,
-        plane="world",
+        plane="near",
     )
 
 
@@ -578,7 +574,7 @@
     )
 
 
-def line_scatter_part(terms, pieces=4):
+def line_scatter_part(terms, pieces=4, kind=jnp.float32):
     line, all_rows, columns = terms.shape
     rows = all_rows // pieces
     step = 32
@@ -602,15 +598,20 @@
             return remote(source, to, down_send.at[i], down_recv.at[i], {"z": z - 1})
 
         def first():
-            pass
+            for d in range(line - 1, 0, -1):
+                for k in range(pieces):
+
+                    @pl.when(z == 0)
+                    def _():
+                        send_up(in_ref.at[d, cut(k), :], d, k).start()
+
+                    @pl.when(z == line - 1)
+                    def _():
+                        send_down(in_ref.at[line - 1 - d, cut(k), :], d, k).start()
 
         def pass_on(d, k):
             @pl.when(z + d < line)
             def _():
-                @pl.when(z == 0)
-                def _():
-                    send_up(in_ref.at[z + d, cut(k), :], d, k).start()
-
                 if d + 1 < line:
 
                     @pl.when(z > 0)
@@ -622,10 +623,6 @@
 
             @pl.when(z - d >= 0)
             def _():
-                @pl.when(z == line - 1)
-                def _():
-                    send_down(in_ref.at[z - d, cut(k), :], d, k).start()
-
                 if d + 1 < line:
 
                     @pl.when(z < line - 1)
@@ -671,7 +668,7 @@
                         send_down(down_stage.at[d - 1, cut(k), :], d, k).wait_send()
 
         middle = [
-            functools.partial(pass_on, d, k) for d in range(line - 1, 0, -1) for k in range(pieces)
+            functools.partial(pass_on, d, k) for d in range(line - 2, 0, -1) for k in range(pieces)
         ]
         middle += [functools.partial(own, k) for k in range(pieces)]
         return first, middle, last
@@ -680,7 +677,7 @@
     buffer = pltpu.VMEM((line - 1, all_rows, columns), jnp.bfloat16)
     return Part(
         [(terms, VMEM)],
-        [(jax.ShapeDtypeStruct((all_rows, columns), jnp.float32), VMEM)],
+        [(jax.ShapeDtypeStruct((all_rows, columns), kind), VMEM)],
         [buffer, buffer, buffer, buffer, sems, sems, sems, sems],
         steps,
         line=True,
@@ -1064,7 +1061,7 @@
             rows_spec(rows, q_columns + HEAD_SIZE),
             rows_spec(rows, q_columns),
         ],
-        compiler_params=kernel_params(32),
+        compiler_params=kernel_params(60),
         cost_estimate=expected(12),
     )(hidden, gain_attn[None], w_attn, cosine, sine, gain_query[None], gain_key[None])
 
@@ -1229,7 +1226,7 @@
             fixed_spec(1, HEAD_SIZE), rows_spec(rows, q_columns), rows_spec(rows, q_columns),
         ],
         out_specs=[rows_spec(rows, columns), pl.BlockSpec((1, 8, HEAD_SIZE), lambda i: (i, 0, 0))],
-        compiler_params=kernel_params(32),
+        compiler_params=kernel_params(60),
         cost_estimate=expected(5),
     )(d_pair, raw, cosine, sine, gain[None], d_query, d_gate)
 
@@ -1273,13 +1270,13 @@
                 for d in range(pieces):
                     for y in range(CORNERS):
                         here = slice(at + d * piece, at + (d + 1) * piece)
-                        parts.append(in_ref[corner_at * CORNERS + y, :, here].astype(jnp.float32))
+                        parts.append(in_ref[corner_at * CORNERS + y, :, here])
                 wide = CORNERS * units
                 ref[:, corner_at * wide : (corner_at + 1) * wide] = jnp.concatenate(parts, axis=1)
 
         return (lambda: None), [functools.partial(some, i) for i in range(CORNERS**2)], (lambda: None)
 
-    out = (jax.ShapeDtypeStruct((rows, ranks * units), jnp.float32), VMEM)
+    out = (jax.ShapeDtypeStruct((rows, ranks * units), blocks.dtype), VMEM)
     return Part([(blocks, VMEM)], [out, out], [], steps)
 
 
@@ -1304,28 +1301,30 @@
         out_shape=[jax.ShapeDtypeStruct(values.shape, jnp.float32), jax.ShapeDtypeStruct((8, width), jnp.float32)],
         in_specs=[some, fixed_spec(1, width), some, some],
         out_specs=[some, fixed_spec(8, width)],
-        compiler_params=kernel_params(32),
+        compiler_params=kernel_params(60),
         cost_estimate=expected(3),
     )(values, gain[None], grads, more)
     return d_values, jnp.sum(term, axis=0)
 
 
 def widen_kernel(in_ref, *out_refs):
-    start = 0
-    for ref in out_refs:
-        width = ref.shape[1]
-        ref[...] = in_ref[0, :, start : start + width].astype(jnp.float32)
-        start += width
+    for rank in range(RANKS):
+        start = 0
+        for ref in out_refs:
+            width = ref.shape[1] // RANKS
+            value = in_ref[rank, :, start : start + width].astype(jnp.float32)
+            ref[:, rank * width : (rank + 1) * width] = value
+            start += width
 
 
 def widen_columns(parts, widths):
     ranks, rows, columns = parts.shape
     return pl.pallas_call(
         widen_kernel,
-        grid=(ranks,),
         out_shape=[jax.ShapeDtypeStruct((rows, ranks * w), jnp.float32) for w in widths],
-        in_specs=[pl.BlockSpec((1, rows, columns), lambda i: (i, 0, 0))],
-        out_specs=[pl.BlockSpec((rows, w), lambda i: (0, i)) for w in widths],
+        in_specs=[VMEM],
+        out_specs=[VMEM] * len(widths),
+        compiler_params=kernel_params(32),
         cost_estimate=expected(3),
     )(parts)
 
@@ -1423,7 +1422,7 @@
         attn_rows, hidden_all, gains, marks, ffn_columns = run(
             [
                 columns_part(attn_columns),
-                later(gather_part(hidden_in), 0.22),
+                between(gather_part(hidden_in), 0.22, 0.8),
                 hello_part(RANKS * data_total, own_gains, marks),
                 split_part(ffn_gate, ffn_up, data_total),
             ],
@@ -1488,19 +1487,21 @@
             branch_all, w_out, query_low, pair, gate_raw, own_marks, marks,
             attended, log_weight, raw, cosine, sine, gain_query,
         )
-        d_pair, result, grad_both = run(
+        out_term = low(contract_first(gated_low, branch_all))
+        d_pair, result, grad_both, out_term = run(
             [
                 line_scatter_part(d_pair),
                 scatter_part(product=(mixed_low, w_down)),
                 swap_part(grad_both),
+                halves_part(out_term, data_total),
             ],
             5,
-            56,
+            58,
             75,
         )
-        branch_all, d_pair = lax.optimization_barrier((branch_all, d_pair))
-        out_term = low(contract_first(gated_low, branch_all))
-        grad_out = lax.psum_scatter(out_term, DATA, scatter_dimension=0, tiled=True)
+        grad_out = lax.psum_scatter(
+            out_term.reshape(-1, out_term.shape[-1]), DATA, scatter_dimension=0, tiled=True
+        ).astype(jnp.float32)
         output = low(middle + result)
         d_raw, key_gain_terms = finish_attention(
             d_pair, raw, cosine, sine, gain_key, d_query, d_gate
@@ -1513,19 +1514,19 @@
         attn_term, d_raw = lax.optimization_barrier((attn_term, d_raw))
         split = attn_term.reshape(CORNERS**2, cells, PLANES, CORNERS, -1, attn_term.shape[1])
         split = jnp.transpose(split, (2, 1, 0, 3, 4, 5)).reshape(PLANES, -1, attn_term.shape[1])
-        d_normed, grad_attn, grad_gate, grad_up = run(
+        grad_attn, d_normed, grad_gate, grad_up = run(
             [
+                line_scatter_part(split, kind=jnp.bfloat16),
                 scatter_part(product=(d_raw, w_attn), transposed=True),
-                line_scatter_part(split),
                 join_part(grad_both, data_total),
             ],
             7,
             56,
             60,
         )
-        grad_attn = low(grad_attn)
         if cells > 1:
             grad_attn = lax.psum_scatter(grad_attn, "cell", scatter_dimension=0, tiled=True)
+        grad_gate, grad_up = grad_gate.astype(jnp.float32), grad_up.astype(jnp.float32)
         grad_attn = grad_attn.reshape(RANKS, -1, attn_term.shape[1])
         input_grad, grad_norm_one_term = norm_rows_back(hidden_in, gain_attn, d_normed, d_middle)
 
@@ -1542,10 +1543,7 @@
             axis=-1,
         )
         terms = jnp.pad(terms, ((0, 0), (0, pad))).reshape((-1,) + tile)
-        grad_attn, small, grad_out = run(
-            [swap_part(grad_attn), spread_part(terms), owners_part(grad_out)], 4, micros=18
-        )
-        grad_out = grad_out.astype(jnp.float32)
+        grad_attn, small = run([swap_part(grad_attn), spread_part(terms)], 4, micros=15)
         small = small.reshape(-1)
         grad_query, grad_key, grad_value, grad_gatew = widen_columns(grad_attn, (a, b - a, c - b, a))
         grad_norm_attn, grad_norm_ffn, grad_query_gain, grad_key_gain = (

time: 779 us -> 754 us (0.968)
  local copies, waits for them, and re-layouts: 55.6 us -> 35.9 us
    unnamed x76 -> x40, local copies, waits for them, and re-layouts: 39.7 us -> 17.8 us
    pallas_call x9, Pallas kernels: 481 us -> 468 us  [run(): pl.pallas_call(functools.partial(run_kernel, parts), out_shape=[shape for...]
  transfers between devices with their start and end apart: 7 -> 7, of which waited for: 3 -> 2; matrix products, arithmetic and copies ran while one was open for 14% -> 16% of each run, Pallas kernels for 58% -> 64%
where the time goes in v6:
time: 754 us; the launch traced here: 745 us
  Pallas kernels  554 us (73%)
  matrix products  70.6 us (9%)
  local copies, waits for them, and re-layouts  35.9 us (5%)
  waiting for transfers between devices  35.3 us (5%)
  other arithmetic  32 us (4%)
  between operations  14.7 us (2%)
    pallas_call x9, Pallas kernels, run(): pl.pallas_call(functools.partial(run_kernel, parts), out_shape=[shape for...  468 us
    dot_general x4, matrix products, contract_first(): lax.dot_general(left, right, (((0,), (0,)), ((), ())), preferred_element_...  43 us
    pallas_call x1, Pallas kernels, attend_back(): pl.pallas_call(attend_back_kernel, grid=(groups,), out_shape=[shape((toke...  35.8 us
    all_gather x1, waiting for transfers between devices, shards(): w_down = lax.all_gather(down_rows, DATA, axis=0, tiled=True)  26.6 us
    unnamed x40, local copies, waits for them, and re-layouts  17.8 us
    pallas_call x1, Pallas kernels, attend(): pl.pallas_call(attend_kernel, grid=(groups,), out_shape=[shape((tokens, w...  17.3 us
    pallas_call x1, Pallas kernels, prepare_attention(): pl.pallas_call(prepare_kernel, grid=(RANKS,), out_shape=[shape((tokens, w...  16 us
  transfers between devices with their start and end apart: 7, of which 2 were waited for; matrix products, arithmetic and copies ran while one was open for 16% of the time, Pallas kernels for 64%

profile of v6, /device:TPU:0, one launch (start us, length us, event | category | flops | bytes accessed | tf_op | source)
XLA Modules:
  0.0 745.1 jit_solution(3417434296579476023)
XLA Ops:
  7.2 1.6 collective-permute-start
  10.9 1.4 fusion.10.refs_2_
  12.3 1.3 pad_add_fusion.refs_3_
  14.6 69.6 %shard_map.263 = (bf16[4,4,2,64,768]{4,3,2,1,0:T(8,128)(2,1)}, bf16[2048,2048]{1,0:T(8,128)(2,1)}, f32[32,8,128]{2,1,0:T(8,128)}, s32[4,32,128]{2,1,0:T(8,128)}, bf16[8,64,1536]{2,1,0:T(8,128)(2,1)}) custom-call(bf16[8,64,768]{2,1,0:T(8,128)(2,1)} %maximum_bitcast_fusion.refs_0_, bf16[256,2048]{1,0:T(8,128)(2,1)} %x_ref.1, f32[8,128]{1,0:T(8,128)} %fusion.10.refs_2_, ...), custom_call_target="tpu_custom_call" | custom-call | bytes 245000000 | tf_op jit(solution)/shard_map/pallas_call | solution.py:149
  89.0 3.7 fusion
  92.7 1.3 pad_maximum_fusion.1.cos_ref
  94.0 1.3 pad_maximum_fusion.2.sin_ref
  95.3 16.0 %shard_map.264 = (bf16[2048,2048]{1,0:T(8,128)(2,1)}, bf16[2048,256]{1,0:T(8,128)(2,1)}, bf16[2048,256]{1,0:T(8,128)(2,1)}, f32[2048,384]{1,0:T(8,128)}, f32[2048,256]{1,0:T(8,128)}) custom-call(bf16[2048,2048]{1,0:T(8,128)(2,1)} %get-tuple-element.66.x_ref, f32[1,2048]{1,0:T(1,128)} %broadcast_in_dim_reshape.16.gain_ref, bf16[2048,768]{1,0:T(8,128)(2,1)} %bitcast.68, ...), custom_call_target="tpu_custom_call" | custom-call | bytes 42000000 | tf_op jit(solution)/shard_map/pallas_call | solution.py:1038
  111.4 73.9 %shard_map.265 = (bf16[4,2048,256]{2,1,0:T(8,128)(2,1)}, bf16[2048,2048]{1,0:T(8,128)(2,1)}, bf16[8,64,1536]{2,1,0:T(8,128)(2,1)}) custom-call(bf16[2048,256]{1,0:T(8,128)(2,1)} %get-tuple-element.72.refs_0_, bf16[256,2048]{1,0:T(8,128)(2,1)} %more_ref.1, bf16[8,64,1536]{2,1,0:T(8,128)(2,1)} %get-tuple-element.73.refs_2_), custom_call_target="tpu_custom_call" | custom-call | bytes 262500000 | tf_op jit(solution)/shard_map/pallas_call | solution.py:149
  186.6 1.2 copy-done.5
  187.8 17.3 %shard_map.266 = (bf16[2048,2048]{1,0:T(8,128)(2,1)}, f32[2048,256]{1,0:T(8,128)}, f32[2048,256]{1,0:T(8,128)}, bf16[2048,256]{1,0:T(8,128)(2,1)S(1)}) custom-call(bf16[2048,256]{1,0:T(8,128)(2,1)S(1)} %copy-done.6, bf16[4,2048,256]{2,1,0:T(8,128)(2,1)} %get-tuple-element.74.kv_ref, f32[2048,256]{1,0:T(8,128)} %get-tuple-element.75.gate_ref, ...), custom_call_target="tpu_custom_call" | custom-call | bytes 63000000 | tf_op jit(solution)/shard_map/pallas_call | solution.py:1117
  205.1 3.4 copy-done.4
  208.5 38.7 %shard_map.267 = f32[256,2048]{1,0:T(8,128)S(1)} custom-call(bf16[8,256,2048]{2,1,0:T(8,128)(2,1)S(1)} %bitcast.63), custom_call_target="tpu_custom_call" | custom-call | bytes 140000000 | tf_op jit(solution)/shard_map/pallas_call | solution.py:149
  247.6 1.3 copy-done.9
  250.2 40.6 %shard_map.268 = bf16[2048,2048]{1,0:T(8,128)(2,1)} custom-call(bf16[256,2048]{1,0:T(8,128)(2,1)} %multiply_convert_fusion.3.refs_0_), custom_call_target="tpu_custom_call" | custom-call | bytes 140000000 | tf_op jit(solution)/shard_map/pallas_call | solution.py:149
  290.8 8.4 %all-gather.9.cloned.1.call-done = bf16[32,64,1536]{2,1,0:T(8,128)(2,1)} async-done(((bf16[8,64,1536]{2,1,0:T(8,128)(2,1)}), bf16[32,64,1536]{2,1,0:T(8,128)(2,1)}) %all-gather.9.cloned.1.call-update) | async-done | bytes 6291472 | tf_op jit(solution)/shard_map/all_gather | solution.py:1358
  299.2 3.6 copy.57
  302.9 3.0 copy-done.15
  305.8 13.4 %fusion.15 = f32[2048,1536]{1,0:T(8,128)S(1)} fusion(bf16[2048,2048]{1,0:T(8,128)(2,1)S(1)} %copy-done.15, bf16[2048,1536]{1,0:T(8,128)(2,1)S(1)} %bitcast.65), kind=kOutput, calls=%fused_computation.50 | convolution fusion | flops 12884901888 | bytes 27262976 | tf_op jit(solution)/shard_map/dot_general | solution.py:949
  319.3 2.1 multiply_convert_fusion.2.refs_1_
  321.4 2.4 copy-done.12
  323.8 1.7 copy-done.13
  325.5 10.5 %convolution_convert_fusion.1 = bf16[768,2048]{1,0:T(8,128)(2,1)} fusion(bf16[2048,768]{1,0:T(8,128)(2,1)S(1)} %multiply_convert_fusion.2.refs_1_, bf16[2048,2048]{1,0:T(8,128)(2,1)} %get-tuple-element.80), kind=kOutput, calls=%fused_computation.6 | convolution fusion | flops 6444023808 | bytes 14680064 | tf_op jit(solution)/shard_map/dot_general | solution.py:959
  336.0 26.6 %all-gather.7.cloned.1.call-done.refs_2_ = bf16[768,2048]{1,0:T(8,128)(2,1)} async-done(((bf16[192,2048]{1,0:T(8,128)(2,1)}), bf16[768,2048]{1,0:T(8,128)(2,1)}) %all-gather.7.cloned.1.call-update) | async-done | bytes 3145744 | tf_op jit(solution)/shard_map/all_gather | solution.py:1441
  362.6 14.2 %multiply_convert_fusion.1 = (bf16[2048,768]{1,0:T(8,128)(2,1)S(1)}, bf16[2048,768]{1,0:T(8,128)(2,1)S(1)}) fusion(f32[2048,1536]{1,0:T(8,128)} %copy-done.12, bf16[2048,2048]{1,0:T(8,128)(2,1)} %get-tuple-element.80, bf16[768,2048]{1,0:T(8,128)(2,1)} %all-gather.7.cloned.1.call-done.refs_2_), kind=kOutput, calls=%fused_computation.3 | convolution fusion | flops 6462898176 | bytes 30408704 | tf_op jit(solution)/shard_map/dot_general | solution.py:953
  376.8 3.1 pad_maximum_fusion.refs_0_
  379.9 15.5 %convolution_convert_fusion = bf16[2048,1536]{1,0:T(8,128)(2,1)S(1)} fusion(bf16[2048,2048]{1,0:T(8,128)(2,1)} %shard_map.268, bf16[2048,768]{1,0:T(8,128)(2,1)S(1)} %get-tuple-element.121, bf16[2048,768]{1,0:T(8,128)(2,1)S(1)} %get-tuple-element.120), kind=kOutput, calls=%fused_computation | convolution fusion | flops 12900630528 | bytes 20971520 | tf_op jit(solution)/shard_map/dot_general | solution.py:959
  395.4 3.4 copy.63
  399.5 47.9 %shard_map.269.grads_ref = f32[256,2048]{1,0:T(8,128)S(1)} custom-call(bf16[2048,1536]{1,0:T(8,128)(2,1)} %pad_maximum_fusion.refs_0_, bf16[2048,1536]{1,0:T(8,128)(2,1)} %bitcast.66), custom_call_target="tpu_custom_call" | custom-call | bytes 157500000 | tf_op jit(solution)/shard_map/pallas_call | solution.py:149
  447.4 1.3 copy-done.3
  448.8 4.9 shard_map.270
  454.5 2.7 convert_element_type.77.refs_0_
  457.3 39.5 %shard_map.271.branch_ref = bf16[2048,2048]{1,0:T(8,128)(2,1)} custom-call(bf16[256,2048]{1,0:T(8,128)(2,1)} %convert_element_type.77.refs_0_), custom_call_target="tpu_custom_call" | custom-call | bytes 140000000 | tf_op jit(solution)/shard_map/pallas_call | solution.py:149
  496.8 2.5 convert_element_type.78
  499.3 35.8 %shard_map.272 = (bf16[2048,256]{1,0:T(8,128)(2,1)}, bf16[2048,256]{1,0:T(8,128)(2,1)}, bf16[4,2048,256]{2,1,0:T(8,128)(2,1)}, f32[4,8,128]{2,1,0:T(8,128)}) custom-call(bf16[2048,2048]{1,0:T(8,128)(2,1)} %shard_map.271.branch_ref, bf16[256,2048]{1,0:T(8,128)(2,1)} %all-gather.5.cloned.1.call-done.wo_ref, bf16[2048,256]{1,0:T(8,128)(2,1)} %get-tuple-element.71.q_ref, ...), custom_call_target="tpu_custom_call" | custom-call | bytes 122500000 | tf_op jit(solution)/shard_map/pallas_call | solution.py:1185
  536.0 6.8 convolution_convert_fusion.3.refs_4_
  542.7 78.0 %shard_map.273 = (f32[2048,256]{1,0:T(8,128)}, f32[256,2048]{1,0:T(8,128)}, bf16[8,64,1536]{2,1,0:T(8,128)(2,1)}, bf16[4,64,2048]{2,1,0:T(8,128)(2,1)}) custom-call(bf16[4,2048,256]{2,1,0:T(8,128)(2,1)} %get-tuple-element.89.refs_0_, bf16[2048,768]{1,0:T(8,128)(2,1)} %copy-done.13, bf16[768,2048]{1,0:T(8,128)(2,1)} %all-gather.7.cloned.1.call-done.refs_2_, ...), custom_call_target="tpu_custom_call" | custom-call | bytes 262500000 | tf_op jit(solution)/shard_map/pallas_call | solution.py:149
  620.8 6.4 shard_map.274
  627.2 10.2 %convolution_convert_fusion.2 = bf16[2048,768]{1,0:T(8,128)(2,1)S(1)} fusion(bf16[2048,2048]{1,0:T(8,128)(2,1)} %get-tuple-element.93, bf16[2048,768]{1,0:T(8,128)(2,1)} %get-tuple-element.99.refs_1_), kind=kOutput, calls=%fused_computation.7 | convolution fusion | flops 6444023808 | bytes 14680064 | tf_op jit(solution)/shard_map/dot_general | solution.py:959
  637.4 2.0 copy.64
  639.4 60.5 %shard_map.275 = (bf16[512,768]{1,0:T(8,128)(2,1)}, f32[256,2048]{1,0:T(8,128)}, bf16[64,6144]{1,0:T(8,128)(2,1)}, bf16[64,6144]{1,0:T(8,128)(2,1)}) custom-call(bf16[4,512,768]{2,1,0:T(8,128)(2,1)} %bitcast.67, bf16[2048,768]{1,0:T(8,128)(2,1)} %get-tuple-element.99.refs_1_, bf16[2048,768]{1,0:T(8,128)(2,1)} %bitcast.69, ...), custom_call_target="tpu_custom_call" | custom-call | bytes 210000000 | tf_op jit(solution)/shard_map/pallas_call | solution.py:149
  700.0 5.0 shard_map.276
  707.5 18.9 %shard_map.277 = (bf16[8,64,768]{2,1,0:T(8,128)(2,1)}, f32[8,128]{1,0:T(8,128)}) custom-call(bf16[8,64,768]{2,1,0:T(8,128)(2,1)} %bitcast.74, f32[32,8,128]{2,1,0:T(8,128)} %bitcast.75), custom_call_target="tpu_custom_call" | custom-call | bytes 52500000 | tf_op jit(solution)/shard_map/pallas_call | solution.py:149
  728.7 2.4 convert_element_type.83
  731.2 1.2 convert_element_type.84
  732.4 1.3 fusion.13
  733.8 1.3 fusion.14
  736.3 1.8 convert_element_type.82
  (79 shorter events, 19.2 us)
Async XLA Ops:
  7.2 1.7 copy-start
  7.2 179.4 %all-gather.5.cloned.1.call-start = ((), (), s32[]{:S(2)}) async-start(), calls=%async_computation.3 | async-start | bytes 1310720 | tf_op jit(solution)/shard_map/all_gather | solution.py:1440
  7.2 77.9 %collective-permute-start = (bf16[64,2048]{1,0:T(8,128)(2,1)}, bf16[64,2048]{1,0:T(8,128)(2,1)S(1)}, u32[]{:S(2)}, u32[]{:S(2)}) collective-permute-start(bf16[64,2048]{1,0:T(8,128)(2,1)} %param.21), channel_id=1, source_target_pairs={{0,0},{1,2},{2,4},{3,6},{4,1},{5,3},{6,5},{7,7},{8,8},{9,10},{10,1... | collective-permute-start | bytes 786440 | tf_op jit(solution)/shard_map/ppermute | solution.py:1433
  85.1 0.7 copy-start.18
  85.9 213.4 %all-gather.9.cloned.1.call-start = ((), (), s32[]{:S(2)}) async-start(), calls=%async_computation.8 | async-start | bytes 7864320 | tf_op jit(solution)/shard_map/all_gather | solution.py:1358
  88.9 97.7 %copy-start.8 = (s32[4,2,2048]{2,1,0:T(2,128)}, s32[4,2,2048]{2,1,0:T(2,128)S(1)}, u32[]{:S(2)}) copy-start(s32[4,2,2048]{2,1,0:T(2,128)S(1)} %reshape.131.keys_ref) | copy-start | bytes 196612
  111.4 75.2 %copy-start.6 = (bf16[2048,256]{1,0:T(8,128)(2,1)S(1)}, bf16[2048,256]{1,0:T(8,128)(2,1)}, u32[]{:S(2)}) copy-start(bf16[2048,256]{1,0:T(8,128)(2,1)} %get-tuple-element.71.q_ref) | copy-start | bytes 3145732
  185.3 177.3 %all-gather.7.cloned.1.call-start = ((), (), s32[]{:S(2)}) async-start(), calls=%async_computation.4 | async-start | bytes 3932160 | tf_op jit(solution)/shard_map/all_gather | solution.py:1441
  185.8 61.5 %copy-start.2 = (s32[4,512,2]{2,1,0:T(8,128)}, s32[4,512,2]{2,1,0:T(8,128)S(1)}, u32[]{:S(2)}) copy-start(s32[4,512,2]{2,1,0:T(8,128)S(1)} %copy.56.own_ref) | copy-start | bytes 49156
  186.0 310.8 %reduce-scatter.4.cloned.1.call-start = ((), (), s32[]{:S(2)}) async-start(), calls=%async_computation.5 | async-start | bytes 3932160 | tf_op jit(solution)/shard_map/reduce_scatter | solution.py:1471
  186.6 1.2 copy-start.5
  187.8 59.4 %copy-start.14 = (bf16[256,2048]{1,0:T(8,128)(2,1)S(1)}, bf16[256,2048]{1,0:T(8,128)(2,1)}, u32[]{:S(2)}) copy-start(bf16[256,2048]{1,0:T(8,128)(2,1)} %x_ref.1) | copy-start | bytes 3145732
  205.1 3.4 copy-start.4
  247.6 1.3 copy-start.9
  299.2 6.6 copy-start.15
  302.9 16.4 %copy-start.11 = (bf16[4,4,2,64,1536]{4,3,2,0,1:T(8,128)(2,1)}, bf16[4,4,2,64,1536]{4,3,2,0,1:T(8,128)(2,1)S(1)}, u32[]{:S(2)}) copy-start(bf16[4,4,2,64,1536]{4,3,2,0,1:T(8,128)(2,1)S(1)} %copy.57) | copy-start | bytes 18874372
  319.3 4.5 copy-start.12
  323.8 1.7 copy-start.13
  336.0 206.8 %reduce-scatter.6.cloned.1.call-start = ((), (), s32[]{:S(2)}) async-start(), calls=%async_computation.6 | async-start | bytes 7864320 | tf_op jit(solution)/shard_map/reduce_scatter | solution.py:1366
  398.8 337.5 %reduce-scatter.8.cloned.1.call-start = ((), (), s32[]{:S(2)}) async-start(), calls=%async_computation.7 | async-start | bytes 1310720 | tf_op jit(solution)/shard_map/reduce_scatter | solution.py:1502
  447.4 1.3 copy-start.3
  700.0 31.2 %copy-start.17 = (bf16[64,6144]{1,0:T(8,128)(2,1)S(1)}, bf16[64,6144]{1,0:T(8,128)(2,1)}, u32[]{:S(2)}) copy-start(bf16[64,6144]{1,0:T(8,128)(2,1)} %get-tuple-element.116) | copy-start | bytes 2359300
  700.0 35.1 %copy-start.10 = (f32[256,2048]{1,0:T(8,128)S(1)}, f32[256,2048]{1,0:T(8,128)}, u32[]{:S(2)}) copy-start(f32[256,2048]{1,0:T(8,128)} %copy-done.9) | copy-start | bytes 6291460
  706.8 31.2 %copy-start.1 = (bf16[64,1024]{1,0:T(8,128)(2,1)S(1)}, bf16[64,1024]{1,0:T(8,128)(2,1)}, u32[]{:S(2)}) copy-start(bf16[64,1024]{1,0:T(8,128)(2,1)} %param.18) | copy-start | bytes 393220
  726.5 1.1 copy-start.7
  727.6 7.5 %copy-start.16 = (f32[256,2048]{1,0:T(8,128)S(1)}, f32[256,2048]{1,0:T(8,128)}, u32[]{:S(2)}) copy-start(f32[256,2048]{1,0:T(8,128)} %get-tuple-element.92) | copy-start | bytes 6291460
Sparse Core Ops, SparseCore 0:
  86.0 26.4 all-gather.4
  185.4 113.7 all-gather.8
  300.8 61.7 all-gather.6
  364.7 58.8 reduce-scatter.3
  425.8 110.7 reduce-scatter.5
  620.9 26.3 reduce-scatter.7

commit v7 on v6

--- a/solution.py
+++ b/solution.py
@@ -70,9 +70,6 @@
 
 
 def greet(plane, line):
-    if plane == "world":
-        everyone(math.prod(lax.axis_size(n) for n in ALL))
-        return
     barrier = pltpu.get_barrier_semaphore()
     near = {"near": neighbours(), "all": [p for p, _ in plane_peers()], None: []}[plane]
     for device in near:
@@ -124,7 +121,7 @@
     ins = take([len(p.inputs) for p in parts])
     outs = take([len(p.outs) for p in parts])
     scratch = take([len(p.scratch) for p in parts])
-    ranks = [None, "near", "all", "world"]
+    ranks = [None, "near", "all"]
     plane = ranks[max(ranks.index(p.plane) for p in parts)]
     greet(plane, any(p.line for p in parts))
     plans = [p.steps(i, o, s) for p, i, o, s in zip(parts, ins, outs, scratch)]
@@ -684,101 +681,6 @@
     )
 
 
-def places():
-    sizes = [lax.axis_size(n) for n in ALL]
-    me = 0
-    for n, size in zip(ALL, sizes):
-        me = me * size + lax.axis_index(n)
-
-    def device(index):
-        where = {}
-        for n, size in reversed(list(zip(ALL, sizes))):
-            where[n] = lax.rem(index, size)
-            index = index // size
-        return where
-
-    return me, device
-
-
-def everyone(total):
-    me, device = places()
-    barrier = pltpu.get_barrier_semaphore()
-
-    def greet_one(d, carry):
-        other = device(lax.rem(me + d, total))
-        pl.semaphore_signal(barrier, inc=1, device_id=other, device_id_type=MESH_ID)
-        return carry
-
-    lax.fori_loop(1, total, greet_one, 0)
-    pl.semaphore_wait(barrier, total - 1)
-    return me, device
-
-
-def hello_part(total, gains, marks):
-    def steps(ins, outs, scratch):
-        gains_ref, marks_ref = ins
-        gains_out, marks_out = outs
-        g_send, g_recv, m_send, m_recv, local = scratch
-        me, device = places()
-        x, c, y = corner()
-        group = x * CORNERS + c
-        keeps = [
-            pltpu.make_async_copy(gains_ref, gains_out.at[me], local.at[0]),
-            pltpu.make_async_copy(marks_ref, marks_out.at[group], local.at[1]),
-        ]
-        near = [(i, dx, dc) for i, (dx, dc) in enumerate([(0, 1), (1, 0), (1, 1)])]
-        sent = []
-
-        def give(d):
-            other = device(lax.rem(me + d, total))
-            return remote(gains_ref, gains_out.at[me], g_send.at[d], g_recv.at[d], other)
-
-        def first():
-            for keep in keeps:
-                keep.start()
-            for i, dx, dc in near:
-                there = {"x": flip(x, dx), "core": flip(c, dc)}
-                copy = remote(marks_ref, marks_out.at[group], m_send.at[i], m_recv.at[i], there)
-                copy.start()
-                sent.append(copy)
-
-            def put(d, carry):
-                give(d).start()
-                return carry
-
-            lax.fori_loop(1, total, put, 0)
-
-        def last():
-            def take(d, carry):
-                source = lax.rem(me + total - d, total)
-                landed(gains_out.at[source], g_recv.at[d], device(source))
-                give(d).wait_send()
-                return carry
-
-            lax.fori_loop(1, total, take, 0)
-            for i, dx, dc in near:
-                there = {"x": flip(x, dx), "core": flip(c, dc)}
-                theirs = flip(x, dx) * CORNERS + flip(c, dc)
-                landed(marks_out.at[theirs], m_recv.at[i], there)
-            for copy in sent:
-                copy.wait_send()
-            for keep in keeps:
-                keep.wait()
-
-        return first, [], last
-
-    return Part(
-        [(gains, VMEM), (marks, VMEM)],
-        [
-            (jax.ShapeDtypeStruct((total,) + gains.shape, gains.dtype), VMEM),
-            (jax.ShapeDtypeStruct((CORNERS**2,) + marks.shape, marks.dtype), VMEM),
-        ],
-        [DMA((total,)), DMA((total,)), DMA((3,)), DMA((3,)), DMA((2,))],
-        steps,
-        plane="world",
-    )
-
-
 def columns_part(blocks):
     ranks, rows, columns = blocks.shape
 
@@ -886,49 +788,126 @@
     )
 
 
-def spread_part(tiles):
-    total = tiles.shape[0]
-
+def tiles_part(tile):
     def steps(ins, outs, scratch):
         (in_ref,), (out_ref,) = ins, outs
-        buffer, send, recv = scratch
-        me, device = places()
-
-        def give(d):
-            other = lax.rem(me + d, total)
-            return remote(in_ref.at[other], buffer.at[me], send.at[d], recv.at[d], device(other))
+        send, recv, up_send, up_recv, down_send, down_recv, local = scratch
+        z = lax.axis_index("z")
+        own = slot(*corner())
+        peers = plane_peers()
+        keep = pltpu.make_async_copy(in_ref, out_ref.at[z, own], local)
+
+        def give(i):
+            return remote(in_ref, out_ref.at[z, own], send.at[i], recv.at[i], peers[i][0])
+
+        def up(t):
+            to = out_ref.at[z - t]
+            return remote(to, to, up_send.at[t], up_recv.at[t], {"z": z + 1})
+
+        def down(t):
+            to = out_ref.at[z + t]
+            return remote(to, to, down_send.at[t], down_recv.at[t], {"z": z - 1})
 
         def first():
-            def put(d, carry):
-                give(d).start()
-                return carry
-
-            lax.fori_loop(1, total, put, 0)
+            keep.start()
+            for i in range(len(peers)):
+                give(i).start()
+
+        def swapped():
+            for i, (there, other) in enumerate(peers):
+                landed(out_ref.at[z, other], recv.at[i], there)
+            keep.wait()
+
+            @pl.when(z < PLANES - 1)
+            def _():
+                up(0).start()
+
+            @pl.when(z > 0)
+            def _():
+                down(0).start()
+
+        def arrive(t):
+            on = t + 1 < PLANES - 1
+
+            @pl.when(z - 1 - t >= 0)
+            def _():
+                landed(out_ref.at[z - 1 - t], up_recv.at[t], {"z": z - 1})
+                if on:
+
+                    @pl.when(z < PLANES - 1)
+                    def _():
+                        up(t + 1).start()
+
+            @pl.when(z + 1 + t < PLANES)
+            def _():
+                landed(out_ref.at[z + 1 + t], down_recv.at[t], {"z": z + 1})
+                if on:
+
+                    @pl.when(z > 0)
+                    def _():
+                        down(t + 1).start()
 
         def last():
-            def take(d, carry):
-                source = lax.rem(me + total - d, total)
-                landed(buffer.at[source], recv.at[d], device(source))
-                give(d).wait_send()
-                return carry
-
-            lax.fori_loop(1, total, take, 0)
-            out_ref[...] = in_ref[me]
-
-            def add(d, carry):
-                out_ref[...] += buffer[lax.rem(me + d, total)]
-                return carry
-
-            lax.fori_loop(1, total, add, 0)
+            for i in range(len(peers)):
+                give(i).wait_send()
+            for t in range(PLANES - 1):
+
+                @pl.when((z < PLANES - 1) & (z - t >= 0))
+                def _():
+                    up(t).wait_send()
+
+                @pl.when((z > 0) & (z + t < PLANES))
+                def _():
+                    down(t).wait_send()
+
+        middle = [swapped] + [functools.partial(arrive, t) for t in range(PLANES - 1)]
+        return first, middle, last
+
+    n = len(OTHERS)
+    line = DMA((PLANES - 1,))
+    return Part(
+        [(tile, VMEM)],
+        [(jax.ShapeDtypeStruct((PLANES, RANKS) + tile.shape, tile.dtype), VMEM)],
+        [DMA((n,)), DMA((n,)), line, line, line, line, DMA(())],
+        steps,
+        plane="all",
+        line=True,
+    )
+
+
+def marks_part(marks):
+    def steps(ins, outs, scratch):
+        (in_ref,), (out_ref,) = ins, outs
+        send, recv, local = scratch
+        x, c, _ = corner()
+        keep = pltpu.make_async_copy(in_ref, out_ref.at[x * CORNERS + c], local)
+        near = []
+        for i, (dx, dc) in enumerate([(0, 1), (1, 0), (1, 1)]):
+            px, pc = flip(x, dx), flip(c, dc)
+            near.append((i, {"x": px, "core": pc}, px * CORNERS + pc))
+
+        def give(i, there):
+            return remote(in_ref, out_ref.at[x * CORNERS + c], send.at[i], recv.at[i], there)
+
+        def first():
+            keep.start()
+            for i, there, _ in near:
+                give(i, there).start()
+
+        def last():
+            for i, there, theirs in near:
+                landed(out_ref.at[theirs], recv.at[i], there)
+                give(i, there).wait_send()
+            keep.wait()
 
         return first, [], last
 
     return Part(
-        [(tiles, VMEM)],
-        [(jax.ShapeDtypeStruct(tiles.shape[1:], tiles.dtype), VMEM)],
-        [pltpu.VMEM(tiles.shape, tiles.dtype), DMA((total,)), DMA((total,))],
+        [(marks, VMEM)],
+        [(jax.ShapeDtypeStruct((CORNERS**2,) + marks.shape, marks.dtype), VMEM)],
+        [DMA((3,)), DMA((3,)), DMA(())],
         steps,
-        plane="world",
+        plane="all",
     )
 
 
@@ -1132,15 +1111,29 @@
 
 def attend_back_kernel(
     branch_ref, wo_ref, q_ref, kv_ref, gate_ref, own_ref, keys_ref, att_ref, log_ref, raw_ref,
-    cos_ref, sin_ref, qg_ref, dq_ref, dgate_ref, dkv_ref, gain_ref,
+    cos_ref, sin_ref, qg_ref, gated_ref, out_ref, dkv_ref, gain_ref, term_ref, term_sum,
 ):
     planes, window = kv_ref.shape[0], kv_ref.shape[1]
     scale = 1.0 / math.sqrt(HEAD_SIZE)
+    turned = jnp.transpose(gated_ref[...])
+
+    @pl.when(pl.program_id(0) == 0)
+    def _():
+        term_sum[...] = dot(turned, branch_ref[...])
+
+    @pl.when(pl.program_id(0) > 0)
+    def _():
+        term_sum[...] += dot(turned, branch_ref[...])
+
+    @pl.when(pl.program_id(0) == pl.num_programs(0) - 1)
+    def _():
+        term_ref[...] = low(term_sum[...])
+
     d_gated = dot_rows(branch_ref[...], wo_ref[...])
     gate = jax.nn.sigmoid(gate_ref[...])
     attended = att_ref[...]
     d_attended = low(d_gated * gate)
-    dgate_ref[...] = low(d_gated * attended * gate * (1.0 - gate))
+    out_ref[:, (REPEAT + 2) * HEAD_SIZE :] = low(d_gated * attended * gate * (1.0 - gate))
     product = d_attended.astype(jnp.float32) * attended
     delta = [jnp.sum(product[:, head(h)], axis=-1, keepdims=True) for h in range(REPEAT)]
     turned_q = [jnp.transpose(q_ref[:, head(h)]) for h in range(REPEAT)]
@@ -1168,12 +1161,14 @@
     for h in range(REPEAT):
         grads = turn_back(d_query[h] * scale, cosine, sine)
         d_raw, by_row = norm_back(raw_ref[:, head(h)], qg_ref[...], grads)
-        dq_ref[:, head(h)] = low(d_raw)
+        out_ref[:, head(h)] = low(d_raw)
         total += jnp.sum(by_row, axis=0, keepdims=True)
     gain_ref[0] = jnp.broadcast_to(total, gain_ref.shape[1:])
 
 
-def attend_back(branch, w_out, query, pair, gate, own, keys, attended, log, raw, cosine, sine, gain):
+def attend_back(
+    branch, w_out, query, pair, gate, own, keys, attended, log, raw, cosine, sine, gain, gated
+):
     tokens, q_columns = query.shape
     groups = own.shape[0]
     window = tokens // groups
@@ -1186,49 +1181,58 @@
         attend_back_kernel,
         grid=(groups,),
         out_shape=[
-            shape((tokens, q_columns), jnp.bfloat16),
-            shape((tokens, q_columns), jnp.bfloat16),
+            shape((tokens, 2 * q_columns + 2 * HEAD_SIZE), jnp.bfloat16),
             shape(pair.shape, jnp.bfloat16),
             shape((groups, 8, HEAD_SIZE), jnp.float32),
+            shape((q_columns, width), jnp.bfloat16),
         ],
         in_specs=[
             rows_spec(window, width), fixed_spec(q_columns, width), columns, kv, columns, mine, marks,
-            columns, columns, rows_spec(window, raw.shape[1]), table, table, fixed_spec(1, HEAD_SIZE),
+            columns, columns, rows_spec(window, raw.shape[1]), table, table, fixed_spec(1, HEAD_SIZE), columns,
         ],
-        out_specs=[columns, columns, kv, pl.BlockSpec((1, 8, HEAD_SIZE), lambda i: (i, 0, 0))],
+        out_specs=[
+            rows_spec(window, 2 * q_columns + 2 * HEAD_SIZE), kv, pl.BlockSpec((1, 8, HEAD_SIZE), lambda i: (i, 0, 0)),
+            fixed_spec(q_columns, width),
+        ],
+        scratch_shapes=[pltpu.VMEM((q_columns, width), jnp.float32)],
         compiler_params=kernel_params(56),
         cost_estimate=expected(35),
-    )(branch, w_out, query, pair, gate, own, keys, attended, log, raw, cosine, sine, gain[None])
-
-
-def finish_kernel(dkv_ref, raw_ref, cos_ref, sin_ref, kg_ref, dq_ref, dgate_ref, out_ref, gain_ref):
+    )(branch, w_out, query, pair, gate, own, keys, attended, log, raw, cosine, sine, gain[None], gated)
+
+
+def finish_kernel(dkv_ref, raw_ref, cos_ref, sin_ref, kg_ref, partial_ref, out_ref, gain_ref):
     grads = turn_back(dkv_ref[:, head(0)], cos_ref[...], sin_ref[...])
-    d_raw, by_row = norm_back(raw_ref[:, head(REPEAT)], kg_ref[...], grads)
-    out_ref[:, : REPEAT * HEAD_SIZE] = dq_ref[...]
-    out_ref[:, head(REPEAT)] = low(d_raw)
-    out_ref[:, head(REPEAT + 1)] = low(dkv_ref[:, head(1)])
-    out_ref[:, (REPEAT + 2) * HEAD_SIZE :] = dgate_ref[...]
+    d_raw, by_row = norm_back(raw_ref[...], kg_ref[...], grads)
+    out_ref[:, head(0)] = low(d_raw)
+    out_ref[:, head(1)] = low(dkv_ref[:, head(1)])
     gain_ref[0] = jnp.broadcast_to(jnp.sum(by_row, axis=0, keepdims=True), gain_ref.shape[1:])
 
 
-def finish_attention(d_pair, raw, cosine, sine, gain, d_query, d_gate, steps=4):
-    tokens, q_columns = d_query.shape
+def finish_attention(d_pair, raw, cosine, sine, gain, partial, steps=4):
+    tokens = d_pair.shape[0]
     rows = tokens // steps
+    table = rows_spec(rows, HEAD_SIZE)
     shape = jax.ShapeDtypeStruct
-    table = rows_spec(rows, HEAD_SIZE)
-    columns = 2 * q_columns + 2 * HEAD_SIZE
     return pl.pallas_call(
         finish_kernel,
         grid=(steps,),
-        out_shape=[shape((tokens, columns), jnp.bfloat16), shape((steps, 8, HEAD_SIZE), jnp.float32)],
+        out_shape=[shape(partial.shape, partial.dtype), shape((steps, 8, HEAD_SIZE), jnp.float32)],
         in_specs=[
-            rows_spec(rows, 2 * HEAD_SIZE), rows_spec(rows, raw.shape[1]), table, table,
-            fixed_spec(1, HEAD_SIZE), rows_spec(rows, q_columns), rows_spec(rows, q_columns),
+            rows_spec(rows, 2 * HEAD_SIZE),
+            pl.BlockSpec((rows, HEAD_SIZE), lambda i: (i, REPEAT)),
+            table,
+            table,
+            fixed_spec(1, HEAD_SIZE),
+            ANYWHERE,
         ],
-        out_specs=[rows_spec(rows, columns), pl.BlockSpec((1, 8, HEAD_SIZE), lambda i: (i, 0, 0))],
+        out_specs=[
+            pl.BlockSpec((rows, 2 * HEAD_SIZE), lambda i: (i, REPEAT // 2)),
+            pl.BlockSpec((1, 8, HEAD_SIZE), lambda i: (i, 0, 0)),
+        ],
+        input_output_aliases={5: 0},
         compiler_params=kernel_params(60),
-        cost_estimate=expected(5),
-    )(d_pair, raw, cosine, sine, gain[None], d_query, d_gate)
+        cost_estimate=expected(4),
+    )(d_pair, raw, cosine, sine, gain[None], partial)
 
 
 def split_part(gate, up, pieces):
@@ -1307,26 +1311,41 @@
     return d_values, jnp.sum(term, axis=0)
 
 
-def widen_kernel(in_ref, *out_refs):
+def widen_kernel(count, in_ref, *refs):
+    weights, refs = refs[:count], refs[count:]
+    others = (len(refs) - count - 1) // 2
+    low_refs, refs = refs[:others], refs[others:]
+    out_refs, along_ref, wide_refs = refs[:count], refs[count], refs[count + 1 :]
+    along = jnp.zeros(along_ref.shape, jnp.float32)
     for rank in range(RANKS):
         start = 0
-        for ref in out_refs:
+        for weight_ref, ref in zip(weights, out_refs):
             width = ref.shape[1] // RANKS
+            place = slice(rank * width, (rank + 1) * width)
             value = in_ref[rank, :, start : start + width].astype(jnp.float32)
-            ref[:, rank * width : (rank + 1) * width] = value
+            ref[:, place] = value
+            product = value * weight_ref[:, place].astype(jnp.float32)
+            along += sum(product[:, head(h)] for h in range(width // HEAD_SIZE))
             start += width
-
-
-def widen_columns(parts, widths):
+    along_ref[...] = jnp.broadcast_to(jnp.sum(along, axis=1, keepdims=True), along_ref.shape)
+    for ref, wide in zip(low_refs, wide_refs):
+        wide[...] = ref[...].astype(jnp.float32)
+
+
+def widen_columns(parts, widths, weights, others):
     ranks, rows, columns = parts.shape
+    shape = jax.ShapeDtypeStruct
+    out_shape = [shape((rows, ranks * w), jnp.float32) for w in widths]
+    out_shape += [shape((rows, HEAD_SIZE), jnp.float32)]
+    out_shape += [shape(o.shape, jnp.float32) for o in others]
     return pl.pallas_call(
-        widen_kernel,
-        out_shape=[jax.ShapeDtypeStruct((rows, ranks * w), jnp.float32) for w in widths],
-        in_specs=[VMEM],
-        out_specs=[VMEM] * len(widths),
+        functools.partial(widen_kernel, len(widths)),
+        out_shape=out_shape,
+        in_specs=[VMEM] * (1 + len(weights) + len(others)),
+        out_specs=[VMEM] * len(out_shape),
         compiler_params=kernel_params(32),
-        cost_estimate=expected(3),
-    )(parts)
+        cost_estimate=expected(4),
+    )(parts, *weights, *others)
 
 
 def make_shards(cells):
@@ -1419,11 +1438,12 @@
                 split_columns(gate_weight),
             ]
         )
-        attn_rows, hidden_all, gains, marks, ffn_columns = run(
+        gains, attn_rows, hidden_all, marks, ffn_columns = run(
             [
+                tiles_part(own_gains),
                 columns_part(attn_columns),
                 between(gather_part(hidden_in), 0.22, 0.8),
-                hello_part(RANKS * data_total, own_gains, marks),
+                marks_part(marks),
                 split_part(ffn_gate, ffn_up, data_total),
             ],
             2,
@@ -1433,6 +1453,10 @@
             (attn_rows, lax.ppermute(out_weight, INNER, to_rank), ffn_down)
         )
         w_attn = join_cells(attn_rows)
+        gains = gains.reshape(PLANES, CORNERS**2, CORNERS, -1)
+        gains = jnp.transpose(gains, (1, 0, 2, 3)).reshape(CORNERS**2, PLANES * CORNERS, -1)
+        if cells > 1:
+            gains = lax.all_gather(gains, "cell", axis=1, tiled=False)
         gains = gains.reshape(RANKS * data_total, -1)
         gain_attn, gain_ffn, gain_query, gain_key = (
             gains[:, a:b].reshape(-1) for a, b in zip(cuts[:-1], cuts[1:])
@@ -1468,9 +1492,7 @@
 
         down_term = low(contract_first(mixed_low, cotangent_all))
         down_term, cotangent_all = lax.optimization_barrier((down_term, cotangent_all))
-        grad_down = lax.psum_scatter(down_term, DATA, scatter_dimension=0, tiled=True).astype(
-            jnp.float32
-        )
+        grad_down = lax.psum_scatter(down_term, DATA, scatter_dimension=0, tiled=True)
         d_mixed = contract_last(cotangent_all, w_down)
         d_up_low = low(d_mixed * gate_ffn * ffn_sig)
         d_gate_ffn_low = low(d_mixed * up_ffn * ffn_sig * (1.0 + gate_ffn * (1.0 - ffn_sig)))
@@ -1483,11 +1505,10 @@
 
         branch_all = gather_tokens(low(d_middle))
         branch_all, grad_down = lax.optimization_barrier((branch_all, grad_down))
-        d_query, d_gate, d_pair, query_gain_terms = attend_back(
+        d_partial, d_pair, query_gain_terms, out_term = attend_back(
             branch_all, w_out, query_low, pair, gate_raw, own_marks, marks,
-            attended, log_weight, raw, cosine, sine, gain_query,
+            attended, log_weight, raw, cosine, sine, gain_query, gated_low,
         )
-        out_term = low(contract_first(gated_low, branch_all))
         d_pair, result, grad_both, out_term = run(
             [
                 line_scatter_part(d_pair),
@@ -1501,10 +1522,10 @@
         )
         grad_out = lax.psum_scatter(
             out_term.reshape(-1, out_term.shape[-1]), DATA, scatter_dimension=0, tiled=True
-        ).astype(jnp.float32)
+        )
         output = low(middle + result)
         d_raw, key_gain_terms = finish_attention(
-            d_pair, raw, cosine, sine, gain_key, d_query, d_gate
+            d_pair, raw, cosine, sine, gain_key, d_partial
         )
         grad_query_gain_term = jnp.sum(query_gain_terms[:, 0], axis=0)
         grad_key_gain_term = jnp.sum(key_gain_terms[:, 0], axis=0)
@@ -1514,40 +1535,49 @@
         attn_term, d_raw = lax.optimization_barrier((attn_term, d_raw))
         split = attn_term.reshape(CORNERS**2, cells, PLANES, CORNERS, -1, attn_term.shape[1])
         split = jnp.transpose(split, (2, 1, 0, 3, 4, 5)).reshape(PLANES, -1, attn_term.shape[1])
-        grad_attn, d_normed, grad_gate, grad_up = run(
+        small = jnp.concatenate(
             [
+                t.reshape(RANKS * data_total, -1)
+                for t in (grad_norm_two_term, grad_query_gain_term, grad_key_gain_term)
+            ],
+            axis=-1,
+        )
+        spare = tile[0] * tile[1] - small.shape[1]
+        small = low(jnp.pad(small, ((0, 0), (0, spare))))
+        small = small.reshape((CORNERS**2, cells, PLANES, CORNERS) + tile)
+        small = jnp.transpose(small, (2, 1, 0, 3, 4, 5)).reshape(PLANES, -1, HEAD_SIZE)
+        small, grad_attn, d_normed, grad_gate, grad_up = run(
+            [
+                line_scatter_part(small, pieces=1),
                 line_scatter_part(split, kind=jnp.bfloat16),
                 scatter_part(product=(d_raw, w_attn), transposed=True),
                 join_part(grad_both, data_total),
             ],
             7,
-            56,
+            58,
             60,
         )
         if cells > 1:
             grad_attn = lax.psum_scatter(grad_attn, "cell", scatter_dimension=0, tiled=True)
-        grad_gate, grad_up = grad_gate.astype(jnp.float32), grad_up.astype(jnp.float32)
+            small = lax.psum_scatter(small, "cell", scatter_dimension=0, tiled=True)
         grad_attn = grad_attn.reshape(RANKS, -1, attn_term.shape[1])
-        input_grad, grad_norm_one_term = norm_rows_back(hidden_in, gain_attn, d_normed, d_middle)
-
-        terms = jnp.concatenate(
-            [
-                t.reshape(RANKS * data_total, -1)
-                for t in (
-                    grad_norm_one_term,
-                    grad_norm_two_term,
-                    grad_query_gain_term,
-                    grad_key_gain_term,
-                )
-            ],
-            axis=-1,
+        grad_attn, small = run(
+            [swap_part(grad_attn), swap_part(small.reshape((RANKS,) + tile))], 4, micros=14
         )
-        terms = jnp.pad(terms, ((0, 0), (0, pad))).reshape((-1,) + tile)
-        grad_attn, small = run([swap_part(grad_attn), spread_part(terms)], 4, micros=15)
-        small = small.reshape(-1)
-        grad_query, grad_key, grad_value, grad_gatew = widen_columns(grad_attn, (a, b - a, c - b, a))
-        grad_norm_attn, grad_norm_ffn, grad_query_gain, grad_key_gain = (
-            small[s:e] for s, e in zip(cuts[:-1], cuts[1:])
+        (
+            grad_query, grad_key, grad_value, grad_gatew, along, grad_gate, grad_up, grad_down, grad_out
+        ) = widen_columns(
+            grad_attn,
+            (a, b - a, c - b, a),
+            (query_weight, key_matrix, value_matrix, gate_weight),
+            (grad_gate, grad_up, grad_down, grad_out),
+        )
+        grad_norm_attn = along[:, 0] / norm_attn.astype(jnp.float32)
+        input_grad = norm_rows_back(hidden_in, gain_attn, d_normed, d_middle)[0]
+        small = jnp.sum(small, axis=0).reshape(-1)
+        ends = [size - cuts[1] for size in cuts]
+        grad_norm_ffn, grad_query_gain, grad_key_gain = (
+            small[s:e] for s, e in zip(ends[1:-1], ends[2:])
         )
         return (
             output,

time: 754 us -> 741 us (0.983)
    convert_element_type x4 -> x0, other arithmetic: 7.89 us -> none  [the longest x1 2.45 us: shards(): lax.psum_scatter(down_term, DATA, scatter_dimension=0, tiled=True)]
    dot_general x4 -> x3, matrix products: 43 us -> 37.5 us  [contract_first(): lax.dot_general(left, right, (((0,), (0,)), ((), ())), preferred_element_...]
    unnamed x40 -> x49, local copies, waits for them, and re-layouts: 17.8 us -> 16.5 us
  transfers between devices with their start and end apart: 7 -> 7, of which waited for: 2 -> 2; matrix products, arithmetic and copies ran while one was open for 16% -> 15% of each run, Pallas kernels for 64% -> 65%
where the time goes in v7:
time: 741 us; the launch traced here: 732 us
  Pallas kernels  555 us (75%)
  matrix products  65.3 us (9%)
  local copies, waits for them, and re-layouts  34.9 us (5%)
  waiting for transfers between devices  33.5 us (5%)
  other arithmetic  26.8 us (4%)
  between operations  14.8 us (2%)
    pallas_call x9, Pallas kernels, run(): pl.pallas_call(functools.partial(run_kernel, parts), out_shape=[shape for...  464 us
    pallas_call x1, Pallas kernels, attend_back(): pl.pallas_call(attend_back_kernel, grid=(groups,), out_shape=[shape((toke...  39.5 us
    dot_general x3, matrix products, contract_first(): lax.dot_general(left, right, (((0,), (0,)), ((), ())), preferred_element_...  37.5 us
    all_gather x1, waiting for transfers between devices, shards(): w_down = lax.all_gather(down_rows, DATA, axis=0, tiled=True)  26.9 us
    pallas_call x1, Pallas kernels, attend(): pl.pallas_call(attend_kernel, grid=(groups,), out_shape=[shape((tokens, w...  17.3 us
    unnamed x49, local copies, waits for them, and re-layouts  16.5 us
    pallas_call x1, Pallas kernels, prepare_attention(): pl.pallas_call(prepare_kernel, grid=(RANKS,), out_shape=[shape((tokens, w...  16 us
  transfers between devices with their start and end apart: 7, of which 2 were waited for; matrix products, arithmetic and copies ran while one was open for 15% of the time, Pallas kernels for 65%

profile of v7, /device:TPU:0, one launch (start us, length us, event | category | flops | bytes accessed | tf_op | source)
XLA Modules:
  0.0 732.3 jit_solution(6398936004225664302)
XLA Ops:
  7.2 1.6 collective-permute-start
  8.8 1.0 copy_bitcast_fusion.2
  9.9 1.1 copy_bitcast_fusion
  10.9 1.4 fusion.15.refs_0_
  12.3 1.3 pad_add_fusion.refs_3_
  14.6 70.3 %shard_map.263 = (f32[4,8,8,128]{3,2,1,0:T(8,128)}, bf16[4,4,2,64,768]{4,3,2,1,0:T(8,128)(2,1)}, bf16[2048,2048]{1,0:T(8,128)(2,1)}, s32[4,32,128]{2,1,0:T(8,128)}, bf16[8,64,1536]{2,1,0:T(8,128)(2,1)}) custom-call(f32[8,128]{1,0:T(8,128)} %fusion.15.refs_0_, bf16[8,64,768]{2,1,0:T(8,128)(2,1)} %maximum_bitcast_fusion.refs_1_, bf16[256,2048]{1,0:T(8,128)(2,1)} %x_ref.1, ...), custom_call_target="tpu_custom_call" | custom-call | bytes 245000000 | tf_op jit(solution)/shard_map/pallas_call | solution.py:146
  84.9 1.0 reshape.135
  89.8 3.7 fusion
  93.5 1.3 pad_maximum_fusion.1.cos_ref
  94.9 1.3 pad_maximum_fusion.2.sin_ref
  96.2 16.0 %shard_map.264 = (bf16[2048,2048]{1,0:T(8,128)(2,1)}, bf16[2048,256]{1,0:T(8,128)(2,1)}, bf16[2048,256]{1,0:T(8,128)(2,1)}, f32[2048,384]{1,0:T(8,128)}, f32[2048,256]{1,0:T(8,128)}) custom-call(bf16[2048,2048]{1,0:T(8,128)(2,1)} %get-tuple-element.71.x_ref, f32[1,2048]{1,0:T(1,128)} %broadcast_in_dim_reshape.16.gain_ref, bf16[2048,768]{1,0:T(8,128)(2,1)} %bitcast.73, ...), custom_call_target="tpu_custom_call" | custom-call | bytes 42000000 | tf_op jit(solution)/shard_map/pallas_call | solution.py:1017
  112.2 73.2 %shard_map.265 = (bf16[4,2048,256]{2,1,0:T(8,128)(2,1)}, bf16[2048,2048]{1,0:T(8,128)(2,1)}, bf16[8,64,1536]{2,1,0:T(8,128)(2,1)}) custom-call(bf16[2048,256]{1,0:T(8,128)(2,1)} %get-tuple-element.77.refs_0_, bf16[256,2048]{1,0:T(8,128)(2,1)} %more_ref.1, bf16[8,64,1536]{2,1,0:T(8,128)(2,1)} %get-tuple-element.78.refs_2_), custom_call_target="tpu_custom_call" | custom-call | bytes 262500000 | tf_op jit(solution)/shard_map/pallas_call | solution.py:146
  186.5 1.2 copy-done.3
  187.7 17.3 %shard_map.266 = (bf16[2048,2048]{1,0:T(8,128)(2,1)}, f32[2048,256]{1,0:T(8,128)}, f32[2048,256]{1,0:T(8,128)}, bf16[2048,256]{1,0:T(8,128)(2,1)S(1)}) custom-call(bf16[2048,256]{1,0:T(8,128)(2,1)S(1)} %copy-done.4, bf16[4,2048,256]{2,1,0:T(8,128)(2,1)} %get-tuple-element.79.kv_ref, f32[2048,256]{1,0:T(8,128)} %get-tuple-element.80.gate_ref, ...), custom_call_target="tpu_custom_call" | custom-call | bytes 63000000 | tf_op jit(solution)/shard_map/pallas_call | solution.py:1096
  205.0 1.0 copy-done.7
  206.0 3.4 copy-done.2
  209.4 39.5 %shard_map.267 = f32[256,2048]{1,0:T(8,128)S(1)} custom-call(bf16[8,256,2048]{2,1,0:T(8,128)(2,1)S(1)} %bitcast.66), custom_call_target="tpu_custom_call" | custom-call | bytes 140000000 | tf_op jit(solution)/shard_map/pallas_call | solution.py:146
  249.4 1.3 copy-done.16
  250.7 1.2 multiply_convert_fusion.3.refs_0_
  251.9 40.1 %shard_map.268 = bf16[2048,2048]{1,0:T(8,128)(2,1)} custom-call(bf16[256,2048]{1,0:T(8,128)(2,1)} %multiply_convert_fusion.3.refs_0_), custom_call_target="tpu_custom_call" | custom-call | bytes 140000000 | tf_op jit(solution)/shard_map/pallas_call | solution.py:146
  292.0 6.2 all-gather.9.cloned.1.call-done
  298.2 3.6 copy.62
  301.9 3.0 copy-done.21
  304.8 13.7 %fusion.19 = f32[2048,1536]{1,0:T(8,128)S(1)} fusion(bf16[2048,2048]{1,0:T(8,128)(2,1)S(1)} %copy-done.21, bf16[2048,1536]{1,0:T(8,128)(2,1)S(1)} %bitcast.70), kind=kOutput, calls=%fused_computation.51 | convolution fusion | flops 12884901888 | bytes 27262976 | tf_op jit(solution)/shard_map/dot_general | solution.py:928
  318.5 2.1 multiply_convert_fusion.2.refs_1_
  320.6 2.4 copy-done.18
  323.0 11.5 %convolution_convert_fusion.1 = bf16[768,2048]{1,0:T(8,128)(2,1)} fusion(bf16[2048,768]{1,0:T(8,128)(2,1)S(1)} %multiply_convert_fusion.2.refs_1_, bf16[2048,2048]{1,0:T(8,128)(2,1)} %get-tuple-element.85), kind=kOutput, calls=%fused_computation.6 | convolution fusion | flops 6444023808 | bytes 14680064 | tf_op jit(solution)/shard_map/dot_general | solution.py:938
  334.6 26.9 %all-gather.7.cloned.1.call-done.refs_2_ = bf16[768,2048]{1,0:T(8,128)(2,1)} async-done(((bf16[192,2048]{1,0:T(8,128)(2,1)}), bf16[768,2048]{1,0:T(8,128)(2,1)}) %all-gather.7.cloned.1.call-update) | async-done | bytes 3145744 | tf_op jit(solution)/shard_map/all_gather | solution.py:1465
  361.6 14.2 %multiply_convert_fusion.1 = (bf16[2048,768]{1,0:T(8,128)(2,1)S(1)}, bf16[2048,768]{1,0:T(8,128)(2,1)S(1)}) fusion(f32[2048,1536]{1,0:T(8,128)} %copy-done.18, bf16[2048,2048]{1,0:T(8,128)(2,1)} %get-tuple-element.85, bf16[768,2048]{1,0:T(8,128)(2,1)} %all-gather.7.cloned.1.call-done.refs_2_), kind=kOutput, calls=%fused_computation.3 | convolution fusion | flops 6462898176 | bytes 30408704 | tf_op jit(solution)/shard_map/dot_general | solution.py:932
  375.8 3.1 pad_maximum_fusion.refs_0_
  378.9 15.5 %convolution_convert_fusion = bf16[2048,1536]{1,0:T(8,128)(2,1)S(1)} fusion(bf16[2048,2048]{1,0:T(8,128)(2,1)} %shard_map.268, bf16[2048,768]{1,0:T(8,128)(2,1)S(1)} %get-tuple-element.131, bf16[2048,768]{1,0:T(8,128)(2,1)S(1)} %get-tuple-element.130), kind=kOutput, calls=%fused_computation | convolution fusion | flops 12900630528 | bytes 20971520 | tf_op jit(solution)/shard_map/dot_general | solution.py:938
  394.4 3.4 copy.68
  398.6 47.7 %shard_map.269.grads_ref = f32[256,2048]{1,0:T(8,128)S(1)} custom-call(bf16[2048,1536]{1,0:T(8,128)(2,1)} %pad_maximum_fusion.refs_0_, bf16[2048,1536]{1,0:T(8,128)(2,1)} %bitcast.71), custom_call_target="tpu_custom_call" | custom-call | bytes 157500000 | tf_op jit(solution)/shard_map/pallas_call | solution.py:146
  446.3 1.4 copy-done.1
  447.6 4.9 shard_map.270
  453.4 2.7 convert_element_type.66.refs_0_
  456.2 39.5 %shard_map.271.branch_ref = bf16[2048,2048]{1,0:T(8,128)(2,1)} custom-call(bf16[256,2048]{1,0:T(8,128)(2,1)} %convert_element_type.66.refs_0_), custom_call_target="tpu_custom_call" | custom-call | bytes 140000000 | tf_op jit(solution)/shard_map/pallas_call | solution.py:146
  495.7 39.5 %shard_map.272 = (bf16[2048,768]{1,0:T(8,128)(2,1)}, bf16[4,2048,256]{2,1,0:T(8,128)(2,1)}, f32[4,8,128]{2,1,0:T(8,128)}, bf16[256,2048]{1,0:T(8,128)(2,1)}) custom-call(bf16[2048,2048]{1,0:T(8,128)(2,1)} %shard_map.271.branch_ref, bf16[256,2048]{1,0:T(8,128)(2,1)} %all-gather.5.cloned.1.call-done.wo_ref, bf16[2048,256]{1,0:T(8,128)(2,1)} %get-tuple-element.76.q_ref, ...), custom_call_target="tpu_custom_call" | custom-call | bytes 122500000 | tf_op jit(solution)/shard_map/pallas_call | solution.py:1180
  536.2 78.1 %shard_map.273 = (f32[2048,256]{1,0:T(8,128)}, f32[256,2048]{1,0:T(8,128)}, bf16[8,64,1536]{2,1,0:T(8,128)(2,1)}, bf16[4,64,2048]{2,1,0:T(8,128)(2,1)}) custom-call(bf16[4,2048,256]{2,1,0:T(8,128)(2,1)} %get-tuple-element.95.refs_0_, bf16[2048,768]{1,0:T(8,128)(2,1)} %copy-done.19, bf16[768,2048]{1,0:T(8,128)(2,1)} %all-gather.7.cloned.1.call-done.refs_2_, ...), custom_call_target="tpu_custom_call" | custom-call | bytes 262500000 | tf_op jit(solution)/shard_map/pallas_call | solution.py:146
  614.3 4.8 shard_map.274
  619.1 10.4 %convolution_convert_fusion.2 = bf16[2048,768]{1,0:T(8,128)(2,1)S(1)} fusion(bf16[2048,2048]{1,0:T(8,128)(2,1)} %get-tuple-element.104, bf16[2048,768]{1,0:T(8,128)(2,1)} %get-tuple-element.107.refs_2_), kind=kOutput, calls=%fused_computation.7 | convolution fusion | flops 6444023808 | bytes 14680064 | tf_op jit(solution)/shard_map/dot_general | solution.py:938
  629.5 2.0 copy.70
  633.1 61.7 %shard_map.275 = (f32[64,128]{1,0:T(8,128)}, bf16[512,768]{1,0:T(8,128)(2,1)}, f32[256,2048]{1,0:T(8,128)}, bf16[64,6144]{1,0:T(8,128)(2,1)}, bf16[64,6144]{1,0:T(8,128)(2,1)}) custom-call(bf16[4,64,128]{2,1,0:T(8,128)(2,1)} %bitcast.81, bf16[4,512,768]{2,1,0:T(8,128)(2,1)} %bitcast.72, bf16[2048,768]{1,0:T(8,128)(2,1)} %get-tuple-element.107.refs_2_, ...), custom_call_target="tpu_custom_call" | custom-call | bytes 210000000 | tf_op jit(solution)/shard_map/pallas_call | solution.py:146
  694.9 5.0 shard_map.276
  699.9 14.2 %shard_map.277 = (bf16[8,64,768]{2,1,0:T(8,128)(2,1)}, f32[8,8,128]{2,1,0:T(8,128)}) custom-call(bf16[8,64,768]{2,1,0:T(8,128)(2,1)} %bitcast.79, f32[8,8,128]{2,1,0:T(8,128)} %bitcast.84), custom_call_target="tpu_custom_call" | custom-call | bytes 49000000 | tf_op jit(solution)/shard_map/pallas_call | solution.py:146
  716.0 3.5 add_convert_fusion
  719.5 1.1 copy-done.11
  721.6 3.0 shard_map.278
  (88 shorter events, 14.0 us)
Async XLA Ops:
  7.2 179.3 %all-gather.5.cloned.1.call-start = ((), (), s32[]{:S(2)}) async-start(), calls=%async_computation.3 | async-start | bytes 1310720 | tf_op jit(solution)/shard_map/all_gather | solution.py:1464
  7.2 78.8 %collective-permute-start = (bf16[64,2048]{1,0:T(8,128)(2,1)}, bf16[64,2048]{1,0:T(8,128)(2,1)S(1)}, u32[]{:S(2)}, u32[]{:S(2)}) collective-permute-start(bf16[64,2048]{1,0:T(8,128)(2,1)} %param.21), channel_id=1, source_target_pairs={{0,0},{1,2},{2,4},{3,6},{4,1},{5,3},{6,5},{7,7},{8,8},{9,10},{10,1... | collective-permute-start | bytes 786440 | tf_op jit(solution)/shard_map/ppermute | solution.py:1453
  86.0 0.7 copy-start.22
  86.7 211.5 %all-gather.9.cloned.1.call-start = ((), (), s32[]{:S(2)}) async-start(), calls=%async_computation.8 | async-start | bytes 7864320 | tf_op jit(solution)/shard_map/all_gather | solution.py:1377
  87.7 98.8 %copy-start.12 = (s32[4,2,2048]{2,1,0:T(2,128)}, s32[4,2,2048]{2,1,0:T(2,128)S(1)}, u32[]{:S(2)}) copy-start(s32[4,2,2048]{2,1,0:T(2,128)S(1)} %reshape.137.keys_ref) | copy-start | bytes 196612
  112.2 74.3 %copy-start.4 = (bf16[2048,256]{1,0:T(8,128)(2,1)S(1)}, bf16[2048,256]{1,0:T(8,128)(2,1)}, u32[]{:S(2)}) copy-start(bf16[2048,256]{1,0:T(8,128)(2,1)} %get-tuple-element.76.q_ref) | copy-start | bytes 3145732
  185.5 176.1 %all-gather.7.cloned.1.call-start = ((), (), s32[]{:S(2)}) async-start(), calls=%async_computation.4 | async-start | bytes 3932160 | tf_op jit(solution)/shard_map/all_gather | solution.py:1465
  186.0 63.0 %copy-start = (s32[4,512,2]{2,1,0:T(8,128)}, s32[4,512,2]{2,1,0:T(8,128)S(1)}, u32[]{:S(2)}) copy-start(s32[4,512,2]{2,1,0:T(8,128)S(1)} %copy.61.own_ref) | copy-start | bytes 49156
  186.2 309.5 %reduce-scatter.4.cloned.1.call-start = ((), (), s32[]{:S(2)}) async-start(), calls=%async_computation.5 | async-start | bytes 3932160 | tf_op jit(solution)/shard_map/reduce_scatter | solution.py:1495
  186.5 1.2 copy-start.3
  187.7 61.3 %copy-start.20 = (bf16[256,2048]{1,0:T(8,128)(2,1)S(1)}, bf16[256,2048]{1,0:T(8,128)(2,1)}, u32[]{:S(2)}) copy-start(bf16[256,2048]{1,0:T(8,128)(2,1)} %x_ref.1) | copy-start | bytes 3145732
  205.0 1.0 copy-start.7
  206.0 3.4 copy-start.2
  249.4 1.3 copy-start.16
  298.2 6.6 copy-start.21
  301.9 16.7 %copy-start.17 = (bf16[4,4,2,64,1536]{4,3,2,0,1:T(8,128)(2,1)}, bf16[4,4,2,64,1536]{4,3,2,0,1:T(8,128)(2,1)S(1)}, u32[]{:S(2)}) copy-start(bf16[4,4,2,64,1536]{4,3,2,0,1:T(8,128)(2,1)S(1)} %copy.62) | copy-start | bytes 18874372
  318.5 4.5 copy-start.18
  323.0 11.5 %copy-start.19 = (bf16[2048,768]{1,0:T(8,128)(2,1)}, bf16[2048,768]{1,0:T(8,128)(2,1)S(1)}, u32[]{:S(2)}) copy-start(bf16[2048,768]{1,0:T(8,128)(2,1)S(1)} %multiply_convert_fusion.2.refs_1_) | copy-start | bytes 9437188
  334.6 201.6 %reduce-scatter.6.cloned.1.call-start = ((), (), s32[]{:S(2)}) async-start(), calls=%async_computation.6 | async-start | bytes 7864320 | tf_op jit(solution)/shard_map/reduce_scatter | solution.py:1385
  397.8 321.6 %reduce-scatter.8.cloned.1.call-start = ((), (), s32[]{:S(2)}) async-start(), calls=%async_computation.7 | async-start | bytes 1310720 | tf_op jit(solution)/shard_map/reduce_scatter | solution.py:1523
  446.3 1.4 copy-start.1
  694.8 24.6 %copy-start.5 = (bf16[64,2048]{1,0:T(8,128)(2,1)S(1)}, bf16[64,2048]{1,0:T(8,128)(2,1)}, u32[]{:S(2)}) copy-start(bf16[64,2048]{1,0:T(8,128)(2,1)} %refs_3_.1) | copy-start | bytes 786436
  694.8 24.6 %copy-start.6 = (bf16[64,2048]{1,0:T(8,128)(2,1)S(1)}, bf16[64,2048]{1,0:T(8,128)(2,1)}, u32[]{:S(2)}) copy-start(bf16[64,2048]{1,0:T(8,128)(2,1)} %refs_0_.1) | copy-start | bytes 786436
  694.9 24.6 %copy-start.8 = (bf16[192,2048]{1,0:T(8,128)(2,1)S(1)}, bf16[192,2048]{1,0:T(8,128)(2,1)}, u32[]{:S(2)}) copy-start(bf16[192,2048]{1,0:T(8,128)(2,1)} %reduce-scatter.4.cloned.1.call-done.refs_6_) | copy-start | bytes 2359300
  694.9 24.6 %copy-start.9 = (bf16[64,6144]{1,0:T(8,128)(2,1)S(1)}, bf16[64,6144]{1,0:T(8,128)(2,1)}, u32[]{:S(2)}) copy-start(bf16[64,6144]{1,0:T(8,128)(2,1)} %get-tuple-element.114.refs_4_) | copy-start | bytes 2359300
  694.9 24.6 %copy-start.10 = (bf16[64,6144]{1,0:T(8,128)(2,1)S(1)}, bf16[64,6144]{1,0:T(8,128)(2,1)}, u32[]{:S(2)}) copy-start(bf16[64,6144]{1,0:T(8,128)(2,1)} %get-tuple-element.115.refs_5_) | copy-start | bytes 2359300
  694.9 24.6 %copy-start.13 = (bf16[64,1024]{1,0:T(8,128)(2,1)S(1)}, bf16[64,1024]{1,0:T(8,128)(2,1)}, u32[]{:S(2)}) copy-start(bf16[64,1024]{1,0:T(8,128)(2,1)} %refs_1_.3) | copy-start | bytes 393220
  694.9 24.6 %copy-start.14 = (bf16[64,1024]{1,0:T(8,128)(2,1)S(1)}, bf16[64,1024]{1,0:T(8,128)(2,1)}, u32[]{:S(2)}) copy-start(bf16[64,1024]{1,0:T(8,128)(2,1)} %refs_2_.3) | copy-start | bytes 393220
  699.9 24.8 %copy-start.23 = (bf16[64]{0:T(256)(128)(2,1)S(1)}, bf16[64]{0:T(256)(128)(2,1)}, u32[]{:S(2)}) copy-start(bf16[64]{0:T(256)(128)(2,1)} %param.22) | copy-start | bytes 388
  719.5 1.1 copy-start.11
  720.7 0.9 copy-start.15
Sparse Core Ops, SparseCore 0:
  86.8 25.5 all-gather.4
  185.6 112.5 all-gather.8
  299.8 61.7 all-gather.6
  363.7 58.8 reduce-scatter.3
  424.8 110.7 reduce-scatter.5
  614.4 27.7 reduce-scatter.7

commit v8 on v7

--- a/solution.py
+++ b/solution.py
@@ -266,7 +266,7 @@
     lax.fori_loop(0, count // step, body, 0)
 
 
-def scatter_part(terms=None, product=None, transposed=False, tile=512):
+def scatter_part(terms=None, product=None, transposed=False, tile=512, more=None):
     if product is None:
         ranks, rows, columns = terms.shape
     else:
@@ -278,6 +278,8 @@
 
     def steps(ins, outs, scratch):
         (out_ref,) = outs
+        extra = [] if more is None else [(ins[-1], 0)]
+        ins = ins if more is None else ins[:-1]
         if product is None:
             (part_ref,) = ins
         else:
@@ -372,7 +374,7 @@
         def own(k):
             landed(x_buf.at[piece(k), :], recv_x.at[k], dev_x)
             landed(y_buf.at[piece(k), :], recv_y.at[k], dev_y)
-            chip(out_ref, O, k, (x_buf, 0), (y_buf, 0))
+            chip(out_ref, O, k, (x_buf, 0), (y_buf, 0), *extra)
 
         def last():
             for copy in sent:
@@ -399,8 +401,9 @@
     core = DMA((4 * n,))
     made = [] if product is None else [low_vmem(RANKS, rows, columns)]
     return Part(
-        [(terms, VMEM)] if product is None else [(left, VMEM), (right, VMEM)],
-        [(jax.ShapeDtypeStruct((rows, columns), jnp.float32), VMEM)],
+        ([(terms, VMEM)] if product is None else [(left, VMEM), (right, VMEM)])
+        + ([] if more is None else [(more, VMEM)]),
+        [(jax.ShapeDtypeStruct((rows, columns), jnp.float32 if more is None else jnp.bfloat16), VMEM)],
         [low_vmem(4, rows, columns), whole, whole, part, part, whole, whole, whole]
         + [core, core, link, link, link, link]
         + made,
@@ -681,11 +684,14 @@
     )
 
 
-def columns_part(blocks):
-    ranks, rows, columns = blocks.shape
+def columns_part(weights):
+    rows = weights[0].shape[0]
+    widths = [w.shape[1] // RANKS for w in weights]
+    ends = [sum(widths[: n + 1]) for n in range(len(widths))]
+    many = len(weights)
 
     def steps(ins, outs, scratch):
-        (in_ref,), (out_ref,) = ins, outs
+        (out_ref,) = outs
         send, recv, up_send, up_recv, down_send, down_recv, local = scratch
         x, c, y = corner()
         z = lax.axis_index("z")
@@ -697,7 +703,13 @@
         def at(i, plane):
             return out_ref.at[spots[i][0], plane, spots[i][1]]
 
-        keep = pltpu.make_async_copy(in_ref.at[own], at(0, z), local)
+        def cut(n, index):
+            return ins[n].at[:, pl.ds(pl.multiple_of(index * widths[n], widths[n]), widths[n])]
+
+        def place(i, n):
+            return at(i, z).at[:, pl.ds(ends[n] - widths[n], widths[n])]
+
+        keeps = [pltpu.make_async_copy(cut(n, own), place(0, n), local.at[n]) for n in range(many)]
         sent = []
 
         def up(t, i, source=None):
@@ -720,15 +732,21 @@
                 down(0, i, source).start()
 
         def first():
-            keep.start()
+            for keep in keeps:
+                keep.start()
             for i, (there, other) in enumerate(peers):
-                copy = remote(in_ref.at[other], at(0, z), send.at[i], recv.at[i], there)
-                copy.start()
-                sent.append(copy)
-            begin(0, in_ref.at[own])
+                for n in range(many):
+                    m = i * many + n
+                    copy = remote(cut(n, other), place(0, n), send.at[m], recv.at[m], there)
+                    copy.start()
+                    sent.append(copy)
+            for keep in keeps:
+                keep.wait()
+            begin(0)
 
         def swapped(i):
-            landed(at(i, z), recv.at[i - 1], peers[i - 1][0])
+            for n in range(many):
+                landed(place(i, n), recv.at[(i - 1) * many + n], peers[i - 1][0])
             begin(i)
 
         def arrive(t, i):
@@ -767,21 +785,19 @@
                     def _():
                         down(t, i).wait_send()
 
-            keep.wait()
-
         middle = [functools.partial(swapped, i) for i in range(1, RANKS)]
         middle += [
             functools.partial(arrive, t, i) for t in range(PLANES - 1) for i in range(RANKS)
         ]
         return first, middle, last
 
-    n = len(OTHERS)
+    n = len(OTHERS) * many
     sems = DMA(((PLANES - 1) * RANKS,))
-    shape = (CORNERS**2, PLANES, CORNERS, rows, columns)
+    shape = (CORNERS**2, PLANES, CORNERS, rows, ends[-1])
     return Part(
-        [(blocks, VMEM)],
-        [(jax.ShapeDtypeStruct(shape, blocks.dtype), ANYWHERE)],
-        [DMA((n,)), DMA((n,)), sems, sems, sems, sems, DMA(())],
+        [(w, VMEM) for w in weights],
+        [(jax.ShapeDtypeStruct(shape, weights[0].dtype), ANYWHERE)],
+        [DMA((n,)), DMA((n,)), sems, sems, sems, sems, DMA((many,))],
         steps,
         plane="all",
         line=True,
@@ -996,6 +1012,13 @@
     gate_ref[...] = raw[:, (REPEAT + 2) * HEAD_SIZE :]
 
 
+def table_specs(rows):
+    return [
+        pl.BlockSpec((rows, HEAD_SIZE), lambda i: (i, 0)),
+        pl.BlockSpec((rows, HEAD_SIZE), lambda i: (i, 1)),
+    ]
+
+
 def rows_spec(rows, columns):
     return pl.BlockSpec((rows, columns), lambda i: (i, 0))
 
@@ -1008,7 +1031,7 @@
     return pltpu.CompilerParams(vmem_limit_bytes=vmem << 20)
 
 
-def prepare_attention(hidden, gain_attn, w_attn, cosine, sine, gain_query, gain_key):
+def prepare_attention(hidden, gain_attn, w_attn, table, gain_query, gain_key):
     tokens, width = hidden.shape
     columns = w_attn.shape[1]
     q_columns = REPEAT * HEAD_SIZE
@@ -1028,8 +1051,7 @@
             rows_spec(rows, width),
             fixed_spec(1, width),
             fixed_spec(width, columns),
-            rows_spec(rows, HEAD_SIZE),
-            rows_spec(rows, HEAD_SIZE),
+            *table_specs(rows),
             fixed_spec(1, HEAD_SIZE),
             fixed_spec(1, HEAD_SIZE),
         ],
@@ -1042,7 +1064,7 @@
         ],
         compiler_params=kernel_params(60),
         cost_estimate=expected(12),
-    )(hidden, gain_attn[None], w_attn, cosine, sine, gain_query[None], gain_key[None])
+    )(hidden, gain_attn[None], w_attn, table, table, gain_query[None], gain_key[None])
 
 
 EXPONENT = math.log2(math.e) / math.sqrt(HEAD_SIZE)
@@ -1167,7 +1189,7 @@
 
 
 def attend_back(
-    branch, w_out, query, pair, gate, own, keys, attended, log, raw, cosine, sine, gain, gated
+    branch, w_out, query, pair, gate, own, keys, attended, log, raw, table, gain, gated
 ):
     tokens, q_columns = query.shape
     groups = own.shape[0]
@@ -1176,7 +1198,6 @@
     kv, mine, marks = group_specs(window)
     shape = jax.ShapeDtypeStruct
     columns = rows_spec(window, q_columns)
-    table = rows_spec(window, HEAD_SIZE)
     return pl.pallas_call(
         attend_back_kernel,
         grid=(groups,),
@@ -1188,7 +1209,7 @@
         ],
         in_specs=[
             rows_spec(window, width), fixed_spec(q_columns, width), columns, kv, columns, mine, marks,
-            columns, columns, rows_spec(window, raw.shape[1]), table, table, fixed_spec(1, HEAD_SIZE), columns,
+            columns, columns, rows_spec(window, raw.shape[1]), *table_specs(window), fixed_spec(1, HEAD_SIZE), columns,
         ],
         out_specs=[
             rows_spec(window, 2 * q_columns + 2 * HEAD_SIZE), kv, pl.BlockSpec((1, 8, HEAD_SIZE), lambda i: (i, 0, 0)),
@@ -1197,7 +1218,7 @@
         scratch_shapes=[pltpu.VMEM((q_columns, width), jnp.float32)],
         compiler_params=kernel_params(56),
         cost_estimate=expected(35),
-    )(branch, w_out, query, pair, gate, own, keys, attended, log, raw, cosine, sine, gain[None], gated)
+    )(branch, w_out, query, pair, gate, own, keys, attended, log, raw, table, table, gain[None], gated)
 
 
 def finish_kernel(dkv_ref, raw_ref, cos_ref, sin_ref, kg_ref, partial_ref, out_ref, gain_ref):
@@ -1208,10 +1229,9 @@
     gain_ref[0] = jnp.broadcast_to(jnp.sum(by_row, axis=0, keepdims=True), gain_ref.shape[1:])
 
 
-def finish_attention(d_pair, raw, cosine, sine, gain, partial, steps=4):
+def finish_attention(d_pair, raw, table, gain, partial, steps=4):
     tokens = d_pair.shape[0]
     rows = tokens // steps
-    table = rows_spec(rows, HEAD_SIZE)
     shape = jax.ShapeDtypeStruct
     return pl.pallas_call(
         finish_kernel,
@@ -1220,8 +1240,7 @@
         in_specs=[
             rows_spec(rows, 2 * HEAD_SIZE),
             pl.BlockSpec((rows, HEAD_SIZE), lambda i: (i, REPEAT)),
-            table,
-            table,
+            *table_specs(rows),
             fixed_spec(1, HEAD_SIZE),
             ANYWHERE,
         ],
@@ -1232,7 +1251,7 @@
         input_output_aliases={5: 0},
         compiler_params=kernel_params(60),
         cost_estimate=expected(4),
-    )(d_pair, raw, cosine, sine, gain[None], partial)
+    )(d_pair, raw, table, table, gain[None], partial)
 
 
 def split_part(gate, up, pieces):
@@ -1311,11 +1330,11 @@
     return d_values, jnp.sum(term, axis=0)
 
 
-def widen_kernel(count, in_ref, *refs):
+def widen_kernel(count, in_ref, small_ref, *refs):
     weights, refs = refs[:count], refs[count:]
-    others = (len(refs) - count - 1) // 2
+    others = (len(refs) - count - 2) // 2
     low_refs, refs = refs[:others], refs[others:]
-    out_refs, along_ref, wide_refs = refs[:count], refs[count], refs[count + 1 :]
+    out_refs, along_ref, total_ref, wide_refs = refs[:count], refs[count], refs[count + 1], refs[count + 2 :]
     along = jnp.zeros(along_ref.shape, jnp.float32)
     for rank in range(RANKS):
         start = 0
@@ -1328,24 +1347,25 @@
             along += sum(product[:, head(h)] for h in range(width // HEAD_SIZE))
             start += width
     along_ref[...] = jnp.broadcast_to(jnp.sum(along, axis=1, keepdims=True), along_ref.shape)
+    total_ref[...] = jnp.sum(small_ref[...], axis=0)
     for ref, wide in zip(low_refs, wide_refs):
-        wide[...] = ref[...].astype(jnp.float32)
-
-
-def widen_columns(parts, widths, weights, others):
+        wide[...] = ref[...].astype(wide.dtype)
+
+
+def widen_columns(parts, small, widths, weights, others):
     ranks, rows, columns = parts.shape
     shape = jax.ShapeDtypeStruct
     out_shape = [shape((rows, ranks * w), jnp.float32) for w in widths]
-    out_shape += [shape((rows, HEAD_SIZE), jnp.float32)]
-    out_shape += [shape(o.shape, jnp.float32) for o in others]
+    out_shape += [shape((rows, HEAD_SIZE), jnp.float32), shape(small.shape[1:], jnp.float32)]
+    out_shape += [shape(o.shape, kind) for o, kind in others]
     return pl.pallas_call(
         functools.partial(widen_kernel, len(widths)),
         out_shape=out_shape,
-        in_specs=[VMEM] * (1 + len(weights) + len(others)),
+        in_specs=[VMEM] * (2 + len(weights) + len(others)),
         out_specs=[VMEM] * len(out_shape),
         compiler_params=kernel_params(32),
         cost_estimate=expected(4),
-    )(parts, *weights, *others)
+    )(parts, small, *weights, *[o for o, _ in others])
 
 
 def make_shards(cells):
@@ -1359,12 +1379,6 @@
 
     def scatter_tokens(terms):
         return run([scatter_part(blocks(terms))], 1, 40)[0]
-
-    def split_columns(weight):
-        return weight.reshape(weight.shape[0], RANKS, -1)
-
-    def send_columns(pieces):
-        return jnp.transpose(jnp.concatenate(pieces, axis=-1), (1, 0, 2))
 
     def join_cells(rows):
         if cells > 1:
@@ -1424,26 +1438,21 @@
         own_gains = jnp.pad(own_gains, (0, pad)).reshape(tile)
         plane = lax.axis_index("z")
         group_start = lax.axis_index("cell") * GROUP_TOKENS
-        marks = jnp.concatenate(
-            [
-                lax.dynamic_slice_in_dim(sequence_numbers, group_start, GROUP_TOKENS),
-                lax.dynamic_slice_in_dim(positions, group_start, GROUP_TOKENS),
-            ]
-        ).reshape(-1, HEAD_SIZE)
-        attn_columns = send_columns(
-            [
-                split_columns(query_weight),
-                split_columns(key_matrix),
-                split_columns(value_matrix),
-                split_columns(gate_weight),
-            ]
+        own_start = group_start + (plane * CORNERS + lax.axis_index("y")) * rows
+        own_table = jnp.concatenate(
+            rope_tables(lax.dynamic_slice_in_dim(positions, own_start, rows)), axis=-1
         )
-        gains, attn_rows, hidden_all, marks, ffn_columns = run(
+        marks = [
+            lax.dynamic_slice_in_dim(m, group_start, GROUP_TOKENS).reshape(-1, HEAD_SIZE)
+            for m in (sequence_numbers, positions)
+        ]
+        gains, attn_rows, table, hidden_all, all_seq, all_pos, ffn_columns = run(
             [
                 tiles_part(own_gains),
-                columns_part(attn_columns),
+                columns_part([query_weight, key_matrix, value_matrix, gate_weight]),
+                between(gather_part(own_table), 0.22, 0.7),
                 between(gather_part(hidden_in), 0.22, 0.8),
-                marks_part(marks),
+                *map(marks_part, marks),
                 split_part(ffn_gate, ffn_up, data_total),
             ],
             2,
@@ -1464,14 +1473,13 @@
         w_out = lax.all_gather(out_rows, DATA, axis=0, tiled=True)
         w_down = lax.all_gather(down_rows, DATA, axis=0, tiled=True)
 
-        marks = marks.reshape(groups, 2, GROUP_TOKENS)
+        marks = jnp.stack([m.reshape(groups, GROUP_TOKENS) for m in (all_seq, all_pos)], axis=1)
         own_marks = lax.dynamic_slice_in_dim(marks, plane * window, window, axis=2)
-        cosine, sine = rope_tables(own_marks[:, 1].reshape(tokens))
         own_marks = jnp.transpose(own_marks, (0, 2, 1))
 
         hidden = hidden_in.astype(jnp.float32)
         normed_input, query_low, pair, raw, gate_raw = prepare_attention(
-            hidden_all, gain_attn, w_attn, cosine, sine, gain_query, gain_key
+            hidden_all, gain_attn, w_attn, table, gain_query, gain_key
         )
         pair, cotangent_all, ffn_columns = run(
             [line_gather_part(pair), gather_part(cotangent), swap_part(ffn_columns)], 3, micros=75
@@ -1507,12 +1515,12 @@
         branch_all, grad_down = lax.optimization_barrier((branch_all, grad_down))
         d_partial, d_pair, query_gain_terms, out_term = attend_back(
             branch_all, w_out, query_low, pair, gate_raw, own_marks, marks,
-            attended, log_weight, raw, cosine, sine, gain_query, gated_low,
+            attended, log_weight, raw, table, gain_query, gated_low,
         )
-        d_pair, result, grad_both, out_term = run(
+        d_pair, output, grad_both, out_term = run(
             [
                 line_scatter_part(d_pair),
-                scatter_part(product=(mixed_low, w_down)),
+                scatter_part(product=(mixed_low, w_down), more=middle),
                 swap_part(grad_both),
                 halves_part(out_term, data_total),
             ],
@@ -1523,9 +1531,8 @@
         grad_out = lax.psum_scatter(
             out_term.reshape(-1, out_term.shape[-1]), DATA, scatter_dimension=0, tiled=True
         )
-        output = low(middle + result)
         d_raw, key_gain_terms = finish_attention(
-            d_pair, raw, cosine, sine, gain_key, d_partial
+            d_pair, raw, table, gain_key, d_partial
         )
         grad_query_gain_term = jnp.sum(query_gain_terms[:, 0], axis=0)
         grad_key_gain_term = jnp.sum(key_gain_terms[:, 0], axis=0)
@@ -1564,17 +1571,20 @@
         grad_attn, small = run(
             [swap_part(grad_attn), swap_part(small.reshape((RANKS,) + tile))], 4, micros=14
         )
+        wide = [(g, jnp.float32) for g in (grad_gate, grad_up, grad_down, grad_out)]
         (
-            grad_query, grad_key, grad_value, grad_gatew, along, grad_gate, grad_up, grad_down, grad_out
+            grad_query, grad_key, grad_value, grad_gatew, along, small,
+            grad_gate, grad_up, grad_down, grad_out, output,
         ) = widen_columns(
             grad_attn,
+            small,
             (a, b - a, c - b, a),
             (query_weight, key_matrix, value_matrix, gate_weight),
-            (grad_gate, grad_up, grad_down, grad_out),
+            wide + [(output, output.dtype)],
         )
         grad_norm_attn = along[:, 0] / norm_attn.astype(jnp.float32)
         input_grad = norm_rows_back(hidden_in, gain_attn, d_normed, d_middle)[0]
-        small = jnp.sum(small, axis=0).reshape(-1)
+        small = small.reshape(-1)
         ends = [size - cuts[1] for size in cuts]
         grad_norm_ffn, grad_query_gain, grad_key_gain = (
             small[s:e] for s, e in zip(ends[1:-1], ends[2:])

time: 741 us -> 738 us (level)
  other arithmetic: 26.8 us -> 16.2 us
    unnamed x49 -> x57, local copies, waits for them, and re-layouts: 16.5 us -> 18.6 us
  transfers between devices with their start and end apart: 7 -> 7, of which waited for: 2 -> 2; matrix products, arithmetic and copies ran while one was open for 15% -> 13% of each run, Pallas kernels for 65% -> 66%
where the time goes in v8:
time: 738 us; the launch traced here: 728 us
  Pallas kernels  561 us (76%)
  matrix products  65.1 us (9%)
  waiting for transfers between devices  35.1 us (5%)
  local copies, waits for them, and re-layouts  34 us (5%)
  other arithmetic  16.2 us (2%)
  between operations  14.8 us (2%)
    pallas_call x9, Pallas kernels, run(): pl.pallas_call(functools.partial(run_kernel, parts), out_shape=[shape for...  470 us
    pallas_call x1, Pallas kernels, attend_back(): pl.pallas_call(attend_back_kernel, grid=(groups,), out_shape=[shape((toke...  39.8 us
    dot_general x3, matrix products, contract_first(): lax.dot_general(left, right, (((0,), (0,)), ((), ())), preferred_element_...  37.4 us
    all_gather x1, waiting for transfers between devices, shards(): w_down = lax.all_gather(down_rows, DATA, axis=0, tiled=True)  27.2 us
    unnamed x57, local copies, waits for them, and re-layouts  18.6 us
    pallas_call x1, Pallas kernels, attend(): pl.pallas_call(attend_kernel, grid=(groups,), out_shape=[shape((tokens, w...  17.3 us
    pallas_call x1, Pallas kernels, prepare_attention(): pl.pallas_call(prepare_kernel, grid=(RANKS,), out_shape=[shape((tokens, w...  16.2 us
  transfers between devices with their start and end apart: 7, of which 2 were waited for; matrix products, arithmetic and copies ran while one was open for 13% of the time, Pallas kernels for 66%

profile of v8, /device:TPU:0, one launch (start us, length us, event | category | flops | bytes accessed | tf_op | source)
XLA Modules:
  0.0 728.3 jit_solution(2723084150897365022)
XLA Ops:
  7.2 1.6 collective-permute-start
  8.8 0.8 dynamic-slice_convert_fusion
  10.1 1.4 fusion.17.refs_0_
  11.5 0.9 pad_maximum_fusion.1.refs_5_
  12.4 73.2 %shard_map.263 = (f32[4,8,8,128]{3,2,1,0:T(8,128)}, bf16[4,4,2,64,768]{4,3,2,1,0:T(8,128)(2,1)}, f32[2048,256]{1,0:T(8,128)}, bf16[2048,2048]{1,0:T(8,128)(2,1)}...) custom-call(f32[8,128]{1,0:T(8,128)} %fusion.17.refs_0_, bf16[64,2048]{1,0:T(8,128)(2,1)} %refs_0_.1, ...), custom_call_target="tpu_custom_call" | custom-call | bytes 245000000 | tf_op jit(solution)/shard_map/pallas_call | solution.py:146
  86.4 1.0 reshape.116
  89.6 16.2 %shard_map.264 = (bf16[2048,2048]{1,0:T(8,128)(2,1)}, bf16[2048,256]{1,0:T(8,128)(2,1)}, bf16[2048,256]{1,0:T(8,128)(2,1)}, f32[2048,384]{1,0:T(8,128)}, f32[2048,256]{1,0:T(8,128)}) custom-call(bf16[2048,2048]{1,0:T(8,128)(2,1)} %get-tuple-element.75.x_ref, f32[1,2048]{1,0:T(1,128)} %broadcast_in_dim_reshape.16.gain_ref, bf16[2048,768]{1,0:T(8,128)(2,1)} %bitcast.55, ...), custom_call_target="tpu_custom_call" | custom-call | bytes 42000000 | tf_op jit(solution)/shard_map/pallas_call | solution.py:1040
  105.8 74.3 %shard_map.265 = (bf16[4,2048,256]{2,1,0:T(8,128)(2,1)}, bf16[2048,2048]{1,0:T(8,128)(2,1)}, bf16[8,64,1536]{2,1,0:T(8,128)(2,1)}) custom-call(bf16[2048,256]{1,0:T(8,128)(2,1)} %get-tuple-element.81.refs_0_, bf16[256,2048]{1,0:T(8,128)(2,1)} %more_ref.1, bf16[8,64,1536]{2,1,0:T(8,128)(2,1)} %get-tuple-element.82.refs_2_), custom_call_target="tpu_custom_call" | custom-call | bytes 262500000 | tf_op jit(solution)/shard_map/pallas_call | solution.py:146
  181.0 1.4 copy-done.3
  182.4 17.3 %shard_map.266 = (bf16[2048,2048]{1,0:T(8,128)(2,1)}, f32[2048,256]{1,0:T(8,128)}, f32[2048,256]{1,0:T(8,128)}, bf16[2048,256]{1,0:T(8,128)(2,1)S(1)}) custom-call(bf16[2048,256]{1,0:T(8,128)(2,1)S(1)} %copy-done.4, bf16[4,2048,256]{2,1,0:T(8,128)(2,1)} %get-tuple-element.83.kv_ref, f32[2048,256]{1,0:T(8,128)} %get-tuple-element.84.gate_ref, ...), custom_call_target="tpu_custom_call" | custom-call | bytes 63000000 | tf_op jit(solution)/shard_map/pallas_call | solution.py:1118
  199.8 1.0 copy-done.5
  200.7 3.4 copy-done.2
  204.1 40.3 %shard_map.267 = f32[256,2048]{1,0:T(8,128)S(1)} custom-call(bf16[8,256,2048]{2,1,0:T(8,128)(2,1)S(1)} %bitcast.49), custom_call_target="tpu_custom_call" | custom-call | bytes 140000000 | tf_op jit(solution)/shard_map/pallas_call | solution.py:146
  244.8 1.3 copy-done.18
  246.2 1.2 multiply_convert_fusion.3.refs_0_
  247.4 40.6 %shard_map.268 = bf16[2048,2048]{1,0:T(8,128)(2,1)} custom-call(bf16[256,2048]{1,0:T(8,128)(2,1)} %multiply_convert_fusion.3.refs_0_), custom_call_target="tpu_custom_call" | custom-call | bytes 140000000 | tf_op jit(solution)/shard_map/pallas_call | solution.py:146
  288.0 7.7 %all-gather.9.cloned.1.call-done = bf16[32,64,1536]{2,1,0:T(8,128)(2,1)} async-done(((bf16[8,64,1536]{2,1,0:T(8,128)(2,1)}), bf16[32,64,1536]{2,1,0:T(8,128)(2,1)}) %all-gather.9.cloned.1.call-update) | async-done | bytes 6291472 | tf_op jit(solution)/shard_map/all_gather | solution.py:1391
  295.6 3.6 copy.66
  299.3 3.0 copy-done.23
  302.2 13.4 %fusion.21 = f32[2048,1536]{1,0:T(8,128)S(1)} fusion(bf16[2048,2048]{1,0:T(8,128)(2,1)S(1)} %copy-done.23, bf16[2048,1536]{1,0:T(8,128)(2,1)S(1)} %bitcast.53), kind=kOutput, calls=%fused_computation.47 | convolution fusion | flops 12884901888 | bytes 27262976 | tf_op jit(solution)/shard_map/dot_general | solution.py:944
  315.7 2.1 multiply_convert_fusion.2.refs_1_
  317.8 2.4 copy-done.20
  320.2 11.5 %convolution_convert_fusion.1 = bf16[768,2048]{1,0:T(8,128)(2,1)} fusion(bf16[2048,768]{1,0:T(8,128)(2,1)S(1)} %multiply_convert_fusion.2.refs_1_, bf16[2048,2048]{1,0:T(8,128)(2,1)} %get-tuple-element.91), kind=kOutput, calls=%fused_computation.6 | convolution fusion | flops 6444023808 | bytes 14680064 | tf_op jit(solution)/shard_map/dot_general | solution.py:954
  331.8 27.2 %all-gather.7.cloned.1.call-done.refs_2_ = bf16[768,2048]{1,0:T(8,128)(2,1)} async-done(((bf16[192,2048]{1,0:T(8,128)(2,1)}), bf16[768,2048]{1,0:T(8,128)(2,1)}) %all-gather.7.cloned.1.call-update) | async-done | bytes 3145744 | tf_op jit(solution)/shard_map/all_gather | solution.py:1474
  359.0 14.2 %multiply_convert_fusion.1 = (bf16[2048,768]{1,0:T(8,128)(2,1)S(1)}, bf16[2048,768]{1,0:T(8,128)(2,1)S(1)}) fusion(f32[2048,1536]{1,0:T(8,128)} %copy-done.20, bf16[2048,2048]{1,0:T(8,128)(2,1)} %get-tuple-element.91, bf16[768,2048]{1,0:T(8,128)(2,1)} %all-gather.7.cloned.1.call-done.refs_2_), kind=kOutput, calls=%fused_computation.3 | convolution fusion | flops 6462898176 | bytes 30408704 | tf_op jit(solution)/shard_map/dot_general | solution.py:948
  373.2 3.1 pad_maximum_fusion.refs_0_
  376.3 15.5 %convolution_convert_fusion = bf16[2048,1536]{1,0:T(8,128)(2,1)S(1)} fusion(bf16[2048,2048]{1,0:T(8,128)(2,1)} %shard_map.268, bf16[2048,768]{1,0:T(8,128)(2,1)S(1)} %get-tuple-element.139, bf16[2048,768]{1,0:T(8,128)(2,1)S(1)} %get-tuple-element.138), kind=kOutput, calls=%fused_computation | convolution fusion | flops 12900630528 | bytes 20971520 | tf_op jit(solution)/shard_map/dot_general | solution.py:954
  391.8 3.4 copy.72
  396.0 47.7 %shard_map.269.grads_ref = f32[256,2048]{1,0:T(8,128)S(1)} custom-call(bf16[2048,1536]{1,0:T(8,128)(2,1)} %pad_maximum_fusion.refs_0_, bf16[2048,1536]{1,0:T(8,128)(2,1)} %bitcast.54), custom_call_target="tpu_custom_call" | custom-call | bytes 157500000 | tf_op jit(solution)/shard_map/pallas_call | solution.py:146
  443.7 1.4 copy-done.1
  445.0 4.9 shard_map.270
  450.0 0.9 reduce_sum.37
  450.9 2.7 convert_element_type.55.refs_0_
  453.6 39.5 %shard_map.271.branch_ref = bf16[2048,2048]{1,0:T(8,128)(2,1)} custom-call(bf16[256,2048]{1,0:T(8,128)(2,1)} %convert_element_type.55.refs_0_), custom_call_target="tpu_custom_call" | custom-call | bytes 140000000 | tf_op jit(solution)/shard_map/pallas_call | solution.py:146
  493.2 39.8 %shard_map.272 = (bf16[2048,768]{1,0:T(8,128)(2,1)}, bf16[4,2048,256]{2,1,0:T(8,128)(2,1)}, f32[4,8,128]{2,1,0:T(8,128)}, bf16[256,2048]{1,0:T(8,128)(2,1)}) custom-call(bf16[2048,2048]{1,0:T(8,128)(2,1)} %shard_map.271.branch_ref, bf16[256,2048]{1,0:T(8,128)(2,1)} %all-gather.5.cloned.1.call-done.wo_ref, bf16[2048,256]{1,0:T(8,128)(2,1)} %get-tuple-element.80.q_ref, ...), custom_call_target="tpu_custom_call" | custom-call | bytes 122500000 | tf_op jit(solution)/shard_map/pallas_call | solution.py:1201
  533.0 0.7 slice_reduce_fusion.2
  533.9 78.2 %shard_map.273 = (f32[2048,256]{1,0:T(8,128)}, bf16[256,2048]{1,0:T(8,128)(2,1)}, bf16[8,64,1536]{2,1,0:T(8,128)(2,1)}, bf16[4,64,2048]{2,1,0:T(8,128)(2,1)}) custom-call(bf16[4,2048,256]{2,1,0:T(8,128)(2,1)} %get-tuple-element.103.refs_0_, bf16[2048,768]{1,0:T(8,128)(2,1)} %copy-done.21, bf16[768,2048]{1,0:T(8,128)(2,1)} %all-gather.7.cloned.1.call-done.refs_2_, ...), custom_call_target="tpu_custom_call" | custom-call | bytes 262500000 | tf_op jit(solution)/shard_map/pallas_call | solution.py:146
  612.2 4.8 shard_map.274
  617.0 10.4 %convolution_convert_fusion.2 = bf16[2048,768]{1,0:T(8,128)(2,1)S(1)} fusion(bf16[2048,2048]{1,0:T(8,128)(2,1)} %get-tuple-element.109, bf16[2048,768]{1,0:T(8,128)(2,1)} %get-tuple-element.112.refs_2_), kind=kOutput, calls=%fused_computation.7 | convolution fusion | flops 6444023808 | bytes 14680064 | tf_op jit(solution)/shard_map/dot_general | solution.py:954
  627.4 2.0 copy.74
  631.0 61.9 %shard_map.275 = (f32[64,128]{1,0:T(8,128)}, bf16[512,768]{1,0:T(8,128)(2,1)}, f32[256,2048]{1,0:T(8,128)}, bf16[64,6144]{1,0:T(8,128)(2,1)}, bf16[64,6144]{1,0:T(8,128)(2,1)}) custom-call(bf16[4,64,128]{2,1,0:T(8,128)(2,1)} %bitcast.64, bf16[4,512,768]{2,1,0:T(8,128)(2,1)} %bitcast.57, bf16[2048,768]{1,0:T(8,128)(2,1)} %get-tuple-element.112.refs_2_, ...), custom_call_target="tpu_custom_call" | custom-call | bytes 210000000 | tf_op jit(solution)/shard_map/pallas_call | solution.py:146
  693.0 4.9 shard_map.278
  697.9 14.2 %shard_map.276 = (bf16[8,64,768]{2,1,0:T(8,128)(2,1)}, f32[8,8,128]{2,1,0:T(8,128)}) custom-call(bf16[8,64,768]{2,1,0:T(8,128)(2,1)} %bitcast.62, f32[8,8,128]{2,1,0:T(8,128)} %bitcast.70), custom_call_target="tpu_custom_call" | custom-call | bytes 49000000 | tf_op jit(solution)/shard_map/pallas_call | solution.py:146
  712.2 1.1 copy-done.11
  713.3 1.1 copy-done.12
  714.5 0.9 copy-done.16
  715.4 0.8 copy-done.17
  716.2 3.4 shard_map.277
  (89 shorter events, 9.1 us)
Async XLA Ops:
  7.2 173.8 %all-gather.5.cloned.1.call-start = ((), (), s32[]{:S(2)}) async-start(), calls=%async_computation.3 | async-start | bytes 1310720 | tf_op jit(solution)/shard_map/all_gather | solution.py:1473
  7.2 78.4 %collective-permute-start = (bf16[64,2048]{1,0:T(8,128)(2,1)}, bf16[64,2048]{1,0:T(8,128)(2,1)S(1)}, u32[]{:S(2)}, u32[]{:S(2)}) collective-permute-start(bf16[64,2048]{1,0:T(8,128)(2,1)} %param.21), channel_id=1, source_target_pairs={{0,0},{1,2},{2,4},{3,6},{4,1},{5,3},{6,5},{7,7},{8,8},{9,10},{10,1... | collective-permute-start | bytes 786440 | tf_op jit(solution)/shard_map/ppermute | solution.py:1462
  85.7 0.7 copy-start.24
  86.4 209.3 %all-gather.9.cloned.1.call-start = ((), (), s32[]{:S(2)}) async-start(), calls=%async_computation.8 | async-start | bytes 7864320 | tf_op jit(solution)/shard_map/all_gather | solution.py:1391
  89.6 90.7 %copy-start.25 = (s32[4,16,128]{2,1,0:T(8,128)S(1)}, s32[4,16,128]{2,1,0:T(8,128)}, u32[]{:S(2)}) copy-start(s32[4,16,128]{2,1,0:T(8,128)} %get-tuple-element.85) | copy-start | bytes 98308
  89.6 90.7 %copy-start.26 = (s32[4,16,128]{2,1,0:T(8,128)S(1)}, s32[4,16,128]{2,1,0:T(8,128)}, u32[]{:S(2)}) copy-start(s32[4,16,128]{2,1,0:T(8,128)} %get-tuple-element.86) | copy-start | bytes 98308
  105.8 75.2 %copy-start.4 = (bf16[2048,256]{1,0:T(8,128)(2,1)S(1)}, bf16[2048,256]{1,0:T(8,128)(2,1)}, u32[]{:S(2)}) copy-start(bf16[2048,256]{1,0:T(8,128)(2,1)} %get-tuple-element.80.q_ref) | copy-start | bytes 3145732
  180.2 178.8 %all-gather.7.cloned.1.call-start = ((), (), s32[]{:S(2)}) async-start(), calls=%async_computation.4 | async-start | bytes 3932160 | tf_op jit(solution)/shard_map/all_gather | solution.py:1474
  180.8 63.6 %copy-start = (s32[4,512,2]{2,1,0:T(8,128)}, s32[4,512,2]{2,1,0:T(8,128)S(1)}, u32[]{:S(2)}) copy-start(s32[4,512,2]{2,1,0:T(8,128)S(1)} %copy.65.own_ref) | copy-start | bytes 49156
  180.8 63.6 %copy-start.13 = (s32[4,2,2048]{2,1,0:T(2,128)}, s32[4,2,2048]{2,1,0:T(2,128)S(1)}, u32[]{:S(2)}) copy-start(s32[4,2,2048]{2,1,0:T(2,128)S(1)} %pad_add_fusion.keys_ref) | copy-start | bytes 196612
  180.9 312.3 %reduce-scatter.4.cloned.1.call-start = ((), (), s32[]{:S(2)}) async-start(), calls=%async_computation.5 | async-start | bytes 3932160 | tf_op jit(solution)/shard_map/reduce_scatter | solution.py:1503
  181.0 1.4 copy-start.3
  182.4 62.0 %copy-start.22 = (bf16[256,2048]{1,0:T(8,128)(2,1)S(1)}, bf16[256,2048]{1,0:T(8,128)(2,1)}, u32[]{:S(2)}) copy-start(bf16[256,2048]{1,0:T(8,128)(2,1)} %x_ref.1) | copy-start | bytes 3145732
  199.8 1.0 copy-start.5
  200.7 3.4 copy-start.2
  244.8 1.4 copy-start.18
  295.6 6.6 copy-start.23
  299.3 16.4 %copy-start.19 = (bf16[4,4,2,64,1536]{4,3,2,0,1:T(8,128)(2,1)}, bf16[4,4,2,64,1536]{4,3,2,0,1:T(8,128)(2,1)S(1)}, u32[]{:S(2)}) copy-start(bf16[4,4,2,64,1536]{4,3,2,0,1:T(8,128)(2,1)S(1)} %copy.66) | copy-start | bytes 18874372
  315.7 4.5 copy-start.20
  320.2 11.5 %copy-start.21 = (bf16[2048,768]{1,0:T(8,128)(2,1)}, bf16[2048,768]{1,0:T(8,128)(2,1)S(1)}, u32[]{:S(2)}) copy-start(bf16[2048,768]{1,0:T(8,128)(2,1)S(1)} %multiply_convert_fusion.2.refs_1_) | copy-start | bytes 9437188
  331.7 202.1 %reduce-scatter.6.cloned.1.call-start = ((), (), s32[]{:S(2)}) async-start(), calls=%async_computation.6 | async-start | bytes 7864320 | tf_op jit(solution)/shard_map/reduce_scatter | solution.py:1399
  395.3 316.9 %reduce-scatter.8.cloned.1.call-start = ((), (), s32[]{:S(2)}) async-start(), calls=%async_computation.7 | async-start | bytes 1310720 | tf_op jit(solution)/shard_map/reduce_scatter | solution.py:1531
  443.7 1.4 copy-start.1
  631.0 81.1 %copy-start.6 = (bf16[256,2048]{1,0:T(8,128)(2,1)S(1)}, bf16[256,2048]{1,0:T(8,128)(2,1)}, u32[]{:S(2)}) copy-start(bf16[256,2048]{1,0:T(8,128)(2,1)} %get-tuple-element.122.refs_8_) | copy-start | bytes 3145732
  631.0 81.1 %copy-start.7 = (bf16[64,2048]{1,0:T(8,128)(2,1)S(1)}, bf16[64,2048]{1,0:T(8,128)(2,1)}, u32[]{:S(2)}) copy-start(bf16[64,2048]{1,0:T(8,128)(2,1)} %refs_0_.1) | copy-start | bytes 786436
  631.0 81.1 %copy-start.8 = (bf16[64,2048]{1,0:T(8,128)(2,1)S(1)}, bf16[64,2048]{1,0:T(8,128)(2,1)}, u32[]{:S(2)}) copy-start(bf16[64,2048]{1,0:T(8,128)(2,1)} %refs_3_.3) | copy-start | bytes 786436
  631.0 81.2 %copy-start.9 = (bf16[192,2048]{1,0:T(8,128)(2,1)S(1)}, bf16[192,2048]{1,0:T(8,128)(2,1)}, u32[]{:S(2)}) copy-start(bf16[192,2048]{1,0:T(8,128)(2,1)} %reduce-scatter.4.cloned.1.call-done.refs_6_) | copy-start | bytes 2359300
  631.0 81.2 %copy-start.14 = (bf16[64,1024]{1,0:T(8,128)(2,1)S(1)}, bf16[64,1024]{1,0:T(8,128)(2,1)}, u32[]{:S(2)}) copy-start(bf16[64,1024]{1,0:T(8,128)(2,1)} %refs_1_.5) | copy-start | bytes 393220
  631.0 81.2 %copy-start.15 = (bf16[64,1024]{1,0:T(8,128)(2,1)S(1)}, bf16[64,1024]{1,0:T(8,128)(2,1)}, u32[]{:S(2)}) copy-start(bf16[64,1024]{1,0:T(8,128)(2,1)} %refs_2_.3) | copy-start | bytes 393220
  693.0 19.2 %copy-start.10 = (bf16[64,6144]{1,0:T(8,128)(2,1)S(1)}, bf16[64,6144]{1,0:T(8,128)(2,1)}, u32[]{:S(2)}) copy-start(bf16[64,6144]{1,0:T(8,128)(2,1)} %get-tuple-element.118.refs_4_) | copy-start | bytes 2359300
  693.0 27.8 %copy-start.27 = (bf16[64]{0:T(256)(128)(2,1)S(1)}, bf16[64]{0:T(256)(128)(2,1)}, u32[]{:S(2)}) copy-start(bf16[64]{0:T(256)(128)(2,1)} %param.22) | copy-start | bytes 388
  712.2 1.1 copy-start.11
  713.3 1.1 copy-start.12
  714.5 0.9 copy-start.16
  715.4 0.8 copy-start.17
Sparse Core Ops, SparseCore 0:
  86.5 27.1 all-gather.4
  180.3 115.3 all-gather.8
  297.2 61.7 all-gather.6
  361.1 58.8 reduce-scatter.3
  422.2 110.7 reduce-scatter.5
  612.3 27.5 reduce-scatter.7

commit v9 on v8

--- a/solution.py
+++ b/solution.py
@@ -1035,11 +1035,12 @@
     tokens, width = hidden.shape
     columns = w_attn.shape[1]
     q_columns = REPEAT * HEAD_SIZE
-    rows = tokens // RANKS
+    steps = RANKS // 2
+    rows = tokens // steps
     shape = jax.ShapeDtypeStruct
     return pl.pallas_call(
         prepare_kernel,
-        grid=(RANKS,),
+        grid=(steps,),
         out_shape=[
             shape((tokens, width), jnp.bfloat16),
             shape((tokens, q_columns), jnp.bfloat16),
@@ -1448,7 +1449,7 @@
         ]
         gains, attn_rows, table, hidden_all, all_seq, all_pos, ffn_columns = run(
             [
-                tiles_part(own_gains),
+                between(tiles_part(own_gains), 0.0, 0.6),
                 columns_part([query_weight, key_matrix, value_matrix, gate_weight]),
                 between(gather_part(own_table), 0.22, 0.7),
                 between(gather_part(hidden_in), 0.22, 0.8),

time: 738 us -> 735 us (level)
  no operation moved by 1% of the time
where the time goes in v9:
time: 735 us; the launch traced here: 728 us
  Pallas kernels  560 us (76%)
  matrix products  65.1 us (9%)
  waiting for transfers between devices  35.3 us (5%)
  local copies, waits for them, and re-layouts  33.8 us (5%)
  other arithmetic  16.2 us (2%)
  between operations  14.8 us (2%)
    pallas_call x9, Pallas kernels, run(): pl.pallas_call(functools.partial(run_kernel, parts), out_shape=[shape for...  469 us
    pallas_call x1, Pallas kernels, attend_back(): pl.pallas_call(attend_back_kernel, grid=(groups,), out_shape=[shape((toke...  39.8 us
    dot_general x3, matrix products, contract_first(): lax.dot_general(left, right, (((0,), (0,)), ((), ())), preferred_element_...  37.4 us
    all_gather x1, waiting for transfers between devices, shards(): w_down = lax.all_gather(down_rows, DATA, axis=0, tiled=True)  27.2 us
    unnamed x57, local copies, waits for them, and re-layouts  18.5 us
    pallas_call x1, Pallas kernels, attend(): pl.pallas_call(attend_kernel, grid=(groups,), out_shape=[shape((tokens, w...  17.3 us
    pallas_call x1, Pallas kernels, prepare_attention(): pl.pallas_call(prepare_kernel, grid=(steps,), out_shape=[shape((tokens, w...  15.8 us
  transfers between devices with their start and end apart: 7, of which 2 were waited for; matrix products, arithmetic and copies ran while one was open for 13% of the time, Pallas kernels for 66%

profile of v9, /device:TPU:0, one launch (start us, length us, event | category | flops | bytes accessed | tf_op | source)
XLA Modules:
  0.0 727.6 jit_solution(9948361216685304114)
XLA Ops:
  7.2 1.6 collective-permute-start
  8.8 0.8 dynamic-slice_convert_fusion
  10.1 1.4 fusion.17.refs_0_
  11.5 0.9 pad_maximum_fusion.1.refs_5_
  12.4 72.5 %shard_map.263 = (f32[4,8,8,128]{3,2,1,0:T(8,128)}, bf16[4,4,2,64,768]{4,3,2,1,0:T(8,128)(2,1)}, f32[2048,256]{1,0:T(8,128)}, bf16[2048,2048]{1,0:T(8,128)(2,1)}...) custom-call(f32[8,128]{1,0:T(8,128)} %fusion.17.refs_0_, bf16[64,2048]{1,0:T(8,128)(2,1)} %refs_0_.1, ...), custom_call_target="tpu_custom_call" | custom-call | bytes 245000000 | tf_op jit(solution)/shard_map/pallas_call | solution.py:146
  85.7 1.0 reshape.116
  88.9 15.8 %shard_map.264 = (bf16[2048,2048]{1,0:T(8,128)(2,1)}, bf16[2048,256]{1,0:T(8,128)(2,1)}, bf16[2048,256]{1,0:T(8,128)(2,1)}, f32[2048,384]{1,0:T(8,128)}, f32[2048,256]{1,0:T(8,128)}) custom-call(bf16[2048,2048]{1,0:T(8,128)(2,1)} %get-tuple-element.75.x_ref, f32[1,2048]{1,0:T(1,128)} %broadcast_in_dim_reshape.16.gain_ref, bf16[2048,768]{1,0:T(8,128)(2,1)} %bitcast.55, ...), custom_call_target="tpu_custom_call" | custom-call | bytes 42000000 | tf_op jit(solution)/shard_map/pallas_call | solution.py:1041
  104.7 74.8 %shard_map.265 = (bf16[4,2048,256]{2,1,0:T(8,128)(2,1)}, bf16[2048,2048]{1,0:T(8,128)(2,1)}, bf16[8,64,1536]{2,1,0:T(8,128)(2,1)}) custom-call(bf16[2048,256]{1,0:T(8,128)(2,1)} %get-tuple-element.81.refs_0_, bf16[256,2048]{1,0:T(8,128)(2,1)} %more_ref.1, bf16[8,64,1536]{2,1,0:T(8,128)(2,1)} %get-tuple-element.82.refs_2_), custom_call_target="tpu_custom_call" | custom-call | bytes 262500000 | tf_op jit(solution)/shard_map/pallas_call | solution.py:146
  180.8 1.2 copy-done.3
  182.0 17.3 %shard_map.266 = (bf16[2048,2048]{1,0:T(8,128)(2,1)}, f32[2048,256]{1,0:T(8,128)}, f32[2048,256]{1,0:T(8,128)}, bf16[2048,256]{1,0:T(8,128)(2,1)S(1)}) custom-call(bf16[2048,256]{1,0:T(8,128)(2,1)S(1)} %copy-done.4, bf16[4,2048,256]{2,1,0:T(8,128)(2,1)} %get-tuple-element.83.kv_ref, f32[2048,256]{1,0:T(8,128)} %get-tuple-element.84.gate_ref, ...), custom_call_target="tpu_custom_call" | custom-call | bytes 63000000 | tf_op jit(solution)/shard_map/pallas_call | solution.py:1119
  199.3 1.0 copy-done.5
  200.3 3.4 copy-done.2
  203.7 39.8 %shard_map.267 = f32[256,2048]{1,0:T(8,128)S(1)} custom-call(bf16[8,256,2048]{2,1,0:T(8,128)(2,1)S(1)} %bitcast.49), custom_call_target="tpu_custom_call" | custom-call | bytes 140000000 | tf_op jit(solution)/shard_map/pallas_call | solution.py:146
  243.9 1.3 copy-done.18
  245.3 1.2 multiply_convert_fusion.3.refs_0_
  246.5 40.6 %shard_map.268 = bf16[2048,2048]{1,0:T(8,128)(2,1)} custom-call(bf16[256,2048]{1,0:T(8,128)(2,1)} %multiply_convert_fusion.3.refs_0_), custom_call_target="tpu_custom_call" | custom-call | bytes 140000000 | tf_op jit(solution)/shard_map/pallas_call | solution.py:146
  287.1 7.9 %all-gather.9.cloned.1.call-done = bf16[32,64,1536]{2,1,0:T(8,128)(2,1)} async-done(((bf16[8,64,1536]{2,1,0:T(8,128)(2,1)}), bf16[32,64,1536]{2,1,0:T(8,128)(2,1)}) %all-gather.9.cloned.1.call-update) | async-done | bytes 6291472 | tf_op jit(solution)/shard_map/all_gather | solution.py:1392
  294.9 3.6 copy.66
  298.6 3.0 copy-done.23
  301.5 13.4 %fusion.21 = f32[2048,1536]{1,0:T(8,128)S(1)} fusion(bf16[2048,2048]{1,0:T(8,128)(2,1)S(1)} %copy-done.23, bf16[2048,1536]{1,0:T(8,128)(2,1)S(1)} %bitcast.53), kind=kOutput, calls=%fused_computation.47 | convolution fusion | flops 12884901888 | bytes 27262976 | tf_op jit(solution)/shard_map/dot_general | solution.py:944
  315.0 2.1 multiply_convert_fusion.2.refs_1_
  317.1 2.4 copy-done.20
  319.5 11.5 %convolution_convert_fusion.1 = bf16[768,2048]{1,0:T(8,128)(2,1)} fusion(bf16[2048,768]{1,0:T(8,128)(2,1)S(1)} %multiply_convert_fusion.2.refs_1_, bf16[2048,2048]{1,0:T(8,128)(2,1)} %get-tuple-element.91), kind=kOutput, calls=%fused_computation.6 | convolution fusion | flops 6444023808 | bytes 14680064 | tf_op jit(solution)/shard_map/dot_general | solution.py:954
  331.1 27.2 %all-gather.7.cloned.1.call-done.refs_2_ = bf16[768,2048]{1,0:T(8,128)(2,1)} async-done(((bf16[192,2048]{1,0:T(8,128)(2,1)}), bf16[768,2048]{1,0:T(8,128)(2,1)}) %all-gather.7.cloned.1.call-update) | async-done | bytes 3145744 | tf_op jit(solution)/shard_map/all_gather | solution.py:1475
  358.3 14.2 %multiply_convert_fusion.1 = (bf16[2048,768]{1,0:T(8,128)(2,1)S(1)}, bf16[2048,768]{1,0:T(8,128)(2,1)S(1)}) fusion(f32[2048,1536]{1,0:T(8,128)} %copy-done.20, bf16[2048,2048]{1,0:T(8,128)(2,1)} %get-tuple-element.91, bf16[768,2048]{1,0:T(8,128)(2,1)} %all-gather.7.cloned.1.call-done.refs_2_), kind=kOutput, calls=%fused_computation.3 | convolution fusion | flops 6462898176 | bytes 30408704 | tf_op jit(solution)/shard_map/dot_general | solution.py:948
  372.5 3.1 pad_maximum_fusion.refs_0_
  375.6 15.5 %convolution_convert_fusion = bf16[2048,1536]{1,0:T(8,128)(2,1)S(1)} fusion(bf16[2048,2048]{1,0:T(8,128)(2,1)} %shard_map.268, bf16[2048,768]{1,0:T(8,128)(2,1)S(1)} %get-tuple-element.139, bf16[2048,768]{1,0:T(8,128)(2,1)S(1)} %get-tuple-element.138), kind=kOutput, calls=%fused_computation | convolution fusion | flops 12900630528 | bytes 20971520 | tf_op jit(solution)/shard_map/dot_general | solution.py:954
  391.1 3.4 copy.72
  395.3 47.7 %shard_map.269.grads_ref = f32[256,2048]{1,0:T(8,128)S(1)} custom-call(bf16[2048,1536]{1,0:T(8,128)(2,1)} %pad_maximum_fusion.refs_0_, bf16[2048,1536]{1,0:T(8,128)(2,1)} %bitcast.54), custom_call_target="tpu_custom_call" | custom-call | bytes 157500000 | tf_op jit(solution)/shard_map/pallas_call | solution.py:146
  443.0 1.4 copy-done.1
  444.3 4.9 shard_map.270
  449.3 0.9 reduce_sum.37
  450.2 2.7 convert_element_type.55.refs_0_
  452.9 39.5 %shard_map.271.branch_ref = bf16[2048,2048]{1,0:T(8,128)(2,1)} custom-call(bf16[256,2048]{1,0:T(8,128)(2,1)} %convert_element_type.55.refs_0_), custom_call_target="tpu_custom_call" | custom-call | bytes 140000000 | tf_op jit(solution)/shard_map/pallas_call | solution.py:146
  492.5 39.8 %shard_map.272 = (bf16[2048,768]{1,0:T(8,128)(2,1)}, bf16[4,2048,256]{2,1,0:T(8,128)(2,1)}, f32[4,8,128]{2,1,0:T(8,128)}, bf16[256,2048]{1,0:T(8,128)(2,1)}) custom-call(bf16[2048,2048]{1,0:T(8,128)(2,1)} %shard_map.271.branch_ref, bf16[256,2048]{1,0:T(8,128)(2,1)} %all-gather.5.cloned.1.call-done.wo_ref, bf16[2048,256]{1,0:T(8,128)(2,1)} %get-tuple-element.80.q_ref, ...), custom_call_target="tpu_custom_call" | custom-call | bytes 122500000 | tf_op jit(solution)/shard_map/pallas_call | solution.py:1202
  532.3 0.7 slice_reduce_fusion.2
  533.2 78.2 %shard_map.273 = (f32[2048,256]{1,0:T(8,128)}, bf16[256,2048]{1,0:T(8,128)(2,1)}, bf16[8,64,1536]{2,1,0:T(8,128)(2,1)}, bf16[4,64,2048]{2,1,0:T(8,128)(2,1)}) custom-call(bf16[4,2048,256]{2,1,0:T(8,128)(2,1)} %get-tuple-element.103.refs_0_, bf16[2048,768]{1,0:T(8,128)(2,1)} %copy-done.21, bf16[768,2048]{1,0:T(8,128)(2,1)} %all-gather.7.cloned.1.call-done.refs_2_, ...), custom_call_target="tpu_custom_call" | custom-call | bytes 262500000 | tf_op jit(solution)/shard_map/pallas_call | solution.py:146
  611.5 4.8 shard_map.274
  616.3 10.4 %convolution_convert_fusion.2 = bf16[2048,768]{1,0:T(8,128)(2,1)S(1)} fusion(bf16[2048,2048]{1,0:T(8,128)(2,1)} %get-tuple-element.109, bf16[2048,768]{1,0:T(8,128)(2,1)} %get-tuple-element.112.refs_2_), kind=kOutput, calls=%fused_computation.7 | convolution fusion | flops 6444023808 | bytes 14680064 | tf_op jit(solution)/shard_map/dot_general | solution.py:954
  626.7 2.0 copy.74
  630.3 61.9 %shard_map.275 = (f32[64,128]{1,0:T(8,128)}, bf16[512,768]{1,0:T(8,128)(2,1)}, f32[256,2048]{1,0:T(8,128)}, bf16[64,6144]{1,0:T(8,128)(2,1)}, bf16[64,6144]{1,0:T(8,128)(2,1)}) custom-call(bf16[4,64,128]{2,1,0:T(8,128)(2,1)} %bitcast.64, bf16[4,512,768]{2,1,0:T(8,128)(2,1)} %bitcast.57, bf16[2048,768]{1,0:T(8,128)(2,1)} %get-tuple-element.112.refs_2_, ...), custom_call_target="tpu_custom_call" | custom-call | bytes 210000000 | tf_op jit(solution)/shard_map/pallas_call | solution.py:146
  692.3 4.9 shard_map.278
  697.2 14.2 %shard_map.276 = (bf16[8,64,768]{2,1,0:T(8,128)(2,1)}, f32[8,8,128]{2,1,0:T(8,128)}) custom-call(bf16[8,64,768]{2,1,0:T(8,128)(2,1)} %bitcast.62, f32[8,8,128]{2,1,0:T(8,128)} %bitcast.70), custom_call_target="tpu_custom_call" | custom-call | bytes 49000000 | tf_op jit(solution)/shard_map/pallas_call | solution.py:146
  711.5 1.1 copy-done.11
  712.6 1.1 copy-done.12
  713.8 0.9 copy-done.16
  714.7 0.8 copy-done.17
  715.5 3.4 shard_map.277
  (89 shorter events, 9.5 us)
Async XLA Ops:
  7.2 173.6 %all-gather.5.cloned.1.call-start = ((), (), s32[]{:S(2)}) async-start(), calls=%async_computation.3 | async-start | bytes 1310720 | tf_op jit(solution)/shard_map/all_gather | solution.py:1474
  7.2 77.7 %collective-permute-start = (bf16[64,2048]{1,0:T(8,128)(2,1)}, bf16[64,2048]{1,0:T(8,128)(2,1)S(1)}, u32[]{:S(2)}, u32[]{:S(2)}) collective-permute-start(bf16[64,2048]{1,0:T(8,128)(2,1)} %param.21), channel_id=1, source_target_pairs={{0,0},{1,2},{2,4},{3,6},{4,1},{5,3},{6,5},{7,7},{8,8},{9,10},{10,1... | collective-permute-start | bytes 786440 | tf_op jit(solution)/shard_map/ppermute | solution.py:1463
  85.0 0.7 copy-start.24
  85.7 209.3 %all-gather.9.cloned.1.call-start = ((), (), s32[]{:S(2)}) async-start(), calls=%async_computation.8 | async-start | bytes 7864320 | tf_op jit(solution)/shard_map/all_gather | solution.py:1392
  88.9 90.7 %copy-start.25 = (s32[4,16,128]{2,1,0:T(8,128)S(1)}, s32[4,16,128]{2,1,0:T(8,128)}, u32[]{:S(2)}) copy-start(s32[4,16,128]{2,1,0:T(8,128)} %get-tuple-element.85) | copy-start | bytes 98308
  88.9 90.7 %copy-start.26 = (s32[4,16,128]{2,1,0:T(8,128)S(1)}, s32[4,16,128]{2,1,0:T(8,128)}, u32[]{:S(2)}) copy-start(s32[4,16,128]{2,1,0:T(8,128)} %get-tuple-element.86) | copy-start | bytes 98308
  104.7 76.1 %copy-start.4 = (bf16[2048,256]{1,0:T(8,128)(2,1)S(1)}, bf16[2048,256]{1,0:T(8,128)(2,1)}, u32[]{:S(2)}) copy-start(bf16[2048,256]{1,0:T(8,128)(2,1)} %get-tuple-element.80.q_ref) | copy-start | bytes 3145732
  179.5 178.8 %all-gather.7.cloned.1.call-start = ((), (), s32[]{:S(2)}) async-start(), calls=%async_computation.4 | async-start | bytes 3932160 | tf_op jit(solution)/shard_map/all_gather | solution.py:1475
  180.1 63.4 %copy-start = (s32[4,512,2]{2,1,0:T(8,128)}, s32[4,512,2]{2,1,0:T(8,128)S(1)}, u32[]{:S(2)}) copy-start(s32[4,512,2]{2,1,0:T(8,128)S(1)} %copy.65.own_ref) | copy-start | bytes 49156
  180.1 63.4 %copy-start.13 = (s32[4,2,2048]{2,1,0:T(2,128)}, s32[4,2,2048]{2,1,0:T(2,128)S(1)}, u32[]{:S(2)}) copy-start(s32[4,2,2048]{2,1,0:T(2,128)S(1)} %pad_add_fusion.keys_ref) | copy-start | bytes 196612
  180.2 312.3 %reduce-scatter.4.cloned.1.call-start = ((), (), s32[]{:S(2)}) async-start(), calls=%async_computation.5 | async-start | bytes 3932160 | tf_op jit(solution)/shard_map/reduce_scatter | solution.py:1504
  180.8 1.2 copy-start.3
  182.0 61.6 %copy-start.22 = (bf16[256,2048]{1,0:T(8,128)(2,1)S(1)}, bf16[256,2048]{1,0:T(8,128)(2,1)}, u32[]{:S(2)}) copy-start(bf16[256,2048]{1,0:T(8,128)(2,1)} %x_ref.1) | copy-start | bytes 3145732
  199.3 1.0 copy-start.5
  200.3 3.4 copy-start.2
  243.9 1.4 copy-start.18
  294.9 6.6 copy-start.23
  298.6 16.4 %copy-start.19 = (bf16[4,4,2,64,1536]{4,3,2,0,1:T(8,128)(2,1)}, bf16[4,4,2,64,1536]{4,3,2,0,1:T(8,128)(2,1)S(1)}, u32[]{:S(2)}) copy-start(bf16[4,4,2,64,1536]{4,3,2,0,1:T(8,128)(2,1)S(1)} %copy.66) | copy-start | bytes 18874372
  315.0 4.5 copy-start.20
  319.5 11.5 %copy-start.21 = (bf16[2048,768]{1,0:T(8,128)(2,1)}, bf16[2048,768]{1,0:T(8,128)(2,1)S(1)}, u32[]{:S(2)}) copy-start(bf16[2048,768]{1,0:T(8,128)(2,1)S(1)} %multiply_convert_fusion.2.refs_1_) | copy-start | bytes 9437188
  331.0 202.1 %reduce-scatter.6.cloned.1.call-start = ((), (), s32[]{:S(2)}) async-start(), calls=%async_computation.6 | async-start | bytes 7864320 | tf_op jit(solution)/shard_map/reduce_scatter | solution.py:1400
  394.5 316.9 %reduce-scatter.8.cloned.1.call-start = ((), (), s32[]{:S(2)}) async-start(), calls=%async_computation.7 | async-start | bytes 1310720 | tf_op jit(solution)/shard_map/reduce_scatter | solution.py:1532
  443.0 1.4 copy-start.1
  630.3 81.1 %copy-start.6 = (bf16[256,2048]{1,0:T(8,128)(2,1)S(1)}, bf16[256,2048]{1,0:T(8,128)(2,1)}, u32[]{:S(2)}) copy-start(bf16[256,2048]{1,0:T(8,128)(2,1)} %get-tuple-element.122.refs_8_) | copy-start | bytes 3145732
  630.3 81.1 %copy-start.7 = (bf16[64,2048]{1,0:T(8,128)(2,1)S(1)}, bf16[64,2048]{1,0:T(8,128)(2,1)}, u32[]{:S(2)}) copy-start(bf16[64,2048]{1,0:T(8,128)(2,1)} %refs_0_.1) | copy-start | bytes 786436
  630.3 81.1 %copy-start.8 = (bf16[64,2048]{1,0:T(8,128)(2,1)S(1)}, bf16[64,2048]{1,0:T(8,128)(2,1)}, u32[]{:S(2)}) copy-start(bf16[64,2048]{1,0:T(8,128)(2,1)} %refs_3_.3) | copy-start | bytes 786436
  630.3 81.2 %copy-start.9 = (bf16[192,2048]{1,0:T(8,128)(2,1)S(1)}, bf16[192,2048]{1,0:T(8,128)(2,1)}, u32[]{:S(2)}) copy-start(bf16[192,2048]{1,0:T(8,128)(2,1)} %reduce-scatter.4.cloned.1.call-done.refs_6_) | copy-start | bytes 2359300
  630.3 81.2 %copy-start.14 = (bf16[64,1024]{1,0:T(8,128)(2,1)S(1)}, bf16[64,1024]{1,0:T(8,128)(2,1)}, u32[]{:S(2)}) copy-start(bf16[64,1024]{1,0:T(8,128)(2,1)} %refs_1_.5) | copy-start | bytes 393220
  630.3 81.2 %copy-start.15 = (bf16[64,1024]{1,0:T(8,128)(2,1)S(1)}, bf16[64,1024]{1,0:T(8,128)(2,1)}, u32[]{:S(2)}) copy-start(bf16[64,1024]{1,0:T(8,128)(2,1)} %refs_2_.3) | copy-start | bytes 393220
  692.3 19.2 %copy-start.10 = (bf16[64,6144]{1,0:T(8,128)(2,1)S(1)}, bf16[64,6144]{1,0:T(8,128)(2,1)}, u32[]{:S(2)}) copy-start(bf16[64,6144]{1,0:T(8,128)(2,1)} %get-tuple-element.118.refs_4_) | copy-start | bytes 2359300
  692.3 27.8 %copy-start.27 = (bf16[64]{0:T(256)(128)(2,1)S(1)}, bf16[64]{0:T(256)(128)(2,1)}, u32[]{:S(2)}) copy-start(bf16[64]{0:T(256)(128)(2,1)} %param.22) | copy-start | bytes 388
  711.5 1.1 copy-start.11
  712.6 1.1 copy-start.12
  713.8 0.9 copy-start.16
  714.7 0.8 copy-start.17
Sparse Core Ops, SparseCore 0:
  85.8 27.4 all-gather.4
  179.6 115.3 all-gather.8
  296.5 61.7 all-gather.6
  360.4 58.8 reduce-scatter.3
  421.5 110.7 reduce-scatter.5
  611.6 27.5 reduce-scatter.7
